TPU v7x, 128 devices: a whole 4x4x4 slice. The times are simulated.
128 devices in a mesh: dom: 32 (over x, z, core), feat: 4 (over y).
Axes of the slice: x: 4, y: 4, z: 4, core: 2. Of those that a mesh axis runs over, the one named last changes fastest.
Arguments:
- features: bfloat16 [32768, 512], P('dom'), may hold values from -96 to 96
- w_query: bfloat16 [512, 512], P(None, 'feat'), may hold values from -0.25 to 0.25
- w_key: bfloat16 [512, 512], P(None, 'feat'), may hold values from -0.25 to 0.25
- w_value: bfloat16 [512, 512], P(None, 'feat'), may hold values from -0.25 to 0.25
- cotangent: bfloat16 [32768, 512], P('dom', 'feat'), may hold values from -6 to 6
- send_rows: int32 [32, 32, 128], P('dom'), may hold values from 0 to 1023, as said below
- halo_count: int32 [32, 32], P(None, 'dom'), may hold values from 0 to 128, as said below
- block_mask: int32 [256, 40], P('dom'), may hold values 0 or 1
- exp_rows: int32 [4, 32768], P(None, 'dom'), may hold values from 0 to 1023, as said below
- global_ids: int32 [128], replicated, may hold values from 0 to 32767, as said below
Outputs:
- attended: bfloat16 [32768, 512], P('dom', 'feat')
- input_grad: bfloat16 [32768, 512], P('dom', 'feat')
Inputs may be any that keep to these rules, and one draw needn't show every extreme that they name: `send_rows`: local row numbers on the sending slab, distinct within each list. `halo_count`: zero from a slab to itself; some receiver gets 128 live slots from every other slab. `exp_rows`: each slab's part of each matching is a permutation of 0 to 1023. `global_ids`: distinct node ids.
All inputs are finite; a program needn't handle non-finite values. No bound on the sum of `block_mask` on one device may be relied on, other than what follows from the above.
Results may differ from a plain program's by a relative error of at most 0.013.
The roundings to bfloat16 on the way count: a program that leaves them out, or rounds other values in their place, can miss the bound.
Values may be sent and summed in bfloat16 or wider, within the bound.
No kernel may reach another device: no remote copies, remote signals or barrier semaphores. Data moves between devices by JAX's collectives and lax.ppermute only.
A program may use at most 128 MiB of HBM per device.

v0:
```python
import math

import jax
import jax.numpy as jnp
from jax import lax
from jax.sharding import PartitionSpec as P

HEAD = 64
BLOCK = 128
EXPANDERS = 4


def swapped_2(value, axis, bit):
    return lax.ppermute(value, axis, [(i, i ^ 1 << bit) for i in range(lax.axis_size(axis))])


def block_allowed(mask_rows, unit, key_live):
    tall = jnp.repeat(mask_rows > 0, unit, axis=0)
    return jnp.repeat(tall, unit, axis=1) & key_live[None, :]


def on_device(
    features,
    w_query,
    w_key,
    w_value,
    cotangent,
    send_rows,
    halo_count,
    block_mask,
    exp_rows,
    global_ids,
):
    node_dev = features.shape[0]
    col_count = w_query.shape[1]
    heads_here = col_count // HEAD
    dom_count = lax.axis_size("dom")
    levels = dom_count.bit_length() - 1
    my_index = lax.axis_index("dom")
    score_scale = 1.0 / math.sqrt(HEAD)
    query = jnp.dot(features, w_query, preferred_element_type=jnp.float32).astype(jnp.bfloat16)
    key_rows = jnp.dot(features, w_key, preferred_element_type=jnp.float32).astype(jnp.bfloat16)
    value_rows = jnp.dot(features, w_value, preferred_element_type=jnp.float32).astype(jnp.bfloat16)
    paired = jnp.concatenate([key_rows, value_rows], axis=1)
    outgoing = paired[send_rows[0]]
    incoming = lax.all_to_all(outgoing, "dom", split_axis=0, concat_axis=0, tiled=True)
    halo_flat = incoming.reshape(dom_count * BLOCK, 2 * col_count)
    slot_live = (jnp.arange(BLOCK, dtype=jnp.int32)[None, :] < halo_count).reshape(-1)
    key_live = jnp.concatenate([jnp.ones((node_dev,), dtype=bool), slot_live])
    cand_key = jnp.concatenate([key_rows, halo_flat[:, :col_count]], axis=0).reshape(
        -1, heads_here, HEAD
    )
    cand_value = jnp.concatenate([value_rows, halo_flat[:, col_count:]], axis=0).reshape(
        -1, heads_here, HEAD
    )
    key_total = cand_key.shape[0]
    partner_list = []
    for matching in range(EXPANDERS):
        swapped = swapped_2(paired, "dom", matching % levels)
        partner_list.append(swapped[exp_rows[matching]])
    partner_pairs = jnp.stack(partner_list)
    is_owner = global_ids // node_dev == my_index
    local_ids = global_ids % node_dev
    picked = jnp.where(is_owner[:, None], paired[local_ids].astype(jnp.float32), 0.0)
    global_pairs = lax.psum(picked.astype(jnp.bfloat16), "dom")
    global_key = global_pairs[:, :col_count].reshape(-1, heads_here, HEAD)
    global_value = global_pairs[:, col_count:].reshape(-1, heads_here, HEAD)
    rows_blk = min(256, node_dev)
    block_count = node_dev // rows_blk
    mask_blk = rows_blk // BLOCK

    def one_block(totals, block_index):
        local_gk, local_gv, global_gk, global_gv = totals
        start = block_index * rows_blk
        query_blk = lax.dynamic_slice_in_dim(query, start, rows_blk, 0).reshape(
            rows_blk, heads_here, HEAD
        )
        grad_blk = lax.dynamic_slice_in_dim(cotangent, start, rows_blk, 0).reshape(
            rows_blk, heads_here, HEAD
        )
        mask_rows = lax.dynamic_slice_in_dim(block_mask, block_index * mask_blk, mask_blk, 0)
        allowed = block_allowed(mask_rows, BLOCK, key_live)
        partner_blk = lax.dynamic_slice_in_dim(partner_pairs, start, rows_blk, 1)
        partner_key = partner_blk[..., :col_count].reshape(EXPANDERS, rows_blk, heads_here, HEAD)
        partner_value = partner_blk[..., col_count:].reshape(EXPANDERS, rows_blk, heads_here, HEAD)
        local_score = (
            jnp.einsum("rhe,khe->rhk", query_blk, cand_key, preferred_element_type=jnp.float32)
            * score_scale
        )
        local_score = jnp.where(allowed[:, None, :], local_score, -jnp.inf)
        partner_score = (
            jnp.einsum("rhe,mrhe->rhm", query_blk, partner_key, preferred_element_type=jnp.float32)
            * score_scale
        )
        global_score = (
            jnp.einsum("rhe,ghe->rhg", query_blk, global_key, preferred_element_type=jnp.float32)
            * score_scale
        )
        top_score = jnp.maximum(
            jnp.maximum(local_score.max(-1), partner_score.max(-1)), global_score.max(-1)
        )[..., None]
        local_exp = jnp.exp(local_score - top_score)
        partner_exp = jnp.exp(partner_score - top_score)
        global_exp = jnp.exp(global_score - top_score)
        denominator = (
            local_exp.sum(-1, keepdims=True)
            + partner_exp.sum(-1, keepdims=True)
            + global_exp.sum(-1, keepdims=True)
        )
        local_prob = local_exp / denominator
        partner_prob = partner_exp / denominator
        global_prob = global_exp / denominator
        local_weight = local_prob.astype(jnp.bfloat16)
        partner_weight = partner_prob.astype(jnp.bfloat16)
        global_weight = global_prob.astype(jnp.bfloat16)
        attended_blk = (
            jnp.einsum("rhk,khe->rhe", local_weight, cand_value, preferred_element_type=jnp.float32)
            + jnp.einsum(
                "rhm,mrhe->rhe", partner_weight, partner_value, preferred_element_type=jnp.float32
            )
            + jnp.einsum(
                "rhg,ghe->rhe", global_weight, global_value, preferred_element_type=jnp.float32
            )
        )
        attended_blk = attended_blk.astype(jnp.bfloat16).reshape(rows_blk, col_count)
        local_dp = jnp.einsum(
            "rhe,khe->rhk", grad_blk, cand_value, preferred_element_type=jnp.float32
        )
        partner_dp = jnp.einsum(
            "rhe,mrhe->rhm", grad_blk, partner_value, preferred_element_type=jnp.float32
        )
        global_dp = jnp.einsum(
            "rhe,ghe->rhg", grad_blk, global_value, preferred_element_type=jnp.float32
        )
        delta = (
            (local_prob * local_dp).sum(-1, keepdims=True)
            + (partner_prob * partner_dp).sum(-1, keepdims=True)
            + (global_prob * global_dp).sum(-1, keepdims=True)
        )
        local_ds = (local_prob * (local_dp - delta) * score_scale).astype(jnp.bfloat16)
        partner_ds = (partner_prob * (partner_dp - delta) * score_scale).astype(jnp.bfloat16)
        global_ds = (global_prob * (global_dp - delta) * score_scale).astype(jnp.bfloat16)
        grad_query_blk = (
            jnp.einsum("rhk,khe->rhe", local_ds, cand_key, preferred_element_type=jnp.float32)
            + jnp.einsum(
                "rhm,mrhe->rhe", partner_ds, partner_key, preferred_element_type=jnp.float32
            )
            + jnp.einsum("rhg,ghe->rhe", global_ds, global_key, preferred_element_type=jnp.float32)
        )
        local_gk = local_gk + jnp.einsum(
            "rhk,rhe->khe", local_ds, query_blk, preferred_element_type=jnp.float32
        )
        local_gv = local_gv + jnp.einsum(
            "rhk,rhe->khe", local_weight, grad_blk, preferred_element_type=jnp.float32
        )
        global_gk = global_gk + jnp.einsum(
            "rhg,rhe->ghe", global_ds, query_blk, preferred_element_type=jnp.float32
        )
        global_gv = global_gv + jnp.einsum(
            "rhg,rhe->ghe", global_weight, grad_blk, preferred_element_type=jnp.float32
        )
        return (
            (local_gk, local_gv, global_gk, global_gv),
            (attended_blk, grad_query_blk.reshape(rows_blk, col_count), partner_ds, partner_weight),
        )

    zero_keys = jnp.zeros((key_total, heads_here, HEAD), jnp.float32)
    zero_globals = jnp.zeros((global_ids.shape[0], heads_here, HEAD), jnp.float32)
    totals, outputs = lax.scan(
        one_block, (zero_keys, zero_keys, zero_globals, zero_globals), jnp.arange(block_count)
    )
    local_gk, local_gv, global_gk, global_gv = totals
    attended_rows, grad_query, partner_ds, partner_weight = outputs
    attended = attended_rows.reshape(node_dev, col_count)
    grad_query = grad_query.reshape(node_dev, col_count)
    partner_ds = partner_ds.reshape(node_dev, heads_here, EXPANDERS)
    partner_weight = partner_weight.reshape(node_dev, heads_here, EXPANDERS)
    key_grads = local_gk.reshape(key_total, col_count)
    value_grads = local_gv.reshape(key_total, col_count)
    pair_grad = jnp.concatenate([key_grads[:node_dev], value_grads[:node_dev]], axis=1)
    halo_back = jnp.concatenate([key_grads[node_dev:], value_grads[node_dev:]], axis=1).reshape(
        dom_count, BLOCK, 2 * col_count
    )
    returned = lax.all_to_all(
        halo_back.astype(jnp.bfloat16), "dom", split_axis=0, concat_axis=0, tiled=True
    )
    pair_grad = pair_grad.at[send_rows[0].reshape(-1)].add(
        returned.reshape(-1, 2 * col_count).astype(jnp.float32)
    )
    for matching in range(EXPANDERS):
        bit_level = matching % levels
        row_order = exp_rows[matching]
        key_term = partner_ds[:, :, matching, None].astype(jnp.float32) * query.reshape(
            node_dev, heads_here, HEAD
        ).astype(jnp.float32)
        value_term = partner_weight[:, :, matching, None].astype(jnp.float32) * cotangent.reshape(
            node_dev, heads_here, HEAD
        ).astype(jnp.float32)
        joined = jnp.concatenate(
            [key_term.reshape(node_dev, col_count), value_term.reshape(node_dev, col_count)], axis=1
        )
        placed = jnp.zeros_like(joined).at[row_order].set(joined)
        pair_grad = pair_grad + swapped_2(placed.astype(jnp.bfloat16), "dom", bit_level).astype(
            placed.dtype
        )
    global_grad = jnp.concatenate(
        [global_gk.reshape(-1, col_count), global_gv.reshape(-1, col_count)], axis=1
    )
    summed = lax.psum(global_grad.astype(jnp.bfloat16), "dom").astype(jnp.float32)
    pair_grad = pair_grad.at[local_ids].add(jnp.where(is_owner[:, None], summed, 0.0))
    feature_terms = (
        jnp.dot(grad_query.astype(jnp.bfloat16), w_query.T, preferred_element_type=jnp.float32)
        + jnp.dot(
            pair_grad[:, :col_count].astype(jnp.bfloat16),
            w_key.T,
            preferred_element_type=jnp.float32,
        )
        + jnp.dot(
            pair_grad[:, col_count:].astype(jnp.bfloat16),
            w_value.T,
            preferred_element_type=jnp.float32,
        )
    )
    input_grad = lax.psum_scatter(feature_terms, "feat", scatter_dimension=1, tiled=True).astype(
        jnp.bfloat16
    )
    return (attended, input_grad)


def solution(mesh):
    return jax.shard_map(
        on_device,
        mesh=mesh,
        in_specs=(
            P("dom", None),
            P(None, "feat"),
            P(None, "feat"),
            P(None, "feat"),
            P("dom", "feat"),
            P("dom", None, None),
            P(None, "dom"),
            P("dom", None),
            P(None, "dom"),
            P(),
        ),
        out_specs=(P("dom", "feat"), P("dom", "feat")),
        check_vma=False,
    )
```

profile of v0, /device:TPU:0, one launch (start us, length us, event | category | flops | bytes accessed | tf_op | source)
XLA Modules:
  0.0 585.5 jit_solution(14606089419128119162)
XLA Ops:
  12.8 3.9 collective-permute-start.2
  17.7 17.0 %gather_fusion = bf16[4096,256]{1,0:T(8,128)(2,1)} fusion(bf16[1024,256]{1,0:T(8,128)(2,1)S(1)} %pad_maximum_fusion.8, s32[4096]{0:T(1024)S(1)} %fusion.59), kind=kCustom, calls=%fused_computation | custom fusion | bytes 4210688 | tf_op jit(solution)/shard_map/gather | solution.py:45
  34.7 5.4 all-to-all-start
  48.9 1.8 copy.112
  51.5 1.8 copy.115
  53.3 93.9 %all-reduce.4.cloned.1.call-done = bf16[128,256]{1,0:T(8,128)(2,1)} async-done(((bf16[128,256]{1,0:T(8,128)(2,1)}), bf16[128,256]{1,0:T(8,128)(2,1)}) %all-reduce.4.cloned.1.call-update) | async-done | bytes 65552 | tf_op jit(solution)/shard_map/psum | solution.py:65
  149.5 5.1 gather_fusion.4
  154.6 3.9 gather_fusion.3
  158.5 4.9 gather_fusion.2
  163.5 4.9 gather_fusion.1
  169.9 3.0 fusion.64
  174.3 2.3 copy.178
  176.6 2.2 pad_maximum_fusion.3
  178.8 2.1 pad_maximum_fusion.2
  181.0 211.5 %while.25 = (s32[]{:T(128)}, f32[5120,2,64]{0,2,1:T(8,128)}, f32[5120,2,64]{0,2,1:T(8,128)}, f32[128,2,64]{0,2,1:T(8,128)}, f32[128,2,64]{0,2,1:T(8,128)}, /*ind...) while((s32[]{:T(128)}, f32[5120,2,64]{0,2,1:T(8,128)}, ...), condition=%wide.region_11.12_spmd.clone, body=%wide.region_1.11_spmd.clone.sunk | while | flops 2151969280 | bytes 260182544 | solution.py:169
  186.2 1.9 broadcast_in_dim.166
  189.0 3.6 bitcast_reduce_fusion.2
  192.6 3.0 fusion.164
  196.6 4.2 fusion.173
  202.2 8.3 %fusion.169 = f32[5120,2,64]{0,2,1:T(8,128)} fusion(bf16[256,2,64]{0,2,1:T(8,128)(2,1)S(1)} %bitcast.353, f32[5120,2,64]{0,2,1:T(8,128)} %get-tuple-element.548, pred[]{:T(512)S(6)} %compare.7, f32[2,256,5120]{2,1,0:T(8,128)} %copy-done.2, f32[256,2]{0,1:T(2,128)S(1)} %add_add_fusion.5, f32[256,2]{0,1:T(2,128)S(1)} %maximum_maximum_fusion.2, ...), kind=kOutput, calls=%fused_computation.25.clone.1 | convolution fusion | flops 349962240 | bytes 17108992 | tf_op jit(solution)/shard_map/while/body/eval_jaxpr/rhk,rhe->khe/dot_general | solution.py:153
  210.6 7.3 %fusion.166 = (f32[256,2]{0,1:T(2,128)S(1)}, f32[2,256,5120]{2,1,0:T(8,128)}) fusion(f32[256,2]{0,1:T(2,128)S(1)} %add_add_fusion.5, f32[256,2]{0,1:T(2,128)S(1)} %maximum_maximum_fusion.2, f32[2,256,5120]{2,1,0:T(8,128)S(1)} %bitcast.324, pred[256,5120]{1,0:T(8,128)(4,1)S(1)} %bitcast_and_fusion.2, bf16[256,2,64]{0,2,1:T(8,128)(2,1)S(1)} %bitcast.354, ...), kind=kOutput, calls=%fused_computation.14.clone.1 | convolution fusion | flops 351272448 | bytes 23664640 | tf_op jit(solution)/shard_map/while/body/eval_jaxpr/rhe,khe->rhk/dot_general | solution.py:126
  218.0 7.1 %fusion.167 = bf16[256,2,5120]{2,0,1:T(8,128)(2,1)S(1)} fusion(f32[2,256,5120]{2,1,0:T(8,128)} %get-tuple-element.506, f32[256,2]{0,1:T(2,128)S(1)} %add_add_fusion.6, f32[256,2]{0,1:T(2,128)S(1)} %add_add_fusion.5, f32[256,2]{0,1:T(2,128)S(1)} %maximum_maximum_fusion.2, f32[2,256,5120]{2,1,0:T(8,128)S(1)} %bitcast.324, ...), kind=kLoop, calls=%fused_computation.17.clone.1 | loop fusion | flops 20971520 | bytes 27531264 | tf_op jit(solution)/shard_map/while/body/eval_jaxpr/convert_element_type | solution.py:140
  226.9 1.7 fusion.172
  237.7 1.9 broadcast_in_dim.166
  240.4 3.6 bitcast_reduce_fusion.2
  244.1 3.0 fusion.164
  248.1 4.2 fusion.173
  254.6 9.1 %fusion.169 = f32[5120,2,64]{0,2,1:T(8,128)} fusion(bf16[256,2,64]{0,2,1:T(8,128)(2,1)S(1)} %bitcast.353, f32[5120,2,64]{0,2,1:T(8,128)} %get-tuple-element.548, pred[]{:T(512)S(6)} %compare.7, f32[2,256,5120]{2,1,0:T(8,128)} %copy-done.2, f32[256,2]{0,1:T(2,128)S(1)} %add_add_fusion.5, f32[256,2]{0,1:T(2,128)S(1)} %maximum_maximum_fusion.2, ...), kind=kOutput, calls=%fused_computation.25.clone.1 | convolution fusion | flops 349962240 | bytes 17108992 | tf_op jit(solution)/shard_map/while/body/eval_jaxpr/rhk,rhe->khe/dot_general | solution.py:153
  263.7 7.3 %fusion.166 = (f32[256,2]{0,1:T(2,128)S(1)}, f32[2,256,5120]{2,1,0:T(8,128)}) fusion(f32[256,2]{0,1:T(2,128)S(1)} %add_add_fusion.5, f32[256,2]{0,1:T(2,128)S(1)} %maximum_maximum_fusion.2, f32[2,256,5120]{2,1,0:T(8,128)S(1)} %bitcast.324, pred[256,5120]{1,0:T(8,128)(4,1)S(1)} %bitcast_and_fusion.2, bf16[256,2,64]{0,2,1:T(8,128)(2,1)S(1)} %bitcast.354, ...), kind=kOutput, calls=%fused_computation.14.clone.1 | convolution fusion | flops 351272448 | bytes 23664640 | tf_op jit(solution)/shard_map/while/body/eval_jaxpr/rhe,khe->rhk/dot_general | solution.py:126
  271.2 7.1 %fusion.167 = bf16[256,2,5120]{2,0,1:T(8,128)(2,1)S(1)} fusion(f32[2,256,5120]{2,1,0:T(8,128)} %get-tuple-element.506, f32[256,2]{0,1:T(2,128)S(1)} %add_add_fusion.6, f32[256,2]{0,1:T(2,128)S(1)} %add_add_fusion.5, f32[256,2]{0,1:T(2,128)S(1)} %maximum_maximum_fusion.2, f32[2,256,5120]{2,1,0:T(8,128)S(1)} %bitcast.324, ...), kind=kLoop, calls=%fused_computation.17.clone.1 | loop fusion | flops 20971520 | bytes 27531264 | tf_op jit(solution)/shard_map/while/body/eval_jaxpr/convert_element_type | solution.py:140
  280.1 1.7 fusion.172
  290.8 1.9 broadcast_in_dim.166
  293.6 3.6 bitcast_reduce_fusion.2
  297.2 3.0 fusion.164
  301.4 4.2 fusion.173
  307.8 9.1 %fusion.169 = f32[5120,2,64]{0,2,1:T(8,128)} fusion(bf16[256,2,64]{0,2,1:T(8,128)(2,1)S(1)} %bitcast.353, f32[5120,2,64]{0,2,1:T(8,128)} %get-tuple-element.548, pred[]{:T(512)S(6)} %compare.7, f32[2,256,5120]{2,1,0:T(8,128)} %copy-done.2, f32[256,2]{0,1:T(2,128)S(1)} %add_add_fusion.5, f32[256,2]{0,1:T(2,128)S(1)} %maximum_maximum_fusion.2, ...), kind=kOutput, calls=%fused_computation.25.clone.1 | convolution fusion | flops 349962240 | bytes 17108992 | tf_op jit(solution)/shard_map/while/body/eval_jaxpr/rhk,rhe->khe/dot_general | solution.py:153
  317.0 7.3 %fusion.166 = (f32[256,2]{0,1:T(2,128)S(1)}, f32[2,256,5120]{2,1,0:T(8,128)}) fusion(f32[256,2]{0,1:T(2,128)S(1)} %add_add_fusion.5, f32[256,2]{0,1:T(2,128)S(1)} %maximum_maximum_fusion.2, f32[2,256,5120]{2,1,0:T(8,128)S(1)} %bitcast.324, pred[256,5120]{1,0:T(8,128)(4,1)S(1)} %bitcast_and_fusion.2, bf16[256,2,64]{0,2,1:T(8,128)(2,1)S(1)} %bitcast.354, ...), kind=kOutput, calls=%fused_computation.14.clone.1 | convolution fusion | flops 351272448 | bytes 23664640 | tf_op jit(solution)/shard_map/while/body/eval_jaxpr/rhe,khe->rhk/dot_general | solution.py:126
  324.4 7.1 %fusion.167 = bf16[256,2,5120]{2,0,1:T(8,128)(2,1)S(1)} fusion(f32[2,256,5120]{2,1,0:T(8,128)} %get-tuple-element.506, f32[256,2]{0,1:T(2,128)S(1)} %add_add_fusion.6, f32[256,2]{0,1:T(2,128)S(1)} %add_add_fusion.5, f32[256,2]{0,1:T(2,128)S(1)} %maximum_maximum_fusion.2, f32[2,256,5120]{2,1,0:T(8,128)S(1)} %bitcast.324, ...), kind=kLoop, calls=%fused_computation.17.clone.1 | loop fusion | flops 20971520 | bytes 27531264 | tf_op jit(solution)/shard_map/while/body/eval_jaxpr/convert_element_type | solution.py:140
  333.3 1.7 fusion.172
  344.0 1.9 broadcast_in_dim.166
  346.8 3.6 bitcast_reduce_fusion.2
  350.5 3.0 fusion.164
  354.4 4.2 fusion.173
  360.9 9.1 %fusion.169 = f32[5120,2,64]{0,2,1:T(8,128)} fusion(bf16[256,2,64]{0,2,1:T(8,128)(2,1)S(1)} %bitcast.353, f32[5120,2,64]{0,2,1:T(8,128)} %get-tuple-element.548, pred[]{:T(512)S(6)} %compare.7, f32[2,256,5120]{2,1,0:T(8,128)} %copy-done.2, f32[256,2]{0,1:T(2,128)S(1)} %add_add_fusion.5, f32[256,2]{0,1:T(2,128)S(1)} %maximum_maximum_fusion.2, ...), kind=kOutput, calls=%fused_computation.25.clone.1 | convolution fusion | flops 349962240 | bytes 17108992 | tf_op jit(solution)/shard_map/while/body/eval_jaxpr/rhk,rhe->khe/dot_general | solution.py:153
  370.1 7.3 %fusion.166 = (f32[256,2]{0,1:T(2,128)S(1)}, f32[2,256,5120]{2,1,0:T(8,128)}) fusion(f32[256,2]{0,1:T(2,128)S(1)} %add_add_fusion.5, f32[256,2]{0,1:T(2,128)S(1)} %maximum_maximum_fusion.2, f32[2,256,5120]{2,1,0:T(8,128)S(1)} %bitcast.324, pred[256,5120]{1,0:T(8,128)(4,1)S(1)} %bitcast_and_fusion.2, bf16[256,2,64]{0,2,1:T(8,128)(2,1)S(1)} %bitcast.354, ...), kind=kOutput, calls=%fused_computation.14.clone.1 | convolution fusion | flops 351272448 | bytes 23664640 | tf_op jit(solution)/shard_map/while/body/eval_jaxpr/rhe,khe->rhk/dot_general | solution.py:126
  377.5 7.1 %fusion.167 = bf16[256,2,5120]{2,0,1:T(8,128)(2,1)S(1)} fusion(f32[2,256,5120]{2,1,0:T(8,128)} %get-tuple-element.506, f32[256,2]{0,1:T(2,128)S(1)} %add_add_fusion.6, f32[256,2]{0,1:T(2,128)S(1)} %add_add_fusion.5, f32[256,2]{0,1:T(2,128)S(1)} %maximum_maximum_fusion.2, f32[2,256,5120]{2,1,0:T(8,128)S(1)} %bitcast.324, ...), kind=kLoop, calls=%fused_computation.17.clone.1 | loop fusion | flops 20971520 | bytes 27531264 | tf_op jit(solution)/shard_map/while/body/eval_jaxpr/convert_element_type | solution.py:140
  398.1 2.1 copy.127
  400.2 5.0 all-to-all-start.1
  409.2 5.5 scatter_custom_fusion
  418.1 5.5 scatter_custom_fusion.1
  425.9 5.5 scatter_custom_fusion.2
  432.7 5.3 scatter_custom_fusion.3
  440.7 3.0 collective-permute-start.6
  450.8 2.5 collective-permute-done.7
  453.3 4.0 collective-permute-done.6
  457.3 10.3 %collective-permute-done.5 = bf16[1024,256]{1,0:T(8,128)(2,1)} collective-permute-done((bf16[1024,256]{1,0:T(8,128)(2,1)}, bf16[1024,256]{1,0:T(8,128)(2,1)}, u32[]{:S(2)}, u32[]{:S(2)}) %collective-permute-start.5) | collective-permute-done | bytes 524320 | tf_op jit(solution)/shard_map/ppermute | solution.py:14
  467.6 1.8 fusion.41
  469.5 4.1 copy.128
  473.5 23.4 %scatter_custom_fusion.4 = f32[1024,256]{1,0:T(8,128)S(1)} fusion(f32[1024,256]{1,0:T(8,128)S(1)} %fusion.41, s32[4096]{0:T(1024)S(1)} %bitcast.365, bf16[4096,256]{1,0:T(8,128)(2,1)} %bitcast.333), kind=kCustom, calls=%fused_computation.82 | custom fusion | flops 2097152 | bytes 3145728 | tf_op jit(solution)/shard_map/scatter-add | solution.py:187
  497.0 46.8 %all-reduce.6.cloned.1.call-done = bf16[128,256]{1,0:T(8,128)(2,1)} async-done(((bf16[128,256]{1,0:T(8,128)(2,1)}), bf16[128,256]{1,0:T(8,128)(2,1)}) %all-reduce.6.cloned.1.call-update) | async-done | bytes 65552 | tf_op jit(solution)/shard_map/psum | solution.py:209
  543.8 2.1 scatter_custom_fusion.5
  546.4 1.9 add_add_fusion.2
  548.2 28.8 %reduce-scatter.2.cloned.1.call-done = f32[1024,128]{1,0:T(8,128)} async-done(((f32[1024,512]{1,0:T(8,128)}), f32[1024,128]{1,0:T(8,128)}) %reduce-scatter.2.cloned.1.call-update) | async-done | bytes 524304 | tf_op jit(solution)/shard_map/reduce_scatter | solution.py:224
  577.0 1.8 convert_element_type.130
  (428 shorter events, 102.9 us)
Async XLA Ops:
  7.2 10.5 %copy-start.27 = (s32[1,32,128]{2,1,0:T(8,128)S(1)}, s32[1,32,128]{2,1,0:T(8,128)}, u32[]{:S(2)}) copy-start(s32[1,32,128]{2,1,0:T(8,128)} %param.17) | copy-start | bytes 49156
  11.1 5.6 copy-start.16
  11.2 138.3 %collective-permute-start.3 = (bf16[1024,256]{1,0:T(8,128)(2,1)S(1)}, bf16[1024,256]{1,0:T(8,128)(2,1)}, u32[]{:S(2)}, u32[]{:S(2)}) collective-permute-start(bf16[1024,256]{1,0:T(8,128)(2,1)S(1)} %pad_maximum_fusion.8), channel_id=1, source_target_pairs={{0,32},{4,36},{8,40},{12,44},{16,48},{20,52},{24,56},{28,60},{32,0... | collective-permute-start | bytes 1572872 | tf_op jit(solution)/shard_map/ppermute | solution.py:14
  12.8 141.7 %collective-permute-start.2 = (bf16[1024,256]{1,0:T(8,128)(2,1)S(1)}, bf16[1024,256]{1,0:T(8,128)(2,1)S(1)}, u32[]{:S(2)}, u32[]{:S(2)}) collective-permute-start(bf16[1024,256]{1,0:T(8,128)(2,1)S(1)} %pad_maximum_fusion.8), channel_id=1, source_target_pairs={{0,16},{4,20},{8,24},{12,28},{16,0},{20,4},{24,8},{28,12},{32,48},... | collective-permute-start | bytes 1572872 | tf_op jit(solution)/shard_map/ppermute | solution.py:14
  16.7 141.8 %collective-permute-start.1 = (bf16[1024,256]{1,0:T(8,128)(2,1)S(1)}, bf16[1024,256]{1,0:T(8,128)(2,1)S(1)}, u32[]{:S(2)}, u32[]{:S(2)}) collective-permute-start(bf16[1024,256]{1,0:T(8,128)(2,1)S(1)} %pad_maximum_fusion.8), channel_id=1, source_target_pairs={{0,8},{4,12},{8,0},{12,4},{16,24},{20,28},{24,16},{28,20},{32,40},... | collective-permute-start | bytes 1572872 | tf_op jit(solution)/shard_map/ppermute | solution.py:14
  17.7 145.7 %collective-permute-start = (bf16[1024,256]{1,0:T(8,128)(2,1)S(1)}, bf16[1024,256]{1,0:T(8,128)(2,1)S(1)}, u32[]{:S(2)}, u32[]{:S(2)}) collective-permute-start(bf16[1024,256]{1,0:T(8,128)(2,1)S(1)} %pad_maximum_fusion.8), channel_id=1, source_target_pairs={{0,4},{4,0},{8,12},{12,8},{16,20},{20,16},{24,28},{28,24},{32,36},... | collective-permute-start | bytes 1572872 | tf_op jit(solution)/shard_map/ppermute | solution.py:14
  34.7 11.0 %copy-start.30 = (s32[4,1024]{1,0:T(4,128)S(1)}, s32[4,1024]{1,0:T(4,128)}, u32[]{:S(2)}) copy-start(s32[4,1024]{1,0:T(4,128)} %param.20) | copy-start | bytes 49156
  34.7 12.3 %copy-start.22 = (bf16[512,128]{1,0:T(8,128)(2,1)S(1)}, bf16[512,128]{1,0:T(8,128)(2,1)}, u32[]{:S(2)}) copy-start(bf16[512,128]{1,0:T(8,128)(2,1)} %param.13) | copy-start | bytes 393220
  34.7 135.2 %all-to-all-start = ((bf16[32,128,256]{2,1,0:T(8,128)(2,1)}), bf16[32,128,256]{2,1,0:T(8,128)(2,1)}, u32[]{:S(2)}, u32[]{:S(2)}) async-start(bf16[32,128,256]{2,1,0:T(8,128)(2,1)} %bitcast.334), calls=%async_computation | async-start | bytes 4194304 | tf_op jit(solution)/shard_map/all_to_all | solution.py:46
  40.0 107.2 %all-reduce.4.cloned.1.call-start = ((), (), s32[]{:S(2)}) async-start(), calls=%async_computation.3 | async-start | bytes 131072 | tf_op jit(solution)/shard_map/psum | solution.py:65
  176.6 4.3 copy-start.9
  176.6 4.3 copy-start.11
  181.1 7.0 %copy-start.6 = (bf16[4,1024,256]{2,1,0:T(8,128)(2,1)}, bf16[4,1024,256]{2,1,0:T(8,128)(2,1)S(1)}, u32[]{:S(2)}) copy-start(bf16[4,1024,256]{2,1,0:T(8,128)(2,1)S(1)} %get-tuple-element.586) | copy-start | bytes 6291460 | tf_op jit(solution)/shard_map/while
  196.6 4.5 copy-start.20
  202.0 8.6 %slice-start = ((s8[10485760]{0:T(1024)(128)(4,1)}), s8[4194304]{0:T(1024)(128)(4,1)S(1)}, s32[]{:S(2)}) async-start(s8[10485760]{0:T(1024)(128)(4,1)} %bitcast.323), calls=%async_computation.6 | async-start | bytes 8388608 | tf_op jit(solution)/shard_map/while
  202.2 8.4 %slice-start.1 = ((s8[10485760]{0:T(1024)(128)(4,1)}), s8[4194304]{0:T(1024)(128)(4,1)S(1)}, s32[]{:S(2)}) async-start(s8[10485760]{0:T(1024)(128)(4,1)} %bitcast.323), calls=%async_computation.7 | async-start | bytes 8388608 | tf_op jit(solution)/shard_map/while
  202.2 8.4 %slice-start.2 = ((s8[10485760]{0:T(1024)(128)(4,1)}), s8[2097152]{0:T(1024)(128)(4,1)S(1)}, s32[]{:S(2)}) async-start(s8[10485760]{0:T(1024)(128)(4,1)} %bitcast.323), calls=%async_computation.8 | async-start | bytes 4194304 | tf_op jit(solution)/shard_map/while
  202.2 8.3 %copy-start.21 = (bf16[5120,2,64]{0,2,1:T(8,128)(2,1)S(1)}, bf16[5120,2,64]{0,2,1:T(8,128)(2,1)}, u32[]{:S(2)}) copy-start(bf16[5120,2,64]{0,2,1:T(8,128)(2,1)} %get-tuple-element.589) | copy-start | bytes 3932164 | tf_op jit(solution)/shard_map/while
  218.0 7.8 %copy-start.13 = (f32[128,2,64]{0,2,1:T(8,128)S(1)}, f32[128,2,64]{0,2,1:T(8,128)}, u32[]{:S(2)}) copy-start(f32[128,2,64]{0,2,1:T(8,128)} %get-tuple-element.549) | copy-start | bytes 196612 | tf_op jit(solution)/shard_map/while
  218.0 8.9 %copy-start.5 = (bf16[5120,2,64]{0,2,1:T(8,128)(2,1)S(1)}, bf16[5120,2,64]{0,2,1:T(8,128)(2,1)}, u32[]{:S(2)}) copy-start(bf16[5120,2,64]{0,2,1:T(8,128)(2,1)} %get-tuple-element.585) | copy-start | bytes 3932164 | tf_op jit(solution)/shard_map/while
  232.6 7.0 %copy-start.6 = (bf16[4,1024,256]{2,1,0:T(8,128)(2,1)}, bf16[4,1024,256]{2,1,0:T(8,128)(2,1)S(1)}, u32[]{:S(2)}) copy-start(bf16[4,1024,256]{2,1,0:T(8,128)(2,1)S(1)} %get-tuple-element.586) | copy-start | bytes 6291460 | tf_op jit(solution)/shard_map/while
  248.1 4.2 copy-start.29
  248.1 4.5 copy-start.20
  254.3 9.4 %slice-start = ((s8[10485760]{0:T(1024)(128)(4,1)}), s8[4194304]{0:T(1024)(128)(4,1)S(1)}, s32[]{:S(2)}) async-start(s8[10485760]{0:T(1024)(128)(4,1)} %bitcast.323), calls=%async_computation.6 | async-start | bytes 8388608 | tf_op jit(solution)/shard_map/while
  254.5 9.2 %slice-start.1 = ((s8[10485760]{0:T(1024)(128)(4,1)}), s8[4194304]{0:T(1024)(128)(4,1)S(1)}, s32[]{:S(2)}) async-start(s8[10485760]{0:T(1024)(128)(4,1)} %bitcast.323), calls=%async_computation.7 | async-start | bytes 8388608 | tf_op jit(solution)/shard_map/while
  254.6 9.2 %slice-start.2 = ((s8[10485760]{0:T(1024)(128)(4,1)}), s8[2097152]{0:T(1024)(128)(4,1)S(1)}, s32[]{:S(2)}) async-start(s8[10485760]{0:T(1024)(128)(4,1)} %bitcast.323), calls=%async_computation.8 | async-start | bytes 4194304 | tf_op jit(solution)/shard_map/while
  254.6 9.2 %copy-start.21 = (bf16[5120,2,64]{0,2,1:T(8,128)(2,1)S(1)}, bf16[5120,2,64]{0,2,1:T(8,128)(2,1)}, u32[]{:S(2)}) copy-start(bf16[5120,2,64]{0,2,1:T(8,128)(2,1)} %get-tuple-element.589) | copy-start | bytes 3932164 | tf_op jit(solution)/shard_map/while
  271.1 7.8 %copy-start.13 = (f32[128,2,64]{0,2,1:T(8,128)S(1)}, f32[128,2,64]{0,2,1:T(8,128)}, u32[]{:S(2)}) copy-start(f32[128,2,64]{0,2,1:T(8,128)} %get-tuple-element.549) | copy-start | bytes 196612 | tf_op jit(solution)/shard_map/while
  271.2 8.9 %copy-start.5 = (bf16[5120,2,64]{0,2,1:T(8,128)(2,1)S(1)}, bf16[5120,2,64]{0,2,1:T(8,128)(2,1)}, u32[]{:S(2)}) copy-start(bf16[5120,2,64]{0,2,1:T(8,128)(2,1)} %get-tuple-element.585) | copy-start | bytes 3932164 | tf_op jit(solution)/shard_map/while
  285.7 7.0 %copy-start.6 = (bf16[4,1024,256]{2,1,0:T(8,128)(2,1)}, bf16[4,1024,256]{2,1,0:T(8,128)(2,1)S(1)}, u32[]{:S(2)}) copy-start(bf16[4,1024,256]{2,1,0:T(8,128)(2,1)S(1)} %get-tuple-element.586) | copy-start | bytes 6291460 | tf_op jit(solution)/shard_map/while
  301.3 4.2 copy-start.29
  301.3 4.5 copy-start.20
  307.5 9.4 %slice-start = ((s8[10485760]{0:T(1024)(128)(4,1)}), s8[4194304]{0:T(1024)(128)(4,1)S(1)}, s32[]{:S(2)}) async-start(s8[10485760]{0:T(1024)(128)(4,1)} %bitcast.323), calls=%async_computation.6 | async-start | bytes 8388608 | tf_op jit(solution)/shard_map/while
  307.8 9.2 %slice-start.1 = ((s8[10485760]{0:T(1024)(128)(4,1)}), s8[4194304]{0:T(1024)(128)(4,1)S(1)}, s32[]{:S(2)}) async-start(s8[10485760]{0:T(1024)(128)(4,1)} %bitcast.323), calls=%async_computation.7 | async-start | bytes 8388608 | tf_op jit(solution)/shard_map/while
  307.8 9.2 %slice-start.2 = ((s8[10485760]{0:T(1024)(128)(4,1)}), s8[2097152]{0:T(1024)(128)(4,1)S(1)}, s32[]{:S(2)}) async-start(s8[10485760]{0:T(1024)(128)(4,1)} %bitcast.323), calls=%async_computation.8 | async-start | bytes 4194304 | tf_op jit(solution)/shard_map/while
  307.8 9.2 %copy-start.21 = (bf16[5120,2,64]{0,2,1:T(8,128)(2,1)S(1)}, bf16[5120,2,64]{0,2,1:T(8,128)(2,1)}, u32[]{:S(2)}) copy-start(bf16[5120,2,64]{0,2,1:T(8,128)(2,1)} %get-tuple-element.589) | copy-start | bytes 3932164 | tf_op jit(solution)/shard_map/while
  324.4 7.8 %copy-start.13 = (f32[128,2,64]{0,2,1:T(8,128)S(1)}, f32[128,2,64]{0,2,1:T(8,128)}, u32[]{:S(2)}) copy-start(f32[128,2,64]{0,2,1:T(8,128)} %get-tuple-element.549) | copy-start | bytes 196612 | tf_op jit(solution)/shard_map/while
  324.4 8.9 %copy-start.5 = (bf16[5120,2,64]{0,2,1:T(8,128)(2,1)S(1)}, bf16[5120,2,64]{0,2,1:T(8,128)(2,1)}, u32[]{:S(2)}) copy-start(bf16[5120,2,64]{0,2,1:T(8,128)(2,1)} %get-tuple-element.585) | copy-start | bytes 3932164 | tf_op jit(solution)/shard_map/while
  339.0 7.0 %copy-start.6 = (bf16[4,1024,256]{2,1,0:T(8,128)(2,1)}, bf16[4,1024,256]{2,1,0:T(8,128)(2,1)S(1)}, u32[]{:S(2)}) copy-start(bf16[4,1024,256]{2,1,0:T(8,128)(2,1)S(1)} %get-tuple-element.586) | copy-start | bytes 6291460 | tf_op jit(solution)/shard_map/while
  354.4 4.5 copy-start.20
  360.6 9.4 %slice-start = ((s8[10485760]{0:T(1024)(128)(4,1)}), s8[4194304]{0:T(1024)(128)(4,1)S(1)}, s32[]{:S(2)}) async-start(s8[10485760]{0:T(1024)(128)(4,1)} %bitcast.323), calls=%async_computation.6 | async-start | bytes 8388608 | tf_op jit(solution)/shard_map/while
  360.9 9.2 %slice-start.1 = ((s8[10485760]{0:T(1024)(128)(4,1)}), s8[4194304]{0:T(1024)(128)(4,1)S(1)}, s32[]{:S(2)}) async-start(s8[10485760]{0:T(1024)(128)(4,1)} %bitcast.323), calls=%async_computation.7 | async-start | bytes 8388608 | tf_op jit(solution)/shard_map/while
  360.9 9.2 %slice-start.2 = ((s8[10485760]{0:T(1024)(128)(4,1)}), s8[2097152]{0:T(1024)(128)(4,1)S(1)}, s32[]{:S(2)}) async-start(s8[10485760]{0:T(1024)(128)(4,1)} %bitcast.323), calls=%async_computation.8 | async-start | bytes 4194304 | tf_op jit(solution)/shard_map/while
  360.9 9.2 %copy-start.21 = (bf16[5120,2,64]{0,2,1:T(8,128)(2,1)S(1)}, bf16[5120,2,64]{0,2,1:T(8,128)(2,1)}, u32[]{:S(2)}) copy-start(bf16[5120,2,64]{0,2,1:T(8,128)(2,1)} %get-tuple-element.589) | copy-start | bytes 3932164 | tf_op jit(solution)/shard_map/while
  377.5 7.8 %copy-start.13 = (f32[128,2,64]{0,2,1:T(8,128)S(1)}, f32[128,2,64]{0,2,1:T(8,128)}, u32[]{:S(2)}) copy-start(f32[128,2,64]{0,2,1:T(8,128)} %get-tuple-element.549) | copy-start | bytes 196612 | tf_op jit(solution)/shard_map/while
  377.5 8.9 %copy-start.5 = (bf16[5120,2,64]{0,2,1:T(8,128)(2,1)S(1)}, bf16[5120,2,64]{0,2,1:T(8,128)(2,1)}, u32[]{:S(2)}) copy-start(bf16[5120,2,64]{0,2,1:T(8,128)(2,1)} %get-tuple-element.585) | copy-start | bytes 3932164 | tf_op jit(solution)/shard_map/while
  400.2 69.2 %all-to-all-start.1 = ((bf16[32,128,256]{1,2,0:T(8,128)(2,1)}), bf16[32,128,256]{1,2,0:T(8,128)(2,1)}, u32[]{:S(2)}, u32[]{:S(2)}) async-start(bf16[32,128,256]{1,2,0:T(8,128)(2,1)} %copy.127), calls=%async_computation.1 | async-start | bytes 4194304 | tf_op jit(solution)/shard_map/all_to_all | solution.py:184
  405.2 138.5 %all-reduce.6.cloned.1.call-start = ((), (), s32[]{:S(2)}) async-start(), calls=%async_computation.4 | async-start | bytes 131072 | tf_op jit(solution)/shard_map/psum | solution.py:209
  416.8 7.7 %copy-start.17 = (f32[1024,128]{0,1:T(8,128)S(1)}, f32[1024,128]{0,1:T(8,128)}, u32[]{:S(2)}) copy-start(f32[1024,128]{0,1:T(8,128)} %get-tuple-element.337) | copy-start | bytes 1572868
  432.4 11.9 %copy-start.28 = (s32[1,32,128]{2,1,0:T(8,128)S(1)}, s32[1,32,128]{2,1,0:T(8,128)}, u32[]{:S(2)}) copy-start(s32[1,32,128]{2,1,0:T(8,128)} %param.17) | copy-start | bytes 49156
  432.7 13.7 %copy-start.15 = (f32[128,2,64]{0,2,1:T(8,128)S(1)}, f32[128,2,64]{0,2,1:T(8,128)}, u32[]{:S(2)}) copy-start(f32[128,2,64]{0,2,1:T(8,128)} %get-tuple-element.642) | copy-start | bytes 196612
  439.0 11.4 %copy-start.23 = (bf16[512,128]{1,0:T(8,128)(2,1)S(1)}, bf16[512,128]{1,0:T(8,128)(2,1)}, u32[]{:S(2)}) copy-start(bf16[512,128]{1,0:T(8,128)(2,1)} %param.13) | copy-start | bytes 393220
  439.0 11.4 %copy-start.26 = (bf16[4,256,128]{2,1,0:T(8,128)(2,1)S(1)}, bf16[4,256,128]{2,1,0:T(8,128)(2,1)}, u32[]{:S(2)}) copy-start(bf16[4,256,128]{2,1,0:T(8,128)(2,1)} %get-tuple-element.645) | copy-start | bytes 786436
  439.0 14.3 %collective-permute-start.7 = (bf16[1024,256]{1,0:T(8,128)(2,1)}, bf16[1024,256]{1,0:T(8,128)(2,1)}, u32[]{:S(2)}, u32[]{:S(2)}) collective-permute-start(bf16[1024,256]{1,0:T(8,128)(2,1)} %convert_element_type.125), channel_id=1, source_target_pairs={{0,32},{4,36},{8,40},{12,44},{16,48},{20,52},{24,56},{28,60},{32,0... | collective-permute-start | bytes 1572872 | tf_op jit(solution)/shard_map/ppermute | solution.py:14
  440.7 16.6 %collective-permute-start.6 = (bf16[1024,256]{1,0:T(8,128)(2,1)}, bf16[1024,256]{1,0:T(8,128)(2,1)}, u32[]{:S(2)}, u32[]{:S(2)}) collective-permute-start(bf16[1024,256]{1,0:T(8,128)(2,1)} %convert_element_type.123), channel_id=1, source_target_pairs={{0,16},{4,20},{8,24},{12,28},{16,0},{20,4},{24,8},{28,12},{32,48},... | collective-permute-start | bytes 1572872 | tf_op jit(solution)/shard_map/ppermute | solution.py:14
  443.7 23.9 %collective-permute-start.5 = (bf16[1024,256]{1,0:T(8,128)(2,1)}, bf16[1024,256]{1,0:T(8,128)(2,1)}, u32[]{:S(2)}, u32[]{:S(2)}) collective-permute-start(bf16[1024,256]{1,0:T(8,128)(2,1)} %convert_element_type.121), channel_id=1, source_target_pairs={{0,8},{4,12},{8,0},{12,4},{16,24},{20,28},{24,16},{28,20},{32,40},... | collective-permute-start | bytes 1572872 | tf_op jit(solution)/shard_map/ppermute | solution.py:14
  444.3 23.4 %collective-permute-start.4 = (bf16[1024,256]{1,0:T(8,128)(2,1)}, bf16[1024,256]{1,0:T(8,128)(2,1)}, u32[]{:S(2)}, u32[]{:S(2)}) collective-permute-start(bf16[1024,256]{1,0:T(8,128)(2,1)} %convert_element_type.119), channel_id=1, source_target_pairs={{0,4},{4,0},{8,12},{12,8},{16,20},{20,16},{24,28},{28,24},{32,36},... | collective-permute-start | bytes 1572872 | tf_op jit(solution)/shard_map/ppermute | solution.py:14
  448.2 128.8 %reduce-scatter.2.cloned.1.call-start = ((), (), s32[]{:S(2)}) async-start(), calls=%async_computation.5 | async-start | bytes 2621440 | tf_op jit(solution)/shard_map/reduce_scatter | solution.py:224
  450.4 17.2 %copy-start.18 = (f32[1024,128]{1,0:T(8,128)S(1)}, f32[1024,128]{1,0:T(8,128)}, u32[]{:S(2)}) copy-start(f32[1024,128]{1,0:T(8,128)} %copy.118) | copy-start | bytes 1572868
  450.4 17.2 %copy-start.19 = (f32[1024,128]{1,0:T(8,128)S(1)}, f32[1024,128]{1,0:T(8,128)}, u32[]{:S(2)}) copy-start(f32[1024,128]{1,0:T(8,128)} %copy.119) | copy-start | bytes 1572868
  473.5 70.2 %copy-start.35 = (pred[128]{0:T(512)(128)(4,1)S(1)}, pred[128]{0:T(512)(128)(4,1)}, u32[]{:S(2)}) copy-start(pred[128]{0:T(512)(128)(4,1)} %fusion.61) | copy-start | bytes 388
  473.5 72.4 %copy-start.24 = (bf16[512,128]{1,0:T(8,128)(2,1)S(1)}, bf16[512,128]{1,0:T(8,128)(2,1)}, u32[]{:S(2)}) copy-start(bf16[512,128]{1,0:T(8,128)(2,1)} %param.14) | copy-start | bytes 393220
  497.0 49.3 %copy-start.25 = (bf16[512,128]{1,0:T(8,128)(2,1)S(1)}, bf16[512,128]{1,0:T(8,128)(2,1)}, u32[]{:S(2)}) copy-start(bf16[512,128]{1,0:T(8,128)(2,1)} %param.15) | copy-start | bytes 393220
  546.3 32.4 %copy-start.1 = (bf16[1024,512]{1,0:T(8,128)(2,1)S(1)}, bf16[1024,512]{1,0:T(8,128)(2,1)}, u32[]{:S(2)}) copy-start(bf16[1024,512]{1,0:T(8,128)(2,1)} %param.12) | copy-start | bytes 3145732
  (45 other events, 127.2 us)
Sparse Core Ops, SparseCore 0:
  45.8 101.4 all-reduce.3
  448.4 95.3 all-reduce.5
  548.4 28.6 reduce-scatter.1
where the time goes:
time: 594 us; the launch traced here: 586 us
  waiting for transfers between devices  186 us (31%)
  matrix products  128 us (22%)
  local copies, waits for them, and re-layouts  118 us (20%)
  other arithmetic  109 us (18%)
  starting transfers between devices  22.3 us (4%)
  between operations  14.5 us (2%)
  loops' own time  7.23 us (1%)
    psum x1, waiting for transfers between devices, on_device(): global_pairs = lax.psum(picked.astype(jnp.bfloat16), 'dom')  93.9 us
    psum x1, waiting for transfers between devices, on_device(): lax.psum(global_grad.astype(jnp.bfloat16), 'dom').astype(jnp.float32)  46.8 us
    dot_general x4, matrix products, one_block(): jnp.einsum('rhk,rhe->khe', local_weight, grad_blk, preferred_element_type...  35.7 us
    dot_general x4, matrix products, one_block(): jnp.einsum('rhe,khe->rhk', grad_blk, cand_value, preferred_element_type=j...  29.3 us
    reduce_scatter x1, waiting for transfers between devices, on_device(): lax.psum_scatter(feature_terms, 'feat', scatter_dimension=1, tiled=True)  28.8 us
    convert_element_type x4, other arithmetic, one_block(): (local_prob * (local_dp - delta) * score_scale).astype(jnp.bfloat16)  28.3 us
    scatter-add x1, other arithmetic, on_device(): pair_grad.at[send_rows[0].reshape(-1)]  23.4 us
    scatter x4, local copies, waits for them, and re-layouts, on_device(): placed = jnp.zeros_like(joined).at[row_order].set(joined)  21.9 us
  transfers between devices with their start and end apart: 13, of which 6 were waited for; matrix products, arithmetic and copies ran while one was open for 21% of the time, Pallas kernels for 0%

commit v1 on v0

v1 whole, which is shorter than its diff:
```python
import math

import jax
import jax.numpy as jnp
from jax import lax
from jax.experimental import pallas as pl
from jax.experimental.pallas import tpu as pltpu
from jax.sharding import PartitionSpec as P

HEAD = 64
BLOCK = 128
EXPANDERS = 4
COLS = 128
NODES_HERE = 1024
Q_BLOCKS = NODES_HERE // BLOCK
SENDERS = 32
GLOBAL_BLOCK = Q_BLOCKS + SENDERS
EMPTY_BLOCK = GLOBAL_BLOCK + 1
KEY_BLOCKS = EMPTY_BLOCK + 1
GROUP = 4
LIST = 48
NEG = -1e30
F32 = jnp.float32
BF16 = jnp.bfloat16


def params():
    return pltpu.CompilerParams(vmem_limit_bytes=56 * 1024 * 1024)


def vmem():
    return pl.BlockSpec(memory_space=pltpu.VMEM)


def smem():
    return pl.BlockSpec(memory_space=pltpu.SMEM)


def iota(shape, dim):
    return lax.broadcasted_iota(jnp.int32, shape, dim)


def dot(a, b):
    return jnp.dot(a, b, preferred_element_type=F32)


def dot_nt(a, b):
    return lax.dot_general(a, b, (((1,), (1,)), ((), ())), preferred_element_type=F32)


def one_hot_rows(row, table_rows):
    column = jnp.broadcast_to(row, (BLOCK, BLOCK)).T
    lanes = iota((BLOCK, BLOCK), 1)
    return jnp.concatenate(
        [(column == lanes + c * BLOCK).astype(F32).astype(BF16) for c in range(table_rows // BLOCK)],
        axis=1,
    )


def project_kernel(x_ref, wq_ref, wk_ref, wv_ref, rows_ref, gid_ref, q_ref, kv_ref, outk_ref, outv_ref, glob_ref):
    x = x_ref[...]
    q_ref[...] = (dot(x, wq_ref[...]).astype(BF16).astype(F32) * (1.0 / math.sqrt(HEAD))).astype(BF16)
    kv_ref[:, :COLS] = dot(x, wk_ref[...]).astype(BF16)
    kv_ref[:, COLS:] = dot(x, wv_ref[...]).astype(BF16)

    def gather(d, carry):
        got = dot(one_hot_rows(rows_ref[pl.ds(d, 1), :], NODES_HERE), kv_ref[...]).astype(BF16)
        outk_ref[d] = got[:, :COLS]
        outv_ref[d] = got[:, COLS:]
        return carry

    lax.fori_loop(0, SENDERS, gather, 0)
    glob_ref[...] = dot(one_hot_rows(gid_ref[...], NODES_HERE), kv_ref[...]).astype(BF16)


def partner_kernel(exp_ref, t0_ref, t1_ref, t2_ref, t3_ref, out_ref):
    for m, table in enumerate((t0_ref, t1_ref, t2_ref, t3_ref)):

        def gather(i, carry):
            b = m * Q_BLOCKS + i
            out_ref[b] = dot(one_hot_rows(exp_ref[pl.ds(b, 1), :], NODES_HERE), table[...]).astype(BF16)
            return carry

        lax.fori_loop(0, Q_BLOCKS, gather, 0)


def plan_kernel(mask_ref, count_ref, list_ref, groups_ref, live_ref):
    for j in range(Q_BLOCKS):
        live_ref[j] = BLOCK
    live_ref[GLOBAL_BLOCK] = BLOCK
    live_ref[EMPTY_BLOCK] = 0

    def copy_count(s, carry):
        live_ref[Q_BLOCKS + s] = count_ref[s]
        return carry

    lax.fori_loop(0, SENDERS, copy_count, 0)

    def per_block(i, carry):
        list_ref[i * LIST] = GLOBAL_BLOCK

        def put(j, n):
            list_ref[i * LIST + n] = j
            used = jnp.logical_and(mask_ref[i * GLOBAL_BLOCK + j] > 0, live_ref[j] > 0)
            return n + used.astype(jnp.int32)

        n = lax.fori_loop(0, GLOBAL_BLOCK, put, 1)
        for extra in range(GROUP):
            list_ref[i * LIST + n + extra] = EMPTY_BLOCK
        groups_ref[i] = (n + GROUP - 1) // GROUP
        return carry

    lax.fori_loop(0, Q_BLOCKS, per_block, 0)


def fill(dst, own_ref, first_col, halo_ref, glob_ref, transposed=False):
    def turn(x):
        return x.T if transposed else x

    def own(j, carry):
        dst[j] = turn(own_ref[pl.ds(pl.multiple_of(j * BLOCK, BLOCK), BLOCK), first_col : first_col + COLS])
        return carry

    def halo(j, carry):
        dst[Q_BLOCKS + j] = turn(halo_ref[j])
        return carry

    lax.fori_loop(0, Q_BLOCKS, own, 0)
    lax.fori_loop(0, SENDERS, halo, 0)
    dst[GLOBAL_BLOCK] = turn(glob_ref[:, first_col : first_col + COLS])
    dst[EMPTY_BLOCK] = jnp.zeros((BLOCK, COLS), BF16)


def stacked(rows):
    lanes = iota((BLOCK, COLS), 1)
    zero = jnp.zeros_like(rows)
    return jnp.concatenate([jnp.where(lanes < HEAD, rows, zero), jnp.where(lanes < HEAD, zero, rows)], axis=0)


def stacked_t(rows):
    turned = rows.T
    subs = iota((COLS, BLOCK), 0)
    zero = jnp.zeros_like(turned)
    return jnp.concatenate([jnp.where(subs < HEAD, turned, zero), jnp.where(subs < HEAD, zero, turned)], axis=1)


def partner_rows(rows, pair_ref, i, first_col):
    total = jnp.zeros((16, BLOCK), F32)
    row_id = iota((16, COLS), 0)
    lane = iota((16, COLS), 1)
    for m in range(EXPANDERS):
        other = pair_ref[m * Q_BLOCKS + i][:, first_col : first_col + COLS]
        prod = rows.astype(F32) * other.astype(F32)
        high = prod.astype(BF16)
        low = (prod - high.astype(F32)).astype(BF16)
        picks = (row_id == jnp.where(lane < HEAD, m, 8 + m)).astype(F32).astype(BF16)
        total = total + dot_nt(picks, high) + dot_nt(picks, low)
    return jnp.concatenate([total[:8], total[8:]], axis=1)


def tall(weights):
    return jnp.concatenate([weights[:, :BLOCK], weights[:, BLOCK:]], axis=0)


def spread(tall_weights):
    turned = tall_weights.T.astype(BF16)
    row_id = iota((16, EXPANDERS * COLS), 0)
    col = iota((16, EXPANDERS * COLS), 1)
    picks = (row_id == (col // COLS) + jnp.where(col % COLS < HEAD, 0, 8)).astype(F32).astype(BF16)
    return dot(turned, picks)


def head_rows(turned):
    return jnp.concatenate([turned[:HEAD, :BLOCK], turned[HEAD:, BLOCK:]], axis=0)


def masked_scores(blocks, k_s, turned_q, live_ref):
    keys = jnp.concatenate([k_s[b] for b in blocks], axis=0)
    scores = dot(keys, turned_q)
    row_id = iota((BLOCK, 2 * BLOCK), 0)
    return jnp.concatenate(
        [
            jnp.where(row_id < live_ref[b], scores[u * BLOCK : (u + 1) * BLOCK], NEG)
            for u, b in enumerate(blocks)
        ],
        axis=0,
    )


def block_ids(list_ref, i, g):
    return [list_ref[i * LIST + g * GROUP + u] for u in range(GROUP)]


def q_rows(i):
    return pl.ds(pl.multiple_of(i * BLOCK, BLOCK), BLOCK)


def score_kernel(list_ref, groups_ref, live_ref, q_ref, kv_ref, hk_ref, glob_ref, pair_ref, lse_ref, sp_ref, k_s):
    fill(k_s, kv_ref, 0, hk_ref, glob_ref)

    def per_block(i, carry):
        rows = q_ref[q_rows(i), :]
        turned_q = stacked_t(rows)
        partner = partner_rows(rows, pair_ref, i, 0)
        partner = jnp.where(iota((8, 2 * BLOCK), 0) < EXPANDERS, partner, NEG)
        sp_ref[i] = partner

        def step(g, state):
            top, total = state
            scores = masked_scores(block_ids(list_ref, i, g), k_s, turned_q, live_ref)
            scores = scores.reshape(GROUP * BLOCK // 8, 8, 2 * BLOCK)
            new_top = jnp.maximum(top, jnp.max(scores, axis=0))
            total = total * jnp.exp(top - new_top) + jnp.sum(jnp.exp(scores - new_top[None]), axis=0)
            return new_top, total

        top, total = lax.fori_loop(0, groups_ref[i], step, (partner, jnp.ones((8, 2 * BLOCK), F32)))
        best = jnp.max(top, axis=0, keepdims=True)
        denominator = jnp.sum(total * jnp.exp(top - best), axis=0, keepdims=True)
        lse_ref[pl.ds(i, 1), :] = best + jnp.log(denominator)
        return carry

    lax.fori_loop(0, Q_BLOCKS, per_block, 0)


def value_kernel(
    list_ref, groups_ref, live_ref, q_ref, kv_ref, hk_ref, hv_ref, glob_ref, pair_ref, cot_ref, lse_ref, sp_ref,
    att_ref, own_ref, halo_ref, gout_ref, wp_ref, dp_ref, delta_ref, k_s, vt_s, acc_s, out_s,
):
    fill(k_s, kv_ref, 0, hk_ref, glob_ref)
    fill(vt_s, kv_ref, COLS, hv_ref, glob_ref, transposed=True)

    def clear(j, carry):
        acc_s[j] = jnp.zeros((BLOCK, COLS), F32)
        return carry

    lax.fori_loop(0, KEY_BLOCKS, clear, 0)

    def per_block(i, carry):
        turned_q = stacked_t(q_ref[q_rows(i), :])
        cot = cot_ref[q_rows(i), :]
        cot_stack = stacked(cot)
        lse = lse_ref[pl.ds(i, 1), :]
        out_s[...] = jnp.zeros((COLS, 2 * BLOCK), F32)

        def step(g, carry):
            blocks = block_ids(list_ref, i, g)
            scores = masked_scores(blocks, k_s, turned_q, live_ref)
            weight = jnp.exp(scores - lse).astype(BF16)
            turned_v = jnp.concatenate([vt_s[b] for b in blocks], axis=1)
            out_s[...] += dot(turned_v, weight)
            grads = dot(weight, cot_stack)
            for u, b in enumerate(blocks):
                acc_s[b] += grads[u * BLOCK : (u + 1) * BLOCK]
            return carry

        lax.fori_loop(0, groups_ref[i], step, 0)
        dprob = partner_rows(cot, pair_ref, i, COLS)
        dp_ref[i] = dprob
        prob = jnp.exp(sp_ref[i] - lse)
        weight = prob.astype(BF16).astype(F32)
        wide = spread(tall(weight))
        wp_ref[i] = tall(weight).astype(BF16)
        attended_t = head_rows(out_s[...])
        prod = attended_t * cot.T.astype(F32)
        delta = jnp.concatenate(
            [jnp.sum(prod[:HEAD], axis=0, keepdims=True), jnp.sum(prod[HEAD:], axis=0, keepdims=True)], axis=1
        )
        delta_ref[pl.ds(i, 1), :] = delta + jnp.sum(prob * dprob, axis=0, keepdims=True)
        attended = attended_t.T
        for m in range(EXPANDERS):
            attended += wide[:, m * COLS : (m + 1) * COLS] * pair_ref[m * Q_BLOCKS + i][:, COLS:].astype(F32)
        att_ref[q_rows(i), :] = attended.astype(BF16)
        return carry

    lax.fori_loop(0, Q_BLOCKS, per_block, 0)
    store_parts(acc_s, own_ref, halo_ref, gout_ref)


def store_parts(acc_s, own_ref, halo_ref, gout_ref):
    def own(j, carry):
        own_ref[q_rows(j), :] = acc_s[j]
        return carry

    def halo(j, carry):
        halo_ref[j] = acc_s[Q_BLOCKS + j].astype(BF16)
        return carry

    lax.fori_loop(0, Q_BLOCKS, own, 0)
    lax.fori_loop(0, SENDERS, halo, 0)
    gout_ref[...] = acc_s[GLOBAL_BLOCK].astype(BF16)


def key_kernel(
    list_ref, groups_ref, live_ref, q_ref, kv_ref, hk_ref, hv_ref, glob_ref, pair_ref, cot_ref, lse_ref, sp_ref,
    dp_ref, delta_ref, gq_ref, own_ref, halo_ref, gout_ref, dsp_ref, k_s, v_s, kt_s, acc_s, out_s,
):
    fill(k_s, kv_ref, 0, hk_ref, glob_ref)
    fill(v_s, kv_ref, COLS, hv_ref, glob_ref)
    fill(kt_s, kv_ref, 0, hk_ref, glob_ref, transposed=True)

    def clear(j, carry):
        acc_s[j] = jnp.zeros((BLOCK, COLS), F32)
        return carry

    lax.fori_loop(0, KEY_BLOCKS, clear, 0)

    def per_block(i, carry):
        rows = q_ref[q_rows(i), :]
        turned_q = stacked_t(rows)
        q_stack = stacked(rows)
        turned_cot = stacked_t(cot_ref[q_rows(i), :])
        lse = lse_ref[pl.ds(i, 1), :]
        delta = delta_ref[pl.ds(i, 1), :]
        out_s[...] = jnp.zeros((COLS, 2 * BLOCK), F32)

        def step(g, carry):
            blocks = block_ids(list_ref, i, g)
            scores = masked_scores(blocks, k_s, turned_q, live_ref)
            values = jnp.concatenate([v_s[b] for b in blocks], axis=0)
            dprob = dot(values, turned_cot)
            dscore = (jnp.exp(scores - lse) * (dprob - delta)).astype(BF16)
            turned_k = jnp.concatenate([kt_s[b] for b in blocks], axis=1)
            out_s[...] += dot(turned_k, dscore)
            grads = dot(dscore, q_stack)
            for u, b in enumerate(blocks):
                acc_s[b] += grads[u * BLOCK : (u + 1) * BLOCK]
            return carry

        lax.fori_loop(0, groups_ref[i], step, 0)
        partner = jnp.exp(sp_ref[i] - lse) * (dp_ref[i] - delta)
        partner = tall(partner.astype(BF16).astype(F32))
        dsp_ref[i] = partner.astype(BF16)
        wide = spread(partner)
        grad_query = head_rows(out_s[...]).T
        for m in range(EXPANDERS):
            grad_query += wide[:, m * COLS : (m + 1) * COLS] * pair_ref[m * Q_BLOCKS + i][:, :COLS].astype(F32)
        gq_ref[q_rows(i), :] = (grad_query * (1.0 / math.sqrt(HEAD))).astype(BF16)
        return carry

    lax.fori_loop(0, Q_BLOCKS, per_block, 0)
    store_parts(acc_s, own_ref, halo_ref, gout_ref)


def scatter_into(acc_s, index_rows, data):
    subs = iota((NODES_HERE, BLOCK), 0)
    hot = jnp.concatenate([(subs == row).astype(F32).astype(BF16) for row in index_rows], axis=1)
    acc_s[...] += dot(hot, data)


def gather_grads(own_ref, ret_ref, rows_ref, part_ref, pexp_ref, others, first_col, gsum_ref, gid_ref, acc_s, term_s):
    acc_s[...] = own_ref[...]

    def halo(t, carry):
        index_rows = [rows_ref[pl.ds(t * GROUP + u, 1), :] for u in range(GROUP)]
        data = jnp.concatenate([ret_ref[t * GROUP + u] for u in range(GROUP)], axis=0)
        scatter_into(acc_s, index_rows, data)
        return carry

    lax.fori_loop(0, SENDERS // GROUP, halo, 0)
    for m, other in enumerate(others):
        row_id = iota((16, COLS), 0)
        lane = iota((16, COLS), 1)
        picks = (row_id == jnp.where(lane < HEAD, m, 8 + m)).astype(F32).astype(BF16)

        def partner(t, carry):
            index_rows, data = [], []
            for u in range(GROUP):
                i = t * GROUP + u
                index_rows.append(pexp_ref[pl.ds(m * Q_BLOCKS + i, 1), :])
                wide = dot(part_ref[m, i].astype(F32).T.astype(BF16), picks)
                rows = other[q_rows(i), first_col : first_col + COLS].astype(F32)
                data.append((wide * rows).astype(BF16))
            scatter_into(acc_s, index_rows, jnp.concatenate(data, axis=0))
            return carry

        lax.fori_loop(0, Q_BLOCKS // GROUP, partner, 0)
    scatter_into(acc_s, [gid_ref[...]], gsum_ref[...])


def value_back_kernel(
    own_ref, ret_ref, rows_ref, part_ref, pexp_ref, o0_ref, o1_ref, o2_ref, o3_ref, gsum_ref, gid_ref, wv_ref,
    grad_ref, acc_s,
):
    gather_grads(
        own_ref, ret_ref, rows_ref, part_ref, pexp_ref, (o0_ref, o1_ref, o2_ref, o3_ref), COLS, gsum_ref, gid_ref,
        acc_s, None,
    )
    grad_ref[...] = acc_s[...].astype(BF16)


def key_back_kernel(
    feat_ref, own_ref, ret_ref, rows_ref, part_ref, pexp_ref, o0_ref, o1_ref, o2_ref, o3_ref, gsum_ref, gid_ref,
    wq_ref, wk_ref, wv_ref, gq_ref, gv_ref, t0_ref, t1_ref, t2_ref, t3_ref, acc_s,
):
    gather_grads(
        own_ref, ret_ref, rows_ref, part_ref, pexp_ref, (o0_ref, o1_ref, o2_ref, o3_ref), 0, gsum_ref, gid_ref,
        acc_s, None,
    )
    grad_key = acc_s[...].astype(BF16)
    for k, out in enumerate((t0_ref, t1_ref, t2_ref, t3_ref)):
        part = pl.ds(pl.multiple_of(((feat_ref[0] + k) % 4) * COLS, COLS), COLS)
        term = dot_nt(gq_ref[...], wq_ref[part, :]) + dot_nt(gv_ref[...], wv_ref[part, :])
        term = term + dot_nt(grad_key, wk_ref[part, :])
        out[...] = term.astype(out.dtype)


def shape(dims, kind=BF16):
    return jax.ShapeDtypeStruct(dims, kind)


def call(kernel, ins, outs, args, scratch=(), name=None, flops=0, out_spaces=None):
    cost = pl.CostEstimate(flops=flops, transcendentals=0, bytes_accessed=4_000_000)
    return pl.pallas_call(
        kernel,
        out_shape=outs,
        in_specs=ins,
        out_specs=out_spaces or tuple(vmem() for _ in outs),
        scratch_shapes=list(scratch),
        compiler_params=params(),
        cost_estimate=cost,
        name=name,
    )(*args)


def reduce_rows(part):
    width = part.shape[1]
    own = lax.all_to_all(part.reshape(SENDERS, 4, width), "dom", 0, 0, tiled=True)
    return own.astype(F32).sum(0).astype(BF16)


def spread_rows(rows):
    width = rows.shape[1]
    copies = jnp.broadcast_to(rows[None], (SENDERS, 4, width))
    return lax.all_to_all(copies, "dom", 0, 0, tiled=True).reshape(BLOCK, width)


def on_device(
    features,
    w_query,
    w_key,
    w_value,
    cotangent,
    send_rows,
    halo_count,
    block_mask,
    exp_rows,
    global_ids,
):
    dom_count = lax.axis_size("dom")
    my_index = lax.axis_index("dom")

    def swapped(value, bit):
        return lax.ppermute(value, "dom", [(i, i ^ (1 << bit)) for i in range(dom_count)])

    rows = send_rows[0]
    local = jnp.where(global_ids // NODES_HERE == my_index, global_ids % NODES_HERE, -1).reshape(1, BLOCK)
    exp_list = exp_rows.reshape(EXPANDERS * Q_BLOCKS, BLOCK)
    pexp = jnp.concatenate(
        [swapped(exp_list[m * Q_BLOCKS : (m + 1) * Q_BLOCKS], m) for m in range(EXPANDERS)], axis=0
    )

    query, paired, out_k, out_v, glob_part = call(
        project_kernel,
        [vmem()] * 6,
        (
            shape((NODES_HERE, COLS)),
            shape((NODES_HERE, 2 * COLS)),
            shape((SENDERS, BLOCK, COLS)),
            shape((SENDERS, BLOCK, COLS)),
            shape((BLOCK, 2 * COLS)),
        ),
        (features, w_query, w_key, w_value, rows, local),
        name="project",
        flops=3_000_000_000,
    )
    halo_k = lax.all_to_all(out_k, "dom", 0, 0, tiled=True)
    glob = spread_rows(reduce_rows(glob_part))
    swaps = [swapped(paired, m) for m in range(EXPANDERS)]
    halo_v = lax.all_to_all(out_v, "dom", 0, 0, tiled=True)
    others = [swapped(jnp.concatenate([query, cotangent], axis=1), m) for m in range(EXPANDERS)]

    plan = call(
        plan_kernel,
        [smem()] * 2,
        (shape((Q_BLOCKS * LIST,), jnp.int32), shape((Q_BLOCKS,), jnp.int32), shape((LIST,), jnp.int32)),
        (block_mask.reshape(-1), halo_count.reshape(-1)),
        name="plan",
        out_spaces=(smem(), smem(), smem()),
    )
    (pairs,) = call(
        partner_kernel,
        [vmem()] * 5,
        (shape((EXPANDERS * Q_BLOCKS, BLOCK, 2 * COLS)),),
        (exp_list, *swaps),
        name="partners",
        flops=2_000_000_000,
    )
    blocks_f = pltpu.VMEM((KEY_BLOCKS, BLOCK, COLS), F32)
    blocks_b = pltpu.VMEM((KEY_BLOCKS, BLOCK, COLS), BF16)
    lse, partner_scores = call(
        score_kernel,
        [smem()] * 3 + [vmem()] * 5,
        (shape((Q_BLOCKS, 2 * BLOCK), F32), shape((Q_BLOCKS, 8, 2 * BLOCK), F32)),
        (*plan, query, paired, halo_k, glob, pairs),
        scratch=[blocks_b],
        name="scores",
        flops=6_000_000_000,
    )
    attended, own_v, back_v, glob_v, weight_p, dprob_p, delta = call(
        value_kernel,
        [smem()] * 3 + [vmem()] * 9,
        (
            shape((NODES_HERE, COLS)),
            shape((NODES_HERE, COLS), F32),
            shape((SENDERS, BLOCK, COLS)),
            shape((BLOCK, COLS)),
            shape((Q_BLOCKS, 16, BLOCK)),
            shape((Q_BLOCKS, 8, 2 * BLOCK), F32),
            shape((Q_BLOCKS, 2 * BLOCK), F32),
        ),
        (*plan, query, paired, halo_k, halo_v, glob, pairs, cotangent, lse, partner_scores),
        scratch=[blocks_b, blocks_b, blocks_f, pltpu.VMEM((COLS, 2 * BLOCK), F32)],
        name="values",
        flops=15_000_000_000,
    )
    returned_v = lax.all_to_all(back_v, "dom", 0, 0, tiled=True)
    wp_back = jnp.stack([swapped(weight_p, m) for m in range(EXPANDERS)])
    gsum_v = spread_rows(reduce_rows(glob_v))
    grad_query, own_k, back_k, glob_k, dscore_p = call(
        key_kernel,
        [smem()] * 3 + [vmem()] * 11,
        (
            shape((NODES_HERE, COLS)),
            shape((NODES_HERE, COLS), F32),
            shape((SENDERS, BLOCK, COLS)),
            shape((BLOCK, COLS)),
            shape((Q_BLOCKS, 16, BLOCK)),
        ),
        (*plan, query, paired, halo_k, halo_v, glob, pairs, cotangent, lse, partner_scores, dprob_p, delta),
        scratch=[blocks_b, blocks_b, blocks_b, blocks_f, pltpu.VMEM((COLS, 2 * BLOCK), F32)],
        name="keys",
        flops=18_000_000_000,
    )
    returned_k = lax.all_to_all(back_k, "dom", 0, 0, tiled=True)
    ds_back = jnp.stack([swapped(dscore_p, m) for m in range(EXPANDERS)])
    gsum_k = spread_rows(reduce_rows(glob_k))
    acc = [pltpu.VMEM((NODES_HERE, COLS), F32)]
    (grad_value,) = call(
        value_back_kernel,
        [vmem()] * 12,
        (shape((NODES_HERE, COLS)),),
        (own_v, returned_v, rows, wp_back, pexp, *others, gsum_v, local, w_value),
        scratch=acc,
        name="value_back",
        flops=5_000_000_000,
    )
    mine, *away = call(
        key_back_kernel,
        [smem()] + [vmem()] * 16,
        (shape((NODES_HERE, COLS), F32),) + tuple(shape((NODES_HERE, COLS)) for _ in range(3)),
        (
            lax.axis_index("feat").reshape(1).astype(jnp.int32), own_k, returned_k, rows, ds_back, pexp, *others,
            gsum_k, local, w_query, w_key, w_value, grad_query, grad_value,
        ),
        scratch=acc,
        name="key_back",
        flops=5_000_000_000,
    )
    for k, term in enumerate(away, 1):
        mine = mine + lax.ppermute(term, "feat", [(i, (i + k) % 4) for i in range(4)]).astype(F32)
    return (attended, mine.astype(BF16))


def solution(mesh):
    return jax.shard_map(
        on_device,
        mesh=mesh,
        in_specs=(
            P("dom", None),
            P(None, "feat"),
            P(None, "feat"),
            P(None, "feat"),
            P("dom", "feat"),
            P("dom", None, None),
            P(None, "dom"),
            P("dom", None),
            P(None, "dom"),
            P(),
        ),
        out_specs=(P("dom", "feat"), P("dom", "feat")),
        check_vma=False,
    )
```

time: 594 us -> 360 us (0.61); the launches traced: 586 us -> 358 us
  Pallas kernels: 0 us -> 139 us
  matrix products: 128 us -> 0 us
  local copies, waits for them, and re-layouts: 118 us -> 6.4 us
  other arithmetic: 109 us -> 4.63 us
  waiting for transfers between devices: 186 us -> 94.4 us
  blocking collectives: 0 us -> 58.9 us
  starting transfers between devices: 22.3 us -> 53.7 us
  between operations: 14.5 us -> 0.89 us
  loops' own time: 7.23 us -> 0 us
    psum x2 -> x0, waiting for transfers between devices: 141 us -> none  [the longest x1 93.9 us: on_device(): global_pairs = lax.psum(picked.astype(jnp.bfloat16), 'dom')]
    pallas_call x0 -> x8, Pallas kernels: none -> 139 us  [call(): pl.pallas_call(kernel, out_shape=outs, in_specs=ins, out_specs=out_spaces...]
    dot_general x54 -> x0, matrix products: 128 us -> none  [the longest x4 35.7 us: one_block(): jnp.einsum('rhk,rhe->khe', local_weight, grad_blk, preferred_element_type...]
    all_to_all x0 -> x4, blocking collectives: none -> 58.9 us  [the longest x2 36.9 us: reduce_rows(): lax.all_to_all(part.reshape(SENDERS, 4, width), 'dom', 0, 0, tiled=True)]
    ppermute x8 -> x23, waiting for transfers between devices: 16.8 us -> 69 us  [the longest x20 55.2 us: swapped(): lax.ppermute(value, 'dom', [(i, i ^ 1 << bit) for i in range(dom_count)])]
    gather x6 -> x0, local copies, waits for them, and re-layouts: 37.4 us -> none  [the longest x4 18.9 us: on_device(): partner_list.append(swapped[exp_rows[matching]])]
    convert_element_type x14 -> x1, other arithmetic: 35.4 us -> 1.87 us  [on_device(): return (attended, mine.astype(BF16))]
    reduce_scatter x1 -> x0, waiting for transfers between devices: 28.8 us -> none  [on_device(): lax.psum_scatter(feature_terms, 'feat', scatter_dimension=1, tiled=True)]
  transfers between devices with their start and end apart: 13 -> 29, of which waited for: 6 -> 13; matrix products, arithmetic and copies ran while one was open for 21% -> 1% of each run, Pallas kernels for 0% -> 13%
where the time goes in v1:
time: 360 us; the launch traced here: 358 us
  Pallas kernels  139 us (39%)
  waiting for transfers between devices  94.4 us (26%)
  blocking collectives  58.9 us (16%)
  starting transfers between devices  53.7 us (15%)
  local copies, waits for them, and re-layouts  6.4 us (2%)
  other arithmetic  4.63 us (1%)
    pallas_call x8, Pallas kernels, call(): pl.pallas_call(kernel, out_shape=outs, in_specs=ins, out_specs=out_spaces...  139 us
    ppermute x20, waiting for transfers between devices, swapped(): lax.ppermute(value, 'dom', [(i, i ^ 1 << bit) for i in range(dom_count)])  55.2 us
    all_to_all x2, blocking collectives, reduce_rows(): lax.all_to_all(part.reshape(SENDERS, 4, width), 'dom', 0, 0, tiled=True)  36.9 us
    ppermute x20, starting transfers between devices, swapped(): lax.ppermute(value, 'dom', [(i, i ^ 1 << bit) for i in range(dom_count)])  23.8 us
    all_to_all x2, blocking collectives, spread_rows(): return lax.all_to_all(copies, 'dom', 0, 0, tiled=True).reshape(BLOCK, width)  21.9 us
    ppermute x3, waiting for transfers between devices, on_device(): lax.ppermute(term, 'feat', [(i, (i + k) % 4) for i in range(4)]).astype(F32)  13.8 us
    all_to_all x1, waiting for transfers between devices, on_device(): halo_k = lax.all_to_all(out_k, 'dom', 0, 0, tiled=True)  10.7 us
    all_to_all x1, waiting for transfers between devices, reduce_rows(): lax.all_to_all(part.reshape(SENDERS, 4, width), 'dom', 0, 0, tiled=True)  7.38 us
  transfers between devices with their start and end apart: 29, of which 13 were waited for; matrix products, arithmetic and copies ran while one was open for 1% of the time, Pallas kernels for 13%

profile of v1, /device:TPU:0, one launch (start us, length us, event | category | flops | bytes accessed | tf_op | source)
XLA Modules:
  0.0 357.7 jit_solution(11265601778739239256)
XLA Ops:
  0.6 1.2 fusion.gid_ref
  1.9 12.6 %project.1 = (bf16[1024,128]{1,0:T(8,128)(2,1)}, bf16[1024,256]{1,0:T(8,128)(2,1)}, bf16[32,128,128]{2,1,0:T(8,128)(2,1)}, bf16[32,128,128]{2,1,0:T(8,128)(2,1)}, bf16[128,256]{1,0:T(8,128)(2,1)}) custom-call(bf16[1024,512]{1,0:T(8,128)(2,1)} %x_ref.1, bf16[512,128]{1,0:T(8,128)(2,1)} %wq_ref.3, bf16[512,128]{1,0:T(8,128)(2,1)} %wk_ref.3, ...), custom_call_target="tpu_custom_call" | custom-call | flops 3000000000 | bytes 4000000 | tf_op jit(solution)/shard_map/project/pallas_call | solution.py:413
  14.5 0.9 reshape.47
  15.4 15.6 %all_to_all.50 = bf16[32,4,256]{2,1,0:T(4,128)(2,1)S(1)} all-to-all(bf16[32,4,256]{2,1,0:T(4,128)(2,1)S(1)} %reshape.47), channel_id=1, replica_groups=mesh['dom'=32,'feat'=4] {'dom'}, dimensions={0} | all-to-all | bytes 131072 | tf_op jit(solution)/shard_map/all_to_all | solution.py:427
  31.0 0.1 reduce_sum.36
  31.0 10.9 %all_to_all.51 = bf16[32,4,256]{2,1,0:T(4,128)(2,1)S(1)} all-to-all(bf16[32,4,256]{2,1,0:T(4,128)(2,1)S(1)} %broadcast_in_dim.8), channel_id=1, replica_groups=mesh['dom'=32,'feat'=4] {'dom'}, dimensions={0} | all-to-all | bytes 131072 | tf_op jit(solution)/shard_map/all_to_all | solution.py:434
  41.9 4.1 %all-to-all-start = ((bf16[32,128,128]{2,1,0:T(8,128)(2,1)}), bf16[32,128,128]{2,1,0:T(8,128)(2,1)S(1)}, u32[]{:S(2)}, u32[]{:S(2)}) async-start(bf16[32,128,128]{2,1,0:T(8,128)(2,1)} %get-tuple-element.33), calls=%async_computation | async-start | bytes 2097152 | tf_op jit(solution)/shard_map/all_to_all | solution.py:476
  46.0 0.2 collective-permute-start
  46.2 1.7 collective-permute-start.1
  47.9 2.7 collective-permute-start.2
  50.6 1.5 collective-permute-start.3
  52.1 10.7 %all-to-all-done.hk_ref = bf16[32,128,128]{2,1,0:T(8,128)(2,1)S(1)} async-done(((bf16[32,128,128]{2,1,0:T(8,128)(2,1)}), bf16[32,128,128]{2,1,0:T(8,128)(2,1)S(1)}, u32[]{:S(2)}, u32[]{:S(2)}) %all-to-all-start) | async-done | bytes 1048608 | tf_op jit(solution)/shard_map/all_to_all | solution.py:476
  62.8 4.5 %all-to-all-start.1 = ((bf16[32,128,128]{2,1,0:T(8,128)(2,1)}), bf16[32,128,128]{2,1,0:T(8,128)(2,1)S(1)}, u32[]{:S(2)}, u32[]{:S(2)}) async-start(bf16[32,128,128]{2,1,0:T(8,128)(2,1)} %get-tuple-element.34), calls=%async_computation.1 | async-start | bytes 2097152 | tf_op jit(solution)/shard_map/all_to_all | solution.py:479
  67.3 0.7 reshape.44.mask_ref
  68.0 0.6 reshape.49.exp_ref
  68.6 4.4 %plan.1 = (s32[384]{0:T(512)}, s32[8]{0:T(128)}, s32[48]{0:T(128)}) custom-call(s32[320]{0:T(512)} %reshape.44.mask_ref, s32[32]{0:T(128)} %bitcast.36), custom_call_target="tpu_custom_call" | custom-call | bytes 4000000 | tf_op jit(solution)/shard_map/plan/pallas_call | solution.py:413
  73.0 0.7 reshape.48.glob_ref
  73.7 19.5 %collective-permute-done.2.t2_ref = bf16[1024,256]{1,0:T(8,128)(2,1)} collective-permute-done((bf16[1024,256]{1,0:T(8,128)(2,1)S(1)}, bf16[1024,256]{1,0:T(8,128)(2,1)}, u32[]{:S(2)}, u32[]{:S(2)}) %collective-permute-start.2) | collective-permute-done | bytes 524320 | tf_op jit(solution)/shard_map/ppermute | solution.py:453
  93.2 11.8 %partners.1.pair_ref = bf16[32,128,256]{2,1,0:T(8,128)(2,1)} custom-call(s32[32,128]{1,0:T(8,128)} %reshape.49.exp_ref, bf16[1024,256]{1,0:T(8,128)(2,1)} %copy-done.12, bf16[1024,256]{1,0:T(8,128)(2,1)} %collective-permute-done.1.t1_ref, bf16[1024,256]{1,0:T(8,128)(2,1)} %collective-permute-done.2.t2_ref, bf16[1024,256]{1,0:T(8,128)(2,1)} %collective-permute-done.3.t3_ref), custom_call_target="tpu_custom_call" | custom-call | flops 2000000000 | bytes 4000000 | tf_op jit(solution)/shard_map/partners/pallas_call | solution.py:413
  105.0 19.2 %scores.1 = (f32[8,256]{1,0:T(8,128)}, f32[8,8,256]{2,1,0:T(8,128)}) custom-call(s32[384]{0:T(512)} %get-tuple-element.28.list_ref, s32[8]{0:T(128)} %get-tuple-element.29.groups_ref, s32[48]{0:T(128)} %get-tuple-element.30.live_ref, bf16[1024,128]{1,0:T(8,128)(2,1)} %get-tuple-element.31.q_ref, bf16[1024,256]{1,0:T(8,128)(2,1)} %get-tuple-element.32.kv_ref, ...), custom_call_target="tpu_custom_call" | custom-call | flops 6000000000 | bytes 4000000 | tf_op jit(solution)/shard_map/scores/pallas_call | solution.py:413
  124.2 1.0 copy-done.3
  125.2 32.4 %values.1 = (bf16[1024,128]{1,0:T(8,128)(2,1)}, f32[1024,128]{1,0:T(8,128)}, bf16[32,128,128]{2,1,0:T(8,128)(2,1)}, bf16[128,128]{1,0:T(8,128)(2,1)}, bf16[8,16,...) custom-call(s32[384]{0:T(512)} %get-tuple-element.28.list_ref, s32[8]{0:T(128)} %get-tuple-element.29.groups_ref, ...), custom_call_target="tpu_custom_call" | custom-call | flops 15000000512 | bytes 4000000 | tf_op jit(solution)/shard_map/values/pallas_call | solution.py:413
  157.6 33.5 %keys.1 = (bf16[1024,128]{1,0:T(8,128)(2,1)}, f32[1024,128]{1,0:T(8,128)}, bf16[32,128,128]{2,1,0:T(8,128)(2,1)}, bf16[128,128]{1,0:T(8,128)(2,1)}, bf16[8,16,128]{2,1,0:T(8,128)(2,1)}) custom-call(s32[384]{0:T(512)} %get-tuple-element.28.list_ref, s32[8]{0:T(128)} %get-tuple-element.29.groups_ref, s32[48]{0:T(128)} %get-tuple-element.30.live_ref, ...), custom_call_target="tpu_custom_call" | custom-call | flops 17999998976 | bytes 4000000 | tf_op jit(solution)/shard_map/keys/pallas_call | solution.py:413
  191.1 21.4 %all_to_all.52 = bf16[32,4,128]{2,1,0:T(4,128)(2,1)S(1)} all-to-all(bf16[32,4,128]{2,1,0:T(4,128)(2,1)} %bitcast.23), channel_id=1, replica_groups=mesh['dom'=32,'feat'=4] {'dom'}, dimensions={0} | all-to-all | bytes 65536 | tf_op jit(solution)/shard_map/all_to_all | solution.py:427
  212.4 3.8 %all-to-all-start.8 = ((bf16[32,4,128]{2,1,0:T(4,128)(2,1)}), bf16[32,4,128]{2,1,0:T(4,128)(2,1)S(1)}, u32[]{:S(2)}, u32[]{:S(2)}) async-start(bf16[32,4,128]{2,1,0:T(4,128)(2,1)} %bitcast.18), calls=%async_computation.8 | async-start | bytes 65536 | tf_op jit(solution)/shard_map/all_to_all | solution.py:427
  216.3 7.4 %all-to-all-done.8 = bf16[32,4,128]{2,1,0:T(4,128)(2,1)S(1)} async-done(((bf16[32,4,128]{2,1,0:T(4,128)(2,1)}), bf16[32,4,128]{2,1,0:T(4,128)(2,1)S(1)}, u32[]{:S(2)}, u32[]{:S(2)}) %all-to-all-start.8) | async-done | bytes 32800 | tf_op jit(solution)/shard_map/all_to_all | solution.py:427
  223.7 0.6 broadcast_in_dim.9
  224.3 3.8 %all-to-all-start.6 = ((bf16[32,4,128]{2,1,0:T(4,128)(2,1)}), bf16[32,4,128]{2,1,0:T(4,128)(2,1)S(1)}, u32[]{:S(2)}, u32[]{:S(2)}) async-start(bf16[32,4,128]{2,1,0:T(4,128)(2,1)} %broadcast_in_dim.9), calls=%async_computation.6 | async-start | bytes 65536 | tf_op jit(solution)/shard_map/all_to_all | solution.py:434
  228.2 7.4 %all-to-all-done.6 = bf16[32,4,128]{2,1,0:T(4,128)(2,1)S(1)} async-done(((bf16[32,4,128]{2,1,0:T(4,128)(2,1)}), bf16[32,4,128]{2,1,0:T(4,128)(2,1)S(1)}, u32[]{:S(2)}, u32[]{:S(2)}) %all-to-all-start.6) | async-done | bytes 32800 | tf_op jit(solution)/shard_map/all_to_all | solution.py:434
  235.6 11.1 %all_to_all.53 = bf16[32,4,128]{2,1,0:T(4,128)(2,1)} all-to-all(bf16[32,4,128]{2,1,0:T(4,128)(2,1)S(1)} %broadcast_in_dim.10), channel_id=1, replica_groups=mesh['dom'=32,'feat'=4] {'dom'}, dimensions={0} | all-to-all | bytes 65536 | tf_op jit(solution)/shard_map/all_to_all | solution.py:434
  246.7 3.9 %all-to-all-start.7 = ((bf16[32,128,128]{2,1,0:T(8,128)(2,1)}), bf16[32,128,128]{2,1,0:T(8,128)(2,1)S(1)}, u32[]{:S(2)}, u32[]{:S(2)}) async-start(bf16[32,128,128]{2,1,0:T(8,128)(2,1)} %get-tuple-element.47), calls=%async_computation.7 | async-start | bytes 2097152 | tf_op jit(solution)/shard_map/all_to_all | solution.py:526
  250.6 0.2 collective-permute-start.8
  250.9 1.7 collective-permute-start.9
  252.6 2.7 collective-permute-start.10
  255.3 1.5 collective-permute-start.11
  256.8 0.1 constant_dynamic-update-slice_fusion.4
  256.9 0.6 collective-permute-start.7
  257.5 0.8 collective-permute-start.6
  258.3 3.4 collective-permute-done.9
  261.8 3.3 collective-permute-done.11
  265.1 0.3 collective-permute-done.7
  265.4 1.5 collective-permute-start.13
  266.9 2.7 collective-permute-start.14
  269.6 2.1 collective-permute-start.15
  271.7 5.5 %all-to-all-start.4 = ((bf16[32,128,128]{2,1,0:T(8,128)(2,1)}), bf16[32,128,128]{2,1,0:T(8,128)(2,1)S(1)}, u32[]{:S(2)}, u32[]{:S(2)}) async-start(bf16[32,128,128]{2,1,0:T(8,128)(2,1)} %get-tuple-element.42), calls=%async_computation.4 | async-start | bytes 2097152 | tf_op jit(solution)/shard_map/all_to_all | solution.py:544
  277.3 1.9 collective-permute-start.19
  279.1 16.3 %collective-permute-done.19 = bf16[8,16,128]{2,1,0:T(8,128)(2,1)S(1)} collective-permute-done((bf16[8,16,128]{2,1,0:T(8,128)(2,1)S(1)}, bf16[8,16,128]{2,1,0:T(8,128)(2,1)S(1)}, u32[]{:S(2)}, u32[]{:S(2)}) %collective-permute-start.19) | collective-permute-done | bytes 32800 | tf_op jit(solution)/shard_map/ppermute | solution.py:453
  295.5 1.1 collective-permute-start.18
  296.6 8.6 %collective-permute-done.18 = bf16[8,16,128]{2,1,0:T(8,128)(2,1)S(1)} collective-permute-done((bf16[8,16,128]{2,1,0:T(8,128)(2,1)S(1)}, bf16[8,16,128]{2,1,0:T(8,128)(2,1)S(1)}, u32[]{:S(2)}, u32[]{:S(2)}) %collective-permute-start.18) | collective-permute-done | bytes 32800 | tf_op jit(solution)/shard_map/ppermute | solution.py:453
  305.2 0.8 collective-permute-start.17
  306.0 3.1 collective-permute-done.17
  309.1 0.7 pad_maximum_fusion.part_ref
  309.8 0.5 collective-permute-done.16
  310.3 0.7 pad_maximum_fusion.1.part_ref
  311.1 0.8 copy-done.10
  311.9 11.9 %value_back.1.gv_ref = bf16[1024,128]{1,0:T(8,128)(2,1)} custom-call(f32[1024,128]{1,0:T(8,128)} %get-tuple-element.46.own_ref, bf16[32,128,128]{2,1,0:T(8,128)(2,1)} %copy-done, s32[32,128]{1,0:T(8,128)} %bitcast.38, bf16[4,8,16,128]{3,2,1,0:T(8,128)(2,1)} %pad_maximum_fusion.1.part_ref, s32[32,128]{1,0:T(8,128)} %copy-done.9, ...), custom_call_target="tpu_custom_call" | custom-call | flops 5000000000 | bytes 4000000 | tf_op jit(solution)/shard_map/value_back/pallas_call | solution.py:413
  323.7 1.0 copy-done.1
  324.7 13.0 %key_back.1 = (f32[1024,128]{1,0:T(8,128)}, bf16[1024,128]{1,0:T(8,128)(2,1)}, bf16[1024,128]{1,0:T(8,128)(2,1)}, bf16[1024,128]{1,0:T(8,128)(2,1)}) custom-call(s32[1]{0:T(128)} %bitcast.3.feat_ref, f32[1024,128]{1,0:T(8,128)} %get-tuple-element.41.own_ref, bf16[32,128,128]{2,1,0:T(8,128)(2,1)} %copy-done.1, s32[32,128]{1,0:T(8,128)} %bitcast.39, ...), custom_call_target="tpu_custom_call" | custom-call | flops 5000000000 | bytes 4000000 | tf_op jit(solution)/shard_map/key_back/pallas_call | solution.py:413
  337.7 2.7 collective-permute-start.22
  340.4 0.6 collective-permute-start.21
  341.1 1.0 collective-permute-start.20
  342.0 10.3 %collective-permute-done.22 = bf16[1024,128]{1,0:T(8,128)(2,1)S(1)} collective-permute-done((bf16[1024,128]{1,0:T(8,128)(2,1)}, bf16[1024,128]{1,0:T(8,128)(2,1)S(1)}, u32[]{:S(2)}, u32[]{:S(2)}) %collective-permute-start.22) | collective-permute-done | bytes 262176 | tf_op jit(solution)/shard_map/ppermute | solution.py:570
  352.3 3.6 collective-permute-done.20
  355.9 1.9 add_convert_fusion
  (57 shorter events, 0.3 us)
Async XLA Ops:
  14.5 31.5 %copy-start.11 = (bf16[1024,256]{1,0:T(8,128)(2,1)S(1)}, bf16[1024,256]{1,0:T(8,128)(2,1)}, u32[]{:S(2)}) copy-start(bf16[1024,256]{1,0:T(8,128)(2,1)} %get-tuple-element.32.kv_ref) | copy-start | bytes 1572868
  41.9 25.4 %copy-start.8 = (s32[8,40]{1,0:T(8,128)S(1)}, s32[8,40]{1,0:T(8,128)}, u32[]{:S(2)}) copy-start(s32[8,40]{1,0:T(8,128)} %param.17) | copy-start | bytes 3844
  41.9 26.0 %copy-start.6 = (s32[4,1024]{1,0:T(4,128)S(1)}, s32[4,1024]{1,0:T(4,128)}, u32[]{:S(2)}) copy-start(s32[4,1024]{1,0:T(4,128)} %param.18) | copy-start | bytes 49156
  41.9 20.9 %all-to-all-start = ((bf16[32,128,128]{2,1,0:T(8,128)(2,1)}), bf16[32,128,128]{2,1,0:T(8,128)(2,1)S(1)}, u32[]{:S(2)}, u32[]{:S(2)}) async-start(bf16[32,128,128]{2,1,0:T(8,128)(2,1)} %get-tuple-element.33), calls=%async_computation | async-start | bytes 2097152 | tf_op jit(solution)/shard_map/all_to_all | solution.py:476
  46.0 27.7 %collective-permute-start = (bf16[1024,256]{1,0:T(8,128)(2,1)S(1)}, bf16[1024,256]{1,0:T(8,128)(2,1)S(1)}, u32[]{:S(2)}, u32[]{:S(2)}) collective-permute-start(bf16[1024,256]{1,0:T(8,128)(2,1)S(1)} %copy-done.11), channel_id=1, source_target_pairs={{0,4},{4,0},{8,12},{12,8},{16,20},{20,16},{24,28},{28,24},{32,36},... | collective-permute-start | bytes 1572872 | tf_op jit(solution)/shard_map/ppermute | solution.py:453
  46.2 27.5 %collective-permute-start.1 = (bf16[1024,256]{1,0:T(8,128)(2,1)S(1)}, bf16[1024,256]{1,0:T(8,128)(2,1)}, u32[]{:S(2)}, u32[]{:S(2)}) collective-permute-start(bf16[1024,256]{1,0:T(8,128)(2,1)S(1)} %copy-done.11), channel_id=1, source_target_pairs={{0,8},{4,12},{8,0},{12,4},{16,24},{20,28},{24,16},{28,20},{32,40},... | collective-permute-start | bytes 1572872 | tf_op jit(solution)/shard_map/ppermute | solution.py:453
  47.9 45.3 %collective-permute-start.2 = (bf16[1024,256]{1,0:T(8,128)(2,1)S(1)}, bf16[1024,256]{1,0:T(8,128)(2,1)}, u32[]{:S(2)}, u32[]{:S(2)}) collective-permute-start(bf16[1024,256]{1,0:T(8,128)(2,1)S(1)} %copy-done.11), channel_id=1, source_target_pairs={{0,16},{4,20},{8,24},{12,28},{16,0},{20,4},{24,8},{28,12},{32,48},... | collective-permute-start | bytes 1572872 | tf_op jit(solution)/shard_map/ppermute | solution.py:453
  50.6 42.6 %collective-permute-start.3 = (bf16[1024,256]{1,0:T(8,128)(2,1)S(1)}, bf16[1024,256]{1,0:T(8,128)(2,1)}, u32[]{:S(2)}, u32[]{:S(2)}) collective-permute-start(bf16[1024,256]{1,0:T(8,128)(2,1)S(1)} %copy-done.11), channel_id=1, source_target_pairs={{0,32},{4,36},{8,40},{12,44},{16,48},{20,52},{24,56},{28,60},{32,0... | collective-permute-start | bytes 1572872 | tf_op jit(solution)/shard_map/ppermute | solution.py:453
  62.8 42.2 %copy-start.2 = (bf16[32,128,128]{2,1,0:T(8,128)(2,1)}, bf16[32,128,128]{2,1,0:T(8,128)(2,1)S(1)}, u32[]{:S(2)}) copy-start(bf16[32,128,128]{2,1,0:T(8,128)(2,1)S(1)} %all-to-all-done.hk_ref) | copy-start | bytes 3145732
  62.8 61.4 %all-to-all-start.1 = ((bf16[32,128,128]{2,1,0:T(8,128)(2,1)}), bf16[32,128,128]{2,1,0:T(8,128)(2,1)S(1)}, u32[]{:S(2)}, u32[]{:S(2)}) async-start(bf16[32,128,128]{2,1,0:T(8,128)(2,1)} %get-tuple-element.34), calls=%async_computation.1 | async-start | bytes 2097152 | tf_op jit(solution)/shard_map/all_to_all | solution.py:479
  73.7 19.5 %copy-start.12 = (bf16[1024,256]{1,0:T(8,128)(2,1)}, bf16[1024,256]{1,0:T(8,128)(2,1)S(1)}, u32[]{:S(2)}) copy-start(bf16[1024,256]{1,0:T(8,128)(2,1)S(1)} %collective-permute-done.t0_ref) | copy-start | bytes 1572868
  124.2 1.0 copy-start.3
  191.1 65.7 %copy-start.5 = (bf16[1024,128]{1,0:T(8,128)(2,1)S(1)}, bf16[1024,128]{1,0:T(8,128)(2,1)}, u32[]{:S(2)}) copy-start(bf16[1024,128]{1,0:T(8,128)(2,1)} %get-tuple-element.31.q_ref) | copy-start | bytes 786436
  191.1 65.8 %copy-start.4 = (bf16[1024,128]{1,0:T(8,128)(2,1)S(1)}, bf16[1024,128]{1,0:T(8,128)(2,1)}, u32[]{:S(2)}) copy-start(bf16[1024,128]{1,0:T(8,128)(2,1)} %cot_ref.3) | copy-start | bytes 786436
  191.1 65.8 %copy-start.14 = (bf16[8,16,128]{2,1,0:T(8,128)(2,1)S(1)}, bf16[8,16,128]{2,1,0:T(8,128)(2,1)}, u32[]{:S(2)}) copy-start(bf16[8,16,128]{2,1,0:T(8,128)(2,1)} %get-tuple-element.43) | copy-start | bytes 98308
  212.4 11.2 %all-to-all-start.8 = ((bf16[32,4,128]{2,1,0:T(4,128)(2,1)}), bf16[32,4,128]{2,1,0:T(4,128)(2,1)S(1)}, u32[]{:S(2)}, u32[]{:S(2)}) async-start(bf16[32,4,128]{2,1,0:T(4,128)(2,1)} %bitcast.18), calls=%async_computation.8 | async-start | bytes 65536 | tf_op jit(solution)/shard_map/all_to_all | solution.py:427
  224.3 11.3 %all-to-all-start.6 = ((bf16[32,4,128]{2,1,0:T(4,128)(2,1)}), bf16[32,4,128]{2,1,0:T(4,128)(2,1)S(1)}, u32[]{:S(2)}, u32[]{:S(2)}) async-start(bf16[32,4,128]{2,1,0:T(4,128)(2,1)} %broadcast_in_dim.9), calls=%async_computation.6 | async-start | bytes 65536 | tf_op jit(solution)/shard_map/all_to_all | solution.py:434
  235.6 36.2 %copy-start.7 = (bf16[32,4,128]{2,1,0:T(4,128)(2,1)}, bf16[32,4,128]{2,1,0:T(4,128)(2,1)S(1)}, u32[]{:S(2)}) copy-start(bf16[32,4,128]{2,1,0:T(4,128)(2,1)S(1)} %all-to-all-done.6) | copy-start | bytes 98308
  246.7 25.1 %all-to-all-start.7 = ((bf16[32,128,128]{2,1,0:T(8,128)(2,1)}), bf16[32,128,128]{2,1,0:T(8,128)(2,1)S(1)}, u32[]{:S(2)}, u32[]{:S(2)}) async-start(bf16[32,128,128]{2,1,0:T(8,128)(2,1)} %get-tuple-element.47), calls=%async_computation.7 | async-start | bytes 2097152 | tf_op jit(solution)/shard_map/all_to_all | solution.py:526
  250.6 26.7 %copy-start.13 = (bf16[8,16,128]{2,1,0:T(8,128)(2,1)S(1)}, bf16[8,16,128]{2,1,0:T(8,128)(2,1)}, u32[]{:S(2)}) copy-start(bf16[8,16,128]{2,1,0:T(8,128)(2,1)} %get-tuple-element.48) | copy-start | bytes 98308
  250.6 6.9 %collective-permute-start.8 = (s32[8,128]{1,0:T(8,128)S(1)}, s32[8,128]{1,0:T(8,128)S(1)}, u32[]{:S(2)}, u32[]{:S(2)}) collective-permute-start(s32[8,128]{1,0:T(8,128)S(1)} %bitcast.35), channel_id=1, source_target_pairs={{0,4},{4,0},{8,12},{12,8},{16,20},{20,16},{24,28},{28,24},{32,36},... | collective-permute-start | bytes 12296 | tf_op jit(solution)/shard_map/ppermute | solution.py:453
  250.9 10.9 %collective-permute-start.9 = (s32[8,128]{1,0:T(8,128)S(1)}, s32[8,128]{1,0:T(8,128)S(1)}, u32[]{:S(2)}, u32[]{:S(2)}) collective-permute-start(s32[8,128]{1,0:T(8,128)S(1)} %bitcast.34), channel_id=1, source_target_pairs={{0,8},{4,12},{8,0},{12,4},{16,24},{20,28},{24,16},{28,20},{32,40},... | collective-permute-start | bytes 12296 | tf_op jit(solution)/shard_map/ppermute | solution.py:453
  252.6 9.2 %collective-permute-start.10 = (s32[8,128]{1,0:T(8,128)S(1)}, s32[8,128]{1,0:T(8,128)S(1)}, u32[]{:S(2)}, u32[]{:S(2)}) collective-permute-start(s32[8,128]{1,0:T(8,128)S(1)} %bitcast.33), channel_id=1, source_target_pairs={{0,16},{4,20},{8,24},{12,28},{16,0},{20,4},{24,8},{28,12},{32,48},... | collective-permute-start | bytes 12296 | tf_op jit(solution)/shard_map/ppermute | solution.py:453
  255.3 9.8 %collective-permute-start.11 = (s32[8,128]{1,0:T(8,128)S(1)}, s32[8,128]{1,0:T(8,128)S(1)}, u32[]{:S(2)}, u32[]{:S(2)}) collective-permute-start(s32[8,128]{1,0:T(8,128)S(1)} %bitcast.32), channel_id=1, source_target_pairs={{0,32},{4,36},{8,40},{12,44},{16,48},{20,52},{24,56},{28,60},{32,0... | collective-permute-start | bytes 12296 | tf_op jit(solution)/shard_map/ppermute | solution.py:453
  256.9 8.5 %collective-permute-start.7 = (bf16[8,16,128]{2,1,0:T(8,128)(2,1)S(1)}, bf16[8,16,128]{2,1,0:T(8,128)(2,1)S(1)}, u32[]{:S(2)}, u32[]{:S(2)}) collective-permute-start(bf16[8,16,128]{2,1,0:T(8,128)(2,1)S(1)} %copy-done.14), channel_id=1, source_target_pairs={{0,32},{4,36},{8,40},{12,44},{16,48},{20,52},{24,56},{28,60},{32,0... | collective-permute-start | bytes 98312 | tf_op jit(solution)/shard_map/ppermute | solution.py:453
  257.5 9.4 %collective-permute-start.6 = (bf16[8,16,128]{2,1,0:T(8,128)(2,1)S(1)}, bf16[8,16,128]{2,1,0:T(8,128)(2,1)S(1)}, u32[]{:S(2)}, u32[]{:S(2)}) collective-permute-start(bf16[8,16,128]{2,1,0:T(8,128)(2,1)S(1)} %copy-done.14), channel_id=1, source_target_pairs={{0,16},{4,20},{8,24},{12,28},{16,0},{20,4},{24,8},{28,12},{32,48},... | collective-permute-start | bytes 98312 | tf_op jit(solution)/shard_map/ppermute | solution.py:453
  261.8 7.9 %collective-permute-start.5 = (bf16[8,16,128]{2,1,0:T(8,128)(2,1)S(1)}, bf16[8,16,128]{2,1,0:T(8,128)(2,1)S(1)}, u32[]{:S(2)}, u32[]{:S(2)}) collective-permute-start(bf16[8,16,128]{2,1,0:T(8,128)(2,1)S(1)} %copy-done.14), channel_id=1, source_target_pairs={{0,8},{4,12},{8,0},{12,4},{16,24},{20,28},{24,16},{28,20},{32,40},... | collective-permute-start | bytes 98312 | tf_op jit(solution)/shard_map/ppermute | solution.py:453
  261.8 15.5 %collective-permute-start.4 = (bf16[8,16,128]{2,1,0:T(8,128)(2,1)S(1)}, bf16[8,16,128]{2,1,0:T(8,128)(2,1)S(1)}, u32[]{:S(2)}, u32[]{:S(2)}) collective-permute-start(bf16[8,16,128]{2,1,0:T(8,128)(2,1)S(1)} %copy-done.14), channel_id=1, source_target_pairs={{0,4},{4,0},{8,12},{12,8},{16,20},{20,16},{24,28},{28,24},{32,36},... | collective-permute-start | bytes 98312 | tf_op jit(solution)/shard_map/ppermute | solution.py:453
  265.1 46.0 %collective-permute-start.12 = (bf16[1024,256]{1,0:T(8,128)(2,1)S(1)}, bf16[1024,256]{1,0:T(8,128)(2,1)S(1)}, u32[]{:S(2)}, u32[]{:S(2)}) collective-permute-start(bf16[1024,256]{1,0:T(8,128)(2,1)S(1)} %constant_dynamic-update-slice_fusion.4), channel_id=1, source_target_pairs={{0,4},{4,0},{8,12},{12,8},{16,20},{20,16},{24,28},{28,24},{32,36},... | collective-permute-start | bytes 1572872 | tf_op jit(solution)/shard_map/ppermute | solution.py:453
  265.4 45.6 %collective-permute-start.13 = (bf16[1024,256]{1,0:T(8,128)(2,1)S(1)}, bf16[1024,256]{1,0:T(8,128)(2,1)}, u32[]{:S(2)}, u32[]{:S(2)}) collective-permute-start(bf16[1024,256]{1,0:T(8,128)(2,1)S(1)} %constant_dynamic-update-slice_fusion.4), channel_id=1, source_target_pairs={{0,8},{4,12},{8,0},{12,4},{16,24},{20,28},{24,16},{28,20},{32,40},... | collective-permute-start | bytes 1572872 | tf_op jit(solution)/shard_map/ppermute | solution.py:453
  266.9 44.1 %collective-permute-start.14 = (bf16[1024,256]{1,0:T(8,128)(2,1)S(1)}, bf16[1024,256]{1,0:T(8,128)(2,1)}, u32[]{:S(2)}, u32[]{:S(2)}) collective-permute-start(bf16[1024,256]{1,0:T(8,128)(2,1)S(1)} %constant_dynamic-update-slice_fusion.4), channel_id=1, source_target_pairs={{0,16},{4,20},{8,24},{12,28},{16,0},{20,4},{24,8},{28,12},{32,48},... | collective-permute-start | bytes 1572872 | tf_op jit(solution)/shard_map/ppermute | solution.py:453
  269.6 41.4 %collective-permute-start.15 = (bf16[1024,256]{1,0:T(8,128)(2,1)S(1)}, bf16[1024,256]{1,0:T(8,128)(2,1)}, u32[]{:S(2)}, u32[]{:S(2)}) collective-permute-start(bf16[1024,256]{1,0:T(8,128)(2,1)S(1)} %constant_dynamic-update-slice_fusion.4), channel_id=1, source_target_pairs={{0,32},{4,36},{8,40},{12,44},{16,48},{20,52},{24,56},{28,60},{32,0... | collective-permute-start | bytes 1572872 | tf_op jit(solution)/shard_map/ppermute | solution.py:453
  271.7 39.3 %copy-start = (bf16[32,128,128]{2,1,0:T(8,128)(2,1)}, bf16[32,128,128]{2,1,0:T(8,128)(2,1)S(1)}, u32[]{:S(2)}) copy-start(bf16[32,128,128]{2,1,0:T(8,128)(2,1)S(1)} %all-to-all-done.7.ret_ref) | copy-start | bytes 3145732
  271.7 52.0 %all-to-all-start.4 = ((bf16[32,128,128]{2,1,0:T(8,128)(2,1)}), bf16[32,128,128]{2,1,0:T(8,128)(2,1)S(1)}, u32[]{:S(2)}, u32[]{:S(2)}) async-start(bf16[32,128,128]{2,1,0:T(8,128)(2,1)} %get-tuple-element.42), calls=%async_computation.4 | async-start | bytes 2097152 | tf_op jit(solution)/shard_map/all_to_all | solution.py:544
  277.3 18.2 %collective-permute-start.19 = (bf16[8,16,128]{2,1,0:T(8,128)(2,1)S(1)}, bf16[8,16,128]{2,1,0:T(8,128)(2,1)S(1)}, u32[]{:S(2)}, u32[]{:S(2)}) collective-permute-start(bf16[8,16,128]{2,1,0:T(8,128)(2,1)S(1)} %copy-done.13), channel_id=1, source_target_pairs={{0,32},{4,36},{8,40},{12,44},{16,48},{20,52},{24,56},{28,60},{32,0... | collective-permute-start | bytes 98312 | tf_op jit(solution)/shard_map/ppermute | solution.py:453
  295.5 9.7 %collective-permute-start.18 = (bf16[8,16,128]{2,1,0:T(8,128)(2,1)S(1)}, bf16[8,16,128]{2,1,0:T(8,128)(2,1)S(1)}, u32[]{:S(2)}, u32[]{:S(2)}) collective-permute-start(bf16[8,16,128]{2,1,0:T(8,128)(2,1)S(1)} %copy-done.13), channel_id=1, source_target_pairs={{0,16},{4,20},{8,24},{12,28},{16,0},{20,4},{24,8},{28,12},{32,48},... | collective-permute-start | bytes 98312 | tf_op jit(solution)/shard_map/ppermute | solution.py:453
  305.2 3.9 %collective-permute-start.17 = (bf16[8,16,128]{2,1,0:T(8,128)(2,1)S(1)}, bf16[8,16,128]{2,1,0:T(8,128)(2,1)S(1)}, u32[]{:S(2)}, u32[]{:S(2)}) collective-permute-start(bf16[8,16,128]{2,1,0:T(8,128)(2,1)S(1)} %copy-done.13), channel_id=1, source_target_pairs={{0,8},{4,12},{8,0},{12,4},{16,24},{20,28},{24,16},{28,20},{32,40},... | collective-permute-start | bytes 98312 | tf_op jit(solution)/shard_map/ppermute | solution.py:453
  306.0 5.0 %copy-start.9 = (s32[32,128]{1,0:T(8,128)}, s32[32,128]{1,0:T(8,128)S(1)}, u32[]{:S(2)}) copy-start(s32[32,128]{1,0:T(8,128)S(1)} %constant_dynamic-update-slice_fusion.pexp_ref) | copy-start | bytes 49156
  309.1 1.2 collective-permute-start.16
  311.0 0.8 copy-start.10
  323.7 1.0 copy-start.1
  337.7 14.6 %collective-permute-start.22 = (bf16[1024,128]{1,0:T(8,128)(2,1)}, bf16[1024,128]{1,0:T(8,128)(2,1)S(1)}, u32[]{:S(2)}, u32[]{:S(2)}) collective-permute-start(bf16[1024,128]{1,0:T(8,128)(2,1)} %get-tuple-element.53), channel_id=1, source_target_pairs={{0,3},{1,0},{2,1},{3,2},{4,7},{5,4},{6,5},{7,6},{8,11},{9,8},{10,9... | collective-permute-start | bytes 786440 | tf_op jit(solution)/shard_map/ppermute | solution.py:570
  340.4 11.9 %collective-permute-start.21 = (bf16[1024,128]{1,0:T(8,128)(2,1)}, bf16[1024,128]{1,0:T(8,128)(2,1)S(1)}, u32[]{:S(2)}, u32[]{:S(2)}) collective-permute-start(bf16[1024,128]{1,0:T(8,128)(2,1)} %get-tuple-element.52), channel_id=1, source_target_pairs={{0,2},{1,3},{2,0},{3,1},{4,6},{5,7},{6,4},{7,5},{8,10},{9,11},{10,... | collective-permute-start | bytes 786440 | tf_op jit(solution)/shard_map/ppermute | solution.py:570
  341.1 14.8 %collective-permute-start.20 = (bf16[1024,128]{1,0:T(8,128)(2,1)}, bf16[1024,128]{1,0:T(8,128)(2,1)S(1)}, u32[]{:S(2)}, u32[]{:S(2)}) collective-permute-start(bf16[1024,128]{1,0:T(8,128)(2,1)} %get-tuple-element.51), channel_id=1, source_target_pairs={{0,1},{1,2},{2,3},{3,0},{4,5},{5,6},{6,7},{7,4},{8,9},{9,10},{10,1... | collective-permute-start | bytes 786440 | tf_op jit(solution)/shard_map/ppermute | solution.py:570

commit v2 on v1

v2 whole, which is shorter than its diff:
```python
import math

import jax
import jax.numpy as jnp
from jax import lax
from jax.experimental import pallas as pl
from jax.experimental.pallas import tpu as pltpu
from jax.sharding import PartitionSpec as P

HEAD = 64
BLOCK = 128
EXPANDERS = 4
COLS = 128
NODES_HERE = 1024
Q_BLOCKS = NODES_HERE // BLOCK
SENDERS = 32
GLOBAL_BLOCK = Q_BLOCKS + SENDERS
EMPTY_BLOCK = GLOBAL_BLOCK + 1
KEY_BLOCKS = EMPTY_BLOCK + 1
GROUP = 4
PAIR = 2
LIST = 56
EXTRA = 16
SLOTS = BLOCK + EXTRA
NEG = -1e30
F32 = jnp.float32
BF16 = jnp.bfloat16


def params():
    return pltpu.CompilerParams(vmem_limit_bytes=56 * 1024 * 1024)


def vmem():
    return pl.BlockSpec(memory_space=pltpu.VMEM)


def smem():
    return pl.BlockSpec(memory_space=pltpu.SMEM)


def iota(shape, dim):
    return lax.broadcasted_iota(jnp.int32, shape, dim)


def dot(a, b):
    return jnp.dot(a, b, preferred_element_type=F32)


def dot_nt(a, b):
    return lax.dot_general(a, b, (((1,), (1,)), ((), ())), preferred_element_type=F32)


def split_index(index):
    return (index & (BLOCK - 1)).astype(F32).astype(BF16), (index >> 7).astype(F32).astype(BF16)


def packed_iota(dim):
    return iota((BLOCK, BLOCK), dim).astype(F32).astype(BF16)


def one_hot_columns(column):
    low, high = split_index(column)
    lanes = jnp.concatenate([packed_iota(1)] * (column.shape[0] // BLOCK), axis=0)
    one, zero = jnp.ones((), BF16), jnp.zeros((), BF16)
    base = jnp.where(low == lanes, one, zero)
    return jnp.concatenate(
        [jnp.where(high == jnp.asarray(c, BF16), base, zero) for c in range(NODES_HERE // BLOCK)], axis=1
    )


def one_hot_of_rows(index_rows):
    columns = [jnp.broadcast_to(row, (BLOCK, BLOCK)).T for row in index_rows]
    return one_hot_columns(jnp.concatenate(columns, axis=0))


def owner_ranks(gid_row):
    owner = jnp.broadcast_to(gid_row >> 10, (BLOCK, BLOCK))
    owner_t = owner.T
    same = owner == owner_t
    subs, lanes = iota((BLOCK, BLOCK), 0), iota((BLOCK, BLOCK), 1)
    row = jnp.sum(jnp.where(jnp.logical_and(same, subs < lanes), 1.0, 0.0), axis=0, keepdims=True)
    col = jnp.sum(jnp.where(jnp.logical_and(same, lanes < subs), 1.0, 0.0), axis=1, keepdims=True)
    row, col = row.astype(jnp.int32), jnp.broadcast_to(col, (BLOCK, BLOCK)).astype(jnp.int32)
    slot_row = jnp.where(row < EXTRA, (gid_row >> 10) * EXTRA + row, -1)
    slot_col = jnp.where(col < EXTRA, owner_t * EXTRA + col, -1)
    return row, slot_row, slot_col


def mine_columns(gid_row, me):
    row, _, _ = owner_ranks(gid_row)
    mine = (gid_row >> 10) == me
    slots = iota((EXTRA, BLOCK), 0)
    hit = jnp.logical_and(jnp.broadcast_to(mine, (EXTRA, BLOCK)), slots == row)
    local = jnp.broadcast_to(gid_row & (NODES_HERE - 1), (EXTRA, BLOCK)) + 1
    return jnp.sum(jnp.where(hit, local, 0).astype(F32), axis=1, keepdims=True).astype(jnp.int32) - 1


def project_kernel(
    me_ref, x_ref, wq_ref, wk_ref, wv_ref, cot_ref, rows_ref, exp_ref, gid_ref, q_ref, kv_ref, outk_ref, outv_ref, away_ref
):
    x = x_ref[...]
    kv_ref[:, :COLS] = dot(x, wk_ref[...]).astype(BF16)
    kv_ref[:, COLS:] = dot(x, wv_ref[...]).astype(BF16)
    query = (dot(x, wq_ref[...]).astype(BF16).astype(F32) * (1.0 / math.sqrt(HEAD))).astype(BF16)
    q_ref[...] = query
    away_ref[:NODES_HERE, :COLS] = query
    away_ref[:NODES_HERE, COLS:] = cot_ref[...]
    low, high = split_index(exp_ref[...])
    away_ref[NODES_HERE:, :COLS] = low
    away_ref[NODES_HERE:, COLS:] = high
    mine = jnp.broadcast_to(mine_columns(gid_ref[...], me_ref[0]), (EXTRA, BLOCK))
    lanes = iota((EXTRA, NODES_HERE), 1)
    hot = (jnp.concatenate([mine] * (NODES_HERE // BLOCK), axis=1) == lanes).astype(F32).astype(BF16)
    extra = dot(hot, kv_ref[...]).astype(BF16)

    def gather(t, carry):
        hot = one_hot_of_rows([rows_ref[pl.ds(t * GROUP + u, 1), :] for u in range(GROUP)])
        got = dot(hot, kv_ref[...]).astype(BF16)
        for u in range(GROUP):
            outk_ref[t * GROUP + u, :BLOCK] = got[u * BLOCK : (u + 1) * BLOCK, :COLS]
            outv_ref[t * GROUP + u, :BLOCK] = got[u * BLOCK : (u + 1) * BLOCK, COLS:]
            outk_ref[t * GROUP + u, BLOCK:] = extra[:, :COLS]
            outv_ref[t * GROUP + u, BLOCK:] = extra[:, COLS:]
        return carry

    lax.fori_loop(0, SENDERS // GROUP, gather, 0)


def partner_kernel(exp_ref, t0_ref, t1_ref, t2_ref, t3_ref, out_ref):
    for m, table in enumerate((t0_ref, t1_ref, t2_ref, t3_ref)):

        def gather(t, carry):
            b = m * Q_BLOCKS + t * GROUP
            got = dot(one_hot_of_rows([exp_ref[pl.ds(b + u, 1), :] for u in range(GROUP)]), table[...]).astype(BF16)
            for u in range(GROUP):
                out_ref[b + u] = got[u * BLOCK : (u + 1) * BLOCK]
            return carry

        lax.fori_loop(0, Q_BLOCKS // GROUP, gather, 0)


def plan_kernel(mask_ref, count_ref, list_ref, groups_ref, live_ref):
    for j in range(Q_BLOCKS):
        live_ref[j] = BLOCK
    live_ref[GLOBAL_BLOCK] = BLOCK
    live_ref[EMPTY_BLOCK] = 0

    def copy_count(s, carry):
        live_ref[Q_BLOCKS + s] = count_ref[s]
        return carry

    lax.fori_loop(0, SENDERS, copy_count, 0)

    def per_block(i, carry):
        list_ref[i * LIST] = GLOBAL_BLOCK

        def put(j, n):
            list_ref[i * LIST + n] = j
            used = jnp.logical_and(mask_ref[i * GLOBAL_BLOCK + j] > 0, live_ref[j] > 0)
            return n + used.astype(jnp.int32)

        n = lax.fori_loop(0, GLOBAL_BLOCK, put, 1)
        for extra in range(GROUP):
            list_ref[i * LIST + n + extra] = EMPTY_BLOCK
        groups_ref[i] = (n + GROUP - 1) // GROUP
        return carry

    lax.fori_loop(0, Q_BLOCKS, per_block, 0)


def fill(dst, own_ref, first_col, halo_ref, gid_ref, glob_ref, transposed=False):
    def turn(x):
        return x.T if transposed else x

    def own(j, carry):
        dst[j] = turn(own_ref[q_rows(j), first_col : first_col + COLS])
        return carry

    def halo(j, carry):
        dst[Q_BLOCKS + j] = turn(halo_ref[j, :BLOCK])
        return carry

    lax.fori_loop(0, Q_BLOCKS, own, 0, unroll=4)
    lax.fori_loop(0, SENDERS, halo, 0, unroll=4)
    slot_col = owner_ranks(gid_ref[...])[2]
    wide = jnp.concatenate([slot_col] * (SENDERS * EXTRA // BLOCK), axis=1)
    hot = (wide == iota((BLOCK, SENDERS * EXTRA), 1)).astype(F32).astype(BF16)
    extra = jnp.concatenate([halo_ref[s, BLOCK:] for s in range(SENDERS)], axis=0)
    rows = dot(hot, extra) + glob_ref[:, first_col : first_col + COLS].astype(F32)
    dst[GLOBAL_BLOCK] = turn(rows.astype(BF16))
    dst[EMPTY_BLOCK] = jnp.zeros((BLOCK, COLS), BF16)


def stacked(rows):
    lanes = iota((BLOCK, COLS), 1)
    zero = jnp.zeros_like(rows)
    return jnp.concatenate([jnp.where(lanes < HEAD, rows, zero), jnp.where(lanes < HEAD, zero, rows)], axis=0)


def stacked_t(rows):
    turned = rows.T
    subs = iota((COLS, BLOCK), 0)
    zero = jnp.zeros_like(turned)
    return jnp.concatenate([jnp.where(subs < HEAD, turned, zero), jnp.where(subs < HEAD, zero, turned)], axis=1)


def partner_rows(rows, pair_ref, i, first_col):
    total = jnp.zeros((16, BLOCK), F32)
    row_id = iota((16, COLS), 0)
    lane = iota((16, COLS), 1)
    for m in range(EXPANDERS):
        other = pair_ref[m * Q_BLOCKS + i][:, first_col : first_col + COLS]
        prod = rows.astype(F32) * other.astype(F32)
        high = prod.astype(BF16)
        low = (prod - high.astype(F32)).astype(BF16)
        picks = (row_id == jnp.where(lane < HEAD, m, 8 + m)).astype(F32).astype(BF16)
        total = total + dot_nt(picks, high) + dot_nt(picks, low)
    return jnp.concatenate([total[:8], total[8:]], axis=1)


def tall(weights):
    return jnp.concatenate([weights[:, :BLOCK], weights[:, BLOCK:]], axis=0)


def spread(tall_weights):
    turned = tall_weights.T.astype(BF16)
    row_id = iota((16, EXPANDERS * COLS), 0)
    col = iota((16, EXPANDERS * COLS), 1)
    picks = (row_id == (col // COLS) + jnp.where(col % COLS < HEAD, 0, 8)).astype(F32).astype(BF16)
    return dot(turned, picks)


def head_rows(turned):
    return jnp.concatenate([turned[:HEAD, :BLOCK], turned[HEAD:, BLOCK:]], axis=0)


def masked_scores(blocks, k_s, turned_q, live_ref):
    keys = jnp.concatenate([k_s[b] for b in blocks], axis=0)
    scores = dot(keys, turned_q)
    row_id = iota((BLOCK, 2 * BLOCK), 0)
    return jnp.concatenate(
        [
            jnp.where(row_id < live_ref[b], scores[u * BLOCK : (u + 1) * BLOCK], NEG)
            for u, b in enumerate(blocks)
        ],
        axis=0,
    )


def score_rows(rows, pair_ref, i):
    partner = partner_rows(rows, pair_ref, i, 0)
    return jnp.where(iota((8, 2 * BLOCK), 0) < EXPANDERS, partner, NEG)


def block_ids(list_ref, i, g):
    return [list_ref[i * LIST + g * GROUP + u] for u in range(GROUP)]


def q_rows(i):
    return pl.ds(pl.multiple_of(i * BLOCK, BLOCK), BLOCK)


def score_kernel(list_ref, groups_ref, live_ref, q_ref, kv_ref, hk_ref, gid_ref, glob_ref, lse_ref, k_s):
    fill(k_s, kv_ref, 0, hk_ref, gid_ref, glob_ref)

    def per_block(i, carry):
        turned_q = stacked_t(q_ref[q_rows(i), :])

        def step(g, state):
            blocks = block_ids(list_ref, i, g)
            new_state = []
            for u in range(GROUP // PAIR):
                top, total = state[u]
                scores = masked_scores(blocks[u * PAIR : (u + 1) * PAIR], k_s, turned_q, live_ref)
                scores = scores.reshape(PAIR * BLOCK // 8, 8, 2 * BLOCK)
                new_top = jnp.maximum(top, jnp.max(scores, axis=0))
                total = total * jnp.exp(top - new_top) + jnp.sum(jnp.exp(scores - new_top[None]), axis=0)
                new_state.append((new_top, total))
            return tuple(new_state)

        init = (jnp.full((8, 2 * BLOCK), NEG, F32), jnp.zeros((8, 2 * BLOCK), F32))
        state = lax.fori_loop(0, groups_ref[i], step, tuple(init for _ in range(GROUP // PAIR)))
        top = jnp.concatenate([t for t, _ in state], axis=0)
        total = jnp.concatenate([t for _, t in state], axis=0)
        best = jnp.max(top, axis=0, keepdims=True)
        denominator = jnp.sum(total * jnp.exp(top - best), axis=0, keepdims=True)
        lse_ref[pl.ds(i, 1), :] = best + jnp.log(denominator)
        return carry

    lax.fori_loop(0, Q_BLOCKS, per_block, 0)


def clear_blocks(acc_s):
    def clear(j, carry):
        acc_s[j] = jnp.zeros((BLOCK, COLS), F32)
        return carry

    lax.fori_loop(0, KEY_BLOCKS, clear, 0)


def value_kernel(
    list_ref, groups_ref, live_ref, q_ref, kv_ref, hk_ref, hv_ref, gid_ref, glob_ref, pair_ref, cot_ref, part_ref,
    att_ref, own_ref, halo_ref, gout_ref, wp_ref, pdp_ref, delta_ref, lse_ref, k_s, vt_s, acc_s, out_s,
):
    fill(k_s, kv_ref, 0, hk_ref, gid_ref, glob_ref)
    fill(vt_s, kv_ref, COLS, hv_ref, gid_ref, glob_ref, transposed=True)
    clear_blocks(acc_s)

    def per_block(i, carry):
        rows = q_ref[q_rows(i), :]
        turned_q = stacked_t(rows)
        cot = cot_ref[q_rows(i), :]
        cot_stack = stacked(cot)
        partner = score_rows(rows, pair_ref, i)
        part = part_ref[pl.ds(i, 1), :]
        best = jnp.maximum(part, jnp.max(partner, axis=0, keepdims=True))
        lse = best + jnp.log(jnp.exp(part - best) + jnp.sum(jnp.exp(partner - best), axis=0, keepdims=True))
        lse_ref[pl.ds(i, 1), :] = lse
        out_s[...] = jnp.zeros((COLS, 2 * BLOCK), F32)

        def step(g, carry):
            blocks = block_ids(list_ref, i, g)
            total = None
            for u in range(0, GROUP, PAIR):
                pair = blocks[u : u + PAIR]
                scores = masked_scores(pair, k_s, turned_q, live_ref)
                weight = jnp.exp(scores - lse).astype(BF16)
                term = dot(jnp.concatenate([vt_s[b] for b in pair], axis=1), weight)
                total = term if total is None else total + term
                grads = dot(weight, cot_stack)
                for w, b in enumerate(pair):
                    acc_s[b] += grads[w * BLOCK : (w + 1) * BLOCK]
            out_s[...] += total
            return carry

        lax.fori_loop(0, groups_ref[i], step, 0)
        dprob = partner_rows(cot, pair_ref, i, COLS)
        prob = jnp.exp(partner - lse)
        weight = prob.astype(BF16).astype(F32)
        wide = spread(tall(weight))
        wp_ref[i] = tall(weight).astype(BF16)
        attended_t = head_rows(out_s[...])
        prod = attended_t * cot.T.astype(F32)
        delta = jnp.concatenate(
            [jnp.sum(prod[:HEAD], axis=0, keepdims=True), jnp.sum(prod[HEAD:], axis=0, keepdims=True)], axis=1
        )
        delta = delta + jnp.sum(prob * dprob, axis=0, keepdims=True)
        delta_ref[pl.ds(i, 1), :] = delta
        pdp_ref[i] = prob * (dprob - delta)
        attended = attended_t.T
        for m in range(EXPANDERS):
            attended += wide[:, m * COLS : (m + 1) * COLS] * pair_ref[m * Q_BLOCKS + i][:, COLS:].astype(F32)
        att_ref[q_rows(i), :] = attended.astype(BF16)
        return carry

    lax.fori_loop(0, Q_BLOCKS, per_block, 0)
    store_parts(acc_s, own_ref, halo_ref, gid_ref, gout_ref)


def store_parts(acc_s, own_ref, halo_ref, gid_ref, gout_ref):
    def own(j, carry):
        own_ref[q_rows(j), :] = acc_s[j]
        return carry

    def halo(j, carry):
        halo_ref[j, :BLOCK] = acc_s[Q_BLOCKS + j].astype(BF16)
        return carry

    lax.fori_loop(0, Q_BLOCKS, own, 0, unroll=2)
    lax.fori_loop(0, SENDERS, halo, 0, unroll=4)
    grads = acc_s[GLOBAL_BLOCK].astype(BF16)
    gout_ref[...] = grads
    slot_row = owner_ranks(gid_ref[...])[1]
    hot = (iota((SENDERS * EXTRA, BLOCK), 0) == slot_row).astype(F32).astype(BF16)
    extra = dot(hot, grads).astype(BF16)
    for s in range(SENDERS):
        halo_ref[s, BLOCK:] = extra[s * EXTRA : (s + 1) * EXTRA]


def key_kernel(
    list_ref, groups_ref, live_ref, q_ref, kv_ref, hk_ref, hv_ref, gid_ref, glob_ref, pair_ref, cot_ref, lse_ref,
    pdp_ref, delta_ref, gq_ref, own_ref, halo_ref, gout_ref, dsp_ref, k_s, v_s, kt_s, acc_s, out_s,
):
    fill(k_s, kv_ref, 0, hk_ref, gid_ref, glob_ref)
    fill(v_s, kv_ref, COLS, hv_ref, gid_ref, glob_ref)
    fill(kt_s, kv_ref, 0, hk_ref, gid_ref, glob_ref, transposed=True)
    clear_blocks(acc_s)

    def per_block(i, carry):
        rows = q_ref[q_rows(i), :]
        turned_q = stacked_t(rows)
        q_stack = stacked(rows)
        turned_cot = stacked_t(cot_ref[q_rows(i), :])
        lse = lse_ref[pl.ds(i, 1), :]
        delta = delta_ref[pl.ds(i, 1), :]
        out_s[...] = jnp.zeros((COLS, 2 * BLOCK), F32)

        def step(g, carry):
            blocks = block_ids(list_ref, i, g)
            total = None
            for u in range(0, GROUP, PAIR):
                pair = blocks[u : u + PAIR]
                scores = masked_scores(pair, k_s, turned_q, live_ref)
                dprob = dot(jnp.concatenate([v_s[b] for b in pair], axis=0), turned_cot)
                dscore = (jnp.exp(scores - lse) * (dprob - delta)).astype(BF16)
                term = dot(jnp.concatenate([kt_s[b] for b in pair], axis=1), dscore)
                total = term if total is None else total + term
                grads = dot(dscore, q_stack)
                for w, b in enumerate(pair):
                    acc_s[b] += grads[w * BLOCK : (w + 1) * BLOCK]
            out_s[...] += total
            return carry

        lax.fori_loop(0, groups_ref[i], step, 0)
        partner = tall(pdp_ref[i].astype(BF16).astype(F32))
        dsp_ref[i] = partner.astype(BF16)
        wide = spread(partner)
        grad_query = head_rows(out_s[...]).T
        for m in range(EXPANDERS):
            grad_query += wide[:, m * COLS : (m + 1) * COLS] * pair_ref[m * Q_BLOCKS + i][:, :COLS].astype(F32)
        gq_ref[q_rows(i), :] = (grad_query * (1.0 / math.sqrt(HEAD))).astype(BF16)
        return carry

    lax.fori_loop(0, Q_BLOCKS, per_block, 0)
    store_parts(acc_s, own_ref, halo_ref, gid_ref, gout_ref)


def scatter_into(acc_s, splits, data):
    subs = packed_iota(0)
    one, zero = jnp.ones((), BF16), jnp.zeros((), BF16)
    bases = [(jnp.where(subs == low, one, zero), jnp.broadcast_to(high, (BLOCK, BLOCK))) for low, high in splits]
    for c in range(NODES_HERE // BLOCK):
        hot = jnp.concatenate([jnp.where(high == jnp.asarray(c, BF16), base, zero) for base, high in bases], axis=1)
        acc_s[c * BLOCK : (c + 1) * BLOCK, :] += dot(hot, data)


def gather_grads(me_ref, own_ref, ret_ref, rows_ref, parts, others, first_col, gid_ref, acc_s):
    acc_s[...] = own_ref[...]

    def halo(t, carry):
        splits = [split_index(rows_ref[pl.ds(t * GROUP + u, 1), :]) for u in range(GROUP)]
        data = jnp.concatenate([ret_ref[t * GROUP + u, :BLOCK] for u in range(GROUP)], axis=0)
        scatter_into(acc_s, splits, data)
        return carry

    lax.fori_loop(0, SENDERS // GROUP, halo, 0)
    row_id = iota((16, COLS), 0)
    lane = iota((16, COLS), 1)
    for m, (part, other) in enumerate(zip(parts, others)):
        picks = (row_id == jnp.where(lane < HEAD, m, 8 + m)).astype(F32).astype(BF16)
        index_low = other[NODES_HERE + m * Q_BLOCKS : NODES_HERE + (m + 1) * Q_BLOCKS, :COLS]
        index_high = other[NODES_HERE + m * Q_BLOCKS : NODES_HERE + (m + 1) * Q_BLOCKS, COLS:]
        for t in range(Q_BLOCKS // GROUP):
            splits, data = [], []
            for u in range(GROUP):
                i = t * GROUP + u
                splits.append((index_low[i : i + 1], index_high[i : i + 1]))
                wide = dot(part[1 if first_col else 0, i].astype(F32).T.astype(BF16), picks)
                rows = other[i * BLOCK : (i + 1) * BLOCK, first_col : first_col + COLS].astype(F32)
                data.append((wide * rows).astype(BF16))
            scatter_into(acc_s, splits, jnp.concatenate(data, axis=0))
    extra = ret_ref[0, BLOCK:].astype(F32)
    for s in range(1, SENDERS):
        extra += ret_ref[s, BLOCK:].astype(F32)
    high = extra.astype(BF16)
    data = jnp.concatenate([high, (extra - high.astype(F32)).astype(BF16)], axis=0)
    mine = jnp.broadcast_to(mine_columns(gid_ref[...], me_ref[0]), (EXTRA, NODES_HERE))
    hot = (mine == iota((EXTRA, NODES_HERE), 1)).astype(F32)
    hot = jnp.concatenate([hot, hot], axis=0).T.astype(BF16)
    acc_s[...] += dot(hot, data)


def value_back_kernel(
    me_ref, own_ref, ret_ref, rows_ref, p0_ref, p1_ref, p2_ref, p3_ref, o0_ref, o1_ref, o2_ref, o3_ref, gid_ref,
    grad_ref, acc_s,
):
    parts, others = (p0_ref, p1_ref, p2_ref, p3_ref), (o0_ref, o1_ref, o2_ref, o3_ref)
    gather_grads(me_ref, own_ref, ret_ref, rows_ref, parts, others, COLS, gid_ref, acc_s)
    grad_ref[...] = acc_s[...].astype(BF16)


def key_back_kernel(
    me_ref, own_ref, ret_ref, rows_ref, p0_ref, p1_ref, p2_ref, p3_ref, o0_ref, o1_ref, o2_ref, o3_ref, gid_ref,
    wq_ref, wk_ref, wv_ref, gq_ref, gv_ref, t0_ref, t1_ref, t2_ref, t3_ref, acc_s,
):
    parts, others = (p0_ref, p1_ref, p2_ref, p3_ref), (o0_ref, o1_ref, o2_ref, o3_ref)
    gather_grads(me_ref, own_ref, ret_ref, rows_ref, parts, others, 0, gid_ref, acc_s)
    grad_key = acc_s[...].astype(BF16)
    for k, out in enumerate((t0_ref, t1_ref, t2_ref, t3_ref)):
        part = pl.ds(pl.multiple_of(((me_ref[1] + k) % 4) * COLS, COLS), COLS)
        term = dot_nt(gq_ref[...], wq_ref[part, :]) + dot_nt(gv_ref[...], wv_ref[part, :])
        term = term + dot_nt(grad_key, wk_ref[part, :])
        out[...] = term.astype(out.dtype)


def shape(dims, kind=BF16):
    return jax.ShapeDtypeStruct(dims, kind)


def call(kernel, ins, outs, args, scratch=(), name=None, flops=0, out_spaces=None):
    cost = pl.CostEstimate(flops=flops, transcendentals=0, bytes_accessed=4_000_000)
    return pl.pallas_call(
        kernel,
        out_shape=outs,
        in_specs=ins,
        out_specs=out_spaces or tuple(vmem() for _ in outs),
        scratch_shapes=list(scratch),
        compiler_params=params(),
        cost_estimate=cost,
        name=name,
    )(*args)


def blocks_of(kind):
    return pltpu.VMEM((KEY_BLOCKS, BLOCK, COLS), kind)


def run_project(me, features, w_query, w_key, w_value, cotangent, rows, exp_list, gids):
    return call(
        project_kernel,
        [smem()] + [vmem()] * 8,
        (
            shape((NODES_HERE, COLS)),
            shape((NODES_HERE, 2 * COLS)),
            shape((SENDERS, SLOTS, COLS)),
            shape((SENDERS, SLOTS, COLS)),
            shape((NODES_HERE + EXPANDERS * Q_BLOCKS, 2 * COLS)),
        ),
        (me, features, w_query, w_key, w_value, cotangent, rows, exp_list, gids),
        name="project",
        flops=3_000_000_000,
    )


def run_plan(block_mask, halo_count):
    return call(
        plan_kernel,
        [smem()] * 2,
        (shape((Q_BLOCKS * LIST,), jnp.int32), shape((Q_BLOCKS,), jnp.int32), shape((LIST,), jnp.int32)),
        (block_mask.reshape(-1), halo_count.reshape(-1)),
        name="plan",
        out_spaces=(smem(), smem(), smem()),
    )


def run_partners(exp_list, swaps):
    return call(
        partner_kernel,
        [vmem()] * 5,
        (shape((EXPANDERS * Q_BLOCKS, BLOCK, 2 * COLS)),),
        (exp_list, *swaps),
        name="partners",
        flops=5_000_000_000,
    )[0]


def run_scores(plan, query, paired, halo_k, gids, glob):
    return call(
        score_kernel,
        [smem()] * 3 + [vmem()] * 5,
        (shape((Q_BLOCKS, 2 * BLOCK), F32),),
        (*plan, query, paired, halo_k, gids, glob),
        scratch=[blocks_of(BF16)],
        name="scores",
        flops=12_000_000_000,
    )[0]


def run_values(plan, query, paired, halo_k, halo_v, gids, glob, pairs, cotangent, part):
    return call(
        value_kernel,
        [smem()] * 3 + [vmem()] * 9,
        (
            shape((NODES_HERE, COLS)),
            shape((NODES_HERE, COLS), F32),
            shape((SENDERS, SLOTS, COLS)),
            shape((BLOCK, COLS)),
            shape((Q_BLOCKS, 16, BLOCK)),
            shape((Q_BLOCKS, 8, 2 * BLOCK), F32),
            shape((Q_BLOCKS, 2 * BLOCK), F32),
            shape((Q_BLOCKS, 2 * BLOCK), F32),
        ),
        (*plan, query, paired, halo_k, halo_v, gids, glob, pairs, cotangent, part),
        scratch=[blocks_of(BF16), blocks_of(BF16), blocks_of(F32), pltpu.VMEM((COLS, 2 * BLOCK), F32)],
        name="values",
        flops=20_000_000_000,
    )


def run_keys(plan, query, paired, halo_k, halo_v, gids, glob, pairs, cotangent, lse, pdp, delta):
    return call(
        key_kernel,
        [smem()] * 3 + [vmem()] * 11,
        (
            shape((NODES_HERE, COLS)),
            shape((NODES_HERE, COLS), F32),
            shape((SENDERS, SLOTS, COLS)),
            shape((BLOCK, COLS)),
            shape((Q_BLOCKS, 16, BLOCK)),
        ),
        (*plan, query, paired, halo_k, halo_v, gids, glob, pairs, cotangent, lse, pdp, delta),
        scratch=[blocks_of(BF16), blocks_of(BF16), blocks_of(BF16), blocks_of(F32), pltpu.VMEM((COLS, 2 * BLOCK), F32)],
        name="keys",
        flops=25_000_000_000,
    )


def run_value_back(me, own_v, returned_v, rows, parts, others, gids):
    return call(
        value_back_kernel,
        [smem()] + [vmem()] * 12,
        (shape((NODES_HERE, COLS)),),
        (me, own_v, returned_v, rows, *parts, *others, gids),
        scratch=[pltpu.VMEM((NODES_HERE, COLS), F32)],
        name="value_back",
        flops=8_000_000_000,
    )[0]


def run_key_back(me, own_k, returned_k, rows, parts, others, gids, w_query, w_key, w_value, grad_query, grad_value):
    return call(
        key_back_kernel,
        [smem()] + [vmem()] * 17,
        (shape((NODES_HERE, COLS), F32),) + tuple(shape((NODES_HERE, COLS)) for _ in range(3)),
        (me, own_k, returned_k, rows, *parts, *others, gids, w_query, w_key, w_value, grad_query, grad_value),
        scratch=[pltpu.VMEM((NODES_HERE, COLS), F32)],
        name="key_back",
        flops=8_000_000_000,
    )


def more_rounds(global_ids):
    owned = (global_ids[None, :] // NODES_HERE == jnp.arange(SENDERS)[:, None]).sum(1)
    return (owned.max() + EXTRA - 1) // EXTRA


def ranks(global_ids):
    owner = global_ids // NODES_HERE
    ids = jnp.arange(BLOCK)
    return owner, ((owner[:, None] == owner[None, :]) & (ids[None, :] < ids[:, None])).sum(1)


def more_globals(rounds, global_ids, my_index, paired):
    def body(state):
        r, glob = state
        owner, rank = ranks(global_ids)
        slot = rank - r * EXTRA
        here = (slot >= 0) & (slot < EXTRA)
        place = jnp.where((owner == my_index) & here, slot, EXTRA)
        rows = jnp.zeros((EXTRA + 1, paired.shape[1]), BF16).at[place].set(paired[global_ids % NODES_HERE])[:EXTRA]
        got = lax.all_to_all(jnp.broadcast_to(rows[None], (SENDERS, *rows.shape)), "dom", 0, 0, tiled=True)
        found = got.reshape(SENDERS * EXTRA, -1)[jnp.clip(owner * EXTRA + slot, 0, SENDERS * EXTRA - 1)]
        return r + 1, jnp.where(here[:, None], found, glob)

    start = (jnp.asarray(1, jnp.int32), jnp.zeros((BLOCK, paired.shape[1]), BF16))
    return lax.while_loop(lambda state: state[0] < rounds, body, start)[1]


def more_grads(rounds, global_ids, my_index, part_k, part_v, own_k, own_v):
    def body(state):
        r, own_k, own_v = state
        owner, rank = ranks(global_ids)
        slot = rank - r * EXTRA
        here = (slot >= 0) & (slot < EXTRA)
        part = jnp.concatenate([part_k, part_v], axis=1)
        place = jnp.where(here, owner * EXTRA + slot, SENDERS * EXTRA)
        rows = jnp.zeros((SENDERS * EXTRA + 1, part.shape[1]), BF16).at[place].set(part)[: SENDERS * EXTRA]
        got = lax.all_to_all(rows.reshape(SENDERS, EXTRA, -1), "dom", 0, 0, tiled=True).astype(F32).sum(0)
        take = (owner == my_index) & here
        add = jnp.where(take[:, None], got[jnp.clip(slot, 0, EXTRA - 1)], 0.0)
        local = global_ids % NODES_HERE
        return r + 1, own_k.at[local].add(add[:, :COLS]), own_v.at[local].add(add[:, COLS:])

    start = (jnp.asarray(1, jnp.int32), own_k, own_v)
    return lax.while_loop(lambda state: state[0] < rounds, body, start)[1:]


def on_device(
    features,
    w_query,
    w_key,
    w_value,
    cotangent,
    send_rows,
    halo_count,
    block_mask,
    exp_rows,
    global_ids,
):
    dom_count = lax.axis_size("dom")
    my_index = lax.axis_index("dom")

    def swapped(value, bit):
        return lax.ppermute(value, "dom", [(i, i ^ (1 << bit)) for i in range(dom_count)])

    rows = send_rows[0]
    gids = global_ids.reshape(1, BLOCK)
    exp_list = exp_rows.reshape(EXPANDERS * Q_BLOCKS, BLOCK)
    me = jnp.stack([my_index, lax.axis_index("feat")]).astype(jnp.int32)
    rounds = more_rounds(global_ids)

    query, paired, out_k, out_v, away = run_project(
        me, features, w_query, w_key, w_value, cotangent, rows, exp_list, gids
    )
    glob = more_globals(rounds, global_ids, my_index, paired)
    out_k, out_v, glob = lax.optimization_barrier((out_k, out_v, glob))
    halo_k = lax.all_to_all(out_k, "dom", 0, 0, tiled=True)
    swaps = [swapped(paired, m) for m in range(EXPANDERS)]
    plan = run_plan(block_mask, halo_count)
    halo_v = lax.all_to_all(out_v, "dom", 0, 0, tiled=True)
    part = run_scores(plan, query, paired, halo_k, gids, glob)
    pairs = run_partners(exp_list, swaps)
    away, part = lax.optimization_barrier((away, part))
    others = [swapped(away, m) for m in range(EXPANDERS)]
    attended, own_v, back_v, glob_v, weight_p, pdp, delta, lse = run_values(
        plan, query, paired, halo_k, halo_v, gids, glob, pairs, cotangent, part
    )
    *others, lse = lax.optimization_barrier((*others, lse))
    returned_v = lax.all_to_all(back_v, "dom", 0, 0, tiled=True)
    grad_query, own_k, back_k, glob_k, dscore_p = run_keys(
        plan, query, paired, halo_k, halo_v, gids, glob, pairs, cotangent, lse, pdp, delta
    )
    own_k, own_v = more_grads(rounds, global_ids, my_index, glob_k, glob_v, own_k, own_v)
    back_k, own_k, own_v = lax.optimization_barrier((back_k, own_k, own_v))
    returned_k = lax.all_to_all(back_k, "dom", 0, 0, tiled=True)
    both = jnp.stack([dscore_p, weight_p])
    parts = [swapped(both, m) for m in range(EXPANDERS)]
    grad_value = run_value_back(me, own_v, returned_v, rows, parts, others, gids)
    mine, *away = run_key_back(
        me, own_k, returned_k, rows, parts, others, gids, w_query, w_key, w_value, grad_query, grad_value
    )
    for k, term in enumerate(away, 1):
        mine = mine + lax.ppermute(term, "feat", [(i, (i + k) % 4) for i in range(4)]).astype(F32)
    return (attended, mine.astype(BF16))


def solution(mesh):
    return jax.shard_map(
        on_device,
        mesh=mesh,
        in_specs=(
            P("dom", None),
            P(None, "feat"),
            P(None, "feat"),
            P(None, "feat"),
            P("dom", "feat"),
            P("dom", None, None),
            P(None, "dom"),
            P("dom", None),
            P(None, "dom"),
            P(),
        ),
        out_specs=(P("dom", "feat"), P("dom", "feat")),
        check_vma=False,
    )
```

time: 360 us -> 265 us (0.74)
  blocking collectives: 58.9 us -> 0 us
  waiting for transfers between devices: 94.4 us -> 74.2 us
  starting transfers between devices: 53.7 us -> 42.2 us
  Pallas kernels: 139 us -> 130 us
    all_to_all x4 -> x0, blocking collectives: 58.9 us -> none  [the longest x2 36.9 us: reduce_rows(): lax.all_to_all(part.reshape(SENDERS, 4, width), 'dom', 0, 0, tiled=True)]
    all_to_all x1, waiting for transfers between devices: 0.01 us -> 18.4 us  [on_device(): returned_v = lax.all_to_all(back_v, 'dom', 0, 0, tiled=True)]
    ppermute x20 -> x12, waiting for transfers between devices: 55.2 us -> 39.8 us  [swapped(): lax.ppermute(value, 'dom', [(i, i ^ 1 << bit) for i in range(dom_count)])]
    all_to_all x2 -> x0, waiting for transfers between devices: 14.8 us -> none  [the longest x1 7.38 us: reduce_rows(): lax.all_to_all(part.reshape(SENDERS, 4, width), 'dom', 0, 0, tiled=True)]
    ppermute x20 -> x12, starting transfers between devices: 23.8 us -> 14.7 us  [swapped(): lax.ppermute(value, 'dom', [(i, i ^ 1 << bit) for i in range(dom_count)])]
    pallas_call x8, Pallas kernels: 139 us -> 130 us  [call(): pl.pallas_call(kernel, out_shape=outs, in_specs=ins, out_specs=out_spaces...]
    all_to_all x2 -> x0, starting transfers between devices: 7.63 us -> none  [the longest x1 3.83 us: spread_rows(): return lax.all_to_all(copies, 'dom', 0, 0, tiled=True).reshape(BLOCK, width)]
    ppermute x3, waiting for transfers between devices: 13.8 us -> 8.94 us  [on_device(): lax.ppermute(term, 'feat', [(i, (i + k) % 4) for i in range(4)]).astype(F32)]
  transfers between devices with their start and end apart: 29 -> 19, of which waited for: 13 -> 7; matrix products, arithmetic and copies ran while one was open for 1% -> 0% of each run, Pallas kernels for 13% -> 27%
where the time goes in v2:
time: 265 us; the launch traced here: 263 us
  Pallas kernels  130 us (49%)
  waiting for transfers between devices  74.2 us (28%)
  starting transfers between devices  42.2 us (16%)
  local copies, waits for them, and re-layouts  9.83 us (4%)
  other arithmetic  4.89 us (2%)
    pallas_call x8, Pallas kernels, call(): pl.pallas_call(kernel, out_shape=outs, in_specs=ins, out_specs=out_spaces...  130 us
    ppermute x12, waiting for transfers between devices, swapped(): lax.ppermute(value, 'dom', [(i, i ^ 1 << bit) for i in range(dom_count)])  39.8 us
    all_to_all x1, waiting for transfers between devices, on_device(): returned_v = lax.all_to_all(back_v, 'dom', 0, 0, tiled=True)  18.4 us
    ppermute x12, starting transfers between devices, swapped(): lax.ppermute(value, 'dom', [(i, i ^ 1 << bit) for i in range(dom_count)])  14.7 us
    ppermute x3, waiting for transfers between devices, on_device(): lax.ppermute(term, 'feat', [(i, (i + k) % 4) for i in range(4)]).astype(F32)  8.94 us
    all_to_all x1, starting transfers between devices, on_device(): halo_k = lax.all_to_all(out_k, 'dom', 0, 0, tiled=True)  8.4 us
    all_to_all x1, waiting for transfers between devices, on_device(): halo_k = lax.all_to_all(out_k, 'dom', 0, 0, tiled=True)  7.1 us
    unnamed x36, local copies, waits for them, and re-layouts  5.97 us
  transfers between devices with their start and end apart: 19, of which 7 were waited for; matrix products, arithmetic and copies ran while one was open for 0% of the time, Pallas kernels for 27%

profile of v2, /device:TPU:0, one launch (start us, length us, event | category | flops | bytes accessed | tf_op | source)
XLA Modules:
  0.0 263.1 jit_solution(883592536197581414)
XLA Ops:
  0.6 0.7 compare_select_fusion.14
  1.3 0.1 convert_reduce_fusion.2
  1.4 0.6 reduce_max.9
  2.7 0.2 convert_reduce_fusion.1
  2.9 1.3 reshape.626.exp_ref
  4.2 0.7 pad_add_fusion.me_ref
  4.9 8.1 %project.1 = (bf16[1024,128]{1,0:T(8,128)(2,1)}, bf16[1024,256]{1,0:T(8,128)(2,1)}, bf16[32,144,128]{2,1,0:T(8,128)(2,1)}, bf16[32,144,128]{2,1,0:T(8,128)(2,1)}, bf16[1056,256]{1,0:T(8,128)(2,1)}) custom-call(s32[2]{0:T(128)} %pad_add_fusion.me_ref, bf16[1024,512]{1,0:T(8,128)(2,1)} %x_ref.1, bf16[512,128]{1,0:T(8,128)(2,1)} %wq_ref.3, ...), custom_call_target="tpu_custom_call" | custom-call | flops 3000000000 | bytes 4000000 | tf_op jit(solution)/shard_map/project/pallas_call | solution.py:503
  13.0 1.9 gather_fusion.2
  14.9 0.0 copy-start.9
  14.9 8.4 %all-to-all-start.2 = ((bf16[32,144,128]{2,1,0:T(8,128)(2,1)}), bf16[32,144,128]{2,1,0:T(8,128)(2,1)S(1)}, u32[]{:S(2)}, u32[]{:S(2)}) async-start(bf16[32,144,128]{2,1,0:T(8,128)(2,1)} %get-tuple-element.628), calls=%async_computation.2 | async-start | bytes 2359296 | tf_op jit(solution)/shard_map/all_to_all | solution.py:708
  23.4 0.4 collective-permute-start
  23.7 1.7 collective-permute-start.1
  25.4 2.7 %collective-permute-start.2 = (bf16[1024,256]{1,0:T(8,128)(2,1)S(1)}, bf16[1024,256]{1,0:T(8,128)(2,1)}, u32[]{:S(2)}, u32[]{:S(2)}) collective-permute-start(bf16[1024,256]{1,0:T(8,128)(2,1)S(1)} %copy-done.4), channel_id=1, source_target_pairs={{0,16},{4,20},{8,24},{12,28},{16,0},{20,4},{24,8},{28,12},{32,48},... | collective-permute-start | bytes 1572872 | tf_op jit(solution)/shard_map/ppermute | solution.py:695
  28.1 1.5 collective-permute-start.3
  29.5 0.7 reshape.624.mask_ref
  30.2 4.5 %plan.1 = (s32[448]{0:T(512)}, s32[8]{0:T(128)}, s32[56]{0:T(128)}) custom-call(s32[320]{0:T(512)} %reshape.624.mask_ref, s32[32]{0:T(128)} %bitcast.105), custom_call_target="tpu_custom_call" | custom-call | bytes 4000000 | tf_op jit(solution)/shard_map/plan/pallas_call | solution.py:503
  34.7 7.1 %all-to-all-done.2.hk_ref = bf16[32,144,128]{2,1,0:T(8,128)(2,1)S(1)} async-done(((bf16[32,144,128]{2,1,0:T(8,128)(2,1)}), bf16[32,144,128]{2,1,0:T(8,128)(2,1)S(1)}, u32[]{:S(2)}, u32[]{:S(2)}) %all-to-all-start.2) | async-done | bytes 1179680 | tf_op jit(solution)/shard_map/all_to_all | solution.py:708
  41.8 1.1 copy-done
  42.9 4.3 %all-to-all-start.3 = ((bf16[32,144,128]{2,1,0:T(8,128)(2,1)}), bf16[32,144,128]{2,1,0:T(8,128)(2,1)S(1)}, u32[]{:S(2)}, u32[]{:S(2)}) async-start(bf16[32,144,128]{2,1,0:T(8,128)(2,1)} %get-tuple-element.629), calls=%async_computation.3 | async-start | bytes 2359296 | tf_op jit(solution)/shard_map/all_to_all | solution.py:711
  47.2 0.0 collective-permute-done.t0_ref
  47.2 3.5 %collective-permute-done.1.t1_ref = bf16[1024,256]{1,0:T(8,128)(2,1)} collective-permute-done((bf16[1024,256]{1,0:T(8,128)(2,1)S(1)}, bf16[1024,256]{1,0:T(8,128)(2,1)}, u32[]{:S(2)}, u32[]{:S(2)}) %collective-permute-start.1) | collective-permute-done | bytes 524320 | tf_op jit(solution)/shard_map/ppermute | solution.py:695
  50.7 22.7 %collective-permute-done.2.t2_ref = bf16[1024,256]{1,0:T(8,128)(2,1)} collective-permute-done((bf16[1024,256]{1,0:T(8,128)(2,1)S(1)}, bf16[1024,256]{1,0:T(8,128)(2,1)}, u32[]{:S(2)}, u32[]{:S(2)}) %collective-permute-start.2) | collective-permute-done | bytes 524320 | tf_op jit(solution)/shard_map/ppermute | solution.py:695
  73.4 0.0 collective-permute-done.3.t3_ref
  73.4 6.8 %partners.1.pair_ref = bf16[32,128,256]{2,1,0:T(8,128)(2,1)} custom-call(s32[32,128]{1,0:T(8,128)} %reshape.626.exp_ref, bf16[1024,256]{1,0:T(8,128)(2,1)} %collective-permute-done.t0_ref, bf16[1024,256]{1,0:T(8,128)(2,1)} %collective-permute-done.1.t1_ref, bf16[1024,256]{1,0:T(8,128)(2,1)} %collective-permute-done.2.t2_ref, ...), custom_call_target="tpu_custom_call" | custom-call | flops 5000000000 | bytes 4000000 | tf_op jit(solution)/shard_map/partners/pallas_call | solution.py:503
  80.2 18.2 %scores.1.part_ref = f32[8,256]{1,0:T(8,128)} custom-call(s32[448]{0:T(512)} %get-tuple-element.620.list_ref, s32[8]{0:T(128)} %get-tuple-element.621.groups_ref, s32[56]{0:T(128)} %get-tuple-element.622.live_ref, bf16[1024,128]{1,0:T(8,128)(2,1)} %get-tuple-element.623.q_ref, bf16[1024,256]{1,0:T(8,128)(2,1)} %get-tuple-element.624.kv_ref, ...), custom_call_target="tpu_custom_call" | custom-call | flops 12000000000 | bytes 4000000 | tf_op jit(solution)/shard_map/scores/pallas_call | solution.py:503
  98.5 0.0 collective-permute-start.4
  98.5 0.0 collective-permute-start.5
  98.5 2.1 collective-permute-start.6
  100.6 1.0 collective-permute-start.7
  101.6 0.0 all-to-all-done.3.hv_ref
  101.6 1.0 copy-done.1
  102.6 32.0 %values.1 = (bf16[1024,128]{1,0:T(8,128)(2,1)}, f32[1024,128]{1,0:T(8,128)S(1)}, bf16[32,144,128]{2,1,0:T(8,128)(2,1)}, bf16[128,128]{1,0:T(8,128)(2,1)}, bf16[8...) custom-call(s32[448]{0:T(512)} %get-tuple-element.620.list_ref, ...), custom_call_target="tpu_custom_call" | custom-call | flops 20000000000 | bytes 4000000 | tf_op jit(solution)/shard_map/values/pallas_call | solution.py:503
  134.6 0.0 collective-permute-done.4.o0_ref
  134.6 0.0 collective-permute-done.5.o1_ref
  134.6 0.0 collective-permute-done.6.o2_ref
  134.6 0.0 collective-permute-done.7.o3_ref
  134.7 0.7 copy-done.10
  135.4 39.7 %keys.1 = (bf16[1024,128]{1,0:T(8,128)(2,1)}, f32[1024,128]{1,0:T(8,128)S(1)}, bf16[32,144,128]{2,1,0:T(8,128)(2,1)}, bf16[128,128]{1,0:T(8,128)(2,1)}, bf16[8,16,128]{2,1,0:T(8,128)(2,1)}) custom-call(s32[448]{0:T(512)} %get-tuple-element.620.list_ref, s32[8]{0:T(128)} %get-tuple-element.621.groups_ref, s32[56]{0:T(128)} %get-tuple-element.622.live_ref, ...), custom_call_target="tpu_custom_call" | custom-call | flops 24999999488 | bytes 4000000 | tf_op jit(solution)/shard_map/keys/pallas_call | solution.py:503
  175.1 0.8 pad_maximum_fusion
  175.9 0.8 copy-done.12
  176.6 5.0 %all-to-all-start.5 = ((bf16[32,144,128]{2,1,0:T(8,128)(2,1)}), bf16[32,144,128]{2,1,0:T(8,128)(2,1)S(1)}, u32[]{:S(2)}, u32[]{:S(2)}) async-start(bf16[32,144,128]{2,1,0:T(8,128)(2,1)} %get-tuple-element.656), calls=%async_computation.5 | async-start | bytes 2359296 | tf_op jit(solution)/shard_map/all_to_all | solution.py:720
  181.7 18.4 %all-to-all-done.5.ret_ref = bf16[32,144,128]{2,1,0:T(8,128)(2,1)S(1)} async-done(((bf16[32,144,128]{2,1,0:T(8,128)(2,1)}), bf16[32,144,128]{2,1,0:T(8,128)(2,1)S(1)}, u32[]{:S(2)}, u32[]{:S(2)}) %all-to-all-start.5) | async-done | bytes 1179680 | tf_op jit(solution)/shard_map/all_to_all | solution.py:720
  200.1 3.9 %all-to-all-start.4 = ((bf16[32,144,128]{2,1,0:T(8,128)(2,1)}), bf16[32,144,128]{2,1,0:T(8,128)(2,1)S(1)}, u32[]{:S(2)}, u32[]{:S(2)}) async-start(bf16[32,144,128]{2,1,0:T(8,128)(2,1)} %get-tuple-element.647), calls=%async_computation.4 | async-start | bytes 2359296 | tf_op jit(solution)/shard_map/all_to_all | solution.py:726
  204.1 3.3 %collective-permute-start.10 = (bf16[2,8,16,128]{3,2,1,0:T(8,128)(2,1)S(1)}, bf16[2,8,16,128]{3,2,1,0:T(8,128)(2,1)S(1)}, u32[]{:S(2)}, u32[]{:S(2)}) collective-permute-start(bf16[2,8,16,128]{3,2,1,0:T(8,128)(2,1)S(1)} %pad_maximum_fusion.1), channel_id=1, source_target_pairs={{0,16},{4,20},{8,24},{12,28},{16,0},{20,4},{24,8},{28,12},{32,48},... | collective-permute-start | bytes 196616 | tf_op jit(solution)/shard_map/ppermute | solution.py:695
  207.4 1.5 collective-permute-start.11
  208.9 0.0 collective-permute-start.8
  208.9 0.6 collective-permute-start.9
  209.4 13.5 %collective-permute-done.10.p2_ref = bf16[2,8,16,128]{3,2,1,0:T(8,128)(2,1)S(1)} collective-permute-done((bf16[2,8,16,128]{3,2,1,0:T(8,128)(2,1)S(1)}, bf16[2,8,16,128]{3,2,1,0:T(8,128)(2,1)S(1)}, u32[]{:S(2)}, u32[]{:S(2)}) %collective-permute-start.10) | collective-permute-done | bytes 65568 | tf_op jit(solution)/shard_map/ppermute | solution.py:695
  223.0 0.0 collective-permute-done.11.p3_ref
  223.0 0.0 collective-permute-done.9.p1_ref
  223.0 0.6 copy-done.14
  223.6 0.0 copy-done.15
  223.6 0.0 copy-done.16
  223.7 0.6 copy-done.17
  224.3 10.0 %value_back.1.gv_ref = bf16[1024,128]{1,0:T(8,128)(2,1)} custom-call(s32[2]{0:T(128)} %pad_add_fusion.me_ref, f32[1024,128]{1,0:T(8,128)S(1)} %get-tuple-element.655.own_ref, bf16[32,144,128]{2,1,0:T(8,128)(2,1)} %copy-done.3, s32[32,128]{1,0:T(8,128)} %bitcast.107, bf16[2,8,16,128]{3,2,1,0:T(8,128)(2,1)} %copy-done.16, bf16[2,8,16,128]{3,2,1,0:T(8,128)(2,1)} %copy-done.17, ...), custom_call_target="tpu_custom_call" | custom-call | flops 8000000000 | bytes 4000000 | tf_op jit(solution)/shard_map/value_back/pallas_call | solution.py:503
  234.3 0.0 all-to-all-done.4.ret_ref
  234.3 1.0 copy-done.2
  235.3 11.1 %key_back.1 = (f32[1024,128]{1,0:T(8,128)}, bf16[1024,128]{1,0:T(8,128)(2,1)}, bf16[1024,128]{1,0:T(8,128)(2,1)}, bf16[1024,128]{1,0:T(8,128)(2,1)}) custom-call(s32[2]{0:T(128)} %pad_add_fusion.me_ref, f32[1024,128]{1,0:T(8,128)S(1)} %copy-done.13, bf16[32,144,128]{2,1,0:T(8,128)(2,1)} %copy-done.2, s32[32,128]{1,0:T(8,128)} %bitcast.108, ...), custom_call_target="tpu_custom_call" | custom-call | flops 8000000000 | bytes 4000000 | tf_op jit(solution)/shard_map/key_back/pallas_call | solution.py:503
  246.4 1.6 collective-permute-start.12
  248.0 2.9 %collective-permute-start.13 = (bf16[1024,128]{1,0:T(8,128)(2,1)}, bf16[1024,128]{1,0:T(8,128)(2,1)S(1)}, u32[]{:S(2)}, u32[]{:S(2)}) collective-permute-start(bf16[1024,128]{1,0:T(8,128)(2,1)} %get-tuple-element.659), channel_id=1, source_target_pairs={{0,2},{1,3},{2,0},{3,1},{4,6},{5,7},{6,4},{7,5},{8,10},{9,11},{10,... | collective-permute-start | bytes 786440 | tf_op jit(solution)/shard_map/ppermute | solution.py:734
  250.9 1.3 collective-permute-start.14
  252.2 3.7 %collective-permute-done.12 = bf16[1024,128]{1,0:T(8,128)(2,1)S(1)} collective-permute-done((bf16[1024,128]{1,0:T(8,128)(2,1)}, bf16[1024,128]{1,0:T(8,128)(2,1)S(1)}, u32[]{:S(2)}, u32[]{:S(2)}) %collective-permute-start.12) | collective-permute-done | bytes 262176 | tf_op jit(solution)/shard_map/ppermute | solution.py:734
  256.0 5.2 %collective-permute-done.13 = bf16[1024,128]{1,0:T(8,128)(2,1)S(1)} collective-permute-done((bf16[1024,128]{1,0:T(8,128)(2,1)}, bf16[1024,128]{1,0:T(8,128)(2,1)S(1)}, u32[]{:S(2)}, u32[]{:S(2)}) %collective-permute-start.13) | collective-permute-done | bytes 262176 | tf_op jit(solution)/shard_map/ppermute | solution.py:734
  261.2 1.9 add_convert_fusion
  (33 shorter events, 0.1 us)
Async XLA Ops:
  4.9 10.0 %copy-start.5 = (s32[128]{0:T(128)S(1)}, s32[128]{0:T(128)}, u32[]{:S(2)}) copy-start(s32[128]{0:T(128)} %param.23) | copy-start | bytes 1540
  14.9 8.4 %copy-start.4 = (bf16[1024,256]{1,0:T(8,128)(2,1)S(1)}, bf16[1024,256]{1,0:T(8,128)(2,1)}, u32[]{:S(2)}) copy-start(bf16[1024,256]{1,0:T(8,128)(2,1)} %get-tuple-element.624.kv_ref) | copy-start | bytes 1572868
  14.9 14.6 %copy-start.9 = (s32[8,40]{1,0:T(8,128)S(1)}, s32[8,40]{1,0:T(8,128)}, u32[]{:S(2)}) copy-start(s32[8,40]{1,0:T(8,128)} %param.21) | copy-start | bytes 3844
  14.9 26.8 %all-to-all-start.2 = ((bf16[32,144,128]{2,1,0:T(8,128)(2,1)}), bf16[32,144,128]{2,1,0:T(8,128)(2,1)S(1)}, u32[]{:S(2)}, u32[]{:S(2)}) async-start(bf16[32,144,128]{2,1,0:T(8,128)(2,1)} %get-tuple-element.628), calls=%async_computation.2 | async-start | bytes 2359296 | tf_op jit(solution)/shard_map/all_to_all | solution.py:708
  23.4 23.8 %collective-permute-start = (bf16[1024,256]{1,0:T(8,128)(2,1)S(1)}, bf16[1024,256]{1,0:T(8,128)(2,1)}, u32[]{:S(2)}, u32[]{:S(2)}) collective-permute-start(bf16[1024,256]{1,0:T(8,128)(2,1)S(1)} %copy-done.4), channel_id=1, source_target_pairs={{0,4},{4,0},{8,12},{12,8},{16,20},{20,16},{24,28},{28,24},{32,36},... | collective-permute-start | bytes 1572872 | tf_op jit(solution)/shard_map/ppermute | solution.py:695
  23.7 27.0 %collective-permute-start.1 = (bf16[1024,256]{1,0:T(8,128)(2,1)S(1)}, bf16[1024,256]{1,0:T(8,128)(2,1)}, u32[]{:S(2)}, u32[]{:S(2)}) collective-permute-start(bf16[1024,256]{1,0:T(8,128)(2,1)S(1)} %copy-done.4), channel_id=1, source_target_pairs={{0,8},{4,12},{8,0},{12,4},{16,24},{20,28},{24,16},{28,20},{32,40},... | collective-permute-start | bytes 1572872 | tf_op jit(solution)/shard_map/ppermute | solution.py:695
  25.4 48.0 %collective-permute-start.2 = (bf16[1024,256]{1,0:T(8,128)(2,1)S(1)}, bf16[1024,256]{1,0:T(8,128)(2,1)}, u32[]{:S(2)}, u32[]{:S(2)}) collective-permute-start(bf16[1024,256]{1,0:T(8,128)(2,1)S(1)} %copy-done.4), channel_id=1, source_target_pairs={{0,16},{4,20},{8,24},{12,28},{16,0},{20,4},{24,8},{28,12},{32,48},... | collective-permute-start | bytes 1572872 | tf_op jit(solution)/shard_map/ppermute | solution.py:695
  28.1 45.4 %collective-permute-start.3 = (bf16[1024,256]{1,0:T(8,128)(2,1)S(1)}, bf16[1024,256]{1,0:T(8,128)(2,1)}, u32[]{:S(2)}, u32[]{:S(2)}) collective-permute-start(bf16[1024,256]{1,0:T(8,128)(2,1)S(1)} %copy-done.4), channel_id=1, source_target_pairs={{0,32},{4,36},{8,40},{12,44},{16,48},{20,52},{24,56},{28,60},{32,0... | collective-permute-start | bytes 1572872 | tf_op jit(solution)/shard_map/ppermute | solution.py:695
  41.8 1.1 copy-start
  42.9 58.7 %all-to-all-start.3 = ((bf16[32,144,128]{2,1,0:T(8,128)(2,1)}), bf16[32,144,128]{2,1,0:T(8,128)(2,1)S(1)}, u32[]{:S(2)}, u32[]{:S(2)}) async-start(bf16[32,144,128]{2,1,0:T(8,128)(2,1)} %get-tuple-element.629), calls=%async_computation.3 | async-start | bytes 2359296 | tf_op jit(solution)/shard_map/all_to_all | solution.py:711
  98.5 36.2 %collective-permute-start.4 = (bf16[1056,256]{1,0:T(8,128)(2,1)}, bf16[1056,256]{1,0:T(8,128)(2,1)S(1)}, u32[]{:S(2)}, u32[]{:S(2)}) collective-permute-start(bf16[1056,256]{1,0:T(8,128)(2,1)} %get-tuple-element.634), channel_id=1, source_target_pairs={{0,4},{4,0},{8,12},{12,8},{16,20},{20,16},{24,28},{28,24},{32,36},... | collective-permute-start | bytes 1622024 | tf_op jit(solution)/shard_map/ppermute | solution.py:695
  98.5 36.2 %collective-permute-start.5 = (bf16[1056,256]{1,0:T(8,128)(2,1)}, bf16[1056,256]{1,0:T(8,128)(2,1)S(1)}, u32[]{:S(2)}, u32[]{:S(2)}) collective-permute-start(bf16[1056,256]{1,0:T(8,128)(2,1)} %get-tuple-element.634), channel_id=1, source_target_pairs={{0,8},{4,12},{8,0},{12,4},{16,24},{20,28},{24,16},{28,20},{32,40},... | collective-permute-start | bytes 1622024 | tf_op jit(solution)/shard_map/ppermute | solution.py:695
  98.5 36.2 %collective-permute-start.6 = (bf16[1056,256]{1,0:T(8,128)(2,1)}, bf16[1056,256]{1,0:T(8,128)(2,1)}, u32[]{:S(2)}, u32[]{:S(2)}) collective-permute-start(bf16[1056,256]{1,0:T(8,128)(2,1)} %get-tuple-element.634), channel_id=1, source_target_pairs={{0,16},{4,20},{8,24},{12,28},{16,0},{20,4},{24,8},{28,12},{32,48},... | collective-permute-start | bytes 1622024 | tf_op jit(solution)/shard_map/ppermute | solution.py:695
  100.6 34.1 %collective-permute-start.7 = (bf16[1056,256]{1,0:T(8,128)(2,1)}, bf16[1056,256]{1,0:T(8,128)(2,1)}, u32[]{:S(2)}, u32[]{:S(2)}) collective-permute-start(bf16[1056,256]{1,0:T(8,128)(2,1)} %get-tuple-element.634), channel_id=1, source_target_pairs={{0,32},{4,36},{8,40},{12,44},{16,48},{20,52},{24,56},{28,60},{32,0... | collective-permute-start | bytes 1622024 | tf_op jit(solution)/shard_map/ppermute | solution.py:695
  101.6 1.0 copy-start.1
  134.6 0.8 copy-start.10
  134.6 40.4 %copy-start.11 = (bf16[1056,256]{1,0:T(8,128)(2,1)}, bf16[1056,256]{1,0:T(8,128)(2,1)S(1)}, u32[]{:S(2)}) copy-start(bf16[1056,256]{1,0:T(8,128)(2,1)S(1)} %collective-permute-done.5.o1_ref) | copy-start | bytes 1622020
  135.4 39.7 %copy-start.8 = (bf16[128,128]{1,0:T(8,128)(2,1)S(1)}, bf16[128,128]{1,0:T(8,128)(2,1)}, u32[]{:S(2)}) copy-start(bf16[128,128]{1,0:T(8,128)(2,1)} %get-tuple-element.643) | copy-start | bytes 98308
  175.9 0.8 copy-start.12
  176.6 23.4 %all-to-all-start.5 = ((bf16[32,144,128]{2,1,0:T(8,128)(2,1)}), bf16[32,144,128]{2,1,0:T(8,128)(2,1)S(1)}, u32[]{:S(2)}, u32[]{:S(2)}) async-start(bf16[32,144,128]{2,1,0:T(8,128)(2,1)} %get-tuple-element.656), calls=%async_computation.5 | async-start | bytes 2359296 | tf_op jit(solution)/shard_map/all_to_all | solution.py:720
  181.7 22.3 %copy-start.6 = (bf16[8,16,128]{2,1,0:T(8,128)(2,1)S(1)}, bf16[8,16,128]{2,1,0:T(8,128)(2,1)}, u32[]{:S(2)}) copy-start(bf16[8,16,128]{2,1,0:T(8,128)(2,1)} %get-tuple-element.649) | copy-start | bytes 98308
  181.7 22.3 %copy-start.7 = (bf16[8,16,128]{2,1,0:T(8,128)(2,1)S(1)}, bf16[8,16,128]{2,1,0:T(8,128)(2,1)}, u32[]{:S(2)}) copy-start(bf16[8,16,128]{2,1,0:T(8,128)(2,1)} %get-tuple-element.648) | copy-start | bytes 98308
  200.1 4.0 %copy-start.3 = (bf16[32,144,128]{2,1,0:T(8,128)(2,1)}, bf16[32,144,128]{2,1,0:T(8,128)(2,1)S(1)}, u32[]{:S(2)}) copy-start(bf16[32,144,128]{2,1,0:T(8,128)(2,1)S(1)} %all-to-all-done.5.ret_ref) | copy-start | bytes 3538948
  200.1 34.2 %all-to-all-start.4 = ((bf16[32,144,128]{2,1,0:T(8,128)(2,1)}), bf16[32,144,128]{2,1,0:T(8,128)(2,1)S(1)}, u32[]{:S(2)}, u32[]{:S(2)}) async-start(bf16[32,144,128]{2,1,0:T(8,128)(2,1)} %get-tuple-element.647), calls=%async_computation.4 | async-start | bytes 2359296 | tf_op jit(solution)/shard_map/all_to_all | solution.py:726
  204.0 31.3 %copy-start.13 = (f32[1024,128]{1,0:T(8,128)S(1)}, f32[1024,128]{1,0:T(8,128)}, u32[]{:S(2)}) copy-start(f32[1024,128]{1,0:T(8,128)} %copy-done.12) | copy-start | bytes 1572868
  204.1 18.9 %collective-permute-start.10 = (bf16[2,8,16,128]{3,2,1,0:T(8,128)(2,1)S(1)}, bf16[2,8,16,128]{3,2,1,0:T(8,128)(2,1)S(1)}, u32[]{:S(2)}, u32[]{:S(2)}) collective-permute-start(bf16[2,8,16,128]{3,2,1,0:T(8,128)(2,1)S(1)} %pad_maximum_fusion.1), channel_id=1, source_target_pairs={{0,16},{4,20},{8,24},{12,28},{16,0},{20,4},{24,8},{28,12},{32,48},... | collective-permute-start | bytes 196616 | tf_op jit(solution)/shard_map/ppermute | solution.py:695
  207.4 15.6 %collective-permute-start.11 = (bf16[2,8,16,128]{3,2,1,0:T(8,128)(2,1)S(1)}, bf16[2,8,16,128]{3,2,1,0:T(8,128)(2,1)S(1)}, u32[]{:S(2)}, u32[]{:S(2)}) collective-permute-start(bf16[2,8,16,128]{3,2,1,0:T(8,128)(2,1)S(1)} %pad_maximum_fusion.1), channel_id=1, source_target_pairs={{0,32},{4,36},{8,40},{12,44},{16,48},{20,52},{24,56},{28,60},{32,0... | collective-permute-start | bytes 196616 | tf_op jit(solution)/shard_map/ppermute | solution.py:695
  208.9 14.1 %collective-permute-start.8 = (bf16[2,8,16,128]{3,2,1,0:T(8,128)(2,1)S(1)}, bf16[2,8,16,128]{3,2,1,0:T(8,128)(2,1)S(1)}, u32[]{:S(2)}, u32[]{:S(2)}) collective-permute-start(bf16[2,8,16,128]{3,2,1,0:T(8,128)(2,1)S(1)} %pad_maximum_fusion.1), channel_id=1, source_target_pairs={{0,4},{4,0},{8,12},{12,8},{16,20},{20,16},{24,28},{28,24},{32,36},... | collective-permute-start | bytes 196616 | tf_op jit(solution)/shard_map/ppermute | solution.py:695
  208.9 14.1 %collective-permute-start.9 = (bf16[2,8,16,128]{3,2,1,0:T(8,128)(2,1)S(1)}, bf16[2,8,16,128]{3,2,1,0:T(8,128)(2,1)S(1)}, u32[]{:S(2)}, u32[]{:S(2)}) collective-permute-start(bf16[2,8,16,128]{3,2,1,0:T(8,128)(2,1)S(1)} %pad_maximum_fusion.1), channel_id=1, source_target_pairs={{0,8},{4,12},{8,0},{12,4},{16,24},{20,28},{24,16},{28,20},{32,40},... | collective-permute-start | bytes 196616 | tf_op jit(solution)/shard_map/ppermute | solution.py:695
  223.0 0.6 copy-start.14
  223.0 0.6 copy-start.15
  223.0 0.7 copy-start.16
  223.7 0.6 copy-start.17
  234.3 1.0 copy-start.2
  246.4 9.5 %collective-permute-start.12 = (bf16[1024,128]{1,0:T(8,128)(2,1)}, bf16[1024,128]{1,0:T(8,128)(2,1)S(1)}, u32[]{:S(2)}, u32[]{:S(2)}) collective-permute-start(bf16[1024,128]{1,0:T(8,128)(2,1)} %get-tuple-element.658), channel_id=1, source_target_pairs={{0,1},{1,2},{2,3},{3,0},{4,5},{5,6},{6,7},{7,4},{8,9},{9,10},{10,1... | collective-permute-start | bytes 786440 | tf_op jit(solution)/shard_map/ppermute | solution.py:734
  248.0 13.2 %collective-permute-start.13 = (bf16[1024,128]{1,0:T(8,128)(2,1)}, bf16[1024,128]{1,0:T(8,128)(2,1)S(1)}, u32[]{:S(2)}, u32[]{:S(2)}) collective-permute-start(bf16[1024,128]{1,0:T(8,128)(2,1)} %get-tuple-element.659), channel_id=1, source_target_pairs={{0,2},{1,3},{2,0},{3,1},{4,6},{5,7},{6,4},{7,5},{8,10},{9,11},{10,... | collective-permute-start | bytes 786440 | tf_op jit(solution)/shard_map/ppermute | solution.py:734
  250.9 10.3 %collective-permute-start.14 = (bf16[1024,128]{1,0:T(8,128)(2,1)}, bf16[1024,128]{1,0:T(8,128)(2,1)S(1)}, u32[]{:S(2)}, u32[]{:S(2)}) collective-permute-start(bf16[1024,128]{1,0:T(8,128)(2,1)} %get-tuple-element.660), channel_id=1, source_target_pairs={{0,3},{1,0},{2,1},{3,2},{4,7},{5,4},{6,5},{7,6},{8,11},{9,8},{10,9... | collective-permute-start | bytes 786440 | tf_op jit(solution)/shard_map/ppermute | solution.py:734

commit v3 on v2

--- a/solution.py
+++ b/solution.py
@@ -17,8 +17,8 @@
 GLOBAL_BLOCK = Q_BLOCKS + SENDERS
 EMPTY_BLOCK = GLOBAL_BLOCK + 1
 KEY_BLOCKS = EMPTY_BLOCK + 1
-GROUP = 4
-PAIR = 2
+GROUP = 8
+PAIR = 4
 LIST = 56
 EXTRA = 16
 SLOTS = BLOCK + EXTRA
@@ -96,6 +96,10 @@
     return jnp.sum(jnp.where(hit, local, 0).astype(F32), axis=1, keepdims=True).astype(jnp.int32) - 1
 
 
+def exp_row(exp_ref, m, i):
+    return exp_ref[m : m + 1, i * BLOCK : (i + 1) * BLOCK]
+
+
 def project_kernel(
     me_ref, x_ref, wq_ref, wk_ref, wv_ref, cot_ref, rows_ref, exp_ref, gid_ref, q_ref, kv_ref, outk_ref, outv_ref, away_ref
 ):
@@ -106,9 +110,10 @@
     q_ref[...] = query
     away_ref[:NODES_HERE, :COLS] = query
     away_ref[:NODES_HERE, COLS:] = cot_ref[...]
-    low, high = split_index(exp_ref[...])
-    away_ref[NODES_HERE:, :COLS] = low
-    away_ref[NODES_HERE:, COLS:] = high
+    for m in range(EXPANDERS):
+        low, high = split_index(jnp.concatenate([exp_row(exp_ref, m, i) for i in range(Q_BLOCKS)], axis=0))
+        away_ref[NODES_HERE + m * Q_BLOCKS : NODES_HERE + (m + 1) * Q_BLOCKS, :COLS] = low
+        away_ref[NODES_HERE + m * Q_BLOCKS : NODES_HERE + (m + 1) * Q_BLOCKS, COLS:] = high
     mine = jnp.broadcast_to(mine_columns(gid_ref[...], me_ref[0]), (EXTRA, BLOCK))
     lanes = iota((EXTRA, NODES_HERE), 1)
     hot = (jnp.concatenate([mine] * (NODES_HERE // BLOCK), axis=1) == lanes).astype(F32).astype(BF16)
@@ -129,15 +134,11 @@
 
 def partner_kernel(exp_ref, t0_ref, t1_ref, t2_ref, t3_ref, out_ref):
     for m, table in enumerate((t0_ref, t1_ref, t2_ref, t3_ref)):
-
-        def gather(t, carry):
-            b = m * Q_BLOCKS + t * GROUP
-            got = dot(one_hot_of_rows([exp_ref[pl.ds(b + u, 1), :] for u in range(GROUP)]), table[...]).astype(BF16)
-            for u in range(GROUP):
-                out_ref[b + u] = got[u * BLOCK : (u + 1) * BLOCK]
-            return carry
-
-        lax.fori_loop(0, Q_BLOCKS // GROUP, gather, 0)
+        for t in range(0, Q_BLOCKS, 4):
+            hot = one_hot_of_rows([exp_row(exp_ref, m, t + u) for u in range(4)])
+            got = dot(hot, table[...]).astype(BF16)
+            for u in range(4):
+                out_ref[m * Q_BLOCKS + t + u] = got[u * BLOCK : (u + 1) * BLOCK]
 
 
 def plan_kernel(mask_ref, count_ref, list_ref, groups_ref, live_ref):
@@ -456,7 +457,7 @@
             for u in range(GROUP):
                 i = t * GROUP + u
                 splits.append((index_low[i : i + 1], index_high[i : i + 1]))
-                wide = dot(part[1 if first_col else 0, i].astype(F32).T.astype(BF16), picks)
+                wide = dot(part[i].astype(F32).T.astype(BF16), picks)
                 rows = other[i * BLOCK : (i + 1) * BLOCK, first_col : first_col + COLS].astype(F32)
                 data.append((wide * rows).astype(BF16))
             scatter_into(acc_s, splits, jnp.concatenate(data, axis=0))
@@ -481,14 +482,14 @@
 
 
 def key_back_kernel(
-    me_ref, own_ref, ret_ref, rows_ref, p0_ref, p1_ref, p2_ref, p3_ref, o0_ref, o1_ref, o2_ref, o3_ref, gid_ref,
+    me_ref, feat_ref, own_ref, ret_ref, rows_ref, p0_ref, p1_ref, p2_ref, p3_ref, o0_ref, o1_ref, o2_ref, o3_ref, gid_ref,
     wq_ref, wk_ref, wv_ref, gq_ref, gv_ref, t0_ref, t1_ref, t2_ref, t3_ref, acc_s,
 ):
     parts, others = (p0_ref, p1_ref, p2_ref, p3_ref), (o0_ref, o1_ref, o2_ref, o3_ref)
     gather_grads(me_ref, own_ref, ret_ref, rows_ref, parts, others, 0, gid_ref, acc_s)
     grad_key = acc_s[...].astype(BF16)
     for k, out in enumerate((t0_ref, t1_ref, t2_ref, t3_ref)):
-        part = pl.ds(pl.multiple_of(((me_ref[1] + k) % 4) * COLS, COLS), COLS)
+        part = pl.ds(pl.multiple_of(((feat_ref[0] + k) % 4) * COLS, COLS), COLS)
         term = dot_nt(gq_ref[...], wq_ref[part, :]) + dot_nt(gv_ref[...], wv_ref[part, :])
         term = term + dot_nt(grad_key, wk_ref[part, :])
         out[...] = term.astype(out.dtype)
@@ -618,12 +619,12 @@
     )[0]
 
 
-def run_key_back(me, own_k, returned_k, rows, parts, others, gids, w_query, w_key, w_value, grad_query, grad_value):
+def run_key_back(me, feat, own_k, returned_k, rows, parts, others, gids, w_query, w_key, w_value, grad_query, grad_value):
     return call(
         key_back_kernel,
-        [smem()] + [vmem()] * 17,
+        [smem()] * 2 + [vmem()] * 17,
         (shape((NODES_HERE, COLS), F32),) + tuple(shape((NODES_HERE, COLS)) for _ in range(3)),
-        (me, own_k, returned_k, rows, *parts, *others, gids, w_query, w_key, w_value, grad_query, grad_value),
+        (me, feat, own_k, returned_k, rows, *parts, *others, gids, w_query, w_key, w_value, grad_query, grad_value),
         scratch=[pltpu.VMEM((NODES_HERE, COLS), F32)],
         name="key_back",
         flops=8_000_000_000,
@@ -648,7 +649,7 @@
         slot = rank - r * EXTRA
         here = (slot >= 0) & (slot < EXTRA)
         place = jnp.where((owner == my_index) & here, slot, EXTRA)
-        rows = jnp.zeros((EXTRA + 1, paired.shape[1]), BF16).at[place].set(paired[global_ids % NODES_HERE])[:EXTRA]
+        rows = jnp.zeros((EXTRA + 1, paired.shape[1]), BF16).at[place].set(paired[jnp.where(here, global_ids % NODES_HERE, 0)])[:EXTRA]
         got = lax.all_to_all(jnp.broadcast_to(rows[None], (SENDERS, *rows.shape)), "dom", 0, 0, tiled=True)
         found = got.reshape(SENDERS * EXTRA, -1)[jnp.clip(owner * EXTRA + slot, 0, SENDERS * EXTRA - 1)]
         return r + 1, jnp.where(here[:, None], found, glob)
@@ -696,13 +697,13 @@
 
     rows = send_rows[0]
     gids = global_ids.reshape(1, BLOCK)
-    exp_list = exp_rows.reshape(EXPANDERS * Q_BLOCKS, BLOCK)
-    me = jnp.stack([my_index, lax.axis_index("feat")]).astype(jnp.int32)
+    me = my_index.reshape(1).astype(jnp.int32)
+    feat = lax.axis_index("feat").reshape(1).astype(jnp.int32)
+
+    query, paired, out_k, out_v, away = run_project(
+        me, features, w_query, w_key, w_value, cotangent, rows, exp_rows, gids
+    )
     rounds = more_rounds(global_ids)
-
-    query, paired, out_k, out_v, away = run_project(
-        me, features, w_query, w_key, w_value, cotangent, rows, exp_list, gids
-    )
     glob = more_globals(rounds, global_ids, my_index, paired)
     out_k, out_v, glob = lax.optimization_barrier((out_k, out_v, glob))
     halo_k = lax.all_to_all(out_k, "dom", 0, 0, tiled=True)
@@ -710,25 +711,26 @@
     plan = run_plan(block_mask, halo_count)
     halo_v = lax.all_to_all(out_v, "dom", 0, 0, tiled=True)
     part = run_scores(plan, query, paired, halo_k, gids, glob)
-    pairs = run_partners(exp_list, swaps)
-    away, part = lax.optimization_barrier((away, part))
+    away, part, *swaps = lax.optimization_barrier((away, part, *swaps))
+    pairs = run_partners(exp_rows, swaps)
     others = [swapped(away, m) for m in range(EXPANDERS)]
     attended, own_v, back_v, glob_v, weight_p, pdp, delta, lse = run_values(
         plan, query, paired, halo_k, halo_v, gids, glob, pairs, cotangent, part
     )
     *others, lse = lax.optimization_barrier((*others, lse))
+    parts_v = [swapped(weight_p, m) for m in range(EXPANDERS)]
     returned_v = lax.all_to_all(back_v, "dom", 0, 0, tiled=True)
     grad_query, own_k, back_k, glob_k, dscore_p = run_keys(
         plan, query, paired, halo_k, halo_v, gids, glob, pairs, cotangent, lse, pdp, delta
     )
+    own_k, returned_v = lax.optimization_barrier((own_k, returned_v))
     own_k, own_v = more_grads(rounds, global_ids, my_index, glob_k, glob_v, own_k, own_v)
     back_k, own_k, own_v = lax.optimization_barrier((back_k, own_k, own_v))
     returned_k = lax.all_to_all(back_k, "dom", 0, 0, tiled=True)
-    both = jnp.stack([dscore_p, weight_p])
-    parts = [swapped(both, m) for m in range(EXPANDERS)]
-    grad_value = run_value_back(me, own_v, returned_v, rows, parts, others, gids)
+    parts_k = [swapped(dscore_p, m) for m in range(EXPANDERS)]
+    grad_value = run_value_back(me, own_v, returned_v, rows, parts_v, others, gids)
     mine, *away = run_key_back(
-        me, own_k, returned_k, rows, parts, others, gids, w_query, w_key, w_value, grad_query, grad_value
+        me, feat, own_k, returned_k, rows, parts_k, others, gids, w_query, w_key, w_value, grad_query, grad_value
     )
     for k, term in enumerate(away, 1):
         mine = mine + lax.ppermute(term, "feat", [(i, (i + k) % 4) for i in range(4)]).astype(F32)

time: 265 us -> 208 us (0.78)
  waiting for transfers between devices: 74.2 us -> 38.9 us
  Pallas kernels: 130 us -> 103 us
  starting transfers between devices: 42.2 us -> 52 us
  local copies, waits for them, and re-layouts: 9.83 us -> 6.79 us
    pallas_call x8, Pallas kernels: 130 us -> 103 us  [call(): pl.pallas_call(kernel, out_shape=outs, in_specs=ins, out_specs=out_spaces...]
    all_to_all x1, waiting for transfers between devices: 18.4 us -> 0.01 us  [on_device(): returned_v = lax.all_to_all(back_v, 'dom', 0, 0, tiled=True)]
    ppermute x12 -> x16, waiting for transfers between devices: 39.8 us -> 23.3 us  [swapped(): lax.ppermute(value, 'dom', [(i, i ^ 1 << bit) for i in range(dom_count)])]
    all_to_all x1, starting transfers between devices: 3.94 us -> 8.98 us  [on_device(): returned_k = lax.all_to_all(back_k, 'dom', 0, 0, tiled=True)]
    ppermute x12 -> x16, starting transfers between devices: 14.7 us -> 17.8 us  [swapped(): lax.ppermute(value, 'dom', [(i, i ^ 1 << bit) for i in range(dom_count)])]
    unnamed x36 -> x42, local copies, waits for them, and re-layouts: 5.97 us -> 6.12 us
  transfers between devices with their start and end apart: 19 -> 23, of which waited for: 7 -> 6; matrix products, arithmetic and copies ran while one was open for 0% -> 1% of each run, Pallas kernels for 27% -> 42%
where the time goes in v3:
time: 208 us; the launch traced here: 206 us
  Pallas kernels  103 us (50%)
  starting transfers between devices  52 us (25%)
  waiting for transfers between devices  38.9 us (19%)
  local copies, waits for them, and re-layouts  6.79 us (3%)
  other arithmetic  4.22 us (2%)
    pallas_call x8, Pallas kernels, call(): pl.pallas_call(kernel, out_shape=outs, in_specs=ins, out_specs=out_spaces...  103 us
    ppermute x16, waiting for transfers between devices, swapped(): lax.ppermute(value, 'dom', [(i, i ^ 1 << bit) for i in range(dom_count)])  23.3 us
    ppermute x16, starting transfers between devices, swapped(): lax.ppermute(value, 'dom', [(i, i ^ 1 << bit) for i in range(dom_count)])  17.8 us
    all_to_all x1, starting transfers between devices, on_device(): returned_k = lax.all_to_all(back_k, 'dom', 0, 0, tiled=True)  8.98 us
    ppermute x3, waiting for transfers between devices, on_device(): lax.ppermute(term, 'feat', [(i, (i + k) % 4) for i in range(4)]).astype(F32)  8.44 us
    all_to_all x1, starting transfers between devices, on_device(): halo_k = lax.all_to_all(out_k, 'dom', 0, 0, tiled=True)  8.26 us
    all_to_all x1, waiting for transfers between devices, on_device(): halo_k = lax.all_to_all(out_k, 'dom', 0, 0, tiled=True)  7.12 us
    all_to_all x1, starting transfers between devices, on_device(): returned_v = lax.all_to_all(back_v, 'dom', 0, 0, tiled=True)  6.81 us
  transfers between devices with their start and end apart: 23, of which 6 were waited for; matrix products, arithmetic and copies ran while one was open for 1% of the time, Pallas kernels for 42%

profile of v3, /device:TPU:0, one launch (start us, length us, event | category | flops | bytes accessed | tf_op | source)
XLA Modules:
  0.0 206.1 jit_solution(880291438776917045)
XLA Ops:
  0.6 0.7 negate_bitcast_fusion
  1.3 0.1 convert_reduce_fusion.2
  1.4 0.6 reduce_max.9
  2.7 0.2 convert_reduce_fusion.1
  2.9 0.0 copy-start.4
  2.9 7.1 %project.1 = (bf16[1024,128]{1,0:T(8,128)(2,1)}, bf16[1024,256]{1,0:T(8,128)(2,1)S(1)}, bf16[32,144,128]{2,1,0:T(8,128)(2,1)}, bf16[32,144,128]{2,1,0:T(8,128)(2,1)}, bf16[1056,256]{1,0:T(8,128)(2,1)}) custom-call(s32[1]{0:T(128)} %bitcast.15.me_ref, bf16[1024,512]{1,0:T(8,128)(2,1)} %x_ref.1, bf16[512,128]{1,0:T(8,128)(2,1)} %wq_ref.3, ...), custom_call_target="tpu_custom_call" | custom-call | flops 3000000000 | bytes 4000000 | tf_op jit(solution)/shard_map/project/pallas_call | solution.py:504
  10.1 0.0 copy-start.6
  10.1 8.3 %all-to-all-start.2 = ((bf16[32,144,128]{2,1,0:T(8,128)(2,1)}), bf16[32,144,128]{2,1,0:T(8,128)(2,1)S(1)}, u32[]{:S(2)}, u32[]{:S(2)}) async-start(bf16[32,144,128]{2,1,0:T(8,128)(2,1)} %get-tuple-element.618), calls=%async_computation.2 | async-start | bytes 2359296 | tf_op jit(solution)/shard_map/all_to_all | solution.py:709
  18.4 0.4 collective-permute-start
  18.7 1.7 collective-permute-start.1
  20.4 2.7 %collective-permute-start.2 = (bf16[1024,256]{1,0:T(8,128)(2,1)S(1)}, bf16[1024,256]{1,0:T(8,128)(2,1)}, u32[]{:S(2)}, u32[]{:S(2)}) collective-permute-start(bf16[1024,256]{1,0:T(8,128)(2,1)S(1)} %get-tuple-element.934), channel_id=1, source_target_pairs={{0,16},{4,20},{8,24},{12,28},{16,0},{20,4},{24,8},{28,12},{32,48},... | collective-permute-start | bytes 1572872 | tf_op jit(solution)/shard_map/ppermute | solution.py:696
  23.1 1.5 collective-permute-start.3
  24.6 0.7 reshape.657.mask_ref
  25.2 4.5 %plan.1 = (s32[448]{0:T(512)}, s32[8]{0:T(128)}, s32[56]{0:T(128)}) custom-call(s32[320]{0:T(512)} %reshape.657.mask_ref, s32[32]{0:T(128)} %bitcast.115), custom_call_target="tpu_custom_call" | custom-call | bytes 4000000 | tf_op jit(solution)/shard_map/plan/pallas_call | solution.py:504
  29.7 7.1 %all-to-all-done.2.hk_ref = bf16[32,144,128]{2,1,0:T(8,128)(2,1)S(1)} async-done(((bf16[32,144,128]{2,1,0:T(8,128)(2,1)}), bf16[32,144,128]{2,1,0:T(8,128)(2,1)S(1)}, u32[]{:S(2)}, u32[]{:S(2)}) %all-to-all-start.2) | async-done | bytes 1179680 | tf_op jit(solution)/shard_map/all_to_all | solution.py:709
  36.8 1.0 copy-done.1
  37.8 4.3 %all-to-all-start.3 = ((bf16[32,144,128]{2,1,0:T(8,128)(2,1)}), bf16[32,144,128]{2,1,0:T(8,128)(2,1)S(1)}, u32[]{:S(2)}, u32[]{:S(2)}) async-start(bf16[32,144,128]{2,1,0:T(8,128)(2,1)} %get-tuple-element.619), calls=%async_computation.3 | async-start | bytes 2359296 | tf_op jit(solution)/shard_map/all_to_all | solution.py:712
  42.1 14.5 %scores.1.part_ref = f32[8,256]{1,0:T(8,128)} custom-call(s32[448]{0:T(512)} %get-tuple-element.610.list_ref, s32[8]{0:T(128)} %get-tuple-element.611.groups_ref, s32[56]{0:T(128)} %get-tuple-element.612.live_ref, bf16[1024,128]{1,0:T(8,128)(2,1)} %get-tuple-element.613.q_ref, bf16[1024,256]{1,0:T(8,128)(2,1)S(1)} %get-tuple-element.934, ...), custom_call_target="tpu_custom_call" | custom-call | flops 12000000000 | bytes 4000000 | tf_op jit(solution)/shard_map/scores/pallas_call | solution.py:504
  56.6 0.0 collective-permute-done.t0_ref
  56.6 0.0 collective-permute-done.1.t1_ref
  56.6 11.8 %collective-permute-done.2.t2_ref = bf16[1024,256]{1,0:T(8,128)(2,1)} collective-permute-done((bf16[1024,256]{1,0:T(8,128)(2,1)S(1)}, bf16[1024,256]{1,0:T(8,128)(2,1)}, u32[]{:S(2)}, u32[]{:S(2)}) %collective-permute-start.2) | collective-permute-done | bytes 524320 | tf_op jit(solution)/shard_map/ppermute | solution.py:696
  68.4 0.0 collective-permute-done.3.t3_ref
  68.4 0.0 collective-permute-start.4
  68.5 0.2 collective-permute-start.5
  68.7 2.2 %collective-permute-start.6 = (bf16[1056,256]{1,0:T(8,128)(2,1)}, bf16[1056,256]{1,0:T(8,128)(2,1)S(1)}, u32[]{:S(2)}, u32[]{:S(2)}) collective-permute-start(bf16[1056,256]{1,0:T(8,128)(2,1)} %get-tuple-element.628), channel_id=1, source_target_pairs={{0,16},{4,20},{8,24},{12,28},{16,0},{20,4},{24,8},{28,12},{32,48},... | collective-permute-start | bytes 1622024 | tf_op jit(solution)/shard_map/ppermute | solution.py:696
  70.8 1.4 collective-permute-start.7
  72.2 5.3 %partners.1.pair_ref = bf16[32,128,256]{2,1,0:T(8,128)(2,1)} custom-call(s32[4,1024]{1,0:T(4,128)} %exp_ref.3, bf16[1024,256]{1,0:T(8,128)(2,1)} %collective-permute-done.t0_ref, bf16[1024,256]{1,0:T(8,128)(2,1)} %collective-permute-done.1.t1_ref, bf16[1024,256]{1,0:T(8,128)(2,1)} %collective-permute-done.2.t2_ref, ...), custom_call_target="tpu_custom_call" | custom-call | flops 5000000000 | bytes 4000000 | tf_op jit(solution)/shard_map/partners/pallas_call | solution.py:504
  77.5 0.0 all-to-all-done.3.hv_ref
  77.5 1.0 copy-done.3
  78.5 24.4 %values.1 = (bf16[1024,128]{1,0:T(8,128)(2,1)}, f32[1024,128]{1,0:T(8,128)}, bf16[32,144,128]{2,1,0:T(8,128)(2,1)}, bf16[128,128]{1,0:T(8,128)(2,1)}, bf16[8,16,...) custom-call(s32[448]{0:T(512)} %get-tuple-element.610.list_ref, ...), custom_call_target="tpu_custom_call" | custom-call | flops 20000000000 | bytes 4000000 | tf_op jit(solution)/shard_map/values/pallas_call | solution.py:504
  102.9 0.0 collective-permute-done.4.o0_ref
  103.0 0.0 collective-permute-done.6.o2_ref
  103.0 0.8 copy-done.7
  103.8 0.2 copy-done.8
  104.0 0.2 copy-done.9
  104.1 6.8 %all-to-all-start.4 = ((bf16[32,144,128]{2,1,0:T(8,128)(2,1)}), bf16[32,144,128]{2,1,0:T(8,128)(2,1)S(1)}, u32[]{:S(2)}, u32[]{:S(2)}) async-start(bf16[32,144,128]{2,1,0:T(8,128)(2,1)} %get-tuple-element.635), calls=%async_computation.4 | async-start | bytes 2359296 | tf_op jit(solution)/shard_map/all_to_all | solution.py:722
  111.0 28.3 %keys.1 = (bf16[1024,128]{1,0:T(8,128)(2,1)}, f32[1024,128]{1,0:T(8,128)S(1)}, bf16[32,144,128]{2,1,0:T(8,128)(2,1)}, bf16[128,128]{1,0:T(8,128)(2,1)}, bf16[8,16,128]{2,1,0:T(8,128)(2,1)}) custom-call(s32[448]{0:T(512)} %get-tuple-element.610.list_ref, s32[8]{0:T(128)} %get-tuple-element.611.groups_ref, s32[56]{0:T(128)} %get-tuple-element.612.live_ref, ...), custom_call_target="tpu_custom_call" | custom-call | flops 24999999488 | bytes 4000000 | tf_op jit(solution)/shard_map/keys/pallas_call | solution.py:504
  139.3 0.8 pad_maximum_fusion
  140.1 1.0 copy-done
  141.1 9.0 %all-to-all-start.5 = ((bf16[32,144,128]{2,1,0:T(8,128)(2,1)}), bf16[32,144,128]{2,1,0:T(8,128)(2,1)S(1)}, u32[]{:S(2)}, u32[]{:S(2)}) async-start(bf16[32,144,128]{2,1,0:T(8,128)(2,1)} %get-tuple-element.643), calls=%async_computation.5 | async-start | bytes 2359296 | tf_op jit(solution)/shard_map/all_to_all | solution.py:729
  150.1 0.4 collective-permute-start.12
  150.4 1.7 collective-permute-start.13
  152.1 2.7 %collective-permute-start.14 = (bf16[8,16,128]{2,1,0:T(8,128)(2,1)S(1)}, bf16[8,16,128]{2,1,0:T(8,128)(2,1)S(1)}, u32[]{:S(2)}, u32[]{:S(2)}) collective-permute-start(bf16[8,16,128]{2,1,0:T(8,128)(2,1)S(1)} %copy-done.11), channel_id=1, source_target_pairs={{0,16},{4,20},{8,24},{12,28},{16,0},{20,4},{24,8},{28,12},{32,48},... | collective-permute-start | bytes 98312 | tf_op jit(solution)/shard_map/ppermute | solution.py:696
  154.8 1.5 collective-permute-start.15
  156.3 0.9 collective-permute-start.10
  157.1 0.6 collective-permute-start.11
  157.7 8.7 %collective-permute-done.13.p1_ref = bf16[8,16,128]{2,1,0:T(8,128)(2,1)S(1)} collective-permute-done((bf16[8,16,128]{2,1,0:T(8,128)(2,1)S(1)}, bf16[8,16,128]{2,1,0:T(8,128)(2,1)S(1)}, u32[]{:S(2)}, u32[]{:S(2)}) %collective-permute-start.13) | collective-permute-done | bytes 32800 | tf_op jit(solution)/shard_map/ppermute | solution.py:696
  166.4 2.7 %collective-permute-done.14.p2_ref = bf16[8,16,128]{2,1,0:T(8,128)(2,1)S(1)} collective-permute-done((bf16[8,16,128]{2,1,0:T(8,128)(2,1)S(1)}, bf16[8,16,128]{2,1,0:T(8,128)(2,1)S(1)}, u32[]{:S(2)}, u32[]{:S(2)}) %collective-permute-start.14) | collective-permute-done | bytes 32800 | tf_op jit(solution)/shard_map/ppermute | solution.py:696
  169.1 0.3 collective-permute-start.9
  169.4 0.3 copy-done.19
  169.7 0.6 copy-done.20
  170.4 8.7 %value_back.1.gv_ref = bf16[1024,128]{1,0:T(8,128)(2,1)} custom-call(s32[1]{0:T(128)} %bitcast.15.me_ref, f32[1024,128]{1,0:T(8,128)S(1)} %get-tuple-element.650.own_ref, bf16[32,144,128]{2,1,0:T(8,128)(2,1)} %copy-done, s32[32,128]{1,0:T(8,128)} %bitcast.117, bf16[8,16,128]{2,1,0:T(8,128)(2,1)} %copy-done.16, bf16[8,16,128]{2,1,0:T(8,128)(2,1)} %copy-done.18, ...), custom_call_target="tpu_custom_call" | custom-call | flops 8000000000 | bytes 4000000 | tf_op jit(solution)/shard_map/value_back/pallas_call | solution.py:504
  179.1 0.5 copy-done.13
  179.7 0.0 copy-done.14
  179.7 0.0 copy-done.15
  179.7 0.0 copy-done.17
  179.7 0.4 copy-done.2
  180.1 9.8 %key_back.1 = (f32[1024,128]{1,0:T(8,128)}, bf16[1024,128]{1,0:T(8,128)(2,1)}, bf16[1024,128]{1,0:T(8,128)(2,1)}, bf16[1024,128]{1,0:T(8,128)(2,1)}) custom-call(s32[1]{0:T(128)} %bitcast.15.me_ref, s32[1]{0:T(128)} %bitcast.20.feat_ref, f32[1024,128]{1,0:T(8,128)S(1)} %get-tuple-element.642.own_ref, bf16[32,144,128]{2,1,0:T(8,128)(2,1)} %copy-done.2, ...), custom_call_target="tpu_custom_call" | custom-call | flops 8000000000 | bytes 4000000 | tf_op jit(solution)/shard_map/key_back/pallas_call | solution.py:504
  190.0 1.6 collective-permute-start.16
  191.5 2.9 %collective-permute-start.17 = (bf16[1024,128]{1,0:T(8,128)(2,1)}, bf16[1024,128]{1,0:T(8,128)(2,1)S(1)}, u32[]{:S(2)}, u32[]{:S(2)}) collective-permute-start(bf16[1024,128]{1,0:T(8,128)(2,1)} %get-tuple-element.655), channel_id=1, source_target_pairs={{0,2},{1,3},{2,0},{3,1},{4,6},{5,7},{6,4},{7,5},{8,10},{9,11},{10,... | collective-permute-start | bytes 786440 | tf_op jit(solution)/shard_map/ppermute | solution.py:736
  194.4 1.3 collective-permute-start.18
  195.8 4.4 %collective-permute-done.16 = bf16[1024,128]{1,0:T(8,128)(2,1)S(1)} collective-permute-done((bf16[1024,128]{1,0:T(8,128)(2,1)}, bf16[1024,128]{1,0:T(8,128)(2,1)S(1)}, u32[]{:S(2)}, u32[]{:S(2)}) %collective-permute-start.16) | collective-permute-done | bytes 262176 | tf_op jit(solution)/shard_map/ppermute | solution.py:736
  200.2 4.1 %collective-permute-done.17 = bf16[1024,128]{1,0:T(8,128)(2,1)S(1)} collective-permute-done((bf16[1024,128]{1,0:T(8,128)(2,1)}, bf16[1024,128]{1,0:T(8,128)(2,1)S(1)}, u32[]{:S(2)}, u32[]{:S(2)}) %collective-permute-start.17) | collective-permute-done | bytes 262176 | tf_op jit(solution)/shard_map/ppermute | solution.py:736
  204.2 1.9 add_convert_fusion
  (42 shorter events, 0.1 us)
Async XLA Ops:
  2.9 7.2 %copy-start.4 = (s32[128]{0:T(128)S(1)}, s32[128]{0:T(128)}, u32[]{:S(2)}) copy-start(s32[128]{0:T(128)} %param.23) | copy-start | bytes 1540
  10.1 14.5 %copy-start.6 = (s32[8,40]{1,0:T(8,128)S(1)}, s32[8,40]{1,0:T(8,128)}, u32[]{:S(2)}) copy-start(s32[8,40]{1,0:T(8,128)} %param.21) | copy-start | bytes 3844
  10.1 26.7 %all-to-all-start.2 = ((bf16[32,144,128]{2,1,0:T(8,128)(2,1)}), bf16[32,144,128]{2,1,0:T(8,128)(2,1)S(1)}, u32[]{:S(2)}, u32[]{:S(2)}) async-start(bf16[32,144,128]{2,1,0:T(8,128)(2,1)} %get-tuple-element.618), calls=%async_computation.2 | async-start | bytes 2359296 | tf_op jit(solution)/shard_map/all_to_all | solution.py:709
  18.4 38.2 %collective-permute-start = (bf16[1024,256]{1,0:T(8,128)(2,1)S(1)}, bf16[1024,256]{1,0:T(8,128)(2,1)}, u32[]{:S(2)}, u32[]{:S(2)}) collective-permute-start(bf16[1024,256]{1,0:T(8,128)(2,1)S(1)} %get-tuple-element.934), channel_id=1, source_target_pairs={{0,4},{4,0},{8,12},{12,8},{16,20},{20,16},{24,28},{28,24},{32,36},... | collective-permute-start | bytes 1572872 | tf_op jit(solution)/shard_map/ppermute | solution.py:696
  18.7 37.9 %collective-permute-start.1 = (bf16[1024,256]{1,0:T(8,128)(2,1)S(1)}, bf16[1024,256]{1,0:T(8,128)(2,1)}, u32[]{:S(2)}, u32[]{:S(2)}) collective-permute-start(bf16[1024,256]{1,0:T(8,128)(2,1)S(1)} %get-tuple-element.934), channel_id=1, source_target_pairs={{0,8},{4,12},{8,0},{12,4},{16,24},{20,28},{24,16},{28,20},{32,40},... | collective-permute-start | bytes 1572872 | tf_op jit(solution)/shard_map/ppermute | solution.py:696
  20.4 48.0 %collective-permute-start.2 = (bf16[1024,256]{1,0:T(8,128)(2,1)S(1)}, bf16[1024,256]{1,0:T(8,128)(2,1)}, u32[]{:S(2)}, u32[]{:S(2)}) collective-permute-start(bf16[1024,256]{1,0:T(8,128)(2,1)S(1)} %get-tuple-element.934), channel_id=1, source_target_pairs={{0,16},{4,20},{8,24},{12,28},{16,0},{20,4},{24,8},{28,12},{32,48},... | collective-permute-start | bytes 1572872 | tf_op jit(solution)/shard_map/ppermute | solution.py:696
  23.1 45.4 %collective-permute-start.3 = (bf16[1024,256]{1,0:T(8,128)(2,1)S(1)}, bf16[1024,256]{1,0:T(8,128)(2,1)}, u32[]{:S(2)}, u32[]{:S(2)}) collective-permute-start(bf16[1024,256]{1,0:T(8,128)(2,1)S(1)} %get-tuple-element.934), channel_id=1, source_target_pairs={{0,32},{4,36},{8,40},{12,44},{16,48},{20,52},{24,56},{28,60},{32,0... | collective-permute-start | bytes 1572872 | tf_op jit(solution)/shard_map/ppermute | solution.py:696
  36.8 1.0 copy-start.1
  37.8 39.7 %all-to-all-start.3 = ((bf16[32,144,128]{2,1,0:T(8,128)(2,1)}), bf16[32,144,128]{2,1,0:T(8,128)(2,1)S(1)}, u32[]{:S(2)}, u32[]{:S(2)}) async-start(bf16[32,144,128]{2,1,0:T(8,128)(2,1)} %get-tuple-element.619), calls=%async_computation.3 | async-start | bytes 2359296 | tf_op jit(solution)/shard_map/all_to_all | solution.py:712
  68.4 34.5 %collective-permute-start.4 = (bf16[1056,256]{1,0:T(8,128)(2,1)}, bf16[1056,256]{1,0:T(8,128)(2,1)S(1)}, u32[]{:S(2)}, u32[]{:S(2)}) collective-permute-start(bf16[1056,256]{1,0:T(8,128)(2,1)} %get-tuple-element.628), channel_id=1, source_target_pairs={{0,4},{4,0},{8,12},{12,8},{16,20},{20,16},{24,28},{28,24},{32,36},... | collective-permute-start | bytes 1622024 | tf_op jit(solution)/shard_map/ppermute | solution.py:696
  68.5 34.5 %collective-permute-start.5 = (bf16[1056,256]{1,0:T(8,128)(2,1)}, bf16[1056,256]{1,0:T(8,128)(2,1)S(1)}, u32[]{:S(2)}, u32[]{:S(2)}) collective-permute-start(bf16[1056,256]{1,0:T(8,128)(2,1)} %get-tuple-element.628), channel_id=1, source_target_pairs={{0,8},{4,12},{8,0},{12,4},{16,24},{20,28},{24,16},{28,20},{32,40},... | collective-permute-start | bytes 1622024 | tf_op jit(solution)/shard_map/ppermute | solution.py:696
  68.7 34.3 %collective-permute-start.6 = (bf16[1056,256]{1,0:T(8,128)(2,1)}, bf16[1056,256]{1,0:T(8,128)(2,1)S(1)}, u32[]{:S(2)}, u32[]{:S(2)}) collective-permute-start(bf16[1056,256]{1,0:T(8,128)(2,1)} %get-tuple-element.628), channel_id=1, source_target_pairs={{0,16},{4,20},{8,24},{12,28},{16,0},{20,4},{24,8},{28,12},{32,48},... | collective-permute-start | bytes 1622024 | tf_op jit(solution)/shard_map/ppermute | solution.py:696
  70.8 32.1 %collective-permute-start.7 = (bf16[1056,256]{1,0:T(8,128)(2,1)}, bf16[1056,256]{1,0:T(8,128)(2,1)}, u32[]{:S(2)}, u32[]{:S(2)}) collective-permute-start(bf16[1056,256]{1,0:T(8,128)(2,1)} %get-tuple-element.628), channel_id=1, source_target_pairs={{0,32},{4,36},{8,40},{12,44},{16,48},{20,52},{24,56},{28,60},{32,0... | collective-permute-start | bytes 1622024 | tf_op jit(solution)/shard_map/ppermute | solution.py:696
  77.5 1.0 copy-start.3
  102.9 0.8 copy-start.7
  103.0 1.0 copy-start.8
  103.0 1.1 copy-start.9
  104.1 35.9 %all-to-all-start.4 = ((bf16[32,144,128]{2,1,0:T(8,128)(2,1)}), bf16[32,144,128]{2,1,0:T(8,128)(2,1)S(1)}, u32[]{:S(2)}, u32[]{:S(2)}) async-start(bf16[32,144,128]{2,1,0:T(8,128)(2,1)} %get-tuple-element.635), calls=%async_computation.4 | async-start | bytes 2359296 | tf_op jit(solution)/shard_map/all_to_all | solution.py:722
  110.9 28.3 %copy-start.5 = (bf16[128,128]{1,0:T(8,128)(2,1)S(1)}, bf16[128,128]{1,0:T(8,128)(2,1)}, u32[]{:S(2)}) copy-start(bf16[128,128]{1,0:T(8,128)(2,1)} %get-tuple-element.639) | copy-start | bytes 98308
  110.9 29.1 %copy-start.10 = (f32[1024,128]{1,0:T(8,128)S(1)}, f32[1024,128]{1,0:T(8,128)}, u32[]{:S(2)}) copy-start(f32[1024,128]{1,0:T(8,128)} %get-tuple-element.878) | copy-start | bytes 1572868
  140.1 1.0 copy-start
  141.1 9.0 %copy-start.11 = (bf16[8,16,128]{2,1,0:T(8,128)(2,1)S(1)}, bf16[8,16,128]{2,1,0:T(8,128)(2,1)}, u32[]{:S(2)}) copy-start(bf16[8,16,128]{2,1,0:T(8,128)(2,1)} %get-tuple-element.652) | copy-start | bytes 98308
  141.1 15.2 %copy-start.12 = (bf16[8,16,128]{2,1,0:T(8,128)(2,1)S(1)}, bf16[8,16,128]{2,1,0:T(8,128)(2,1)}, u32[]{:S(2)}) copy-start(bf16[8,16,128]{2,1,0:T(8,128)(2,1)} %get-tuple-element.644) | copy-start | bytes 98308
  141.1 38.0 %all-to-all-start.5 = ((bf16[32,144,128]{2,1,0:T(8,128)(2,1)}), bf16[32,144,128]{2,1,0:T(8,128)(2,1)S(1)}, u32[]{:S(2)}, u32[]{:S(2)}) async-start(bf16[32,144,128]{2,1,0:T(8,128)(2,1)} %get-tuple-element.643), calls=%async_computation.5 | async-start | bytes 2359296 | tf_op jit(solution)/shard_map/all_to_all | solution.py:729
  150.1 7.0 %collective-permute-start.12 = (bf16[8,16,128]{2,1,0:T(8,128)(2,1)S(1)}, bf16[8,16,128]{2,1,0:T(8,128)(2,1)S(1)}, u32[]{:S(2)}, u32[]{:S(2)}) collective-permute-start(bf16[8,16,128]{2,1,0:T(8,128)(2,1)S(1)} %copy-done.11), channel_id=1, source_target_pairs={{0,4},{4,0},{8,12},{12,8},{16,20},{20,16},{24,28},{28,24},{32,36},... | collective-permute-start | bytes 98312 | tf_op jit(solution)/shard_map/ppermute | solution.py:696
  150.4 15.9 %collective-permute-start.13 = (bf16[8,16,128]{2,1,0:T(8,128)(2,1)S(1)}, bf16[8,16,128]{2,1,0:T(8,128)(2,1)S(1)}, u32[]{:S(2)}, u32[]{:S(2)}) collective-permute-start(bf16[8,16,128]{2,1,0:T(8,128)(2,1)S(1)} %copy-done.11), channel_id=1, source_target_pairs={{0,8},{4,12},{8,0},{12,4},{16,24},{20,28},{24,16},{28,20},{32,40},... | collective-permute-start | bytes 98312 | tf_op jit(solution)/shard_map/ppermute | solution.py:696
  152.1 17.0 %collective-permute-start.14 = (bf16[8,16,128]{2,1,0:T(8,128)(2,1)S(1)}, bf16[8,16,128]{2,1,0:T(8,128)(2,1)S(1)}, u32[]{:S(2)}, u32[]{:S(2)}) collective-permute-start(bf16[8,16,128]{2,1,0:T(8,128)(2,1)S(1)} %copy-done.11), channel_id=1, source_target_pairs={{0,16},{4,20},{8,24},{12,28},{16,0},{20,4},{24,8},{28,12},{32,48},... | collective-permute-start | bytes 98312 | tf_op jit(solution)/shard_map/ppermute | solution.py:696
  154.8 14.6 %collective-permute-start.15 = (bf16[8,16,128]{2,1,0:T(8,128)(2,1)S(1)}, bf16[8,16,128]{2,1,0:T(8,128)(2,1)S(1)}, u32[]{:S(2)}, u32[]{:S(2)}) collective-permute-start(bf16[8,16,128]{2,1,0:T(8,128)(2,1)S(1)} %copy-done.11), channel_id=1, source_target_pairs={{0,32},{4,36},{8,40},{12,44},{16,48},{20,52},{24,56},{28,60},{32,0... | collective-permute-start | bytes 98312 | tf_op jit(solution)/shard_map/ppermute | solution.py:696
  156.3 22.8 %collective-permute-start.10 = (bf16[8,16,128]{2,1,0:T(8,128)(2,1)S(1)}, bf16[8,16,128]{2,1,0:T(8,128)(2,1)S(1)}, u32[]{:S(2)}, u32[]{:S(2)}) collective-permute-start(bf16[8,16,128]{2,1,0:T(8,128)(2,1)S(1)} %copy-done.12), channel_id=1, source_target_pairs={{0,16},{4,20},{8,24},{12,28},{16,0},{20,4},{24,8},{28,12},{32,48},... | collective-permute-start | bytes 98312 | tf_op jit(solution)/shard_map/ppermute | solution.py:696
  157.1 12.3 %copy-start.16 = (bf16[8,16,128]{2,1,0:T(8,128)(2,1)}, bf16[8,16,128]{2,1,0:T(8,128)(2,1)S(1)}, u32[]{:S(2)}) copy-start(bf16[8,16,128]{2,1,0:T(8,128)(2,1)S(1)} %collective-permute-done.12.p0_ref) | copy-start | bytes 98308
  157.1 21.9 %collective-permute-start.11 = (bf16[8,16,128]{2,1,0:T(8,128)(2,1)S(1)}, bf16[8,16,128]{2,1,0:T(8,128)(2,1)S(1)}, u32[]{:S(2)}, u32[]{:S(2)}) collective-permute-start(bf16[8,16,128]{2,1,0:T(8,128)(2,1)S(1)} %copy-done.12), channel_id=1, source_target_pairs={{0,32},{4,36},{8,40},{12,44},{16,48},{20,52},{24,56},{28,60},{32,0... | collective-permute-start | bytes 98312 | tf_op jit(solution)/shard_map/ppermute | solution.py:696
  166.4 3.1 %copy-start.18 = (bf16[8,16,128]{2,1,0:T(8,128)(2,1)}, bf16[8,16,128]{2,1,0:T(8,128)(2,1)S(1)}, u32[]{:S(2)}) copy-start(bf16[8,16,128]{2,1,0:T(8,128)(2,1)S(1)} %collective-permute-done.13.p1_ref) | copy-start | bytes 98308
  166.4 12.7 %collective-permute-start.8 = (bf16[8,16,128]{2,1,0:T(8,128)(2,1)S(1)}, bf16[8,16,128]{2,1,0:T(8,128)(2,1)S(1)}, u32[]{:S(2)}, u32[]{:S(2)}) collective-permute-start(bf16[8,16,128]{2,1,0:T(8,128)(2,1)S(1)} %copy-done.12), channel_id=1, source_target_pairs={{0,4},{4,0},{8,12},{12,8},{16,20},{20,16},{24,28},{28,24},{32,36},... | collective-permute-start | bytes 98312 | tf_op jit(solution)/shard_map/ppermute | solution.py:696
  169.1 0.6 copy-start.19
  169.1 10.0 %collective-permute-start.9 = (bf16[8,16,128]{2,1,0:T(8,128)(2,1)S(1)}, bf16[8,16,128]{2,1,0:T(8,128)(2,1)S(1)}, u32[]{:S(2)}, u32[]{:S(2)}) collective-permute-start(bf16[8,16,128]{2,1,0:T(8,128)(2,1)S(1)} %copy-done.12), channel_id=1, source_target_pairs={{0,8},{4,12},{8,0},{12,4},{16,24},{20,28},{24,16},{28,20},{32,40},... | collective-permute-start | bytes 98312 | tf_op jit(solution)/shard_map/ppermute | solution.py:696
  169.7 0.6 copy-start.20
  179.0 0.6 copy-start.13
  179.1 0.6 copy-start.14
  179.1 0.6 copy-start.15
  179.1 0.6 copy-start.17
  179.1 1.0 copy-start.2
  190.0 10.2 %collective-permute-start.16 = (bf16[1024,128]{1,0:T(8,128)(2,1)}, bf16[1024,128]{1,0:T(8,128)(2,1)S(1)}, u32[]{:S(2)}, u32[]{:S(2)}) collective-permute-start(bf16[1024,128]{1,0:T(8,128)(2,1)} %get-tuple-element.654), channel_id=1, source_target_pairs={{0,1},{1,2},{2,3},{3,0},{4,5},{5,6},{6,7},{7,4},{8,9},{9,10},{10,1... | collective-permute-start | bytes 786440 | tf_op jit(solution)/shard_map/ppermute | solution.py:736
  191.5 12.7 %collective-permute-start.17 = (bf16[1024,128]{1,0:T(8,128)(2,1)}, bf16[1024,128]{1,0:T(8,128)(2,1)S(1)}, u32[]{:S(2)}, u32[]{:S(2)}) collective-permute-start(bf16[1024,128]{1,0:T(8,128)(2,1)} %get-tuple-element.655), channel_id=1, source_target_pairs={{0,2},{1,3},{2,0},{3,1},{4,6},{5,7},{6,4},{7,5},{8,10},{9,11},{10,... | collective-permute-start | bytes 786440 | tf_op jit(solution)/shard_map/ppermute | solution.py:736
  194.4 9.8 %collective-permute-start.18 = (bf16[1024,128]{1,0:T(8,128)(2,1)}, bf16[1024,128]{1,0:T(8,128)(2,1)S(1)}, u32[]{:S(2)}, u32[]{:S(2)}) collective-permute-start(bf16[1024,128]{1,0:T(8,128)(2,1)} %get-tuple-element.656), channel_id=1, source_target_pairs={{0,3},{1,0},{2,1},{3,2},{4,7},{5,4},{6,5},{7,6},{8,11},{9,8},{10,9... | collective-permute-start | bytes 786440 | tf_op jit(solution)/shard_map/ppermute | solution.py:736

commit v4 on v3

--- a/solution.py
+++ b/solution.py
@@ -101,8 +101,11 @@
 
 
 def project_kernel(
-    me_ref, x_ref, wq_ref, wk_ref, wv_ref, cot_ref, rows_ref, exp_ref, gid_ref, q_ref, kv_ref, outk_ref, outv_ref, away_ref
+    me_ref, x_ref, wq_ref, wk_ref, wv_ref, cot_ref, rows_ref, exp_ref, gid_ref, q_ref, kv_ref, outk_ref, outv_ref, away_ref,
+    rounds_ref,
 ):
+    most = jnp.max(owner_ranks(gid_ref[...])[0].astype(F32)).astype(jnp.int32)
+    rounds_ref[0] = (most + EXTRA) // EXTRA
     x = x_ref[...]
     kv_ref[:, :COLS] = dot(x, wk_ref[...]).astype(BF16)
     kv_ref[:, COLS:] = dot(x, wv_ref[...]).astype(BF16)
@@ -132,13 +135,56 @@
     lax.fori_loop(0, SENDERS // GROUP, gather, 0)
 
 
-def partner_kernel(exp_ref, t0_ref, t1_ref, t2_ref, t3_ref, out_ref):
-    for m, table in enumerate((t0_ref, t1_ref, t2_ref, t3_ref)):
-        for t in range(0, Q_BLOCKS, 4):
-            hot = one_hot_of_rows([exp_row(exp_ref, m, t + u) for u in range(4)])
-            got = dot(hot, table[...]).astype(BF16)
-            for u in range(4):
-                out_ref[m * Q_BLOCKS + t + u] = got[u * BLOCK : (u + 1) * BLOCK]
+def partner_kernel(m, exp_ref, table, q_ref, cot_ref, out_ref, sp_ref, dp_ref):
+    sums = [jnp.zeros((16, BLOCK), F32), jnp.zeros((16, BLOCK), F32)]
+    for t in range(0, Q_BLOCKS, 4):
+        hot = one_hot_of_rows([exp_row(exp_ref, m, t + u) for u in range(4)])
+        got = dot(hot, table[...]).astype(BF16)
+        for u in range(4):
+            i = t + u
+            pair = got[u * BLOCK : (u + 1) * BLOCK]
+            out_ref[i] = pair
+            here = slice(i * BLOCK, (i + 1) * BLOCK)
+            sums[0] += head_sums(q_ref[here, :], pair[:, :COLS], i)
+            sums[1] += head_sums(cot_ref[here, :], pair[:, COLS:], i)
+    sp_ref[...] = flat(sums[0])
+    dp_ref[...] = flat(sums[1])
+
+
+def head_picks(i):
+    return (iota((16, COLS), 0) == jnp.where(iota((16, COLS), 1) < HEAD, i, 8 + i)).astype(F32).astype(BF16)
+
+
+def head_sums(a, b, i):
+    prod = a.astype(F32) * b.astype(F32)
+    high = prod.astype(BF16)
+    low = (prod - high.astype(F32)).astype(BF16)
+    return dot_nt(head_picks(i), high) + dot_nt(head_picks(i), low)
+
+
+def flat(x):
+    return jnp.concatenate([x[:8], x[8:]], axis=1)
+
+
+def tall(x):
+    return jnp.concatenate([x[:, :BLOCK], x[:, BLOCK:]], axis=0)
+
+
+def turned_weights(tall_rows):
+    return tall_rows.astype(F32).T.astype(BF16)
+
+
+def prepare_kernel(q_ref, cot_ref, qt_ref, qs_ref, ct_ref, cs_ref):
+    def one(i, carry):
+        q = q_ref[q_rows(i), :]
+        cot = cot_ref[q_rows(i), :]
+        qt_ref[i] = stacked_t(q)
+        qs_ref[i] = stacked(q)
+        ct_ref[i] = stacked_t(cot)
+        cs_ref[i] = stacked(cot)
+        return carry
+
+    lax.fori_loop(0, Q_BLOCKS, one, 0, unroll=2)
 
 
 def plan_kernel(mask_ref, count_ref, list_ref, groups_ref, live_ref):
@@ -170,16 +216,17 @@
     lax.fori_loop(0, Q_BLOCKS, per_block, 0)
 
 
-def fill(dst, own_ref, first_col, halo_ref, gid_ref, glob_ref, transposed=False):
-    def turn(x):
-        return x.T if transposed else x
-
+def fill(dst, dst_t, own_ref, first_col, halo_ref, gid_ref, glob_ref):
     def own(j, carry):
-        dst[j] = turn(own_ref[q_rows(j), first_col : first_col + COLS])
+        block = own_ref[q_rows(j), first_col : first_col + COLS]
+        dst[j] = block
+        dst_t[j] = block.T
         return carry
 
     def halo(j, carry):
-        dst[Q_BLOCKS + j] = turn(halo_ref[j, :BLOCK])
+        block = halo_ref[j, :BLOCK]
+        dst[Q_BLOCKS + j] = block
+        dst_t[Q_BLOCKS + j] = block.T
         return carry
 
     lax.fori_loop(0, Q_BLOCKS, own, 0, unroll=4)
@@ -188,9 +235,15 @@
     wide = jnp.concatenate([slot_col] * (SENDERS * EXTRA // BLOCK), axis=1)
     hot = (wide == iota((BLOCK, SENDERS * EXTRA), 1)).astype(F32).astype(BF16)
     extra = jnp.concatenate([halo_ref[s, BLOCK:] for s in range(SENDERS)], axis=0)
-    rows = dot(hot, extra) + glob_ref[:, first_col : first_col + COLS].astype(F32)
-    dst[GLOBAL_BLOCK] = turn(rows.astype(BF16))
+    rows = (dot(hot, extra) + glob_ref[:, first_col : first_col + COLS].astype(F32)).astype(BF16)
+    dst[GLOBAL_BLOCK] = rows
+    dst_t[GLOBAL_BLOCK] = rows.T
     dst[EMPTY_BLOCK] = jnp.zeros((BLOCK, COLS), BF16)
+    dst_t[EMPTY_BLOCK] = jnp.zeros((BLOCK, COLS), BF16)
+
+
+def turn_kernel(kv_ref, hv_ref, gid_ref, glob_ref, v_ref, vt_ref):
+    fill(v_ref, vt_ref, kv_ref, COLS, hv_ref, gid_ref, glob_ref)
 
 
 def stacked(rows):
@@ -204,32 +257,6 @@
     subs = iota((COLS, BLOCK), 0)
     zero = jnp.zeros_like(turned)
     return jnp.concatenate([jnp.where(subs < HEAD, turned, zero), jnp.where(subs < HEAD, zero, turned)], axis=1)
-
-
-def partner_rows(rows, pair_ref, i, first_col):
-    total = jnp.zeros((16, BLOCK), F32)
-    row_id = iota((16, COLS), 0)
-    lane = iota((16, COLS), 1)
-    for m in range(EXPANDERS):
-        other = pair_ref[m * Q_BLOCKS + i][:, first_col : first_col + COLS]
-        prod = rows.astype(F32) * other.astype(F32)
-        high = prod.astype(BF16)
-        low = (prod - high.astype(F32)).astype(BF16)
-        picks = (row_id == jnp.where(lane < HEAD, m, 8 + m)).astype(F32).astype(BF16)
-        total = total + dot_nt(picks, high) + dot_nt(picks, low)
-    return jnp.concatenate([total[:8], total[8:]], axis=1)
-
-
-def tall(weights):
-    return jnp.concatenate([weights[:, :BLOCK], weights[:, BLOCK:]], axis=0)
-
-
-def spread(tall_weights):
-    turned = tall_weights.T.astype(BF16)
-    row_id = iota((16, EXPANDERS * COLS), 0)
-    col = iota((16, EXPANDERS * COLS), 1)
-    picks = (row_id == (col // COLS) + jnp.where(col % COLS < HEAD, 0, 8)).astype(F32).astype(BF16)
-    return dot(turned, picks)
 
 
 def head_rows(turned):
@@ -249,11 +276,6 @@
     )
 
 
-def score_rows(rows, pair_ref, i):
-    partner = partner_rows(rows, pair_ref, i, 0)
-    return jnp.where(iota((8, 2 * BLOCK), 0) < EXPANDERS, partner, NEG)
-
-
 def block_ids(list_ref, i, g):
     return [list_ref[i * LIST + g * GROUP + u] for u in range(GROUP)]
 
@@ -262,11 +284,13 @@
     return pl.ds(pl.multiple_of(i * BLOCK, BLOCK), BLOCK)
 
 
-def score_kernel(list_ref, groups_ref, live_ref, q_ref, kv_ref, hk_ref, gid_ref, glob_ref, lse_ref, k_s):
-    fill(k_s, kv_ref, 0, hk_ref, gid_ref, glob_ref)
+def score_kernel(
+    list_ref, groups_ref, live_ref, qt_ref, kv_ref, hk_ref, gid_ref, glob_ref, lse_ref, k_s, kt_ref
+):
+    fill(k_s, kt_ref, kv_ref, 0, hk_ref, gid_ref, glob_ref)
 
     def per_block(i, carry):
-        turned_q = stacked_t(q_ref[q_rows(i), :])
+        turned_q = qt_ref[i]
 
         def step(g, state):
             blocks = block_ids(list_ref, i, g)
@@ -301,24 +325,25 @@
 
 
 def value_kernel(
-    list_ref, groups_ref, live_ref, q_ref, kv_ref, hk_ref, hv_ref, gid_ref, glob_ref, pair_ref, cot_ref, part_ref,
-    att_ref, own_ref, halo_ref, gout_ref, wp_ref, pdp_ref, delta_ref, lse_ref, k_s, vt_s, acc_s, out_s,
+    list_ref, groups_ref, live_ref, k_s, vt_s, qt_ref, ct_ref, cs_ref, part_ref, sp_ref, dp_ref,
+    p0_ref, p1_ref, p2_ref, p3_ref, gid_ref,
+    att_ref, own_ref, halo_ref, gout_ref, back_ref, delta_ref, lse_ref, acc_s, out_s,
 ):
-    fill(k_s, kv_ref, 0, hk_ref, gid_ref, glob_ref)
-    fill(vt_s, kv_ref, COLS, hv_ref, gid_ref, glob_ref, transposed=True)
     clear_blocks(acc_s)
+    part = part_ref[...]
+    best = part
+    for m in range(EXPANDERS):
+        best = jnp.maximum(best, sp_ref[m])
+    total = jnp.exp(part - best)
+    for m in range(EXPANDERS):
+        total += jnp.exp(sp_ref[m] - best)
+    lse_ref[...] = best + jnp.log(total)
 
     def per_block(i, carry):
-        rows = q_ref[q_rows(i), :]
-        turned_q = stacked_t(rows)
-        cot = cot_ref[q_rows(i), :]
-        cot_stack = stacked(cot)
-        partner = score_rows(rows, pair_ref, i)
-        part = part_ref[pl.ds(i, 1), :]
-        best = jnp.maximum(part, jnp.max(partner, axis=0, keepdims=True))
-        lse = best + jnp.log(jnp.exp(part - best) + jnp.sum(jnp.exp(partner - best), axis=0, keepdims=True))
-        lse_ref[pl.ds(i, 1), :] = lse
-        out_s[...] = jnp.zeros((COLS, 2 * BLOCK), F32)
+        turned_q = qt_ref[i]
+        cot_stack = cs_ref[i]
+        lse = lse_ref[pl.ds(i, 1), :]
+        out_s[i] = jnp.zeros((COLS, 2 * BLOCK), F32)
 
         def step(g, carry):
             blocks = block_ids(list_ref, i, g)
@@ -332,31 +357,40 @@
                 grads = dot(weight, cot_stack)
                 for w, b in enumerate(pair):
                     acc_s[b] += grads[w * BLOCK : (w + 1) * BLOCK]
-            out_s[...] += total
+            out_s[i] += total
             return carry
 
         lax.fori_loop(0, groups_ref[i], step, 0)
-        dprob = partner_rows(cot, pair_ref, i, COLS)
-        prob = jnp.exp(partner - lse)
-        weight = prob.astype(BF16).astype(F32)
-        wide = spread(tall(weight))
-        wp_ref[i] = tall(weight).astype(BF16)
-        attended_t = head_rows(out_s[...])
-        prod = attended_t * cot.T.astype(F32)
-        delta = jnp.concatenate(
-            [jnp.sum(prod[:HEAD], axis=0, keepdims=True), jnp.sum(prod[HEAD:], axis=0, keepdims=True)], axis=1
-        )
-        delta = delta + jnp.sum(prob * dprob, axis=0, keepdims=True)
-        delta_ref[pl.ds(i, 1), :] = delta
-        pdp_ref[i] = prob * (dprob - delta)
-        attended = attended_t.T
-        for m in range(EXPANDERS):
-            attended += wide[:, m * COLS : (m + 1) * COLS] * pair_ref[m * Q_BLOCKS + i][:, COLS:].astype(F32)
-        att_ref[q_rows(i), :] = attended.astype(BF16)
+        delta_ref[pl.ds(i, 1), :] = jnp.sum(out_s[i] * ct_ref[i].astype(F32), axis=0, keepdims=True)
         return carry
 
     lax.fori_loop(0, Q_BLOCKS, per_block, 0)
+    lse = lse_ref[...]
+    probs = [jnp.exp(sp_ref[m] - lse) for m in range(EXPANDERS)]
+    delta = delta_ref[...]
+    for m in range(EXPANDERS):
+        delta += probs[m] * dp_ref[m]
+    delta_ref[...] = delta
+    turned = []
+    for m in range(EXPANDERS):
+        weight = tall(probs[m]).astype(BF16)
+        turned.append(turned_weights(weight))
+        back_ref[m, 0] = tall(probs[m] * (dp_ref[m] - delta)).astype(BF16)
+        back_ref[m, 1] = weight
+    for i in range(Q_BLOCKS):
+        attended = head_rows(out_s[i]).T
+        for m, pair_ref in enumerate((p0_ref, p1_ref, p2_ref, p3_ref)):
+            attended += dot(turned[m], head_picks(i)) * pair_ref[i][:, COLS:].astype(F32)
+        att_ref[i * BLOCK : (i + 1) * BLOCK, :] = attended.astype(BF16)
     store_parts(acc_s, own_ref, halo_ref, gid_ref, gout_ref)
+
+
+def clear_blocks(acc_s):
+    def clear(j, carry):
+        acc_s[j] = jnp.zeros((BLOCK, COLS), F32)
+        return carry
+
+    lax.fori_loop(0, KEY_BLOCKS, clear, 0, unroll=2)
 
 
 def store_parts(acc_s, own_ref, halo_ref, gid_ref, gout_ref):
@@ -380,22 +414,19 @@
 
 
 def key_kernel(
-    list_ref, groups_ref, live_ref, q_ref, kv_ref, hk_ref, hv_ref, gid_ref, glob_ref, pair_ref, cot_ref, lse_ref,
-    pdp_ref, delta_ref, gq_ref, own_ref, halo_ref, gout_ref, dsp_ref, k_s, v_s, kt_s, acc_s, out_s,
+    list_ref, groups_ref, live_ref, k_s, kt_s, v_s, qt_ref, qs_ref, ct_ref, lse_ref, delta_ref, back_ref,
+    p0_ref, p1_ref, p2_ref, p3_ref, gid_ref,
+    gq_ref, own_ref, halo_ref, gout_ref, acc_s, out_s,
 ):
-    fill(k_s, kv_ref, 0, hk_ref, gid_ref, glob_ref)
-    fill(v_s, kv_ref, COLS, hv_ref, gid_ref, glob_ref)
-    fill(kt_s, kv_ref, 0, hk_ref, gid_ref, glob_ref, transposed=True)
     clear_blocks(acc_s)
 
     def per_block(i, carry):
-        rows = q_ref[q_rows(i), :]
-        turned_q = stacked_t(rows)
-        q_stack = stacked(rows)
-        turned_cot = stacked_t(cot_ref[q_rows(i), :])
+        turned_q = qt_ref[i]
+        q_stack = qs_ref[i]
+        turned_cot = ct_ref[i]
         lse = lse_ref[pl.ds(i, 1), :]
         delta = delta_ref[pl.ds(i, 1), :]
-        out_s[...] = jnp.zeros((COLS, 2 * BLOCK), F32)
+        out_s[i] = jnp.zeros((COLS, 2 * BLOCK), F32)
 
         def step(g, carry):
             blocks = block_ids(list_ref, i, g)
@@ -410,20 +441,19 @@
                 grads = dot(dscore, q_stack)
                 for w, b in enumerate(pair):
                     acc_s[b] += grads[w * BLOCK : (w + 1) * BLOCK]
-            out_s[...] += total
+            out_s[i] += total
             return carry
 
         lax.fori_loop(0, groups_ref[i], step, 0)
-        partner = tall(pdp_ref[i].astype(BF16).astype(F32))
-        dsp_ref[i] = partner.astype(BF16)
-        wide = spread(partner)
-        grad_query = head_rows(out_s[...]).T
-        for m in range(EXPANDERS):
-            grad_query += wide[:, m * COLS : (m + 1) * COLS] * pair_ref[m * Q_BLOCKS + i][:, :COLS].astype(F32)
-        gq_ref[q_rows(i), :] = (grad_query * (1.0 / math.sqrt(HEAD))).astype(BF16)
         return carry
 
     lax.fori_loop(0, Q_BLOCKS, per_block, 0)
+    turned = [turned_weights(back_ref[m, 0]) for m in range(EXPANDERS)]
+    for i in range(Q_BLOCKS):
+        grad_query = head_rows(out_s[i]).T
+        for m, pair_ref in enumerate((p0_ref, p1_ref, p2_ref, p3_ref)):
+            grad_query += dot(turned[m], head_picks(i)) * pair_ref[i][:, :COLS].astype(F32)
+        gq_ref[i * BLOCK : (i + 1) * BLOCK, :] = (grad_query * (1.0 / math.sqrt(HEAD))).astype(BF16)
     store_parts(acc_s, own_ref, halo_ref, gid_ref, gout_ref)
 
 
@@ -446,10 +476,8 @@
         return carry
 
     lax.fori_loop(0, SENDERS // GROUP, halo, 0)
-    row_id = iota((16, COLS), 0)
-    lane = iota((16, COLS), 1)
     for m, (part, other) in enumerate(zip(parts, others)):
-        picks = (row_id == jnp.where(lane < HEAD, m, 8 + m)).astype(F32).astype(BF16)
+        turned = turned_weights(part[1 if first_col else 0])
         index_low = other[NODES_HERE + m * Q_BLOCKS : NODES_HERE + (m + 1) * Q_BLOCKS, :COLS]
         index_high = other[NODES_HERE + m * Q_BLOCKS : NODES_HERE + (m + 1) * Q_BLOCKS, COLS:]
         for t in range(Q_BLOCKS // GROUP):
@@ -457,7 +485,7 @@
             for u in range(GROUP):
                 i = t * GROUP + u
                 splits.append((index_low[i : i + 1], index_high[i : i + 1]))
-                wide = dot(part[i].astype(F32).T.astype(BF16), picks)
+                wide = dot(turned, head_picks(i))
                 rows = other[i * BLOCK : (i + 1) * BLOCK, first_col : first_col + COLS].astype(F32)
                 data.append((wide * rows).astype(BF16))
             scatter_into(acc_s, splits, jnp.concatenate(data, axis=0))
@@ -527,10 +555,12 @@
             shape((SENDERS, SLOTS, COLS)),
             shape((SENDERS, SLOTS, COLS)),
             shape((NODES_HERE + EXPANDERS * Q_BLOCKS, 2 * COLS)),
+            shape((1,), jnp.int32),
         ),
         (me, features, w_query, w_key, w_value, cotangent, rows, exp_list, gids),
         name="project",
         flops=3_000_000_000,
+        out_spaces=(*(vmem() for _ in range(5)), smem()),
     )
 
 
@@ -545,63 +575,88 @@
     )
 
 
-def run_partners(exp_list, swaps):
-    return call(
-        partner_kernel,
-        [vmem()] * 5,
-        (shape((EXPANDERS * Q_BLOCKS, BLOCK, 2 * COLS)),),
-        (exp_list, *swaps),
-        name="partners",
-        flops=5_000_000_000,
-    )[0]
-
-
-def run_scores(plan, query, paired, halo_k, gids, glob):
+def run_partner(m, exp_rows, swap, query, cotangent):
+    return call(
+        lambda *refs: partner_kernel(m, *refs),
+        [vmem()] * 4,
+        (
+            shape((Q_BLOCKS, BLOCK, 2 * COLS)),
+            shape((Q_BLOCKS, 2 * BLOCK), F32),
+            shape((Q_BLOCKS, 2 * BLOCK), F32),
+        ),
+        (exp_rows, swap, query, cotangent),
+        name="partner%d" % m,
+        flops=1_500_000_000,
+    )
+
+
+def run_prepare(query, cotangent):
+    wide, high = shape((Q_BLOCKS, COLS, 2 * BLOCK)), shape((Q_BLOCKS, 2 * BLOCK, COLS))
+    return call(
+        prepare_kernel, [vmem()] * 2, (wide, high, wide, high), (query, cotangent), name="prepare", flops=2_000_000_000
+    )
+
+
+def run_scores(plan, turned_q, paired, halo_k, gids, glob):
     return call(
         score_kernel,
         [smem()] * 3 + [vmem()] * 5,
-        (shape((Q_BLOCKS, 2 * BLOCK), F32),),
-        (*plan, query, paired, halo_k, gids, glob),
-        scratch=[blocks_of(BF16)],
+        (
+            shape((Q_BLOCKS, 2 * BLOCK), F32),
+            shape((KEY_BLOCKS, BLOCK, COLS)),
+            shape((KEY_BLOCKS, COLS, BLOCK)),
+        ),
+        (*plan, turned_q, paired, halo_k, gids, glob),
         name="scores",
         flops=12_000_000_000,
-    )[0]
-
-
-def run_values(plan, query, paired, halo_k, halo_v, gids, glob, pairs, cotangent, part):
+    )
+
+
+def run_turn(paired, halo_v, gids, glob):
+    return call(
+        turn_kernel,
+        [vmem()] * 4,
+        (shape((KEY_BLOCKS, BLOCK, COLS)), shape((KEY_BLOCKS, COLS, BLOCK))),
+        (paired, halo_v, gids, glob),
+        name="turn",
+        flops=2_000_000_000,
+    )
+
+
+def run_values(plan, keys, turned_v, prepared, part, scores, dprobs, pairs, gids):
+    turned_q, _, turned_cot, cot_stack = prepared
     return call(
         value_kernel,
-        [smem()] * 3 + [vmem()] * 9,
+        [smem()] * 3 + [vmem()] * 13,
         (
             shape((NODES_HERE, COLS)),
             shape((NODES_HERE, COLS), F32),
             shape((SENDERS, SLOTS, COLS)),
             shape((BLOCK, COLS)),
-            shape((Q_BLOCKS, 16, BLOCK)),
-            shape((Q_BLOCKS, 8, 2 * BLOCK), F32),
+            shape((EXPANDERS, 2, 16, BLOCK)),
             shape((Q_BLOCKS, 2 * BLOCK), F32),
             shape((Q_BLOCKS, 2 * BLOCK), F32),
         ),
-        (*plan, query, paired, halo_k, halo_v, gids, glob, pairs, cotangent, part),
-        scratch=[blocks_of(BF16), blocks_of(BF16), blocks_of(F32), pltpu.VMEM((COLS, 2 * BLOCK), F32)],
+        (*plan, keys, turned_v, turned_q, turned_cot, cot_stack, part, scores, dprobs, *pairs, gids),
+        scratch=[blocks_of(F32), pltpu.VMEM((Q_BLOCKS, COLS, 2 * BLOCK), F32)],
         name="values",
         flops=20_000_000_000,
     )
 
 
-def run_keys(plan, query, paired, halo_k, halo_v, gids, glob, pairs, cotangent, lse, pdp, delta):
+def run_keys(plan, keys, turned_k, values, prepared, lse, delta, back, pairs, gids):
+    turned_q, q_stack, turned_cot, _ = prepared
     return call(
         key_kernel,
-        [smem()] * 3 + [vmem()] * 11,
+        [smem()] * 3 + [vmem()] * 14,
         (
             shape((NODES_HERE, COLS)),
             shape((NODES_HERE, COLS), F32),
             shape((SENDERS, SLOTS, COLS)),
             shape((BLOCK, COLS)),
-            shape((Q_BLOCKS, 16, BLOCK)),
         ),
-        (*plan, query, paired, halo_k, halo_v, gids, glob, pairs, cotangent, lse, pdp, delta),
-        scratch=[blocks_of(BF16), blocks_of(BF16), blocks_of(BF16), blocks_of(F32), pltpu.VMEM((COLS, 2 * BLOCK), F32)],
+        (*plan, keys, turned_k, values, turned_q, q_stack, turned_cot, lse, delta, back, *pairs, gids),
+        scratch=[blocks_of(F32), pltpu.VMEM((Q_BLOCKS, COLS, 2 * BLOCK), F32)],
         name="keys",
         flops=25_000_000_000,
     )
@@ -629,11 +684,6 @@
         name="key_back",
         flops=8_000_000_000,
     )
-
-
-def more_rounds(global_ids):
-    owned = (global_ids[None, :] // NODES_HERE == jnp.arange(SENDERS)[:, None]).sum(1)
-    return (owned.max() + EXTRA - 1) // EXTRA
 
 
 def ranks(global_ids):
@@ -700,37 +750,41 @@
     me = my_index.reshape(1).astype(jnp.int32)
     feat = lax.axis_index("feat").reshape(1).astype(jnp.int32)
 
-    query, paired, out_k, out_v, away = run_project(
+    query, paired, out_k, out_v, away, rounds = run_project(
         me, features, w_query, w_key, w_value, cotangent, rows, exp_rows, gids
     )
-    rounds = more_rounds(global_ids)
+    rounds = rounds[0]
     glob = more_globals(rounds, global_ids, my_index, paired)
     out_k, out_v, glob = lax.optimization_barrier((out_k, out_v, glob))
     halo_k = lax.all_to_all(out_k, "dom", 0, 0, tiled=True)
     swaps = [swapped(paired, m) for m in range(EXPANDERS)]
     plan = run_plan(block_mask, halo_count)
+    prepared = run_prepare(query, cotangent)
     halo_v = lax.all_to_all(out_v, "dom", 0, 0, tiled=True)
-    part = run_scores(plan, query, paired, halo_k, gids, glob)
+    part, keys, turned_k = run_scores(plan, prepared[0], paired, halo_k, gids, glob)
     away, part, *swaps = lax.optimization_barrier((away, part, *swaps))
-    pairs = run_partners(exp_rows, swaps)
+    joined = {m: run_partner(m, exp_rows, swaps[m], query, cotangent) for m in (0, 1, 3)}
+    values, turned_v = run_turn(paired, halo_v, gids, glob)
+    swaps[2], values, joined = lax.optimization_barrier((swaps[2], values, joined))
+    joined[2] = run_partner(2, exp_rows, swaps[2], query, cotangent)
+    pairs, scores, dprobs = zip(*[joined[m] for m in range(EXPANDERS)])
     others = [swapped(away, m) for m in range(EXPANDERS)]
-    attended, own_v, back_v, glob_v, weight_p, pdp, delta, lse = run_values(
-        plan, query, paired, halo_k, halo_v, gids, glob, pairs, cotangent, part
+    attended, own_v, back_v, glob_v, back, delta, lse = run_values(
+        plan, keys, turned_v, prepared, part, jnp.stack(scores), jnp.stack(dprobs), pairs, gids
     )
     *others, lse = lax.optimization_barrier((*others, lse))
-    parts_v = [swapped(weight_p, m) for m in range(EXPANDERS)]
+    parts = [swapped(back[m], m) for m in range(EXPANDERS)]
     returned_v = lax.all_to_all(back_v, "dom", 0, 0, tiled=True)
-    grad_query, own_k, back_k, glob_k, dscore_p = run_keys(
-        plan, query, paired, halo_k, halo_v, gids, glob, pairs, cotangent, lse, pdp, delta
-    )
-    own_k, returned_v = lax.optimization_barrier((own_k, returned_v))
+    grad_query, own_k, back_k, glob_k = run_keys(
+        plan, keys, turned_k, values, prepared, lse, delta, back, pairs, gids
+    )
+    own_k, returned_v, *parts = lax.optimization_barrier((own_k, returned_v, *parts))
     own_k, own_v = more_grads(rounds, global_ids, my_index, glob_k, glob_v, own_k, own_v)
     back_k, own_k, own_v = lax.optimization_barrier((back_k, own_k, own_v))
     returned_k = lax.all_to_all(back_k, "dom", 0, 0, tiled=True)
-    parts_k = [swapped(dscore_p, m) for m in range(EXPANDERS)]
-    grad_value = run_value_back(me, own_v, returned_v, rows, parts_v, others, gids)
+    grad_value = run_value_back(me, own_v, returned_v, rows, parts, others, gids)
     mine, *away = run_key_back(
-        me, feat, own_k, returned_k, rows, parts_k, others, gids, w_query, w_key, w_value, grad_query, grad_value
+        me, feat, own_k, returned_k, rows, parts, others, gids, w_query, w_key, w_value, grad_query, grad_value
     )
     for k, term in enumerate(away, 1):
         mine = mine + lax.ppermute(term, "feat", [(i, (i + k) % 4) for i in range(4)]).astype(F32)

time: 208 us -> 209 us (level)
  Pallas kernels: 103 us -> 111 us
  starting transfers between devices: 52 us -> 47.1 us
  waiting for transfers between devices: 38.9 us -> 35.6 us
    ppermute x16 -> x12, waiting for transfers between devices: 23.3 us -> 10.6 us  [swapped(): lax.ppermute(value, 'dom', [(i, i ^ 1 << bit) for i in range(dom_count)])]
    all_to_all x1, waiting for transfers between devices: 0.01 us -> 9.65 us  [on_device(): returned_k = lax.all_to_all(back_k, 'dom', 0, 0, tiled=True)]
    pallas_call x8 -> x13, Pallas kernels: 103 us -> 111 us  [call(): pl.pallas_call(kernel, out_shape=outs, in_specs=ins, out_specs=out_spaces...]
    ppermute x16 -> x12, starting transfers between devices: 17.8 us -> 15 us  [swapped(): lax.ppermute(value, 'dom', [(i, i ^ 1 << bit) for i in range(dom_count)])]
    all_to_all x1, waiting for transfers between devices: 7.12 us -> 4.41 us  [on_device(): halo_k = lax.all_to_all(out_k, 'dom', 0, 0, tiled=True)]
    ppermute x3, waiting for transfers between devices: 8.44 us -> 10.9 us  [on_device(): lax.ppermute(term, 'feat', [(i, (i + k) % 4) for i in range(4)]).astype(F32)]
    unnamed x42 -> x44, local copies, waits for them, and re-layouts: 6.12 us -> 5.11 us
  transfers between devices with their start and end apart: 23 -> 19, of which waited for: 6 -> 5; matrix products, arithmetic and copies ran while one was open for 1% -> 2% of each run, Pallas kernels for 42% -> 45%
where the time goes in v4:
time: 209 us; the launch traced here: 207 us
  Pallas kernels  111 us (53%)
  starting transfers between devices  47.1 us (23%)
  waiting for transfers between devices  35.6 us (17%)
  local copies, waits for them, and re-layouts  6.53 us (3%)
  other arithmetic  4.81 us (2%)
    pallas_call x13, Pallas kernels, call(): pl.pallas_call(kernel, out_shape=outs, in_specs=ins, out_specs=out_spaces...  111 us
    ppermute x12, starting transfers between devices, swapped(): lax.ppermute(value, 'dom', [(i, i ^ 1 << bit) for i in range(dom_count)])  15 us
    ppermute x3, waiting for transfers between devices, on_device(): lax.ppermute(term, 'feat', [(i, (i + k) % 4) for i in range(4)]).astype(F32)  10.9 us
    ppermute x12, waiting for transfers between devices, swapped(): lax.ppermute(value, 'dom', [(i, i ^ 1 << bit) for i in range(dom_count)])  10.6 us
    all_to_all x1, waiting for transfers between devices, on_device(): returned_k = lax.all_to_all(back_k, 'dom', 0, 0, tiled=True)  9.65 us
    all_to_all x1, starting transfers between devices, on_device(): returned_k = lax.all_to_all(back_k, 'dom', 0, 0, tiled=True)  8.82 us
    all_to_all x1, starting transfers between devices, on_device(): halo_k = lax.all_to_all(out_k, 'dom', 0, 0, tiled=True)  8.24 us
    ppermute x3, starting transfers between devices, on_device(): lax.ppermute(term, 'feat', [(i, (i + k) % 4) for i in range(4)]).astype(F32)  5.84 us
  transfers between devices with their start and end apart: 19, of which 5 were waited for; matrix products, arithmetic and copies ran while one was open for 2% of the time, Pallas kernels for 45%

profile of v4, /device:TPU:0, one launch (start us, length us, event | category | flops | bytes accessed | tf_op | source)
XLA Modules:
  0.0 207.4 jit_solution(11763693035045045987)
XLA Ops:
  0.6 0.7 negate_bitcast_fusion
  1.3 0.2 convert_reduce_fusion.1
  1.5 0.0 copy-start.4
  1.5 7.1 %project.1 = (bf16[1024,128]{1,0:T(8,128)(2,1)}, bf16[1024,256]{1,0:T(8,128)(2,1)S(1)}, bf16[32,144,128]{2,1,0:T(8,128)(2,1)}, bf16[32,144,128]{2,1,0:T(8,128)(2...) custom-call(s32[1]{0:T(128)} %bitcast.15.me_ref, bf16[1024,512]{1,0:T(8,128)(2,1)} %x_ref.1, bf16[512,128]{1,0:T(8,128)(2,1)} %wq_ref.3, ...), custom_call_target="tpu_custom_call" | custom-call | flops 3000000000 | bytes 4000000 | tf_op jit(solution)/shard_map/project/pallas_call | solution.py:532
  8.7 0.6 while.34
  9.3 0.0 copy-start.12
  9.3 8.2 %all-to-all-start.2 = ((bf16[32,144,128]{2,1,0:T(8,128)(2,1)}), bf16[32,144,128]{2,1,0:T(8,128)(2,1)S(1)}, u32[]{:S(2)}, u32[]{:S(2)}) async-start(bf16[32,144,128]{2,1,0:T(8,128)(2,1)} %get-tuple-element.655), calls=%async_computation.2 | async-start | bytes 2359296 | tf_op jit(solution)/shard_map/all_to_all | solution.py:759
  17.6 0.4 collective-permute-start
  17.9 1.7 collective-permute-start.1
  19.6 2.7 %collective-permute-start.2 = (bf16[1024,256]{1,0:T(8,128)(2,1)S(1)}, bf16[1024,256]{1,0:T(8,128)(2,1)}, u32[]{:S(2)}, u32[]{:S(2)}) collective-permute-start(bf16[1024,256]{1,0:T(8,128)(2,1)S(1)} %get-tuple-element.1014), channel_id=1, source_target_pairs={{0,16},{4,20},{8,24},{12,28},{16,0},{20,4},{24,8},{28,12},{32,48},... | collective-permute-start | bytes 1572872 | tf_op jit(solution)/shard_map/ppermute | solution.py:746
  22.3 1.5 collective-permute-start.3
  23.8 0.7 reshape.638.mask_ref
  24.4 4.5 %plan.1 = (s32[448]{0:T(512)}, s32[8]{0:T(128)}, s32[56]{0:T(128)}) custom-call(s32[320]{0:T(512)} %reshape.638.mask_ref, s32[32]{0:T(128)} %bitcast.141), custom_call_target="tpu_custom_call" | custom-call | bytes 4000000 | tf_op jit(solution)/shard_map/plan/pallas_call | solution.py:532
  28.9 2.7 %prepare.1 = (bf16[8,128,256]{2,1,0:T(8,128)(2,1)}, bf16[8,256,128]{2,1,0:T(8,128)(2,1)}, bf16[8,128,256]{2,1,0:T(8,128)(2,1)}, bf16[8,256,128]{2,1,0:T(8,128)(2,1)}) custom-call(bf16[1024,128]{1,0:T(8,128)(2,1)} %get-tuple-element.648.q_ref.refs_2_, bf16[1024,128]{1,0:T(8,128)(2,1)} %refs_3_.7), custom_call_target="tpu_custom_call" | custom-call | flops 2000000000 | bytes 4000000 | tf_op jit(solution)/shard_map/prepare/pallas_call | solution.py:532
  31.6 4.4 %all-to-all-done.2.hk_ref = bf16[32,144,128]{2,1,0:T(8,128)(2,1)S(1)} async-done(((bf16[32,144,128]{2,1,0:T(8,128)(2,1)}), bf16[32,144,128]{2,1,0:T(8,128)(2,1)S(1)}, u32[]{:S(2)}, u32[]{:S(2)}) %all-to-all-start.2) | async-done | bytes 1179680 | tf_op jit(solution)/shard_map/all_to_all | solution.py:759
  36.0 1.1 copy-done.2
  37.1 4.3 %all-to-all-start.3 = ((bf16[32,144,128]{2,1,0:T(8,128)(2,1)}), bf16[32,144,128]{2,1,0:T(8,128)(2,1)S(1)}, u32[]{:S(2)}, u32[]{:S(2)}) async-start(bf16[32,144,128]{2,1,0:T(8,128)(2,1)} %get-tuple-element.658), calls=%async_computation.3 | async-start | bytes 2359296 | tf_op jit(solution)/shard_map/all_to_all | solution.py:763
  41.4 15.6 %scores.1 = (f32[8,256]{1,0:T(8,128)}, bf16[42,128,128]{2,1,0:T(8,128)(2,1)}, bf16[42,128,128]{2,1,0:T(8,128)(2,1)}) custom-call(s32[448]{0:T(512)} %get-tuple-element.645.list_ref, s32[8]{0:T(128)} %get-tuple-element.646.groups_ref, s32[56]{0:T(128)} %get-tuple-element.647.live_ref, bf16[8,128,256]{2,1,0:T(8,128)(2,1)} %get-tuple-element.649.qt_ref, ...), custom_call_target="tpu_custom_call" | custom-call | flops 12000000000 | bytes 4000000 | tf_op jit(solution)/shard_map/scores/pallas_call | solution.py:532
  57.0 10.6 %collective-permute-done.2.refs_1_ = bf16[1024,256]{1,0:T(8,128)(2,1)} collective-permute-done((bf16[1024,256]{1,0:T(8,128)(2,1)S(1)}, bf16[1024,256]{1,0:T(8,128)(2,1)}, u32[]{:S(2)}, u32[]{:S(2)}) %collective-permute-start.2) | collective-permute-done | bytes 524320 | tf_op jit(solution)/shard_map/ppermute | solution.py:746
  67.6 0.0 collective-permute-start.4
  67.6 0.3 collective-permute-start.5
  67.9 2.1 %collective-permute-start.6 = (bf16[1056,256]{1,0:T(8,128)(2,1)}, bf16[1056,256]{1,0:T(8,128)(2,1)S(1)}, u32[]{:S(2)}, u32[]{:S(2)}) collective-permute-start(bf16[1056,256]{1,0:T(8,128)(2,1)} %get-tuple-element.696), channel_id=1, source_target_pairs={{0,16},{4,20},{8,24},{12,28},{16,0},{20,4},{24,8},{28,12},{32,48},... | collective-permute-start | bytes 1622024 | tf_op jit(solution)/shard_map/ppermute | solution.py:746
  70.0 1.4 collective-permute-start.7
  71.4 3.6 %partner3.1 = (bf16[8,128,256]{2,1,0:T(8,128)(2,1)}, f32[8,256]{1,0:T(8,128)}, f32[8,256]{1,0:T(8,128)}) custom-call(s32[4,1024]{1,0:T(4,128)} %refs_0_.7, bf16[1024,256]{1,0:T(8,128)(2,1)} %collective-permute-done.3.refs_1_, bf16[1024,128]{1,0:T(8,128)(2,1)} %get-tuple-element.648.q_ref.refs_2_, bf16[1024,128]{1,0:T(8,128)(2,1)} %refs_3_.7), custom_call_target="tpu_custom_call" | custom-call | flops 1500000000 | bytes 4000000 | tf_op jit(solution)/shard_map/partner3/pallas_call | solution.py:532
  75.0 3.6 %partner1.1 = (bf16[8,128,256]{2,1,0:T(8,128)(2,1)}, f32[8,256]{1,0:T(8,128)}, f32[8,256]{1,0:T(8,128)}) custom-call(s32[4,1024]{1,0:T(4,128)} %refs_0_.7, bf16[1024,256]{1,0:T(8,128)(2,1)} %collective-permute-done.1.refs_1_, bf16[1024,128]{1,0:T(8,128)(2,1)} %get-tuple-element.648.q_ref.refs_2_, bf16[1024,128]{1,0:T(8,128)(2,1)} %refs_3_.7), custom_call_target="tpu_custom_call" | custom-call | flops 1500000000 | bytes 4000000 | tf_op jit(solution)/shard_map/partner1/pallas_call | solution.py:532
  78.6 3.6 %partner0.1 = (bf16[8,128,256]{2,1,0:T(8,128)(2,1)}, f32[8,256]{1,0:T(8,128)}, f32[8,256]{1,0:T(8,128)}) custom-call(s32[4,1024]{1,0:T(4,128)} %refs_0_.7, bf16[1024,256]{1,0:T(8,128)(2,1)} %collective-permute-done.refs_1_, bf16[1024,128]{1,0:T(8,128)(2,1)} %get-tuple-element.648.q_ref.refs_2_, bf16[1024,128]{1,0:T(8,128)(2,1)} %refs_3_.7), custom_call_target="tpu_custom_call" | custom-call | flops 1500000000 | bytes 4000000 | tf_op jit(solution)/shard_map/partner0/pallas_call | solution.py:532
  82.2 0.0 all-to-all-done.3.hv_ref
  82.2 1.0 copy-done.1
  83.3 4.0 %turn.1 = (bf16[42,128,128]{2,1,0:T(8,128)(2,1)}, bf16[42,128,128]{2,1,0:T(8,128)(2,1)}) custom-call(bf16[1024,256]{1,0:T(8,128)(2,1)S(1)} %get-tuple-element.1014, bf16[32,144,128]{2,1,0:T(8,128)(2,1)} %copy-done.1, s32[1,128]{1,0:T(1,128)S(1)} %bitcast.128, bf16[128,256]{1,0:T(8,128)(2,1)S(1)} %get-tuple-element.656.glob_ref), custom_call_target="tpu_custom_call" | custom-call | flops 2000000000 | bytes 4000000 | tf_op jit(solution)/shard_map/turn/pallas_call | solution.py:532
  87.3 3.7 %partner2.1 = (bf16[8,128,256]{2,1,0:T(8,128)(2,1)}, f32[8,256]{1,0:T(8,128)}, f32[8,256]{1,0:T(8,128)}) custom-call(s32[4,1024]{1,0:T(4,128)} %refs_0_.7, bf16[1024,256]{1,0:T(8,128)(2,1)} %collective-permute-done.2.refs_1_, bf16[1024,128]{1,0:T(8,128)(2,1)} %get-tuple-element.648.q_ref.refs_2_, bf16[1024,128]{1,0:T(8,128)(2,1)} %refs_3_.7), custom_call_target="tpu_custom_call" | custom-call | flops 1500000000 | bytes 4000000 | tf_op jit(solution)/shard_map/partner2/pallas_call | solution.py:532
  91.0 1.3 pad_maximum_fusion.1
  92.3 19.1 %values.1 = (bf16[1024,128]{1,0:T(8,128)(2,1)}, f32[1024,128]{1,0:T(8,128)S(1)}, bf16[32,144,128]{2,1,0:T(8,128)(2,1)}, bf16[128,128]{1,0:T(8,128)(2,1)}, bf16[4...) custom-call(s32[448]{0:T(512)} %get-tuple-element.645.list_ref, s32[8]{0:T(128)} %get-tuple-element.646.groups_ref, ...), custom_call_target="tpu_custom_call" | custom-call | flops 20000000000 | bytes 4000000 | tf_op jit(solution)/shard_map/values/pallas_call | solution.py:532
  111.5 0.8 slice_bitcast_fusion
  112.2 1.6 collective-permute-start.10
  113.8 0.0 collective-permute-done.4.o0_ref
  113.8 2.3 %collective-permute-start.11 = (bf16[2,16,128]{2,1,0:T(8,128)(2,1)S(1)}, bf16[2,16,128]{2,1,0:T(8,128)(2,1)S(1)}, u32[]{:S(2)}, u32[]{:S(2)}) collective-permute-start(bf16[2,16,128]{2,1,0:T(8,128)(2,1)S(1)} %get-tuple-element.773), channel_id=1, source_target_pairs={{0,32},{4,36},{8,40},{12,44},{16,48},{20,52},{24,56},{28,60},{32,0... | collective-permute-start | bytes 24584 | tf_op jit(solution)/shard_map/ppermute | solution.py:746
  116.1 0.0 collective-permute-done.5.o1_ref
  116.1 0.0 collective-permute-start.8
  116.1 1.2 collective-permute-start.9
  117.3 0.0 collective-permute-done.7.o3_ref
  117.4 4.8 %all-to-all-start.4 = ((bf16[32,144,128]{2,1,0:T(8,128)(2,1)}), bf16[32,144,128]{2,1,0:T(8,128)(2,1)S(1)}, u32[]{:S(2)}, u32[]{:S(2)}) async-start(bf16[32,144,128]{2,1,0:T(8,128)(2,1)} %get-tuple-element.703), calls=%async_computation.4 | async-start | bytes 2359296 | tf_op jit(solution)/shard_map/all_to_all | solution.py:777
  122.2 25.1 %keys.1 = (bf16[1024,128]{1,0:T(8,128)(2,1)}, f32[1024,128]{1,0:T(8,128)S(1)}, bf16[32,144,128]{2,1,0:T(8,128)(2,1)}, bf16[128,128]{1,0:T(8,128)(2,1)}) custom-call(s32[448]{0:T(512)} %get-tuple-element.645.list_ref, s32[8]{0:T(128)} %get-tuple-element.646.groups_ref, s32[56]{0:T(128)} %get-tuple-element.647.live_ref, ...), custom_call_target="tpu_custom_call" | custom-call | flops 24999999488 | bytes 4000000 | tf_op jit(solution)/shard_map/keys/pallas_call | solution.py:532
  147.3 0.8 pad_maximum_fusion
  148.1 0.0 collective-permute-done.10.p2_ref
  148.1 0.0 collective-permute-done.11.p3_ref
  148.1 0.0 collective-permute-done.8.p0_ref
  148.2 0.5 copy-done.18
  148.7 0.0 copy-done.19
  148.7 0.0 copy-done.20
  148.7 0.0 copy-done.21
  148.7 0.5 copy-done
  149.2 0.6 while.35
  149.9 0.8 copy-done.16
  150.7 8.8 %all-to-all-start.5 = ((bf16[32,144,128]{2,1,0:T(8,128)(2,1)}), bf16[32,144,128]{2,1,0:T(8,128)(2,1)S(1)}, u32[]{:S(2)}, u32[]{:S(2)}) async-start(bf16[32,144,128]{2,1,0:T(8,128)(2,1)} %get-tuple-element.711), calls=%async_computation.5 | async-start | bytes 2359296 | tf_op jit(solution)/shard_map/all_to_all | solution.py:784
  159.5 8.7 %value_back.1.gv_ref = bf16[1024,128]{1,0:T(8,128)(2,1)} custom-call(s32[1]{0:T(128)} %bitcast.15.me_ref, f32[1024,128]{1,0:T(8,128)S(1)} %get-tuple-element.721.own_ref, bf16[32,144,128]{2,1,0:T(8,128)(2,1)} %copy-done, s32[32,128]{1,0:T(8,128)} %bitcast.143, bf16[2,16,128]{2,1,0:T(8,128)(2,1)} %copy-done.20, bf16[2,16,128]{2,1,0:T(8,128)(2,1)} %copy-done.21, ...), custom_call_target="tpu_custom_call" | custom-call | flops 8000000000 | bytes 4000000 | tf_op jit(solution)/shard_map/value_back/pallas_call | solution.py:532
  168.2 9.6 %all-to-all-done.5.ret_ref = bf16[32,144,128]{2,1,0:T(8,128)(2,1)S(1)} async-done(((bf16[32,144,128]{2,1,0:T(8,128)(2,1)}), bf16[32,144,128]{2,1,0:T(8,128)(2,1)S(1)}, u32[]{:S(2)}, u32[]{:S(2)}) %all-to-all-start.5) | async-done | bytes 1179680 | tf_op jit(solution)/shard_map/all_to_all | solution.py:784
  177.9 1.1 copy-done.3
  179.0 9.8 %key_back.1 = (f32[1024,128]{1,0:T(8,128)}, bf16[1024,128]{1,0:T(8,128)(2,1)}, bf16[1024,128]{1,0:T(8,128)(2,1)}, bf16[1024,128]{1,0:T(8,128)(2,1)}) custom-call(s32[1]{0:T(128)} %bitcast.15.me_ref, s32[1]{0:T(128)} %bitcast.29.feat_ref, f32[1024,128]{1,0:T(8,128)S(1)} %copy-done.17, bf16[32,144,128]{2,1,0:T(8,128)(2,1)} %copy-done.3, s32[32,128]{1,0:T(8,128)} %bitcast.144, ...), custom_call_target="tpu_custom_call" | custom-call | flops 8000000000 | bytes 4000000 | tf_op jit(solution)/shard_map/key_back/pallas_call | solution.py:532
  188.8 1.6 collective-permute-start.12
  190.4 2.9 %collective-permute-start.13 = (bf16[1024,128]{1,0:T(8,128)(2,1)}, bf16[1024,128]{1,0:T(8,128)(2,1)S(1)}, u32[]{:S(2)}, u32[]{:S(2)}) collective-permute-start(bf16[1024,128]{1,0:T(8,128)(2,1)} %get-tuple-element.725), channel_id=1, source_target_pairs={{0,2},{1,3},{2,0},{3,1},{4,6},{5,7},{6,4},{7,5},{8,10},{9,11},{10,... | collective-permute-start | bytes 786440 | tf_op jit(solution)/shard_map/ppermute | solution.py:790
  193.3 1.3 collective-permute-start.14
  194.6 4.1 %collective-permute-done.12 = bf16[1024,128]{1,0:T(8,128)(2,1)S(1)} collective-permute-done((bf16[1024,128]{1,0:T(8,128)(2,1)}, bf16[1024,128]{1,0:T(8,128)(2,1)S(1)}, u32[]{:S(2)}, u32[]{:S(2)}) %collective-permute-start.12) | collective-permute-done | bytes 262176 | tf_op jit(solution)/shard_map/ppermute | solution.py:790
  198.7 6.8 %collective-permute-done.13 = bf16[1024,128]{1,0:T(8,128)(2,1)S(1)} collective-permute-done((bf16[1024,128]{1,0:T(8,128)(2,1)}, bf16[1024,128]{1,0:T(8,128)(2,1)S(1)}, u32[]{:S(2)}, u32[]{:S(2)}) %collective-permute-start.13) | collective-permute-done | bytes 262176 | tf_op jit(solution)/shard_map/ppermute | solution.py:790
  205.5 1.9 add_convert_fusion
  (41 shorter events, 0.1 us)
Async XLA Ops:
  1.5 7.2 %copy-start.4 = (s32[128]{0:T(128)S(1)}, s32[128]{0:T(128)}, u32[]{:S(2)}) copy-start(s32[128]{0:T(128)} %param.23) | copy-start | bytes 1540
  9.3 14.4 %copy-start.12 = (s32[8,40]{1,0:T(8,128)S(1)}, s32[8,40]{1,0:T(8,128)}, u32[]{:S(2)}) copy-start(s32[8,40]{1,0:T(8,128)} %param.21) | copy-start | bytes 3844
  9.3 26.7 %all-to-all-start.2 = ((bf16[32,144,128]{2,1,0:T(8,128)(2,1)}), bf16[32,144,128]{2,1,0:T(8,128)(2,1)S(1)}, u32[]{:S(2)}, u32[]{:S(2)}) async-start(bf16[32,144,128]{2,1,0:T(8,128)(2,1)} %get-tuple-element.655), calls=%async_computation.2 | async-start | bytes 2359296 | tf_op jit(solution)/shard_map/all_to_all | solution.py:759
  17.6 39.4 %collective-permute-start = (bf16[1024,256]{1,0:T(8,128)(2,1)S(1)}, bf16[1024,256]{1,0:T(8,128)(2,1)}, u32[]{:S(2)}, u32[]{:S(2)}) collective-permute-start(bf16[1024,256]{1,0:T(8,128)(2,1)S(1)} %get-tuple-element.1014), channel_id=1, source_target_pairs={{0,4},{4,0},{8,12},{12,8},{16,20},{20,16},{24,28},{28,24},{32,36},... | collective-permute-start | bytes 1572872 | tf_op jit(solution)/shard_map/ppermute | solution.py:746
  17.9 39.1 %collective-permute-start.1 = (bf16[1024,256]{1,0:T(8,128)(2,1)S(1)}, bf16[1024,256]{1,0:T(8,128)(2,1)}, u32[]{:S(2)}, u32[]{:S(2)}) collective-permute-start(bf16[1024,256]{1,0:T(8,128)(2,1)S(1)} %get-tuple-element.1014), channel_id=1, source_target_pairs={{0,8},{4,12},{8,0},{12,4},{16,24},{20,28},{24,16},{28,20},{32,40},... | collective-permute-start | bytes 1572872 | tf_op jit(solution)/shard_map/ppermute | solution.py:746
  19.6 48.0 %collective-permute-start.2 = (bf16[1024,256]{1,0:T(8,128)(2,1)S(1)}, bf16[1024,256]{1,0:T(8,128)(2,1)}, u32[]{:S(2)}, u32[]{:S(2)}) collective-permute-start(bf16[1024,256]{1,0:T(8,128)(2,1)S(1)} %get-tuple-element.1014), channel_id=1, source_target_pairs={{0,16},{4,20},{8,24},{12,28},{16,0},{20,4},{24,8},{28,12},{32,48},... | collective-permute-start | bytes 1572872 | tf_op jit(solution)/shard_map/ppermute | solution.py:746
  22.3 45.3 %collective-permute-start.3 = (bf16[1024,256]{1,0:T(8,128)(2,1)S(1)}, bf16[1024,256]{1,0:T(8,128)(2,1)}, u32[]{:S(2)}, u32[]{:S(2)}) collective-permute-start(bf16[1024,256]{1,0:T(8,128)(2,1)S(1)} %get-tuple-element.1014), channel_id=1, source_target_pairs={{0,32},{4,36},{8,40},{12,44},{16,48},{20,52},{24,56},{28,60},{32,0... | collective-permute-start | bytes 1572872 | tf_op jit(solution)/shard_map/ppermute | solution.py:746
  36.0 1.1 copy-start.2
  37.1 45.2 %all-to-all-start.3 = ((bf16[32,144,128]{2,1,0:T(8,128)(2,1)}), bf16[32,144,128]{2,1,0:T(8,128)(2,1)S(1)}, u32[]{:S(2)}, u32[]{:S(2)}) async-start(bf16[32,144,128]{2,1,0:T(8,128)(2,1)} %get-tuple-element.658), calls=%async_computation.3 | async-start | bytes 2359296 | tf_op jit(solution)/shard_map/all_to_all | solution.py:763
  67.6 46.2 %collective-permute-start.4 = (bf16[1056,256]{1,0:T(8,128)(2,1)}, bf16[1056,256]{1,0:T(8,128)(2,1)S(1)}, u32[]{:S(2)}, u32[]{:S(2)}) collective-permute-start(bf16[1056,256]{1,0:T(8,128)(2,1)} %get-tuple-element.696), channel_id=1, source_target_pairs={{0,4},{4,0},{8,12},{12,8},{16,20},{20,16},{24,28},{28,24},{32,36},... | collective-permute-start | bytes 1622024 | tf_op jit(solution)/shard_map/ppermute | solution.py:746
  67.6 48.5 %collective-permute-start.5 = (bf16[1056,256]{1,0:T(8,128)(2,1)}, bf16[1056,256]{1,0:T(8,128)(2,1)S(1)}, u32[]{:S(2)}, u32[]{:S(2)}) collective-permute-start(bf16[1056,256]{1,0:T(8,128)(2,1)} %get-tuple-element.696), channel_id=1, source_target_pairs={{0,8},{4,12},{8,0},{12,4},{16,24},{20,28},{24,16},{28,20},{32,40},... | collective-permute-start | bytes 1622024 | tf_op jit(solution)/shard_map/ppermute | solution.py:746
  67.9 48.2 %collective-permute-start.6 = (bf16[1056,256]{1,0:T(8,128)(2,1)}, bf16[1056,256]{1,0:T(8,128)(2,1)S(1)}, u32[]{:S(2)}, u32[]{:S(2)}) collective-permute-start(bf16[1056,256]{1,0:T(8,128)(2,1)} %get-tuple-element.696), channel_id=1, source_target_pairs={{0,16},{4,20},{8,24},{12,28},{16,0},{20,4},{24,8},{28,12},{32,48},... | collective-permute-start | bytes 1622024 | tf_op jit(solution)/shard_map/ppermute | solution.py:746
  70.0 47.3 %collective-permute-start.7 = (bf16[1056,256]{1,0:T(8,128)(2,1)}, bf16[1056,256]{1,0:T(8,128)(2,1)}, u32[]{:S(2)}, u32[]{:S(2)}) collective-permute-start(bf16[1056,256]{1,0:T(8,128)(2,1)} %get-tuple-element.696), channel_id=1, source_target_pairs={{0,32},{4,36},{8,40},{12,44},{16,48},{20,52},{24,56},{28,60},{32,0... | collective-permute-start | bytes 1622024 | tf_op jit(solution)/shard_map/ppermute | solution.py:746
  82.2 1.0 copy-start.1
  87.3 3.7 %copy-start.6 = (f32[8,256]{1,0:T(8,128)S(1)}, f32[8,256]{1,0:T(8,128)}, u32[]{:S(2)}) copy-start(f32[8,256]{1,0:T(8,128)} %get-tuple-element.683) | copy-start | bytes 24580
  87.3 3.7 %copy-start.7 = (f32[8,256]{1,0:T(8,128)S(1)}, f32[8,256]{1,0:T(8,128)}, u32[]{:S(2)}) copy-start(f32[8,256]{1,0:T(8,128)} %get-tuple-element.687) | copy-start | bytes 24580
  87.3 3.7 %copy-start.8 = (f32[8,256]{1,0:T(8,128)S(1)}, f32[8,256]{1,0:T(8,128)}, u32[]{:S(2)}) copy-start(f32[8,256]{1,0:T(8,128)} %get-tuple-element.680) | copy-start | bytes 24580
  87.3 3.7 %copy-start.9 = (f32[8,256]{1,0:T(8,128)S(1)}, f32[8,256]{1,0:T(8,128)}, u32[]{:S(2)}) copy-start(f32[8,256]{1,0:T(8,128)} %get-tuple-element.685) | copy-start | bytes 24580
  87.3 3.7 %copy-start.10 = (f32[8,256]{1,0:T(8,128)S(1)}, f32[8,256]{1,0:T(8,128)}, u32[]{:S(2)}) copy-start(f32[8,256]{1,0:T(8,128)} %get-tuple-element.679) | copy-start | bytes 24580
  87.3 3.7 %copy-start.11 = (f32[8,256]{1,0:T(8,128)S(1)}, f32[8,256]{1,0:T(8,128)}, u32[]{:S(2)}) copy-start(f32[8,256]{1,0:T(8,128)} %get-tuple-element.684) | copy-start | bytes 24580
  112.2 35.8 %collective-permute-start.10 = (bf16[2,16,128]{2,1,0:T(8,128)(2,1)S(1)}, bf16[2,16,128]{2,1,0:T(8,128)(2,1)S(1)}, u32[]{:S(2)}, u32[]{:S(2)}) collective-permute-start(bf16[2,16,128]{2,1,0:T(8,128)(2,1)S(1)} %get-tuple-element.774), channel_id=1, source_target_pairs={{0,16},{4,20},{8,24},{12,28},{16,0},{20,4},{24,8},{28,12},{32,48},... | collective-permute-start | bytes 24584 | tf_op jit(solution)/shard_map/ppermute | solution.py:746
  113.8 3.5 %copy-start.13 = (bf16[1056,256]{1,0:T(8,128)(2,1)}, bf16[1056,256]{1,0:T(8,128)(2,1)S(1)}, u32[]{:S(2)}) copy-start(bf16[1056,256]{1,0:T(8,128)(2,1)S(1)} %collective-permute-done.4.o0_ref) | copy-start | bytes 1622020
  113.8 34.3 %collective-permute-start.11 = (bf16[2,16,128]{2,1,0:T(8,128)(2,1)S(1)}, bf16[2,16,128]{2,1,0:T(8,128)(2,1)S(1)}, u32[]{:S(2)}, u32[]{:S(2)}) collective-permute-start(bf16[2,16,128]{2,1,0:T(8,128)(2,1)S(1)} %get-tuple-element.773), channel_id=1, source_target_pairs={{0,32},{4,36},{8,40},{12,44},{16,48},{20,52},{24,56},{28,60},{32,0... | collective-permute-start | bytes 24584 | tf_op jit(solution)/shard_map/ppermute | solution.py:746
  116.1 1.3 copy-start.14
  116.1 32.0 %collective-permute-start.8 = (bf16[2,16,128]{2,1,0:T(8,128)(2,1)S(1)}, bf16[2,16,128]{2,1,0:T(8,128)(2,1)S(1)}, u32[]{:S(2)}, u32[]{:S(2)}) collective-permute-start(bf16[2,16,128]{2,1,0:T(8,128)(2,1)S(1)} %get-tuple-element.776), channel_id=1, source_target_pairs={{0,4},{4,0},{8,12},{12,8},{16,20},{20,16},{24,28},{28,24},{32,36},... | collective-permute-start | bytes 24584 | tf_op jit(solution)/shard_map/ppermute | solution.py:746
  116.1 1.2 copy-start.15
  116.1 32.0 %collective-permute-start.9 = (bf16[2,16,128]{2,1,0:T(8,128)(2,1)S(1)}, bf16[2,16,128]{2,1,0:T(8,128)(2,1)S(1)}, u32[]{:S(2)}, u32[]{:S(2)}) collective-permute-start(bf16[2,16,128]{2,1,0:T(8,128)(2,1)S(1)} %get-tuple-element.775), channel_id=1, source_target_pairs={{0,8},{4,12},{8,0},{12,4},{16,24},{20,28},{24,16},{28,20},{32,40},... | collective-permute-start | bytes 24584 | tf_op jit(solution)/shard_map/ppermute | solution.py:746
  117.4 30.8 %all-to-all-start.4 = ((bf16[32,144,128]{2,1,0:T(8,128)(2,1)}), bf16[32,144,128]{2,1,0:T(8,128)(2,1)S(1)}, u32[]{:S(2)}, u32[]{:S(2)}) async-start(bf16[32,144,128]{2,1,0:T(8,128)(2,1)} %get-tuple-element.703), calls=%async_computation.4 | async-start | bytes 2359296 | tf_op jit(solution)/shard_map/all_to_all | solution.py:777
  122.2 25.1 %copy-start.5 = (bf16[128,128]{1,0:T(8,128)(2,1)S(1)}, bf16[128,128]{1,0:T(8,128)(2,1)}, u32[]{:S(2)}) copy-start(bf16[128,128]{1,0:T(8,128)(2,1)} %get-tuple-element.707) | copy-start | bytes 98308
  148.1 0.6 copy-start.18
  148.1 0.6 copy-start.19
  148.1 0.6 copy-start.20
  148.1 0.6 copy-start.21
  148.1 1.1 copy-start
  149.9 0.8 copy-start.16
  150.7 27.2 %all-to-all-start.5 = ((bf16[32,144,128]{2,1,0:T(8,128)(2,1)}), bf16[32,144,128]{2,1,0:T(8,128)(2,1)S(1)}, u32[]{:S(2)}, u32[]{:S(2)}) async-start(bf16[32,144,128]{2,1,0:T(8,128)(2,1)} %get-tuple-element.711), calls=%async_computation.5 | async-start | bytes 2359296 | tf_op jit(solution)/shard_map/all_to_all | solution.py:784
  159.5 19.4 %copy-start.17 = (f32[1024,128]{1,0:T(8,128)S(1)}, f32[1024,128]{1,0:T(8,128)}, u32[]{:S(2)}) copy-start(f32[1024,128]{1,0:T(8,128)} %copy-done.16) | copy-start | bytes 1572868
  177.9 1.1 copy-start.3
  188.8 10.0 %collective-permute-start.12 = (bf16[1024,128]{1,0:T(8,128)(2,1)}, bf16[1024,128]{1,0:T(8,128)(2,1)S(1)}, u32[]{:S(2)}, u32[]{:S(2)}) collective-permute-start(bf16[1024,128]{1,0:T(8,128)(2,1)} %get-tuple-element.724), channel_id=1, source_target_pairs={{0,1},{1,2},{2,3},{3,0},{4,5},{5,6},{6,7},{7,4},{8,9},{9,10},{10,1... | collective-permute-start | bytes 786440 | tf_op jit(solution)/shard_map/ppermute | solution.py:790
  190.4 15.2 %collective-permute-start.13 = (bf16[1024,128]{1,0:T(8,128)(2,1)}, bf16[1024,128]{1,0:T(8,128)(2,1)S(1)}, u32[]{:S(2)}, u32[]{:S(2)}) collective-permute-start(bf16[1024,128]{1,0:T(8,128)(2,1)} %get-tuple-element.725), channel_id=1, source_target_pairs={{0,2},{1,3},{2,0},{3,1},{4,6},{5,7},{6,4},{7,5},{8,10},{9,11},{10,... | collective-permute-start | bytes 786440 | tf_op jit(solution)/shard_map/ppermute | solution.py:790
  193.3 12.3 %collective-permute-start.14 = (bf16[1024,128]{1,0:T(8,128)(2,1)}, bf16[1024,128]{1,0:T(8,128)(2,1)S(1)}, u32[]{:S(2)}, u32[]{:S(2)}) collective-permute-start(bf16[1024,128]{1,0:T(8,128)(2,1)} %get-tuple-element.726), channel_id=1, source_target_pairs={{0,3},{1,0},{2,1},{3,2},{4,7},{5,4},{6,5},{7,6},{8,11},{9,8},{10,9... | collective-permute-start | bytes 786440 | tf_op jit(solution)/shard_map/ppermute | solution.py:790

commit v5 on v4

--- a/solution.py
+++ b/solution.py
@@ -22,6 +22,8 @@
 LIST = 56
 EXTRA = 16
 SLOTS = BLOCK + EXTRA
+PART_ROWS = 32
+BACK = SLOTS + PART_ROWS
 NEG = -1e30
 F32 = jnp.float32
 BF16 = jnp.bfloat16
@@ -101,14 +103,18 @@
 
 
 def project_kernel(
-    me_ref, x_ref, wq_ref, wk_ref, wv_ref, cot_ref, rows_ref, exp_ref, gid_ref, q_ref, kv_ref, outk_ref, outv_ref, away_ref,
-    rounds_ref,
+    me_ref, x_ref, wq_ref, wk_ref, wv_ref, cot_ref, rows_ref, exp_ref, gid_ref, q_ref, k_ref, v_ref, outk_ref, outv_ref,
+    away_ref, rounds_ref, kv_ref,
 ):
     most = jnp.max(owner_ranks(gid_ref[...])[0].astype(F32)).astype(jnp.int32)
     rounds_ref[0] = (most + EXTRA) // EXTRA
     x = x_ref[...]
-    kv_ref[:, :COLS] = dot(x, wk_ref[...]).astype(BF16)
-    kv_ref[:, COLS:] = dot(x, wv_ref[...]).astype(BF16)
+    keys = dot(x, wk_ref[...]).astype(BF16)
+    values = dot(x, wv_ref[...]).astype(BF16)
+    k_ref[...] = keys
+    v_ref[...] = values
+    kv_ref[:, :COLS] = keys
+    kv_ref[:, COLS:] = values
     query = (dot(x, wq_ref[...]).astype(BF16).astype(F32) * (1.0 / math.sqrt(HEAD))).astype(BF16)
     q_ref[...] = query
     away_ref[:NODES_HERE, :COLS] = query
@@ -135,31 +141,79 @@
     lax.fori_loop(0, SENDERS // GROUP, gather, 0)
 
 
-def partner_kernel(m, exp_ref, table, q_ref, cot_ref, out_ref, sp_ref, dp_ref):
-    sums = [jnp.zeros((16, BLOCK), F32), jnp.zeros((16, BLOCK), F32)]
+def gather_partner(exp_ref, m, table):
+    blocks = []
     for t in range(0, Q_BLOCKS, 4):
         hot = one_hot_of_rows([exp_row(exp_ref, m, t + u) for u in range(4)])
         got = dot(hot, table[...]).astype(BF16)
-        for u in range(4):
-            i = t + u
-            pair = got[u * BLOCK : (u + 1) * BLOCK]
-            out_ref[i] = pair
-            here = slice(i * BLOCK, (i + 1) * BLOCK)
-            sums[0] += head_sums(q_ref[here, :], pair[:, :COLS], i)
-            sums[1] += head_sums(cot_ref[here, :], pair[:, COLS:], i)
-    sp_ref[...] = flat(sums[0])
-    dp_ref[...] = flat(sums[1])
+        blocks += [got[u * BLOCK : (u + 1) * BLOCK] for u in range(4)]
+    return blocks
+
+
+def sum_picks():
+    sub = iota((2 * Q_BLOCKS * COLS, 16), 0)
+    col = iota((2 * Q_BLOCKS * COLS, 16), 1)
+    return (col == (sub >> 8) + jnp.where((sub & (COLS - 1)) < HEAD, 0, 8)).astype(F32).astype(BF16)
+
+
+def head_sums(a_ref, blocks, picks):
+    parts = []
+    for i, b in enumerate(blocks):
+        prod = a_ref[i * BLOCK : (i + 1) * BLOCK, :].astype(F32) * b.astype(F32)
+        high = prod.astype(BF16)
+        parts += [high, (prod - high.astype(F32)).astype(BF16)]
+    return flat(dot(jnp.concatenate(parts, axis=1), picks).T)
+
+
+def partner_key_kernel(exp_ref, t0_ref, t1_ref, t2_ref, t3_ref, q_ref, out_ref, sp_ref):
+    picks = sum_picks()
+    for m, table in enumerate((t0_ref, t1_ref, t2_ref, t3_ref)):
+        blocks = gather_partner(exp_ref, m, table)
+        for i, block in enumerate(blocks):
+            out_ref[m * Q_BLOCKS + i] = block
+        sp_ref[m] = head_sums(q_ref, blocks, picks)
 
 
 def head_picks(i):
     return (iota((16, COLS), 0) == jnp.where(iota((16, COLS), 1) < HEAD, i, 8 + i)).astype(F32).astype(BF16)
 
 
-def head_sums(a, b, i):
-    prod = a.astype(F32) * b.astype(F32)
-    high = prod.astype(BF16)
-    low = (prod - high.astype(F32)).astype(BF16)
-    return dot_nt(head_picks(i), high) + dot_nt(head_picks(i), low)
+def finish_kernel(
+    me_ref, exp_ref, t0_ref, t1_ref, t2_ref, t3_ref, cot_ref, out_t_ref, sp_ref, lse_ref, local_ref, _, att_ref, back_ref,
+    delta_ref, message_ref, sems,
+):
+    picks = sum_picks()
+    lse = lse_ref[...]
+    delta = local_ref[...]
+    totals = [head_rows(out_t_ref[i]).T for i in range(Q_BLOCKS)]
+    probs, dprobs = [], []
+    for m, table in enumerate((t0_ref, t1_ref, t2_ref, t3_ref)):
+        blocks = gather_partner(exp_ref, m, table)
+        prob = jnp.exp(sp_ref[m] - lse)
+        dprob = head_sums(cot_ref, blocks, picks)
+        delta += prob * dprob
+        weight = tall(prob).astype(BF16)
+        back_ref[m, 16:] = weight
+        turned = turned_weights(weight)
+        for i, block in enumerate(blocks):
+            totals[i] += dot(turned, head_picks(i)) * block.astype(F32)
+        probs.append(prob)
+        dprobs.append(dprob)
+    delta_ref[...] = delta
+    for m in range(EXPANDERS):
+        back_ref[m, :16] = tall(probs[m] * (dprobs[m] - delta)).astype(BF16)
+    copies = [
+        pltpu.make_async_copy(
+            back_ref.at[m], message_ref.at[me_ref[0] ^ (1 << m), pl.ds(SLOTS, PART_ROWS)], sems.at[m]
+        )
+        for m in range(EXPANDERS)
+    ]
+    for copy in copies:
+        copy.start()
+    for i in range(Q_BLOCKS):
+        att_ref[i * BLOCK : (i + 1) * BLOCK, :] = totals[i].astype(BF16)
+    for copy in copies:
+        copy.wait()
 
 
 def flat(x):
@@ -216,9 +270,9 @@
     lax.fori_loop(0, Q_BLOCKS, per_block, 0)
 
 
-def fill(dst, dst_t, own_ref, first_col, halo_ref, gid_ref, glob_ref):
+def fill(dst, dst_t, first_col, own_ref, halo_ref, gid_ref, glob_ref):
     def own(j, carry):
-        block = own_ref[q_rows(j), first_col : first_col + COLS]
+        block = own_ref[q_rows(j), :]
         dst[j] = block
         dst_t[j] = block.T
         return carry
@@ -242,8 +296,8 @@
     dst_t[EMPTY_BLOCK] = jnp.zeros((BLOCK, COLS), BF16)
 
 
-def turn_kernel(kv_ref, hv_ref, gid_ref, glob_ref, v_ref, vt_ref):
-    fill(v_ref, vt_ref, kv_ref, COLS, hv_ref, gid_ref, glob_ref)
+def turn_kernel(own_ref, hv_ref, gid_ref, glob_ref, v_ref, vt_ref):
+    fill(v_ref, vt_ref, COLS, own_ref, hv_ref, gid_ref, glob_ref)
 
 
 def stacked(rows):
@@ -285,9 +339,9 @@
 
 
 def score_kernel(
-    list_ref, groups_ref, live_ref, qt_ref, kv_ref, hk_ref, gid_ref, glob_ref, lse_ref, k_s, kt_ref
+    list_ref, groups_ref, live_ref, qt_ref, own_ref, hk_ref, gid_ref, glob_ref, lse_ref, k_s, kt_ref
 ):
-    fill(k_s, kt_ref, kv_ref, 0, hk_ref, gid_ref, glob_ref)
+    fill(k_s, kt_ref, 0, own_ref, hk_ref, gid_ref, glob_ref)
 
     def per_block(i, carry):
         turned_q = qt_ref[i]
@@ -316,18 +370,9 @@
     lax.fori_loop(0, Q_BLOCKS, per_block, 0)
 
 
-def clear_blocks(acc_s):
-    def clear(j, carry):
-        acc_s[j] = jnp.zeros((BLOCK, COLS), F32)
-        return carry
-
-    lax.fori_loop(0, KEY_BLOCKS, clear, 0)
-
-
 def value_kernel(
-    list_ref, groups_ref, live_ref, k_s, vt_s, qt_ref, ct_ref, cs_ref, part_ref, sp_ref, dp_ref,
-    p0_ref, p1_ref, p2_ref, p3_ref, gid_ref,
-    att_ref, own_ref, halo_ref, gout_ref, back_ref, delta_ref, lse_ref, acc_s, out_s,
+    list_ref, groups_ref, live_ref, k_s, vt_s, qt_ref, ct_ref, cs_ref, part_ref, sp_ref, gid_ref,
+    own_ref, halo_ref, gout_ref, out_s, delta_ref, lse_ref, acc_s,
 ):
     clear_blocks(acc_s)
     part = part_ref[...]
@@ -365,23 +410,6 @@
         return carry
 
     lax.fori_loop(0, Q_BLOCKS, per_block, 0)
-    lse = lse_ref[...]
-    probs = [jnp.exp(sp_ref[m] - lse) for m in range(EXPANDERS)]
-    delta = delta_ref[...]
-    for m in range(EXPANDERS):
-        delta += probs[m] * dp_ref[m]
-    delta_ref[...] = delta
-    turned = []
-    for m in range(EXPANDERS):
-        weight = tall(probs[m]).astype(BF16)
-        turned.append(turned_weights(weight))
-        back_ref[m, 0] = tall(probs[m] * (dp_ref[m] - delta)).astype(BF16)
-        back_ref[m, 1] = weight
-    for i in range(Q_BLOCKS):
-        attended = head_rows(out_s[i]).T
-        for m, pair_ref in enumerate((p0_ref, p1_ref, p2_ref, p3_ref)):
-            attended += dot(turned[m], head_picks(i)) * pair_ref[i][:, COLS:].astype(F32)
-        att_ref[i * BLOCK : (i + 1) * BLOCK, :] = attended.astype(BF16)
     store_parts(acc_s, own_ref, halo_ref, gid_ref, gout_ref)
 
 
@@ -410,12 +438,11 @@
     hot = (iota((SENDERS * EXTRA, BLOCK), 0) == slot_row).astype(F32).astype(BF16)
     extra = dot(hot, grads).astype(BF16)
     for s in range(SENDERS):
-        halo_ref[s, BLOCK:] = extra[s * EXTRA : (s + 1) * EXTRA]
+        halo_ref[s, BLOCK:SLOTS] = extra[s * EXTRA : (s + 1) * EXTRA]
 
 
 def key_kernel(
-    list_ref, groups_ref, live_ref, k_s, kt_s, v_s, qt_ref, qs_ref, ct_ref, lse_ref, delta_ref, back_ref,
-    p0_ref, p1_ref, p2_ref, p3_ref, gid_ref,
+    list_ref, groups_ref, live_ref, k_s, kt_s, v_s, qt_ref, qs_ref, ct_ref, lse_ref, delta_ref, back_ref, pair_ref, gid_ref,
     gq_ref, own_ref, halo_ref, gout_ref, acc_s, out_s,
 ):
     clear_blocks(acc_s)
@@ -448,11 +475,11 @@
         return carry
 
     lax.fori_loop(0, Q_BLOCKS, per_block, 0)
-    turned = [turned_weights(back_ref[m, 0]) for m in range(EXPANDERS)]
+    turned = [turned_weights(back_ref[m, :16]) for m in range(EXPANDERS)]
     for i in range(Q_BLOCKS):
         grad_query = head_rows(out_s[i]).T
-        for m, pair_ref in enumerate((p0_ref, p1_ref, p2_ref, p3_ref)):
-            grad_query += dot(turned[m], head_picks(i)) * pair_ref[i][:, :COLS].astype(F32)
+        for m in range(EXPANDERS):
+            grad_query += dot(turned[m], head_picks(i)) * pair_ref[m * Q_BLOCKS + i].astype(F32)
         gq_ref[i * BLOCK : (i + 1) * BLOCK, :] = (grad_query * (1.0 / math.sqrt(HEAD))).astype(BF16)
     store_parts(acc_s, own_ref, halo_ref, gid_ref, gout_ref)
 
@@ -466,9 +493,7 @@
         acc_s[c * BLOCK : (c + 1) * BLOCK, :] += dot(hot, data)
 
 
-def gather_grads(me_ref, own_ref, ret_ref, rows_ref, parts, others, first_col, gid_ref, acc_s):
-    acc_s[...] = own_ref[...]
-
+def add_halo(acc_s, me_ref, ret_ref, rows_ref, gid_ref):
     def halo(t, carry):
         splits = [split_index(rows_ref[pl.ds(t * GROUP + u, 1), :]) for u in range(GROUP)]
         data = jnp.concatenate([ret_ref[t * GROUP + u, :BLOCK] for u in range(GROUP)], axis=0)
@@ -476,8 +501,20 @@
         return carry
 
     lax.fori_loop(0, SENDERS // GROUP, halo, 0)
+    extra = ret_ref[0, BLOCK:SLOTS].astype(F32)
+    for s in range(1, SENDERS):
+        extra += ret_ref[s, BLOCK:SLOTS].astype(F32)
+    high = extra.astype(BF16)
+    data = jnp.concatenate([high, (extra - high.astype(F32)).astype(BF16)], axis=0)
+    mine = jnp.broadcast_to(mine_columns(gid_ref[...], me_ref[0]), (EXTRA, NODES_HERE))
+    hot = (mine == iota((EXTRA, NODES_HERE), 1)).astype(F32)
+    hot = jnp.concatenate([hot, hot], axis=0).T.astype(BF16)
+    acc_s[...] += dot(hot, data)
+
+
+def add_partners(acc_s, parts, others, first_col):
     for m, (part, other) in enumerate(zip(parts, others)):
-        turned = turned_weights(part[1 if first_col else 0])
+        turned = turned_weights(part)
         index_low = other[NODES_HERE + m * Q_BLOCKS : NODES_HERE + (m + 1) * Q_BLOCKS, :COLS]
         index_high = other[NODES_HERE + m * Q_BLOCKS : NODES_HERE + (m + 1) * Q_BLOCKS, COLS:]
         for t in range(Q_BLOCKS // GROUP):
@@ -489,45 +526,44 @@
                 rows = other[i * BLOCK : (i + 1) * BLOCK, first_col : first_col + COLS].astype(F32)
                 data.append((wide * rows).astype(BF16))
             scatter_into(acc_s, splits, jnp.concatenate(data, axis=0))
-    extra = ret_ref[0, BLOCK:].astype(F32)
-    for s in range(1, SENDERS):
-        extra += ret_ref[s, BLOCK:].astype(F32)
-    high = extra.astype(BF16)
-    data = jnp.concatenate([high, (extra - high.astype(F32)).astype(BF16)], axis=0)
-    mine = jnp.broadcast_to(mine_columns(gid_ref[...], me_ref[0]), (EXTRA, NODES_HERE))
-    hot = (mine == iota((EXTRA, NODES_HERE), 1)).astype(F32)
-    hot = jnp.concatenate([hot, hot], axis=0).T.astype(BF16)
-    acc_s[...] += dot(hot, data)
+
+
+def feature_part(feat_ref, k):
+    return pl.ds(pl.multiple_of(((feat_ref[0] + k) % 4) * COLS, COLS), COLS)
 
 
 def value_back_kernel(
-    me_ref, own_ref, ret_ref, rows_ref, p0_ref, p1_ref, p2_ref, p3_ref, o0_ref, o1_ref, o2_ref, o3_ref, gid_ref,
-    grad_ref, acc_s,
+    me_ref, feat_ref, ownv_ref, ret_ref, ownk_ref, rows_ref, o0_ref, o1_ref, o2_ref, o3_ref, gid_ref, wq_ref, wv_ref,
+    gq_ref, accv_s, acck_ref, pre_ref,
 ):
-    parts, others = (p0_ref, p1_ref, p2_ref, p3_ref), (o0_ref, o1_ref, o2_ref, o3_ref)
-    gather_grads(me_ref, own_ref, ret_ref, rows_ref, parts, others, COLS, gid_ref, acc_s)
-    grad_ref[...] = acc_s[...].astype(BF16)
+    others = (o0_ref, o1_ref, o2_ref, o3_ref)
+    parts = [ret_ref[me_ref[0] ^ (1 << m), SLOTS:] for m in range(EXPANDERS)]
+    accv_s[...] = ownv_ref[...]
+    add_halo(accv_s, me_ref, ret_ref, rows_ref, gid_ref)
+    add_partners(accv_s, [part[16:] for part in parts], others, COLS)
+    acck_ref[...] = ownk_ref[...]
+    add_partners(acck_ref, [part[:16] for part in parts], others, 0)
+    grad_value = accv_s[...].astype(BF16)
+    for k in range(4):
+        part = feature_part(feat_ref, k)
+        pre_ref[k] = dot_nt(gq_ref[...], wq_ref[part, :]) + dot_nt(grad_value, wv_ref[part, :])
 
 
 def key_back_kernel(
-    me_ref, feat_ref, own_ref, ret_ref, rows_ref, p0_ref, p1_ref, p2_ref, p3_ref, o0_ref, o1_ref, o2_ref, o3_ref, gid_ref,
-    wq_ref, wk_ref, wv_ref, gq_ref, gv_ref, t0_ref, t1_ref, t2_ref, t3_ref, acc_s,
+    me_ref, feat_ref, acck_ref, ret_ref, rows_ref, gid_ref, wk_ref, pre_ref, t0_ref, t1_ref, t2_ref, t3_ref, acc_s
 ):
-    parts, others = (p0_ref, p1_ref, p2_ref, p3_ref), (o0_ref, o1_ref, o2_ref, o3_ref)
-    gather_grads(me_ref, own_ref, ret_ref, rows_ref, parts, others, 0, gid_ref, acc_s)
+    acc_s[...] = acck_ref[...]
+    add_halo(acc_s, me_ref, ret_ref, rows_ref, gid_ref)
     grad_key = acc_s[...].astype(BF16)
-    for k, out in enumerate((t0_ref, t1_ref, t2_ref, t3_ref)):
-        part = pl.ds(pl.multiple_of(((feat_ref[0] + k) % 4) * COLS, COLS), COLS)
-        term = dot_nt(gq_ref[...], wq_ref[part, :]) + dot_nt(gv_ref[...], wv_ref[part, :])
-        term = term + dot_nt(grad_key, wk_ref[part, :])
-        out[...] = term.astype(out.dtype)
+    for k, out in ((1, t1_ref), (2, t2_ref), (3, t3_ref), (0, t0_ref)):
+        out[...] = (pre_ref[k] + dot_nt(grad_key, wk_ref[feature_part(feat_ref, k), :])).astype(out.dtype)
 
 
 def shape(dims, kind=BF16):
     return jax.ShapeDtypeStruct(dims, kind)
 
 
-def call(kernel, ins, outs, args, scratch=(), name=None, flops=0, out_spaces=None):
+def call(kernel, ins, outs, args, scratch=(), name=None, flops=0, out_spaces=None, aliases={}):
     cost = pl.CostEstimate(flops=flops, transcendentals=0, bytes_accessed=4_000_000)
     return pl.pallas_call(
         kernel,
@@ -537,6 +573,7 @@
         scratch_shapes=list(scratch),
         compiler_params=params(),
         cost_estimate=cost,
+        input_output_aliases=aliases,
         name=name,
     )(*args)
 
@@ -551,7 +588,8 @@
         [smem()] + [vmem()] * 8,
         (
             shape((NODES_HERE, COLS)),
-            shape((NODES_HERE, 2 * COLS)),
+            shape((NODES_HERE, COLS)),
+            shape((NODES_HERE, COLS)),
             shape((SENDERS, SLOTS, COLS)),
             shape((SENDERS, SLOTS, COLS)),
             shape((NODES_HERE + EXPANDERS * Q_BLOCKS, 2 * COLS)),
@@ -560,7 +598,8 @@
         (me, features, w_query, w_key, w_value, cotangent, rows, exp_list, gids),
         name="project",
         flops=3_000_000_000,
-        out_spaces=(*(vmem() for _ in range(5)), smem()),
+        out_spaces=(*(vmem() for _ in range(6)), smem()),
+        scratch=[pltpu.VMEM((NODES_HERE, 2 * COLS), BF16)],
     )
 
 
@@ -575,18 +614,34 @@
     )
 
 
-def run_partner(m, exp_rows, swap, query, cotangent):
-    return call(
-        lambda *refs: partner_kernel(m, *refs),
-        [vmem()] * 4,
+def run_partner_keys(exp_rows, swaps, query):
+    return call(
+        partner_key_kernel,
+        [vmem()] * 6,
+        (shape((EXPANDERS * Q_BLOCKS, BLOCK, COLS)), shape((EXPANDERS, Q_BLOCKS, 2 * BLOCK), F32)),
+        (exp_rows, *swaps, query),
+        name="partners",
+        flops=5_000_000_000,
+    )
+
+
+def run_finish(me, exp_rows, swaps, cotangent, out_t, scores, lse, local, back_v):
+    anywhere = pl.BlockSpec(memory_space=pl.ANY)
+    return call(
+        finish_kernel,
+        [smem()] + [vmem()] * 10 + [anywhere],
         (
-            shape((Q_BLOCKS, BLOCK, 2 * COLS)),
+            shape((NODES_HERE, COLS)),
+            shape((EXPANDERS, PART_ROWS, BLOCK)),
             shape((Q_BLOCKS, 2 * BLOCK), F32),
-            shape((Q_BLOCKS, 2 * BLOCK), F32),
+            shape((SENDERS, BACK, COLS)),
         ),
-        (exp_rows, swap, query, cotangent),
-        name="partner%d" % m,
-        flops=1_500_000_000,
+        (me, exp_rows, *swaps, cotangent, out_t, scores, lse, local, back_v),
+        name="finish",
+        flops=5_000_000_000,
+        out_spaces=(vmem(), vmem(), vmem(), anywhere),
+        scratch=[pltpu.SemaphoreType.DMA((EXPANDERS,))],
+        aliases={11: 3},
     )
 
 
@@ -597,7 +652,7 @@
     )
 
 
-def run_scores(plan, turned_q, paired, halo_k, gids, glob):
+def run_scores(plan, turned_q, own, halo_k, gids, glob):
     return call(
         score_kernel,
         [smem()] * 3 + [vmem()] * 5,
@@ -606,39 +661,38 @@
             shape((KEY_BLOCKS, BLOCK, COLS)),
             shape((KEY_BLOCKS, COLS, BLOCK)),
         ),
-        (*plan, turned_q, paired, halo_k, gids, glob),
+        (*plan, turned_q, own, halo_k, gids, glob),
         name="scores",
         flops=12_000_000_000,
     )
 
 
-def run_turn(paired, halo_v, gids, glob):
+def run_turn(own, halo_v, gids, glob):
     return call(
         turn_kernel,
         [vmem()] * 4,
         (shape((KEY_BLOCKS, BLOCK, COLS)), shape((KEY_BLOCKS, COLS, BLOCK))),
-        (paired, halo_v, gids, glob),
+        (own, halo_v, gids, glob),
         name="turn",
         flops=2_000_000_000,
     )
 
 
-def run_values(plan, keys, turned_v, prepared, part, scores, dprobs, pairs, gids):
+def run_values(plan, keys, turned_v, prepared, part, scores, gids):
     turned_q, _, turned_cot, cot_stack = prepared
     return call(
         value_kernel,
-        [smem()] * 3 + [vmem()] * 13,
+        [smem()] * 3 + [vmem()] * 8,
         (
-            shape((NODES_HERE, COLS)),
             shape((NODES_HERE, COLS), F32),
-            shape((SENDERS, SLOTS, COLS)),
+            shape((SENDERS, BACK, COLS)),
             shape((BLOCK, COLS)),
-            shape((EXPANDERS, 2, 16, BLOCK)),
+            shape((Q_BLOCKS, COLS, 2 * BLOCK), F32),
             shape((Q_BLOCKS, 2 * BLOCK), F32),
             shape((Q_BLOCKS, 2 * BLOCK), F32),
         ),
-        (*plan, keys, turned_v, turned_q, turned_cot, cot_stack, part, scores, dprobs, *pairs, gids),
-        scratch=[blocks_of(F32), pltpu.VMEM((Q_BLOCKS, COLS, 2 * BLOCK), F32)],
+        (*plan, keys, turned_v, turned_q, turned_cot, cot_stack, part, scores, gids),
+        scratch=[blocks_of(F32)],
         name="values",
         flops=20_000_000_000,
     )
@@ -648,38 +702,37 @@
     turned_q, q_stack, turned_cot, _ = prepared
     return call(
         key_kernel,
-        [smem()] * 3 + [vmem()] * 14,
+        [smem()] * 3 + [vmem()] * 11,
         (
             shape((NODES_HERE, COLS)),
             shape((NODES_HERE, COLS), F32),
             shape((SENDERS, SLOTS, COLS)),
             shape((BLOCK, COLS)),
         ),
-        (*plan, keys, turned_k, values, turned_q, q_stack, turned_cot, lse, delta, back, *pairs, gids),
+        (*plan, keys, turned_k, values, turned_q, q_stack, turned_cot, lse, delta, back, pairs, gids),
         scratch=[blocks_of(F32), pltpu.VMEM((Q_BLOCKS, COLS, 2 * BLOCK), F32)],
         name="keys",
         flops=25_000_000_000,
     )
 
 
-def run_value_back(me, own_v, returned_v, rows, parts, others, gids):
+def run_value_back(me, feat, own_v, returned_v, own_k, rows, others, gids, w_query, w_value, grad_query):
     return call(
         value_back_kernel,
-        [smem()] + [vmem()] * 12,
-        (shape((NODES_HERE, COLS)),),
-        (me, own_v, returned_v, rows, *parts, *others, gids),
-        scratch=[pltpu.VMEM((NODES_HERE, COLS), F32)],
+        [smem()] * 2 + [vmem()] * 12,
+        (shape((NODES_HERE, COLS), F32), shape((NODES_HERE, COLS), F32), shape((4, NODES_HERE, COLS), F32)),
+        (me, feat, own_v, returned_v, own_k, rows, *others, gids, w_query, w_value, grad_query),
         name="value_back",
-        flops=8_000_000_000,
-    )[0]
-
-
-def run_key_back(me, feat, own_k, returned_k, rows, parts, others, gids, w_query, w_key, w_value, grad_query, grad_value):
+        flops=12_000_000_000,
+    )[1:]
+
+
+def run_key_back(me, feat, own_k, returned_k, rows, gids, w_key, pre):
     return call(
         key_back_kernel,
-        [smem()] * 2 + [vmem()] * 17,
+        [smem()] * 2 + [vmem()] * 6,
         (shape((NODES_HERE, COLS), F32),) + tuple(shape((NODES_HERE, COLS)) for _ in range(3)),
-        (me, feat, own_k, returned_k, rows, *parts, *others, gids, w_query, w_key, w_value, grad_query, grad_value),
+        (me, feat, own_k, returned_k, rows, gids, w_key, pre),
         scratch=[pltpu.VMEM((NODES_HERE, COLS), F32)],
         name="key_back",
         flops=8_000_000_000,
@@ -692,19 +745,21 @@
     return owner, ((owner[:, None] == owner[None, :]) & (ids[None, :] < ids[:, None])).sum(1)
 
 
-def more_globals(rounds, global_ids, my_index, paired):
+def more_globals(rounds, global_ids, my_index, own_k, own_v):
     def body(state):
         r, glob = state
         owner, rank = ranks(global_ids)
         slot = rank - r * EXTRA
         here = (slot >= 0) & (slot < EXTRA)
         place = jnp.where((owner == my_index) & here, slot, EXTRA)
-        rows = jnp.zeros((EXTRA + 1, paired.shape[1]), BF16).at[place].set(paired[jnp.where(here, global_ids % NODES_HERE, 0)])[:EXTRA]
+        local = jnp.where(here, global_ids % NODES_HERE, 0)
+        found = jnp.concatenate([own_k[local], own_v[local]], axis=1)
+        rows = jnp.zeros((EXTRA + 1, 2 * COLS), BF16).at[place].set(found)[:EXTRA]
         got = lax.all_to_all(jnp.broadcast_to(rows[None], (SENDERS, *rows.shape)), "dom", 0, 0, tiled=True)
         found = got.reshape(SENDERS * EXTRA, -1)[jnp.clip(owner * EXTRA + slot, 0, SENDERS * EXTRA - 1)]
         return r + 1, jnp.where(here[:, None], found, glob)
 
-    start = (jnp.asarray(1, jnp.int32), jnp.zeros((BLOCK, paired.shape[1]), BF16))
+    start = (jnp.asarray(1, jnp.int32), jnp.zeros((BLOCK, 2 * COLS), BF16))
     return lax.while_loop(lambda state: state[0] < rounds, body, start)[1]
 
 
@@ -750,42 +805,42 @@
     me = my_index.reshape(1).astype(jnp.int32)
     feat = lax.axis_index("feat").reshape(1).astype(jnp.int32)
 
-    query, paired, out_k, out_v, away, rounds = run_project(
+    query, own_keys, own_values, out_k, out_v, away, rounds = run_project(
         me, features, w_query, w_key, w_value, cotangent, rows, exp_rows, gids
     )
     rounds = rounds[0]
-    glob = more_globals(rounds, global_ids, my_index, paired)
+    glob = more_globals(rounds, global_ids, my_index, own_keys, own_values)
     out_k, out_v, glob = lax.optimization_barrier((out_k, out_v, glob))
     halo_k = lax.all_to_all(out_k, "dom", 0, 0, tiled=True)
-    swaps = [swapped(paired, m) for m in range(EXPANDERS)]
+    key_swaps = [swapped(own_keys, m) for m in range(EXPANDERS)]
     plan = run_plan(block_mask, halo_count)
     prepared = run_prepare(query, cotangent)
     halo_v = lax.all_to_all(out_v, "dom", 0, 0, tiled=True)
-    part, keys, turned_k = run_scores(plan, prepared[0], paired, halo_k, gids, glob)
-    away, part, *swaps = lax.optimization_barrier((away, part, *swaps))
-    joined = {m: run_partner(m, exp_rows, swaps[m], query, cotangent) for m in (0, 1, 3)}
-    values, turned_v = run_turn(paired, halo_v, gids, glob)
-    swaps[2], values, joined = lax.optimization_barrier((swaps[2], values, joined))
-    joined[2] = run_partner(2, exp_rows, swaps[2], query, cotangent)
-    pairs, scores, dprobs = zip(*[joined[m] for m in range(EXPANDERS)])
+    part, keys, turned_k = run_scores(plan, prepared[0], own_keys, halo_k, gids, glob)
+    own_values_late, part = lax.optimization_barrier((own_values, part))
+    part, *key_swaps = lax.optimization_barrier((part, *key_swaps))
+    value_swaps = [swapped(own_values_late, m) for m in range(EXPANDERS)]
+    pairs, scores = run_partner_keys(exp_rows, key_swaps, query)
+    values, turned_v = run_turn(own_values, halo_v, gids, glob)
+    away, scores = lax.optimization_barrier((away, scores))
     others = [swapped(away, m) for m in range(EXPANDERS)]
-    attended, own_v, back_v, glob_v, back, delta, lse = run_values(
-        plan, keys, turned_v, prepared, part, jnp.stack(scores), jnp.stack(dprobs), pairs, gids
-    )
-    *others, lse = lax.optimization_barrier((*others, lse))
-    parts = [swapped(back[m], m) for m in range(EXPANDERS)]
+    own_v, back_v, glob_v, out_t, local, lse = run_values(plan, keys, turned_v, prepared, part, scores, gids)
+    out_t, *value_swaps = lax.optimization_barrier((out_t, *value_swaps))
+    attended, back, delta, back_v = run_finish(
+        me, exp_rows, value_swaps, cotangent, out_t, scores, lse, local, back_v
+    )
     returned_v = lax.all_to_all(back_v, "dom", 0, 0, tiled=True)
     grad_query, own_k, back_k, glob_k = run_keys(
         plan, keys, turned_k, values, prepared, lse, delta, back, pairs, gids
     )
-    own_k, returned_v, *parts = lax.optimization_barrier((own_k, returned_v, *parts))
+    own_k, returned_v, *others = lax.optimization_barrier((own_k, returned_v, *others))
     own_k, own_v = more_grads(rounds, global_ids, my_index, glob_k, glob_v, own_k, own_v)
     back_k, own_k, own_v = lax.optimization_barrier((back_k, own_k, own_v))
     returned_k = lax.all_to_all(back_k, "dom", 0, 0, tiled=True)
-    grad_value = run_value_back(me, own_v, returned_v, rows, parts, others, gids)
-    mine, *away = run_key_back(
-        me, feat, own_k, returned_k, rows, parts, others, gids, w_query, w_key, w_value, grad_query, grad_value
-    )
+    own_k, pre = run_value_back(
+        me, feat, own_v, returned_v, own_k, rows, others, gids, w_query, w_value, grad_query
+    )
+    mine, *away = run_key_back(me, feat, own_k, returned_k, rows, gids, w_key, pre)
     for k, term in enumerate(away, 1):
         mine = mine + lax.ppermute(term, "feat", [(i, (i + k) % 4) for i in range(4)]).astype(F32)
     return (attended, mine.astype(BF16))

time: 209 us -> 191 us (0.914)
  waiting for transfers between devices: 35.6 us -> 20.4 us
  starting transfers between devices: 47.1 us -> 56.7 us
  Pallas kernels: 111 us -> 103 us
  local copies, waits for them, and re-layouts: 6.53 us -> 4.13 us
    ppermute x12, waiting for transfers between devices: 10.6 us -> 0.03 us  [swapped(): lax.ppermute(value, 'dom', [(i, i ^ 1 << bit) for i in range(dom_count)])]
    pallas_call x13 -> x11, Pallas kernels: 111 us -> 103 us  [call(): pl.pallas_call(kernel, out_shape=outs, in_specs=ins, out_specs=out_spaces...]
    all_to_all x1, waiting for transfers between devices: 9.65 us -> 4.99 us  [on_device(): returned_k = lax.all_to_all(back_k, 'dom', 0, 0, tiled=True)]
    ppermute x12, starting transfers between devices: 15 us -> 19 us  [swapped(): lax.ppermute(value, 'dom', [(i, i ^ 1 << bit) for i in range(dom_count)])]
    all_to_all x1, starting transfers between devices: 8.82 us -> 12 us  [on_device(): returned_k = lax.all_to_all(back_k, 'dom', 0, 0, tiled=True)]
    all_to_all x1, starting transfers between devices: 4.81 us -> 7.28 us  [on_device(): returned_v = lax.all_to_all(back_v, 'dom', 0, 0, tiled=True)]
    unnamed x44 -> x26, local copies, waits for them, and re-layouts: 5.11 us -> 3.46 us
  transfers between devices with their start and end apart: 19 -> 19, of which waited for: 5 -> 4; matrix products, arithmetic and copies ran while one was open for 2% -> 1% of each run, Pallas kernels for 45% -> 47%
where the time goes in v5:
time: 191 us; the launch traced here: 190 us
  Pallas kernels  103 us (54%)
  starting transfers between devices  56.7 us (30%)
  waiting for transfers between devices  20.4 us (11%)
  local copies, waits for them, and re-layouts  4.13 us (2%)
  other arithmetic  3.47 us (2%)
    pallas_call x11, Pallas kernels, call(): pl.pallas_call(kernel, out_shape=outs, in_specs=ins, out_specs=out_spaces...  103 us
    ppermute x12, starting transfers between devices, swapped(): lax.ppermute(value, 'dom', [(i, i ^ 1 << bit) for i in range(dom_count)])  19 us
    all_to_all x1, starting transfers between devices, on_device(): returned_k = lax.all_to_all(back_k, 'dom', 0, 0, tiled=True)  12 us
    ppermute x3, waiting for transfers between devices, on_device(): lax.ppermute(term, 'feat', [(i, (i + k) % 4) for i in range(4)]).astype(F32)  10.9 us
    all_to_all x1, starting transfers between devices, on_device(): halo_k = lax.all_to_all(out_k, 'dom', 0, 0, tiled=True)  8.27 us
    all_to_all x1, starting transfers between devices, on_device(): returned_v = lax.all_to_all(back_v, 'dom', 0, 0, tiled=True)  7.28 us
    ppermute x3, starting transfers between devices, on_device(): lax.ppermute(term, 'feat', [(i, (i + k) % 4) for i in range(4)]).astype(F32)  5.83 us
    all_to_all x1, waiting for transfers between devices, on_device(): returned_k = lax.all_to_all(back_k, 'dom', 0, 0, tiled=True)  4.99 us
  transfers between devices with their start and end apart: 19, of which 4 were waited for; matrix products, arithmetic and copies ran while one was open for 1% of the time, Pallas kernels for 47%

profile of v5, /device:TPU:0, one launch (start us, length us, event | category | flops | bytes accessed | tf_op | source)
XLA Modules:
  0.0 190.1 jit_solution(6334374738220068157)
XLA Ops:
  0.6 0.7 negate_bitcast_fusion
  1.3 0.2 convert_reduce_fusion.1
  1.5 0.0 copy-start.4
  1.5 7.1 %project.1 = (bf16[1024,128]{1,0:T(8,128)(2,1)}, bf16[1024,128]{1,0:T(8,128)(2,1)S(1)}, bf16[1024,128]{1,0:T(8,128)(2,1)S(1)}, bf16[32,144,128]{2,1,0:T(8,128)(2...) custom-call(s32[1]{0:T(128)} %bitcast.14.me_ref, bf16[1024,512]{1,0:T(8,128)(2,1)} %x_ref.1, ...), custom_call_target="tpu_custom_call" | custom-call | flops 3000000000 | bytes 4000000 | tf_op jit(solution)/shard_map/project/pallas_call | solution.py:568
  8.7 0.6 while.34
  9.3 0.0 copy-start.6
  9.3 8.3 %all-to-all-start.2 = ((bf16[32,144,128]{2,1,0:T(8,128)(2,1)}), bf16[32,144,128]{2,1,0:T(8,128)(2,1)S(1)}, u32[]{:S(2)}, u32[]{:S(2)}) async-start(bf16[32,144,128]{2,1,0:T(8,128)(2,1)} %get-tuple-element.668), calls=%async_computation.2 | async-start | bytes 2359296 | tf_op jit(solution)/shard_map/all_to_all | solution.py:814
  17.6 0.4 collective-permute-start
  17.9 1.7 collective-permute-start.1
  19.6 2.7 %collective-permute-start.2 = (bf16[1024,128]{1,0:T(8,128)(2,1)S(1)}, bf16[1024,128]{1,0:T(8,128)(2,1)}, u32[]{:S(2)}, u32[]{:S(2)}) collective-permute-start(bf16[1024,128]{1,0:T(8,128)(2,1)S(1)} %get-tuple-element.1006), channel_id=1, source_target_pairs={{0,16},{4,20},{8,24},{12,28},{16,0},{20,4},{24,8},{28,12},{32,48},... | collective-permute-start | bytes 786440 | tf_op jit(solution)/shard_map/ppermute | solution.py:801
  22.3 1.5 collective-permute-start.3
  23.8 0.7 reshape.639.mask_ref
  24.4 4.5 %plan.1 = (s32[448]{0:T(512)}, s32[8]{0:T(128)}, s32[56]{0:T(128)}) custom-call(s32[320]{0:T(512)} %reshape.639.mask_ref, s32[32]{0:T(128)} %bitcast.117), custom_call_target="tpu_custom_call" | custom-call | bytes 4000000 | tf_op jit(solution)/shard_map/plan/pallas_call | solution.py:568
  28.9 2.7 %prepare.1 = (bf16[8,128,256]{2,1,0:T(8,128)(2,1)}, bf16[8,256,128]{2,1,0:T(8,128)(2,1)}, bf16[8,128,256]{2,1,0:T(8,128)(2,1)}, bf16[8,256,128]{2,1,0:T(8,128)(2,1)}) custom-call(bf16[1024,128]{1,0:T(8,128)(2,1)} %get-tuple-element.660.q_ref, bf16[1024,128]{1,0:T(8,128)(2,1)} %cot_ref.5), custom_call_target="tpu_custom_call" | custom-call | flops 2000000000 | bytes 4000000 | tf_op jit(solution)/shard_map/prepare/pallas_call | solution.py:568
  31.6 4.4 %all-to-all-done.2.hk_ref = bf16[32,144,128]{2,1,0:T(8,128)(2,1)S(1)} async-done(((bf16[32,144,128]{2,1,0:T(8,128)(2,1)}), bf16[32,144,128]{2,1,0:T(8,128)(2,1)S(1)}, u32[]{:S(2)}, u32[]{:S(2)}) %all-to-all-start.2) | async-done | bytes 1179680 | tf_op jit(solution)/shard_map/all_to_all | solution.py:814
  36.0 4.3 %all-to-all-start.3 = ((bf16[32,144,128]{2,1,0:T(8,128)(2,1)}), bf16[32,144,128]{2,1,0:T(8,128)(2,1)S(1)}, u32[]{:S(2)}, u32[]{:S(2)}) async-start(bf16[32,144,128]{2,1,0:T(8,128)(2,1)} %get-tuple-element.671), calls=%async_computation.3 | async-start | bytes 2359296 | tf_op jit(solution)/shard_map/all_to_all | solution.py:818
  40.3 0.0 copy-done.2
  40.4 14.2 %scores.1 = (f32[8,256]{1,0:T(8,128)}, bf16[42,128,128]{2,1,0:T(8,128)(2,1)}, bf16[42,128,128]{2,1,0:T(8,128)(2,1)}) custom-call(s32[448]{0:T(512)} %get-tuple-element.657.list_ref, s32[8]{0:T(128)} %get-tuple-element.658.groups_ref, s32[56]{0:T(128)} %get-tuple-element.659.live_ref, bf16[8,128,256]{2,1,0:T(8,128)(2,1)} %get-tuple-element.661.qt_ref, ...), custom_call_target="tpu_custom_call" | custom-call | flops 12000000000 | bytes 4000000 | tf_op jit(solution)/shard_map/scores/pallas_call | solution.py:568
  54.5 2.2 %collective-permute-start.4 = (bf16[1024,128]{1,0:T(8,128)(2,1)S(1)}, bf16[1024,128]{1,0:T(8,128)(2,1)}, u32[]{:S(2)}, u32[]{:S(2)}) collective-permute-start(bf16[1024,128]{1,0:T(8,128)(2,1)S(1)} %get-tuple-element.1001), channel_id=1, source_target_pairs={{0,4},{4,0},{8,12},{12,8},{16,20},{20,16},{24,28},{28,24},{32,36},... | collective-permute-start | bytes 786440 | tf_op jit(solution)/shard_map/ppermute | solution.py:801
  56.7 0.0 collective-permute-done.t0_ref
  56.7 2.1 %collective-permute-start.5 = (bf16[1024,128]{1,0:T(8,128)(2,1)S(1)}, bf16[1024,128]{1,0:T(8,128)(2,1)}, u32[]{:S(2)}, u32[]{:S(2)}) collective-permute-start(bf16[1024,128]{1,0:T(8,128)(2,1)S(1)} %get-tuple-element.1001), channel_id=1, source_target_pairs={{0,8},{4,12},{8,0},{12,4},{16,24},{20,28},{24,16},{28,20},{32,40},... | collective-permute-start | bytes 786440 | tf_op jit(solution)/shard_map/ppermute | solution.py:801
  58.8 0.0 collective-permute-done.1.t1_ref
  58.8 3.1 %collective-permute-start.6 = (bf16[1024,128]{1,0:T(8,128)(2,1)S(1)}, bf16[1024,128]{1,0:T(8,128)(2,1)}, u32[]{:S(2)}, u32[]{:S(2)}) collective-permute-start(bf16[1024,128]{1,0:T(8,128)(2,1)S(1)} %get-tuple-element.1001), channel_id=1, source_target_pairs={{0,16},{4,20},{8,24},{12,28},{16,0},{20,4},{24,8},{28,12},{32,48},... | collective-permute-start | bytes 786440 | tf_op jit(solution)/shard_map/ppermute | solution.py:801
  62.0 0.0 collective-permute-done.2.t2_ref
  62.0 0.6 collective-permute-start.7
  62.6 0.0 collective-permute-done.3.t3_ref
  62.6 5.4 %partners.1 = (bf16[32,128,128]{2,1,0:T(8,128)(2,1)}, f32[4,8,256]{2,1,0:T(8,128)}) custom-call(s32[4,1024]{1,0:T(4,128)} %exp_ref.5, bf16[1024,128]{1,0:T(8,128)(2,1)} %copy-done.13, bf16[1024,128]{1,0:T(8,128)(2,1)} %copy-done.14, bf16[1024,128]{1,0:T(8,128)(2,1)} %collective-permute-done.2.t2_ref, bf16[1024,128]{1,0:T(8,128)(2,1)} %collective-permute-done.3.t3_ref, ...), custom_call_target="tpu_custom_call" | custom-call | flops 5000000000 | bytes 4000000 | tf_op jit(solution)/shard_map/partners/pallas_call | solution.py:568
  68.0 0.8 collective-permute-start.10
  68.7 0.0 all-to-all-done.3.hv_ref
  68.7 1.0 copy-done.1
  69.8 4.0 %turn.1 = (bf16[42,128,128]{2,1,0:T(8,128)(2,1)}, bf16[42,128,128]{2,1,0:T(8,128)(2,1)}) custom-call(bf16[1024,128]{1,0:T(8,128)(2,1)S(1)} %get-tuple-element.1001, bf16[32,144,128]{2,1,0:T(8,128)(2,1)} %copy-done.1, s32[1,128]{1,0:T(1,128)S(1)} %bitcast.112, bf16[128,256]{1,0:T(8,128)(2,1)S(1)} %get-tuple-element.669.glob_ref), custom_call_target="tpu_custom_call" | custom-call | flops 2000000000 | bytes 4000000 | tf_op jit(solution)/shard_map/turn/pallas_call | solution.py:568
  73.8 16.6 %values.1 = (f32[1024,128]{1,0:T(8,128)}, bf16[32,176,128]{2,1,0:T(8,128)(2,1)}, bf16[128,128]{1,0:T(8,128)(2,1)}, f32[8,128,256]{2,1,0:T(8,128)}, f32[8,256]{1,0:T(8,128)}, /*index=5*/f32[8,256]{1,0:T(8,128)}) custom-call(s32[448]{0:T(512)} %get-tuple-element.657.list_ref, s32[8]{0:T(128)} %get-tuple-element.658.groups_ref, s32[56]{0:T(128)} %get-tuple-element.659.live_ref, ...), custom_call_target="tpu_custom_call" | custom-call | flops 20000000000 | bytes 4000000 | tf_op jit(solution)/shard_map/values/pallas_call | solution.py:568
  90.4 0.0 collective-permute-done.4.t0_ref
  90.4 3.5 %collective-permute-start.11 = (bf16[1056,256]{1,0:T(8,128)(2,1)S(1)}, bf16[1056,256]{1,0:T(8,128)(2,1)S(1)}, u32[]{:S(2)}, u32[]{:S(2)}) collective-permute-start(bf16[1056,256]{1,0:T(8,128)(2,1)S(1)} %copy-done.7), channel_id=1, source_target_pairs={{0,32},{4,36},{8,40},{12,44},{16,48},{20,52},{24,56},{28,60},{32,0... | collective-permute-start | bytes 1622024 | tf_op jit(solution)/shard_map/ppermute | solution.py:801
  93.9 0.0 collective-permute-done.5.t1_ref
  93.9 0.0 collective-permute-start.8
  93.9 0.0 collective-permute-done.6.t2_ref
  93.9 0.5 collective-permute-start.9
  94.4 0.0 collective-permute-done.7.t3_ref
  94.4 6.6 %finish.1 = (bf16[1024,128]{1,0:T(8,128)(2,1)}, bf16[4,32,128]{2,1,0:T(8,128)(2,1)}, f32[8,256]{1,0:T(8,128)}, bf16[32,176,128]{2,1,0:T(8,128)(2,1)}) custom-call(s32[1]{0:T(128)} %bitcast.14.me_ref, s32[4,1024]{1,0:T(4,128)} %exp_ref.5, bf16[1024,128]{1,0:T(8,128)(2,1)} %collective-permute-done.4.t0_ref, ...), custom_call_target="tpu_custom_call", output_to_operand_aliasing={{3}: (11, {})} | custom-call | flops 5000000000 | bytes 4000000 | tf_op jit(solution)/shard_map/finish/pallas_call | solution.py:568
  101.0 7.3 %all-to-all-start.4 = ((bf16[32,176,128]{2,1,0:T(8,128)(2,1)}), bf16[32,176,128]{2,1,0:T(8,128)(2,1)S(1)}, u32[]{:S(2)}, u32[]{:S(2)}) async-start(bf16[32,176,128]{2,1,0:T(8,128)(2,1)} %get-tuple-element.704), calls=%async_computation.4 | async-start | bytes 2883584 | tf_op jit(solution)/shard_map/all_to_all | solution.py:832
  108.3 22.3 %keys.1 = (bf16[1024,128]{1,0:T(8,128)(2,1)}, f32[1024,128]{1,0:T(8,128)}, bf16[32,144,128]{2,1,0:T(8,128)(2,1)}, bf16[128,128]{1,0:T(8,128)(2,1)}) custom-call(s32[448]{0:T(512)} %get-tuple-element.657.list_ref, s32[8]{0:T(128)} %get-tuple-element.658.groups_ref, s32[56]{0:T(128)} %get-tuple-element.659.live_ref, ...), custom_call_target="tpu_custom_call" | custom-call | flops 24999999488 | bytes 4000000 | tf_op jit(solution)/shard_map/keys/pallas_call | solution.py:568
  130.7 0.8 pad_maximum_fusion
  131.4 0.0 collective-permute-done.10.o2_ref
  131.5 0.0 collective-permute-done.11.o3_ref
  131.5 0.0 collective-permute-done.8.o0_ref
  131.5 0.0 collective-permute-done.9.o1_ref
  131.5 0.0 all-to-all-done.4.ret_ref
  131.5 0.8 copy-done.8
  132.3 0.2 copy-done.9
  132.4 0.5 copy-done
  132.9 0.6 while.35
  133.5 12.0 %all-to-all-start.5 = ((bf16[32,144,128]{2,1,0:T(8,128)(2,1)}), bf16[32,144,128]{2,1,0:T(8,128)(2,1)S(1)}, u32[]{:S(2)}, u32[]{:S(2)}) async-start(bf16[32,144,128]{2,1,0:T(8,128)(2,1)} %get-tuple-element.721), calls=%async_computation.5 | async-start | bytes 2359296 | tf_op jit(solution)/shard_map/all_to_all | solution.py:839
  145.6 13.2 %value_back.1 = (f32[1024,128]{1,0:T(8,128)}, f32[1024,128]{1,0:T(8,128)}, f32[4,1024,128]{2,1,0:T(8,128)}) custom-call(s32[1]{0:T(128)} %bitcast.14.me_ref, s32[1]{0:T(128)} %bitcast.21.feat_ref, f32[1024,128]{1,0:T(8,128)S(1)} %copy-done.12, bf16[32,176,128]{2,1,0:T(8,128)(2,1)} %copy-done, f32[1024,128]{1,0:T(8,128)} %get-tuple-element.714.ownk_ref, ...), custom_call_target="tpu_custom_call" | custom-call | flops 12000000000 | bytes 4000000 | tf_op jit(solution)/shard_map/value_back/pallas_call | solution.py:568
  158.7 5.0 %all-to-all-done.5.ret_ref = bf16[32,144,128]{2,1,0:T(8,128)(2,1)S(1)} async-done(((bf16[32,144,128]{2,1,0:T(8,128)(2,1)}), bf16[32,144,128]{2,1,0:T(8,128)(2,1)S(1)}, u32[]{:S(2)}, u32[]{:S(2)}) %all-to-all-start.5) | async-done | bytes 1179680 | tf_op jit(solution)/shard_map/all_to_all | solution.py:839
  163.7 1.0 copy-done.3
  164.7 6.7 %key_back.1 = (f32[1024,128]{1,0:T(8,128)}, bf16[1024,128]{1,0:T(8,128)(2,1)}, bf16[1024,128]{1,0:T(8,128)(2,1)}, bf16[1024,128]{1,0:T(8,128)(2,1)}) custom-call(s32[1]{0:T(128)} %bitcast.14.me_ref, s32[1]{0:T(128)} %bitcast.21.feat_ref, f32[1024,128]{1,0:T(8,128)} %get-tuple-element.720.acck_ref, bf16[32,144,128]{2,1,0:T(8,128)(2,1)} %copy-done.3, ...), custom_call_target="tpu_custom_call" | custom-call | flops 8000000000 | bytes 4000000 | tf_op jit(solution)/shard_map/key_back/pallas_call | solution.py:568
  171.5 1.6 collective-permute-start.12
  173.1 2.9 %collective-permute-start.13 = (bf16[1024,128]{1,0:T(8,128)(2,1)}, bf16[1024,128]{1,0:T(8,128)(2,1)S(1)}, u32[]{:S(2)}, u32[]{:S(2)}) collective-permute-start(bf16[1024,128]{1,0:T(8,128)(2,1)} %get-tuple-element.725), channel_id=1, source_target_pairs={{0,2},{1,3},{2,0},{3,1},{4,6},{5,7},{6,4},{7,5},{8,10},{9,11},{10,... | collective-permute-start | bytes 786440 | tf_op jit(solution)/shard_map/ppermute | solution.py:845
  176.0 1.3 collective-permute-start.14
  177.3 4.1 %collective-permute-done.12 = bf16[1024,128]{1,0:T(8,128)(2,1)S(1)} collective-permute-done((bf16[1024,128]{1,0:T(8,128)(2,1)}, bf16[1024,128]{1,0:T(8,128)(2,1)S(1)}, u32[]{:S(2)}, u32[]{:S(2)}) %collective-permute-start.12) | collective-permute-done | bytes 262176 | tf_op jit(solution)/shard_map/ppermute | solution.py:845
  181.4 6.8 %collective-permute-done.13 = bf16[1024,128]{1,0:T(8,128)(2,1)S(1)} collective-permute-done((bf16[1024,128]{1,0:T(8,128)(2,1)}, bf16[1024,128]{1,0:T(8,128)(2,1)S(1)}, u32[]{:S(2)}, u32[]{:S(2)}) %collective-permute-start.13) | collective-permute-done | bytes 262176 | tf_op jit(solution)/shard_map/ppermute | solution.py:845
  188.2 0.0 collective-permute-done.14
  188.2 1.9 add_convert_fusion
  (19 shorter events, 0.0 us)
Async XLA Ops:
  1.5 7.2 %copy-start.4 = (s32[128]{0:T(128)S(1)}, s32[128]{0:T(128)}, u32[]{:S(2)}) copy-start(s32[128]{0:T(128)} %param.23) | copy-start | bytes 1540
  9.3 14.5 %copy-start.6 = (s32[8,40]{1,0:T(8,128)S(1)}, s32[8,40]{1,0:T(8,128)}, u32[]{:S(2)}) copy-start(s32[8,40]{1,0:T(8,128)} %param.21) | copy-start | bytes 3844
  9.3 26.7 %all-to-all-start.2 = ((bf16[32,144,128]{2,1,0:T(8,128)(2,1)}), bf16[32,144,128]{2,1,0:T(8,128)(2,1)S(1)}, u32[]{:S(2)}, u32[]{:S(2)}) async-start(bf16[32,144,128]{2,1,0:T(8,128)(2,1)} %get-tuple-element.668), calls=%async_computation.2 | async-start | bytes 2359296 | tf_op jit(solution)/shard_map/all_to_all | solution.py:814
  17.6 39.2 %collective-permute-start = (bf16[1024,128]{1,0:T(8,128)(2,1)S(1)}, bf16[1024,128]{1,0:T(8,128)(2,1)S(1)}, u32[]{:S(2)}, u32[]{:S(2)}) collective-permute-start(bf16[1024,128]{1,0:T(8,128)(2,1)S(1)} %get-tuple-element.1006), channel_id=1, source_target_pairs={{0,4},{4,0},{8,12},{12,8},{16,20},{20,16},{24,28},{28,24},{32,36},... | collective-permute-start | bytes 786440 | tf_op jit(solution)/shard_map/ppermute | solution.py:801
  17.9 40.9 %collective-permute-start.1 = (bf16[1024,128]{1,0:T(8,128)(2,1)S(1)}, bf16[1024,128]{1,0:T(8,128)(2,1)S(1)}, u32[]{:S(2)}, u32[]{:S(2)}) collective-permute-start(bf16[1024,128]{1,0:T(8,128)(2,1)S(1)} %get-tuple-element.1006), channel_id=1, source_target_pairs={{0,8},{4,12},{8,0},{12,4},{16,24},{20,28},{24,16},{28,20},{32,40},... | collective-permute-start | bytes 786440 | tf_op jit(solution)/shard_map/ppermute | solution.py:801
  19.6 42.4 %collective-permute-start.2 = (bf16[1024,128]{1,0:T(8,128)(2,1)S(1)}, bf16[1024,128]{1,0:T(8,128)(2,1)}, u32[]{:S(2)}, u32[]{:S(2)}) collective-permute-start(bf16[1024,128]{1,0:T(8,128)(2,1)S(1)} %get-tuple-element.1006), channel_id=1, source_target_pairs={{0,16},{4,20},{8,24},{12,28},{16,0},{20,4},{24,8},{28,12},{32,48},... | collective-permute-start | bytes 786440 | tf_op jit(solution)/shard_map/ppermute | solution.py:801
  22.3 40.3 %collective-permute-start.3 = (bf16[1024,128]{1,0:T(8,128)(2,1)S(1)}, bf16[1024,128]{1,0:T(8,128)(2,1)}, u32[]{:S(2)}, u32[]{:S(2)}) collective-permute-start(bf16[1024,128]{1,0:T(8,128)(2,1)S(1)} %get-tuple-element.1006), channel_id=1, source_target_pairs={{0,32},{4,36},{8,40},{12,44},{16,48},{20,52},{24,56},{28,60},{32,0... | collective-permute-start | bytes 786440 | tf_op jit(solution)/shard_map/ppermute | solution.py:801
  36.0 4.3 %copy-start.2 = (bf16[32,144,128]{2,1,0:T(8,128)(2,1)}, bf16[32,144,128]{2,1,0:T(8,128)(2,1)S(1)}, u32[]{:S(2)}) copy-start(bf16[32,144,128]{2,1,0:T(8,128)(2,1)S(1)} %all-to-all-done.2.hk_ref) | copy-start | bytes 3538948
  36.0 32.7 %all-to-all-start.3 = ((bf16[32,144,128]{2,1,0:T(8,128)(2,1)}), bf16[32,144,128]{2,1,0:T(8,128)(2,1)S(1)}, u32[]{:S(2)}, u32[]{:S(2)}) async-start(bf16[32,144,128]{2,1,0:T(8,128)(2,1)} %get-tuple-element.671), calls=%async_computation.3 | async-start | bytes 2359296 | tf_op jit(solution)/shard_map/all_to_all | solution.py:818
  54.5 13.4 %copy-start.7 = (bf16[1056,256]{1,0:T(8,128)(2,1)S(1)}, bf16[1056,256]{1,0:T(8,128)(2,1)}, u32[]{:S(2)}) copy-start(bf16[1056,256]{1,0:T(8,128)(2,1)} %get-tuple-element.705) | copy-start | bytes 1622020
  54.5 35.9 %collective-permute-start.4 = (bf16[1024,128]{1,0:T(8,128)(2,1)S(1)}, bf16[1024,128]{1,0:T(8,128)(2,1)}, u32[]{:S(2)}, u32[]{:S(2)}) collective-permute-start(bf16[1024,128]{1,0:T(8,128)(2,1)S(1)} %get-tuple-element.1001), channel_id=1, source_target_pairs={{0,4},{4,0},{8,12},{12,8},{16,20},{20,16},{24,28},{28,24},{32,36},... | collective-permute-start | bytes 786440 | tf_op jit(solution)/shard_map/ppermute | solution.py:801
  56.7 5.8 %copy-start.13 = (bf16[1024,128]{1,0:T(8,128)(2,1)}, bf16[1024,128]{1,0:T(8,128)(2,1)S(1)}, u32[]{:S(2)}) copy-start(bf16[1024,128]{1,0:T(8,128)(2,1)S(1)} %collective-permute-done.t0_ref) | copy-start | bytes 786436
  56.7 37.1 %collective-permute-start.5 = (bf16[1024,128]{1,0:T(8,128)(2,1)S(1)}, bf16[1024,128]{1,0:T(8,128)(2,1)}, u32[]{:S(2)}, u32[]{:S(2)}) collective-permute-start(bf16[1024,128]{1,0:T(8,128)(2,1)S(1)} %get-tuple-element.1001), channel_id=1, source_target_pairs={{0,8},{4,12},{8,0},{12,4},{16,24},{20,28},{24,16},{28,20},{32,40},... | collective-permute-start | bytes 786440 | tf_op jit(solution)/shard_map/ppermute | solution.py:801
  58.8 3.8 %copy-start.14 = (bf16[1024,128]{1,0:T(8,128)(2,1)}, bf16[1024,128]{1,0:T(8,128)(2,1)S(1)}, u32[]{:S(2)}) copy-start(bf16[1024,128]{1,0:T(8,128)(2,1)S(1)} %collective-permute-done.1.t1_ref) | copy-start | bytes 786436
  58.8 35.1 %collective-permute-start.6 = (bf16[1024,128]{1,0:T(8,128)(2,1)S(1)}, bf16[1024,128]{1,0:T(8,128)(2,1)}, u32[]{:S(2)}, u32[]{:S(2)}) collective-permute-start(bf16[1024,128]{1,0:T(8,128)(2,1)S(1)} %get-tuple-element.1001), channel_id=1, source_target_pairs={{0,16},{4,20},{8,24},{12,28},{16,0},{20,4},{24,8},{28,12},{32,48},... | collective-permute-start | bytes 786440 | tf_op jit(solution)/shard_map/ppermute | solution.py:801
  62.0 32.4 %collective-permute-start.7 = (bf16[1024,128]{1,0:T(8,128)(2,1)S(1)}, bf16[1024,128]{1,0:T(8,128)(2,1)}, u32[]{:S(2)}, u32[]{:S(2)}) collective-permute-start(bf16[1024,128]{1,0:T(8,128)(2,1)S(1)} %get-tuple-element.1001), channel_id=1, source_target_pairs={{0,32},{4,36},{8,40},{12,44},{16,48},{20,52},{24,56},{28,60},{32,0... | collective-permute-start | bytes 786440 | tf_op jit(solution)/shard_map/ppermute | solution.py:801
  68.0 63.5 %collective-permute-start.10 = (bf16[1056,256]{1,0:T(8,128)(2,1)S(1)}, bf16[1056,256]{1,0:T(8,128)(2,1)S(1)}, u32[]{:S(2)}, u32[]{:S(2)}) collective-permute-start(bf16[1056,256]{1,0:T(8,128)(2,1)S(1)} %copy-done.7), channel_id=1, source_target_pairs={{0,16},{4,20},{8,24},{12,28},{16,0},{20,4},{24,8},{28,12},{32,48},... | collective-permute-start | bytes 1622024 | tf_op jit(solution)/shard_map/ppermute | solution.py:801
  68.7 1.0 copy-start.1
  90.4 41.1 %collective-permute-start.11 = (bf16[1056,256]{1,0:T(8,128)(2,1)S(1)}, bf16[1056,256]{1,0:T(8,128)(2,1)S(1)}, u32[]{:S(2)}, u32[]{:S(2)}) collective-permute-start(bf16[1056,256]{1,0:T(8,128)(2,1)S(1)} %copy-done.7), channel_id=1, source_target_pairs={{0,32},{4,36},{8,40},{12,44},{16,48},{20,52},{24,56},{28,60},{32,0... | collective-permute-start | bytes 1622024 | tf_op jit(solution)/shard_map/ppermute | solution.py:801
  93.9 37.6 %collective-permute-start.8 = (bf16[1056,256]{1,0:T(8,128)(2,1)S(1)}, bf16[1056,256]{1,0:T(8,128)(2,1)}, u32[]{:S(2)}, u32[]{:S(2)}) collective-permute-start(bf16[1056,256]{1,0:T(8,128)(2,1)S(1)} %copy-done.7), channel_id=1, source_target_pairs={{0,4},{4,0},{8,12},{12,8},{16,20},{20,16},{24,28},{28,24},{32,36},... | collective-permute-start | bytes 1622024 | tf_op jit(solution)/shard_map/ppermute | solution.py:801
  93.9 37.6 %collective-permute-start.9 = (bf16[1056,256]{1,0:T(8,128)(2,1)S(1)}, bf16[1056,256]{1,0:T(8,128)(2,1)}, u32[]{:S(2)}, u32[]{:S(2)}) collective-permute-start(bf16[1056,256]{1,0:T(8,128)(2,1)S(1)} %copy-done.7), channel_id=1, source_target_pairs={{0,8},{4,12},{8,0},{12,4},{16,24},{20,28},{24,16},{28,20},{32,40},... | collective-permute-start | bytes 1622024 | tf_op jit(solution)/shard_map/ppermute | solution.py:801
  101.0 30.5 %all-to-all-start.4 = ((bf16[32,176,128]{2,1,0:T(8,128)(2,1)}), bf16[32,176,128]{2,1,0:T(8,128)(2,1)S(1)}, u32[]{:S(2)}, u32[]{:S(2)}) async-start(bf16[32,176,128]{2,1,0:T(8,128)(2,1)} %get-tuple-element.704), calls=%async_computation.4 | async-start | bytes 2883584 | tf_op jit(solution)/shard_map/all_to_all | solution.py:832
  108.3 22.3 %copy-start.5 = (bf16[128,128]{1,0:T(8,128)(2,1)S(1)}, bf16[128,128]{1,0:T(8,128)(2,1)}, u32[]{:S(2)}) copy-start(bf16[128,128]{1,0:T(8,128)(2,1)} %get-tuple-element.709) | copy-start | bytes 98308
  131.4 0.8 copy-start.8
  131.5 1.0 copy-start.9
  131.5 1.4 copy-start
  133.5 12.0 %copy-start.12 = (f32[1024,128]{1,0:T(8,128)S(1)}, f32[1024,128]{1,0:T(8,128)}, u32[]{:S(2)}) copy-start(f32[1024,128]{1,0:T(8,128)} %get-tuple-element.712.ownv_ref) | copy-start | bytes 1572868
  133.5 30.2 %all-to-all-start.5 = ((bf16[32,144,128]{2,1,0:T(8,128)(2,1)}), bf16[32,144,128]{2,1,0:T(8,128)(2,1)S(1)}, u32[]{:S(2)}, u32[]{:S(2)}) async-start(bf16[32,144,128]{2,1,0:T(8,128)(2,1)} %get-tuple-element.721), calls=%async_computation.5 | async-start | bytes 2359296 | tf_op jit(solution)/shard_map/all_to_all | solution.py:839
  163.7 1.0 copy-start.3
  171.5 10.0 %collective-permute-start.12 = (bf16[1024,128]{1,0:T(8,128)(2,1)}, bf16[1024,128]{1,0:T(8,128)(2,1)S(1)}, u32[]{:S(2)}, u32[]{:S(2)}) collective-permute-start(bf16[1024,128]{1,0:T(8,128)(2,1)} %get-tuple-element.724), channel_id=1, source_target_pairs={{0,1},{1,2},{2,3},{3,0},{4,5},{5,6},{6,7},{7,4},{8,9},{9,10},{10,1... | collective-permute-start | bytes 786440 | tf_op jit(solution)/shard_map/ppermute | solution.py:845
  173.1 15.2 %collective-permute-start.13 = (bf16[1024,128]{1,0:T(8,128)(2,1)}, bf16[1024,128]{1,0:T(8,128)(2,1)S(1)}, u32[]{:S(2)}, u32[]{:S(2)}) collective-permute-start(bf16[1024,128]{1,0:T(8,128)(2,1)} %get-tuple-element.725), channel_id=1, source_target_pairs={{0,2},{1,3},{2,0},{3,1},{4,6},{5,7},{6,4},{7,5},{8,10},{9,11},{10,... | collective-permute-start | bytes 786440 | tf_op jit(solution)/shard_map/ppermute | solution.py:845
  176.0 12.3 %collective-permute-start.14 = (bf16[1024,128]{1,0:T(8,128)(2,1)}, bf16[1024,128]{1,0:T(8,128)(2,1)S(1)}, u32[]{:S(2)}, u32[]{:S(2)}) collective-permute-start(bf16[1024,128]{1,0:T(8,128)(2,1)} %get-tuple-element.726), channel_id=1, source_target_pairs={{0,3},{1,0},{2,1},{3,2},{4,7},{5,4},{6,5},{7,6},{8,11},{9,8},{10,9... | collective-permute-start | bytes 786440 | tf_op jit(solution)/shard_map/ppermute | solution.py:845

commit v6 on v5

--- a/solution.py
+++ b/solution.py
@@ -30,7 +30,7 @@
 
 
 def params():
-    return pltpu.CompilerParams(vmem_limit_bytes=56 * 1024 * 1024)
+    return pltpu.CompilerParams(vmem_limit_bytes=20 * 1024 * 1024)
 
 
 def vmem():

time: 191 us -> 197 us (1.031)
  local copies, waits for them, and re-layouts: 4.13 us -> 31.3 us
  Pallas kernels: 103 us -> 91.5 us
  starting transfers between devices: 56.7 us -> 52.5 us
  waiting for transfers between devices: 20.4 us -> 17.4 us
    unnamed x26 -> x98, local copies, waits for them, and re-layouts: 3.46 us -> 31.3 us
    pallas_call x11, Pallas kernels: 103 us -> 91.5 us  [call(): pl.pallas_call(kernel, out_shape=outs, in_specs=ins, out_specs=out_spaces...]
    ppermute x12, starting transfers between devices: 19 us -> 16.1 us  [swapped(): lax.ppermute(value, 'dom', [(i, i ^ 1 << bit) for i in range(dom_count)])]
    all_to_all x1, waiting for transfers between devices: 4.99 us -> 2.54 us  [on_device(): returned_k = lax.all_to_all(back_k, 'dom', 0, 0, tiled=True)]
  transfers between devices with their start and end apart: 19 -> 19, of which waited for: 4 -> 4; matrix products, arithmetic and copies ran while one was open for 1% -> 0% of each run, Pallas kernels for 47% -> 41%
where the time goes in v6:
time: 197 us
  Pallas kernels  91.5 us (46%)
  starting transfers between devices  52.5 us (27%)
  local copies, waits for them, and re-layouts  31.3 us (16%)
  waiting for transfers between devices  17.4 us (9%)
    pallas_call x11, Pallas kernels, call(): pl.pallas_call(kernel, out_shape=outs, in_specs=ins, out_specs=out_spaces...  91.5 us
    unnamed x98, local copies, waits for them, and re-layouts  31.3 us
    ppermute x12, starting transfers between devices, swapped(): lax.ppermute(value, 'dom', [(i, i ^ 1 << bit) for i in range(dom_count)])  16.1 us
    ppermute x3, waiting for transfers between devices, on_device(): lax.ppermute(term, 'feat', [(i, (i + k) % 4) for i in range(4)]).astype(F32)  10.7 us
    all_to_all x1, starting transfers between devices, on_device(): returned_k = lax.all_to_all(back_k, 'dom', 0, 0, tiled=True)  10.3 us
    all_to_all x1, starting transfers between devices, on_device(): halo_k = lax.all_to_all(out_k, 'dom', 0, 0, tiled=True)  8.39 us
    all_to_all x1, starting transfers between devices, on_device(): returned_v = lax.all_to_all(back_v, 'dom', 0, 0, tiled=True)  7.47 us
    ppermute x3, starting transfers between devices, on_device(): lax.ppermute(term, 'feat', [(i, (i + k) % 4) for i in range(4)]).astype(F32)  5.89 us
  transfers between devices with their start and end apart: 19, of which 4 were waited for; matrix products, arithmetic and copies ran while one was open for 0% of the time, Pallas kernels for 41%

profile of v6, /device:TPU:0, one launch (start us, length us, event | category | flops | bytes accessed | tf_op | source)
XLA Modules:
  0.0 196.6 jit_solution(14162878492877229620)
XLA Ops:
  0.6 0.7 negate_bitcast_fusion
  1.5 1.2 copy-done.1
  2.7 0.9 copy-done.4
  3.7 0.9 copy-done.7
  4.6 0.9 copy-done.9
  5.5 0.9 copy-done.11
  6.4 0.7 copy-done.13
  7.1 0.7 copy-done.15
  7.8 6.4 %project.1 = (bf16[1024,128]{1,0:T(8,128)(2,1)S(1)}, bf16[1024,128]{1,0:T(8,128)(2,1)}, bf16[1024,128]{1,0:T(8,128)(2,1)}, bf16[32,144,128]{2,1,0:T(8,128)(2,1)}...) custom-call(s32[1]{0:T(128)} %bitcast.14.me_ref, bf16[1024,512]{1,0:T(8,128)(2,1)S(1)} %copy-done.1, ...), custom_call_target="tpu_custom_call" | custom-call | flops 3000000000 | bytes 4000000 | tf_op jit(solution)/shard_map/project/pallas_call | solution.py:568
  14.9 8.4 %all-to-all-start.2 = ((bf16[32,144,128]{2,1,0:T(8,128)(2,1)}), bf16[32,144,128]{2,1,0:T(8,128)(2,1)S(1)}, u32[]{:S(2)}, u32[]{:S(2)}) async-start(bf16[32,144,128]{2,1,0:T(8,128)(2,1)} %get-tuple-element.668), calls=%async_computation.2 | async-start | bytes 2359296 | tf_op jit(solution)/shard_map/all_to_all | solution.py:814
  23.6 1.7 collective-permute-start.1
  25.3 2.7 %collective-permute-start.2 = (bf16[1024,128]{1,0:T(8,128)(2,1)}, bf16[1024,128]{1,0:T(8,128)(2,1)}, u32[]{:S(2)}, u32[]{:S(2)}) collective-permute-start(bf16[1024,128]{1,0:T(8,128)(2,1)} %get-tuple-element.926.own_ref), channel_id=1, source_target_pairs={{0,16},{4,20},{8,24},{12,28},{16,0},{20,4},{24,8},{28,12},{32,48},... | collective-permute-start | bytes 786440 | tf_op jit(solution)/shard_map/ppermute | solution.py:801
  28.0 1.5 collective-permute-start.3
  29.5 4.4 %plan.1 = (s32[448]{0:T(512)S(1)}, s32[8]{0:T(128)S(1)}, s32[56]{0:T(128)S(1)}) custom-call(s32[320]{0:T(512)S(1)} %reshape.639.mask_ref, s32[32]{0:T(128)S(1)} %bitcast.109), custom_call_target="tpu_custom_call" | custom-call | bytes 4000000 | tf_op jit(solution)/shard_map/plan/pallas_call | solution.py:568
  34.4 0.8 copy-done.19
  35.2 0.8 copy-done.23
  36.0 0.8 copy-done.25
  36.8 0.8 copy-done.28
  37.6 4.1 %all-to-all-done.2.hk_ref = bf16[32,144,128]{2,1,0:T(8,128)(2,1)S(1)} async-done(((bf16[32,144,128]{2,1,0:T(8,128)(2,1)}), bf16[32,144,128]{2,1,0:T(8,128)(2,1)S(1)}, u32[]{:S(2)}, u32[]{:S(2)}) %all-to-all-start.2) | async-done | bytes 1179680 | tf_op jit(solution)/shard_map/all_to_all | solution.py:814
  41.7 4.3 %all-to-all-start.3 = ((bf16[32,144,128]{2,1,0:T(8,128)(2,1)}), bf16[32,144,128]{2,1,0:T(8,128)(2,1)S(1)}, u32[]{:S(2)}, u32[]{:S(2)}) async-start(bf16[32,144,128]{2,1,0:T(8,128)(2,1)} %get-tuple-element.671), calls=%async_computation.3 | async-start | bytes 2359296 | tf_op jit(solution)/shard_map/all_to_all | solution.py:818
  46.0 1.0 copy-done.20
  47.1 13.7 %scores.1 = (f32[8,256]{1,0:T(8,128)S(1)}, bf16[42,128,128]{2,1,0:T(8,128)(2,1)S(1)}, bf16[42,128,128]{2,1,0:T(8,128)(2,1)S(1)}) custom-call(s32[448]{0:T(512)S(1)} %get-tuple-element.657.list_ref, s32[8]{0:T(128)S(1)} %get-tuple-element.658.groups_ref, s32[56]{0:T(128)S(1)} %get-tuple-element.659.live_ref, bf16[8,128,256]{2,1,0:T(8,128)(2,1)S(1)} %copy-done.20, ...), custom_call_target="tpu_custom_call" | custom-call | flops 12000000000 | bytes 4000000 | tf_op jit(solution)/shard_map/scores/pallas_call | solution.py:568
  60.8 1.1 copy-done.38
  61.9 1.7 collective-permute-start.4
  63.6 0.7 collective-permute-start.5
  64.3 2.6 %collective-permute-start.6 = (bf16[1024,128]{1,0:T(8,128)(2,1)}, bf16[1024,128]{1,0:T(8,128)(2,1)}, u32[]{:S(2)}, u32[]{:S(2)}) collective-permute-start(bf16[1024,128]{1,0:T(8,128)(2,1)} %get-tuple-element.686.own_ref), channel_id=1, source_target_pairs={{0,16},{4,20},{8,24},{12,28},{16,0},{20,4},{24,8},{28,12},{32,48},... | collective-permute-start | bytes 786440 | tf_op jit(solution)/shard_map/ppermute | solution.py:801
  66.9 1.9 collective-permute-start.7
  68.8 4.2 %partners.1 = (bf16[32,128,128]{2,1,0:T(8,128)(2,1)S(1)}, f32[4,8,256]{2,1,0:T(8,128)S(1)}) custom-call(s32[4,1024]{1,0:T(4,128)S(1)} %copy-done.14, bf16[1024,128]{1,0:T(8,128)(2,1)S(1)} %collective-permute-done.t0_ref, bf16[1024,128]{1,0:T(8,128)(2,1)S(1)} %collective-permute-done.1.t1_ref, bf16[1024,128]{1,0:T(8,128)(2,1)} %collective-permute-done.2.t2_ref, ...), custom_call_target="tpu_custom_call" | custom-call | flops 5000000000 | bytes 4000000 | tf_op jit(solution)/shard_map/partners/pallas_call | solution.py:568
  73.1 1.0 copy-done.32
  74.1 0.9 collective-permute-start.10
  75.0 2.3 %turn.1 = (bf16[42,128,128]{2,1,0:T(8,128)(2,1)S(1)}, bf16[42,128,128]{2,1,0:T(8,128)(2,1)S(1)}) custom-call(bf16[1024,128]{1,0:T(8,128)(2,1)} %get-tuple-element.686.own_ref, bf16[32,144,128]{2,1,0:T(8,128)(2,1)S(1)} %all-to-all-done.3.hv_ref, s32[1,128]{1,0:T(1,128)S(1)} %bitcast.116, bf16[128,256]{1,0:T(8,128)(2,1)S(1)} %get-tuple-element.669.glob_ref), custom_call_target="tpu_custom_call" | custom-call | flops 2000000000 | bytes 4000000 | tf_op jit(solution)/shard_map/turn/pallas_call | solution.py:568
  77.3 1.1 copy-done.17
  78.5 16.5 %values.1 = (f32[1024,128]{1,0:T(8,128)}, bf16[32,176,128]{2,1,0:T(8,128)(2,1)}, bf16[128,128]{1,0:T(8,128)(2,1)S(1)}, f32[8,128,256]{2,1,0:T(8,128)S(1)}, f32[8,256]{1,0:T(8,128)S(1)}, /*index=5*/f32[8,256]{1,0:T(8,128)S(1)}) custom-call(s32[448]{0:T(512)S(1)} %get-tuple-element.657.list_ref, s32[8]{0:T(128)S(1)} %get-tuple-element.658.groups_ref, ...), custom_call_target="tpu_custom_call" | custom-call | flops 20000000000 | bytes 4000000 | tf_op jit(solution)/shard_map/values/pallas_call | solution.py:568
  95.0 0.8 collective-permute-start.8
  95.8 1.2 collective-permute-start.9
  97.1 6.1 %finish.1 = (bf16[1024,128]{1,0:T(8,128)(2,1)}, bf16[4,32,128]{2,1,0:T(8,128)(2,1)S(1)}, f32[8,256]{1,0:T(8,128)S(1)}, bf16[32,176,128]{2,1,0:T(8,128)(2,1)}) custom-call(s32[1]{0:T(128)} %bitcast.14.me_ref, s32[4,1024]{1,0:T(4,128)S(1)} %copy-done.14, bf16[1024,128]{1,0:T(8,128)(2,1)S(1)} %collective-permute-done.4.t0_ref, ...), custom_call_target="tpu_custom_call", output_to_operand_aliasing={{3}: (11, {})} | custom-call | flops 5000000000 | bytes 4000000 | tf_op jit(solution)/shard_map/finish/pallas_call | solution.py:568
  103.1 7.5 %all-to-all-start.4 = ((bf16[32,176,128]{2,1,0:T(8,128)(2,1)}), bf16[32,176,128]{2,1,0:T(8,128)(2,1)S(1)}, u32[]{:S(2)}, u32[]{:S(2)}) async-start(bf16[32,176,128]{2,1,0:T(8,128)(2,1)} %get-tuple-element.704), calls=%async_computation.4 | async-start | bytes 2883584 | tf_op jit(solution)/shard_map/all_to_all | solution.py:832
  110.6 1.3 copy-done.18
  112.0 1.0 copy-done.22
  113.0 1.0 copy-done.24
  114.0 1.0 copy-done.27
  115.1 1.2 copy-done.33
  116.3 1.3 copy-done.40
  117.7 1.3 copy-done.42
  119.0 22.3 %keys.1 = (bf16[1024,128]{1,0:T(8,128)(2,1)S(1)}, f32[1024,128]{1,0:T(8,128)}, bf16[32,144,128]{2,1,0:T(8,128)(2,1)}, bf16[128,128]{1,0:T(8,128)(2,1)S(1)}) custom-call(s32[448]{0:T(512)S(1)} %get-tuple-element.657.list_ref, s32[8]{0:T(128)S(1)} %get-tuple-element.658.groups_ref, s32[56]{0:T(128)S(1)} %get-tuple-element.659.live_ref, ...), custom_call_target="tpu_custom_call" | custom-call | flops 24999999488 | bytes 4000000 | tf_op jit(solution)/shard_map/keys/pallas_call | solution.py:568
  141.3 0.7 copy-done.43
  142.1 0.8 copy-done.2
  143.5 10.3 %all-to-all-start.5 = ((bf16[32,144,128]{2,1,0:T(8,128)(2,1)}), bf16[32,144,128]{2,1,0:T(8,128)(2,1)S(1)}, u32[]{:S(2)}, u32[]{:S(2)}) async-start(bf16[32,144,128]{2,1,0:T(8,128)(2,1)} %get-tuple-element.721), calls=%async_computation.5 | async-start | bytes 2359296 | tf_op jit(solution)/shard_map/all_to_all | solution.py:839
  153.8 1.0 copy-done.3
  154.8 0.9 copy-done.44
  155.8 11.5 %value_back.1 = (f32[1024,128]{1,0:T(8,128)}, f32[1024,128]{1,0:T(8,128)S(1)}, f32[4,1024,128]{2,1,0:T(8,128)S(1)}) custom-call(s32[1]{0:T(128)} %bitcast.14.me_ref, s32[1]{0:T(128)} %bitcast.21.feat_ref, f32[1024,128]{1,0:T(8,128)} %get-tuple-element.712.ownv_ref, bf16[32,176,128]{2,1,0:T(8,128)(2,1)S(1)} %all-to-all-done.4.ret_ref, ...), custom_call_target="tpu_custom_call" | custom-call | flops 12000000000 | bytes 4000000 | tf_op jit(solution)/shard_map/value_back/pallas_call | solution.py:568
  167.3 1.3 copy-done.34
  168.6 0.8 copy-done.36
  169.4 2.5 %all-to-all-done.5.ret_ref = bf16[32,144,128]{2,1,0:T(8,128)(2,1)S(1)} async-done(((bf16[32,144,128]{2,1,0:T(8,128)(2,1)}), bf16[32,144,128]{2,1,0:T(8,128)(2,1)S(1)}, u32[]{:S(2)}, u32[]{:S(2)}) %all-to-all-start.5) | async-done | bytes 1179680 | tf_op jit(solution)/shard_map/all_to_all | solution.py:839
  171.9 0.9 copy-done.12
  172.8 1.6 copy-done.35
  174.4 1.0 copy-done.37
  175.5 3.6 %key_back.1 = (f32[1024,128]{1,0:T(8,128)S(1)}, bf16[1024,128]{1,0:T(8,128)(2,1)S(1)}, bf16[1024,128]{1,0:T(8,128)(2,1)S(1)}, bf16[1024,128]{1,0:T(8,128)(2,1)S(1)}) custom-call(s32[1]{0:T(128)} %bitcast.14.me_ref, s32[1]{0:T(128)} %bitcast.21.feat_ref, f32[1024,128]{1,0:T(8,128)S(1)} %copy-done.37, bf16[32,144,128]{2,1,0:T(8,128)(2,1)S(1)} %all-to-all-done.5.ret_ref, ...), custom_call_target="tpu_custom_call" | custom-call | flops 8000000000 | bytes 4000000 | tf_op jit(solution)/shard_map/key_back/pallas_call | solution.py:568
  179.1 1.6 collective-permute-start.12
  180.7 2.9 %collective-permute-start.13 = (bf16[1024,128]{1,0:T(8,128)(2,1)S(1)}, bf16[1024,128]{1,0:T(8,128)(2,1)S(1)}, u32[]{:S(2)}, u32[]{:S(2)}) collective-permute-start(bf16[1024,128]{1,0:T(8,128)(2,1)S(1)} %get-tuple-element.725), channel_id=1, source_target_pairs={{0,2},{1,3},{2,0},{3,1},{4,6},{5,7},{6,4},{7,5},{8,10},{9,11},{10,... | collective-permute-start | bytes 786440 | tf_op jit(solution)/shard_map/ppermute | solution.py:845
  183.6 1.3 collective-permute-start.14
  185.0 3.9 %collective-permute-done.12 = bf16[1024,128]{1,0:T(8,128)(2,1)S(1)} collective-permute-done((bf16[1024,128]{1,0:T(8,128)(2,1)S(1)}, bf16[1024,128]{1,0:T(8,128)(2,1)S(1)}, u32[]{:S(2)}, u32[]{:S(2)}) %collective-permute-start.12) | collective-permute-done | bytes 262176 | tf_op jit(solution)/shard_map/ppermute | solution.py:845
  188.9 6.8 %collective-permute-done.13 = bf16[1024,128]{1,0:T(8,128)(2,1)S(1)} collective-permute-done((bf16[1024,128]{1,0:T(8,128)(2,1)S(1)}, bf16[1024,128]{1,0:T(8,128)(2,1)S(1)}, u32[]{:S(2)}, u32[]{:S(2)}) %collective-permute-start.13) | collective-permute-done | bytes 262176 | tf_op jit(solution)/shard_map/ppermute | solution.py:845
  195.7 0.8 add_convert_fusion
  (91 shorter events, 2.4 us)
Async XLA Ops:
  1.5 1.2 copy-start.1
  2.7 0.9 copy-start.4
  3.7 0.9 copy-start.7
  4.6 0.9 copy-start.9
  5.5 0.9 copy-start.11
  7.8 6.4 %copy-start.45 = (s32[128]{0:T(128)S(1)}, s32[128]{0:T(128)}, u32[]{:S(2)}) copy-start(s32[128]{0:T(128)} %param.23) | copy-start | bytes 1540
  14.2 19.7 %copy-start.30 = (bf16[1024,128]{1,0:T(8,128)(2,1)}, bf16[1024,128]{1,0:T(8,128)(2,1)S(1)}, u32[]{:S(2)}) copy-start(bf16[1024,128]{1,0:T(8,128)(2,1)S(1)} %get-tuple-element.660.q_ref) | copy-start | bytes 786436
  14.8 19.1 %copy-start.46 = (s32[128]{0:T(128)}, s32[128]{0:T(128)S(1)}, u32[]{:S(2)}) copy-start(s32[128]{0:T(128)S(1)} %get-tuple-element.1024) | copy-start | bytes 1540
  14.8 14.6 %copy-start.48 = (s32[8,40]{1,0:T(8,128)S(1)}, s32[8,40]{1,0:T(8,128)}, u32[]{:S(2)}) copy-start(s32[8,40]{1,0:T(8,128)} %param.21) | copy-start | bytes 3844
  14.9 14.7 %copy-start = (s32[32,1]{0,1:T(1,128)S(1)}, s32[32,1]{0,1:T(1,128)}, u32[]{:S(2)}) copy-start(s32[32,1]{0,1:T(1,128)} %param.20) | copy-start | bytes 388
  14.9 19.1 %copy-start.5 = (bf16[1024,128]{1,0:T(8,128)(2,1)S(1)}, bf16[1024,128]{1,0:T(8,128)(2,1)}, u32[]{:S(2)}) copy-start(bf16[1024,128]{1,0:T(8,128)(2,1)} %cot_ref.5) | copy-start | bytes 786436
  14.9 26.8 %all-to-all-start.2 = ((bf16[32,144,128]{2,1,0:T(8,128)(2,1)}), bf16[32,144,128]{2,1,0:T(8,128)(2,1)S(1)}, u32[]{:S(2)}, u32[]{:S(2)}) async-start(bf16[32,144,128]{2,1,0:T(8,128)(2,1)} %get-tuple-element.668), calls=%async_computation.2 | async-start | bytes 2359296 | tf_op jit(solution)/shard_map/all_to_all | solution.py:814
  23.3 40.3 %collective-permute-start = (bf16[1024,128]{1,0:T(8,128)(2,1)}, bf16[1024,128]{1,0:T(8,128)(2,1)S(1)}, u32[]{:S(2)}, u32[]{:S(2)}) collective-permute-start(bf16[1024,128]{1,0:T(8,128)(2,1)} %get-tuple-element.926.own_ref), channel_id=1, source_target_pairs={{0,4},{4,0},{8,12},{12,8},{16,20},{20,16},{24,28},{28,24},{32,36},... | collective-permute-start | bytes 786440 | tf_op jit(solution)/shard_map/ppermute | solution.py:801
  23.6 40.6 %collective-permute-start.1 = (bf16[1024,128]{1,0:T(8,128)(2,1)}, bf16[1024,128]{1,0:T(8,128)(2,1)S(1)}, u32[]{:S(2)}, u32[]{:S(2)}) collective-permute-start(bf16[1024,128]{1,0:T(8,128)(2,1)} %get-tuple-element.926.own_ref), channel_id=1, source_target_pairs={{0,8},{4,12},{8,0},{12,4},{16,24},{20,28},{24,16},{28,20},{32,40},... | collective-permute-start | bytes 786440 | tf_op jit(solution)/shard_map/ppermute | solution.py:801
  25.3 41.6 %collective-permute-start.2 = (bf16[1024,128]{1,0:T(8,128)(2,1)}, bf16[1024,128]{1,0:T(8,128)(2,1)}, u32[]{:S(2)}, u32[]{:S(2)}) collective-permute-start(bf16[1024,128]{1,0:T(8,128)(2,1)} %get-tuple-element.926.own_ref), channel_id=1, source_target_pairs={{0,16},{4,20},{8,24},{12,28},{16,0},{20,4},{24,8},{28,12},{32,48},... | collective-permute-start | bytes 786440 | tf_op jit(solution)/shard_map/ppermute | solution.py:801
  28.0 40.8 %collective-permute-start.3 = (bf16[1024,128]{1,0:T(8,128)(2,1)}, bf16[1024,128]{1,0:T(8,128)(2,1)}, u32[]{:S(2)}, u32[]{:S(2)}) collective-permute-start(bf16[1024,128]{1,0:T(8,128)(2,1)} %get-tuple-element.926.own_ref), channel_id=1, source_target_pairs={{0,32},{4,36},{8,40},{12,44},{16,48},{20,52},{24,56},{28,60},{32,0... | collective-permute-start | bytes 786440 | tf_op jit(solution)/shard_map/ppermute | solution.py:801
  34.4 0.8 copy-start.19
  36.0 0.8 copy-start.25
  36.8 0.8 copy-start.28
  41.7 33.3 %all-to-all-start.3 = ((bf16[32,144,128]{2,1,0:T(8,128)(2,1)}), bf16[32,144,128]{2,1,0:T(8,128)(2,1)S(1)}, u32[]{:S(2)}, u32[]{:S(2)}) async-start(bf16[32,144,128]{2,1,0:T(8,128)(2,1)} %get-tuple-element.671), calls=%async_computation.3 | async-start | bytes 2359296 | tf_op jit(solution)/shard_map/all_to_all | solution.py:818
  46.0 1.0 copy-start.20
  47.1 21.8 %copy-start.14 = (s32[4,1024]{1,0:T(4,128)S(1)}, s32[4,1024]{1,0:T(4,128)}, u32[]{:S(2)}) copy-start(s32[4,1024]{1,0:T(4,128)} %exp_ref.5) | copy-start | bytes 49156
  47.1 21.8 %copy-start.31 = (bf16[1024,128]{1,0:T(8,128)(2,1)S(1)}, bf16[1024,128]{1,0:T(8,128)(2,1)}, u32[]{:S(2)}) copy-start(bf16[1024,128]{1,0:T(8,128)(2,1)} %copy-done.30) | copy-start | bytes 786436
  60.8 1.1 copy-start.38
  61.9 11.2 %copy-start.41 = (bf16[42,128,128]{2,1,0:T(8,128)(2,1)}, bf16[42,128,128]{2,1,0:T(8,128)(2,1)S(1)}, u32[]{:S(2)}) copy-start(bf16[42,128,128]{2,1,0:T(8,128)(2,1)S(1)} %get-tuple-element.696.kt_s) | copy-start | bytes 4128772
  61.9 33.1 %collective-permute-start.4 = (bf16[1024,128]{1,0:T(8,128)(2,1)}, bf16[1024,128]{1,0:T(8,128)(2,1)S(1)}, u32[]{:S(2)}, u32[]{:S(2)}) collective-permute-start(bf16[1024,128]{1,0:T(8,128)(2,1)} %get-tuple-element.686.own_ref), channel_id=1, source_target_pairs={{0,4},{4,0},{8,12},{12,8},{16,20},{20,16},{24,28},{28,24},{32,36},... | collective-permute-start | bytes 786440 | tf_op jit(solution)/shard_map/ppermute | solution.py:801
  63.6 31.4 %collective-permute-start.5 = (bf16[1024,128]{1,0:T(8,128)(2,1)}, bf16[1024,128]{1,0:T(8,128)(2,1)}, u32[]{:S(2)}, u32[]{:S(2)}) collective-permute-start(bf16[1024,128]{1,0:T(8,128)(2,1)} %get-tuple-element.686.own_ref), channel_id=1, source_target_pairs={{0,8},{4,12},{8,0},{12,4},{16,24},{20,28},{24,16},{28,20},{32,40},... | collective-permute-start | bytes 786440 | tf_op jit(solution)/shard_map/ppermute | solution.py:801
  64.3 31.5 %collective-permute-start.6 = (bf16[1024,128]{1,0:T(8,128)(2,1)}, bf16[1024,128]{1,0:T(8,128)(2,1)}, u32[]{:S(2)}, u32[]{:S(2)}) collective-permute-start(bf16[1024,128]{1,0:T(8,128)(2,1)} %get-tuple-element.686.own_ref), channel_id=1, source_target_pairs={{0,16},{4,20},{8,24},{12,28},{16,0},{20,4},{24,8},{28,12},{32,48},... | collective-permute-start | bytes 786440 | tf_op jit(solution)/shard_map/ppermute | solution.py:801
  66.9 30.2 %collective-permute-start.7 = (bf16[1024,128]{1,0:T(8,128)(2,1)}, bf16[1024,128]{1,0:T(8,128)(2,1)}, u32[]{:S(2)}, u32[]{:S(2)}) collective-permute-start(bf16[1024,128]{1,0:T(8,128)(2,1)} %get-tuple-element.686.own_ref), channel_id=1, source_target_pairs={{0,32},{4,36},{8,40},{12,44},{16,48},{20,52},{24,56},{28,60},{32,0... | collective-permute-start | bytes 786440 | tf_op jit(solution)/shard_map/ppermute | solution.py:801
  73.1 1.0 copy-start.32
  74.1 4.4 %copy-start.21 = (bf16[8,128,256]{2,1,0:T(8,128)(2,1)S(1)}, bf16[8,128,256]{2,1,0:T(8,128)(2,1)}, u32[]{:S(2)}) copy-start(bf16[8,128,256]{2,1,0:T(8,128)(2,1)} %copy-done.19) | copy-start | bytes 1572868
  74.1 68.0 %collective-permute-start.10 = (bf16[1056,256]{1,0:T(8,128)(2,1)S(1)}, bf16[1056,256]{1,0:T(8,128)(2,1)S(1)}, u32[]{:S(2)}, u32[]{:S(2)}) collective-permute-start(bf16[1056,256]{1,0:T(8,128)(2,1)S(1)} %get-tuple-element.705), channel_id=1, source_target_pairs={{0,16},{4,20},{8,24},{12,28},{16,0},{20,4},{24,8},{28,12},{32,48},... | collective-permute-start | bytes 1622024 | tf_op jit(solution)/shard_map/ppermute | solution.py:801
  75.0 3.5 %copy-start.26 = (bf16[8,128,256]{2,1,0:T(8,128)(2,1)S(1)}, bf16[8,128,256]{2,1,0:T(8,128)(2,1)}, u32[]{:S(2)}) copy-start(bf16[8,128,256]{2,1,0:T(8,128)(2,1)} %copy-done.25) | copy-start | bytes 1572868
  75.0 3.5 %copy-start.29 = (bf16[8,256,128]{2,1,0:T(8,128)(2,1)S(1)}, bf16[8,256,128]{2,1,0:T(8,128)(2,1)}, u32[]{:S(2)}) copy-start(bf16[8,256,128]{2,1,0:T(8,128)(2,1)} %copy-done.28) | copy-start | bytes 1572868
  75.0 3.5 %copy-start.39 = (bf16[42,128,128]{2,1,0:T(8,128)(2,1)S(1)}, bf16[42,128,128]{2,1,0:T(8,128)(2,1)}, u32[]{:S(2)}) copy-start(bf16[42,128,128]{2,1,0:T(8,128)(2,1)} %copy-done.38) | copy-start | bytes 4128772
  77.3 1.1 copy-start.17
  78.5 18.6 %copy-start.6 = (bf16[1024,128]{1,0:T(8,128)(2,1)S(1)}, bf16[1024,128]{1,0:T(8,128)(2,1)}, u32[]{:S(2)}) copy-start(bf16[1024,128]{1,0:T(8,128)(2,1)} %cot_ref.5) | copy-start | bytes 786436
  95.0 47.1 %collective-permute-start.11 = (bf16[1056,256]{1,0:T(8,128)(2,1)S(1)}, bf16[1056,256]{1,0:T(8,128)(2,1)S(1)}, u32[]{:S(2)}, u32[]{:S(2)}) collective-permute-start(bf16[1056,256]{1,0:T(8,128)(2,1)S(1)} %get-tuple-element.705), channel_id=1, source_target_pairs={{0,32},{4,36},{8,40},{12,44},{16,48},{20,52},{24,56},{28,60},{32,0... | collective-permute-start | bytes 1622024 | tf_op jit(solution)/shard_map/ppermute | solution.py:801
  95.0 47.1 %collective-permute-start.8 = (bf16[1056,256]{1,0:T(8,128)(2,1)S(1)}, bf16[1056,256]{1,0:T(8,128)(2,1)}, u32[]{:S(2)}, u32[]{:S(2)}) collective-permute-start(bf16[1056,256]{1,0:T(8,128)(2,1)S(1)} %get-tuple-element.705), channel_id=1, source_target_pairs={{0,4},{4,0},{8,12},{12,8},{16,20},{20,16},{24,28},{28,24},{32,36},... | collective-permute-start | bytes 1622024 | tf_op jit(solution)/shard_map/ppermute | solution.py:801
  95.8 46.3 %collective-permute-start.9 = (bf16[1056,256]{1,0:T(8,128)(2,1)S(1)}, bf16[1056,256]{1,0:T(8,128)(2,1)}, u32[]{:S(2)}, u32[]{:S(2)}) collective-permute-start(bf16[1056,256]{1,0:T(8,128)(2,1)S(1)} %get-tuple-element.705), channel_id=1, source_target_pairs={{0,8},{4,12},{8,0},{12,4},{16,24},{20,28},{24,16},{28,20},{32,40},... | collective-permute-start | bytes 1622024 | tf_op jit(solution)/shard_map/ppermute | solution.py:801
  103.1 39.0 %all-to-all-start.4 = ((bf16[32,176,128]{2,1,0:T(8,128)(2,1)}), bf16[32,176,128]{2,1,0:T(8,128)(2,1)S(1)}, u32[]{:S(2)}, u32[]{:S(2)}) async-start(bf16[32,176,128]{2,1,0:T(8,128)(2,1)} %get-tuple-element.704), calls=%async_computation.4 | async-start | bytes 2883584 | tf_op jit(solution)/shard_map/all_to_all | solution.py:832
  110.6 1.3 copy-start.18
  112.0 1.0 copy-start.22
  113.0 1.0 copy-start.24
  114.0 1.0 copy-start.27
  115.1 1.2 copy-start.33
  116.3 1.3 copy-start.40
  117.7 1.3 copy-start.42
  119.0 23.1 %copy-start.47 = (s32[128]{0:T(128)S(1)}, s32[128]{0:T(128)}, u32[]{:S(2)}) copy-start(s32[128]{0:T(128)} %copy-done.46) | copy-start | bytes 1540
  142.1 0.8 copy-start.2
  143.5 10.3 %copy-start.8 = (bf16[512,128]{1,0:T(8,128)(2,1)S(1)}, bf16[512,128]{1,0:T(8,128)(2,1)}, u32[]{:S(2)}) copy-start(bf16[512,128]{1,0:T(8,128)(2,1)} %wq_ref.3) | copy-start | bytes 393220
  143.5 10.3 %copy-start.10 = (bf16[512,128]{1,0:T(8,128)(2,1)S(1)}, bf16[512,128]{1,0:T(8,128)(2,1)}, u32[]{:S(2)}) copy-start(bf16[512,128]{1,0:T(8,128)(2,1)} %wv_ref.3) | copy-start | bytes 393220
  143.5 10.3 %copy-start.16 = (s32[1,32,128]{2,1,0:T(8,128)S(1)}, s32[1,32,128]{2,1,0:T(8,128)}, u32[]{:S(2)}) copy-start(s32[1,32,128]{2,1,0:T(8,128)} %param.19) | copy-start | bytes 49156
  143.5 28.4 %all-to-all-start.5 = ((bf16[32,144,128]{2,1,0:T(8,128)(2,1)}), bf16[32,144,128]{2,1,0:T(8,128)(2,1)S(1)}, u32[]{:S(2)}, u32[]{:S(2)}) async-start(bf16[32,144,128]{2,1,0:T(8,128)(2,1)} %get-tuple-element.721), calls=%async_computation.5 | async-start | bytes 2359296 | tf_op jit(solution)/shard_map/all_to_all | solution.py:839
  153.8 1.0 copy-start.3
  154.8 0.9 copy-start.44
  167.3 1.3 copy-start.34
  168.6 0.8 copy-start.36
  171.9 0.9 copy-start.12
  172.8 1.6 copy-start.35
  174.4 1.0 copy-start.37
  179.1 9.8 %collective-permute-start.12 = (bf16[1024,128]{1,0:T(8,128)(2,1)S(1)}, bf16[1024,128]{1,0:T(8,128)(2,1)S(1)}, u32[]{:S(2)}, u32[]{:S(2)}) collective-permute-start(bf16[1024,128]{1,0:T(8,128)(2,1)S(1)} %get-tuple-element.724), channel_id=1, source_target_pairs={{0,1},{1,2},{2,3},{3,0},{4,5},{5,6},{6,7},{7,4},{8,9},{9,10},{10,1... | collective-permute-start | bytes 786440 | tf_op jit(solution)/shard_map/ppermute | solution.py:845
  180.7 15.0 %collective-permute-start.13 = (bf16[1024,128]{1,0:T(8,128)(2,1)S(1)}, bf16[1024,128]{1,0:T(8,128)(2,1)S(1)}, u32[]{:S(2)}, u32[]{:S(2)}) collective-permute-start(bf16[1024,128]{1,0:T(8,128)(2,1)S(1)} %get-tuple-element.725), channel_id=1, source_target_pairs={{0,2},{1,3},{2,0},{3,1},{4,6},{5,7},{6,4},{7,5},{8,10},{9,11},{10,... | collective-permute-start | bytes 786440 | tf_op jit(solution)/shard_map/ppermute | solution.py:845
  183.6 12.1 %collective-permute-start.14 = (bf16[1024,128]{1,0:T(8,128)(2,1)S(1)}, bf16[1024,128]{1,0:T(8,128)(2,1)S(1)}, u32[]{:S(2)}, u32[]{:S(2)}) collective-permute-start(bf16[1024,128]{1,0:T(8,128)(2,1)S(1)} %get-tuple-element.726), channel_id=1, source_target_pairs={{0,3},{1,0},{2,1},{3,2},{4,7},{5,4},{6,5},{7,6},{8,11},{9,8},{10,9... | collective-permute-start | bytes 786440 | tf_op jit(solution)/shard_map/ppermute | solution.py:845
  (4 other events, 2.9 us)

commit v7 on v6

--- a/solution.py
+++ b/solution.py
@@ -1,3 +1,4 @@
+import functools
 import math
 
 import jax
@@ -29,8 +30,8 @@
 BF16 = jnp.bfloat16
 
 
-def params():
-    return pltpu.CompilerParams(vmem_limit_bytes=20 * 1024 * 1024)
+def params(mib):
+    return pltpu.CompilerParams(vmem_limit_bytes=mib * 1024 * 1024)
 
 
 def vmem():
@@ -179,24 +180,21 @@
 
 
 def finish_kernel(
-    me_ref, exp_ref, t0_ref, t1_ref, t2_ref, t3_ref, cot_ref, out_t_ref, sp_ref, lse_ref, local_ref, _, att_ref, back_ref,
+    me_ref, exp_ref, t0_ref, t1_ref, t2_ref, t3_ref, cot_ref, sp_ref, lse_ref, local_ref, _, pair_ref, back_ref,
     delta_ref, message_ref, sems,
 ):
     picks = sum_picks()
     lse = lse_ref[...]
     delta = local_ref[...]
-    totals = [head_rows(out_t_ref[i]).T for i in range(Q_BLOCKS)]
     probs, dprobs = [], []
     for m, table in enumerate((t0_ref, t1_ref, t2_ref, t3_ref)):
         blocks = gather_partner(exp_ref, m, table)
         prob = jnp.exp(sp_ref[m] - lse)
         dprob = head_sums(cot_ref, blocks, picks)
         delta += prob * dprob
-        weight = tall(prob).astype(BF16)
-        back_ref[m, 16:] = weight
-        turned = turned_weights(weight)
+        back_ref[m, 16:] = tall(prob).astype(BF16)
         for i, block in enumerate(blocks):
-            totals[i] += dot(turned, head_picks(i)) * block.astype(F32)
+            pair_ref[m * Q_BLOCKS + i] = block
         probs.append(prob)
         dprobs.append(dprob)
     delta_ref[...] = delta
@@ -210,10 +208,21 @@
     ]
     for copy in copies:
         copy.start()
-    for i in range(Q_BLOCKS):
-        att_ref[i * BLOCK : (i + 1) * BLOCK, :] = totals[i].astype(BF16)
     for copy in copies:
         copy.wait()
+
+
+def join_partners(out_ref, out_t_ref, part_rows, pair_ref, scale):
+    turned = [turned_weights(rows) for rows in part_rows]
+    for i in range(Q_BLOCKS):
+        total = head_rows(out_t_ref[i]).T
+        for m in range(EXPANDERS):
+            total += dot(turned[m], head_picks(i)) * pair_ref[m * Q_BLOCKS + i].astype(F32)
+        out_ref[i * BLOCK : (i + 1) * BLOCK, :] = (total * scale).astype(BF16)
+
+
+def attend_kernel(out_t_ref, back_ref, pair_ref, att_ref):
+    join_partners(att_ref, out_t_ref, [back_ref[m, 16:] for m in range(EXPANDERS)], pair_ref, 1.0)
 
 
 def flat(x):
@@ -241,7 +250,7 @@
     lax.fori_loop(0, Q_BLOCKS, one, 0, unroll=2)
 
 
-def plan_kernel(mask_ref, count_ref, list_ref, groups_ref, live_ref):
+def plan_kernel(mask_ref, count_ref, list_ref, groups_ref, tail_ref, live_ref):
     for j in range(Q_BLOCKS):
         live_ref[j] = BLOCK
     live_ref[GLOBAL_BLOCK] = BLOCK
@@ -264,7 +273,8 @@
         n = lax.fori_loop(0, GLOBAL_BLOCK, put, 1)
         for extra in range(GROUP):
             list_ref[i * LIST + n + extra] = EMPTY_BLOCK
-        groups_ref[i] = (n + GROUP - 1) // GROUP
+        groups_ref[i] = (n + PAIR - 1) // GROUP
+        tail_ref[i] = jnp.logical_and(n % GROUP > 0, n % GROUP <= PAIR).astype(jnp.int32)
         return carry
 
     lax.fori_loop(0, Q_BLOCKS, per_block, 0)
@@ -330,8 +340,8 @@
     )
 
 
-def block_ids(list_ref, i, g):
-    return [list_ref[i * LIST + g * GROUP + u] for u in range(GROUP)]
+def block_ids(list_ref, i, g, size):
+    return [list_ref[i * LIST + g * GROUP + u] for u in range(size)]
 
 
 def q_rows(i):
@@ -339,27 +349,29 @@
 
 
 def score_kernel(
-    list_ref, groups_ref, live_ref, qt_ref, own_ref, hk_ref, gid_ref, glob_ref, lse_ref, k_s, kt_ref
+    list_ref, groups_ref, tail_ref, live_ref, qt_ref, own_ref, hk_ref, gid_ref, glob_ref, lse_ref, k_s, kt_ref
 ):
     fill(k_s, kt_ref, 0, own_ref, hk_ref, gid_ref, glob_ref)
 
     def per_block(i, carry):
         turned_q = qt_ref[i]
 
-        def step(g, state):
-            blocks = block_ids(list_ref, i, g)
+        def step(size, g, state):
+            blocks = block_ids(list_ref, i, g, size)
             new_state = []
-            for u in range(GROUP // PAIR):
+            for u in range(size // PAIR):
                 top, total = state[u]
                 scores = masked_scores(blocks[u * PAIR : (u + 1) * PAIR], k_s, turned_q, live_ref)
                 scores = scores.reshape(PAIR * BLOCK // 8, 8, 2 * BLOCK)
                 new_top = jnp.maximum(top, jnp.max(scores, axis=0))
                 total = total * jnp.exp(top - new_top) + jnp.sum(jnp.exp(scores - new_top[None]), axis=0)
                 new_state.append((new_top, total))
-            return tuple(new_state)
+            return tuple(new_state) + tuple(state[size // PAIR :])
 
         init = (jnp.full((8, 2 * BLOCK), NEG, F32), jnp.zeros((8, 2 * BLOCK), F32))
-        state = lax.fori_loop(0, groups_ref[i], step, tuple(init for _ in range(GROUP // PAIR)))
+        state = tuple(init for _ in range(GROUP // PAIR))
+        state = lax.fori_loop(0, groups_ref[i], functools.partial(step, GROUP), state)
+        state = lax.fori_loop(groups_ref[i], groups_ref[i] + tail_ref[i], functools.partial(step, PAIR), state)
         top = jnp.concatenate([t for t, _ in state], axis=0)
         total = jnp.concatenate([t for _, t in state], axis=0)
         best = jnp.max(top, axis=0, keepdims=True)
@@ -371,7 +383,7 @@
 
 
 def value_kernel(
-    list_ref, groups_ref, live_ref, k_s, vt_s, qt_ref, ct_ref, cs_ref, part_ref, sp_ref, gid_ref,
+    list_ref, groups_ref, tail_ref, live_ref, k_s, vt_s, qt_ref, ct_ref, cs_ref, part_ref, sp_ref, gid_ref,
     own_ref, halo_ref, gout_ref, out_s, delta_ref, lse_ref, acc_s,
 ):
     clear_blocks(acc_s)
@@ -390,10 +402,10 @@
         lse = lse_ref[pl.ds(i, 1), :]
         out_s[i] = jnp.zeros((COLS, 2 * BLOCK), F32)
 
-        def step(g, carry):
-            blocks = block_ids(list_ref, i, g)
+        def step(size, g, carry):
+            blocks = block_ids(list_ref, i, g, size)
             total = None
-            for u in range(0, GROUP, PAIR):
+            for u in range(0, size, PAIR):
                 pair = blocks[u : u + PAIR]
                 scores = masked_scores(pair, k_s, turned_q, live_ref)
                 weight = jnp.exp(scores - lse).astype(BF16)
@@ -405,7 +417,8 @@
             out_s[i] += total
             return carry
 
-        lax.fori_loop(0, groups_ref[i], step, 0)
+        lax.fori_loop(0, groups_ref[i], functools.partial(step, GROUP), 0)
+        lax.fori_loop(groups_ref[i], groups_ref[i] + tail_ref[i], functools.partial(step, PAIR), 0)
         delta_ref[pl.ds(i, 1), :] = jnp.sum(out_s[i] * ct_ref[i].astype(F32), axis=0, keepdims=True)
         return carry
 
@@ -442,8 +455,8 @@
 
 
 def key_kernel(
-    list_ref, groups_ref, live_ref, k_s, kt_s, v_s, qt_ref, qs_ref, ct_ref, lse_ref, delta_ref, back_ref, pair_ref, gid_ref,
-    gq_ref, own_ref, halo_ref, gout_ref, acc_s, out_s,
+    list_ref, groups_ref, tail_ref, live_ref, k_s, kt_s, v_s, qt_ref, qs_ref, ct_ref, lse_ref, delta_ref, gid_ref,
+    out_s, own_ref, halo_ref, gout_ref, acc_s,
 ):
     clear_blocks(acc_s)
 
@@ -455,10 +468,10 @@
         delta = delta_ref[pl.ds(i, 1), :]
         out_s[i] = jnp.zeros((COLS, 2 * BLOCK), F32)
 
-        def step(g, carry):
-            blocks = block_ids(list_ref, i, g)
+        def step(size, g, carry):
+            blocks = block_ids(list_ref, i, g, size)
             total = None
-            for u in range(0, GROUP, PAIR):
+            for u in range(0, size, PAIR):
                 pair = blocks[u : u + PAIR]
                 scores = masked_scores(pair, k_s, turned_q, live_ref)
                 dprob = dot(jnp.concatenate([v_s[b] for b in pair], axis=0), turned_cot)
@@ -471,16 +484,11 @@
             out_s[i] += total
             return carry
 
-        lax.fori_loop(0, groups_ref[i], step, 0)
+        lax.fori_loop(0, groups_ref[i], functools.partial(step, GROUP), 0)
+        lax.fori_loop(groups_ref[i], groups_ref[i] + tail_ref[i], functools.partial(step, PAIR), 0)
         return carry
 
     lax.fori_loop(0, Q_BLOCKS, per_block, 0)
-    turned = [turned_weights(back_ref[m, :16]) for m in range(EXPANDERS)]
-    for i in range(Q_BLOCKS):
-        grad_query = head_rows(out_s[i]).T
-        for m in range(EXPANDERS):
-            grad_query += dot(turned[m], head_picks(i)) * pair_ref[m * Q_BLOCKS + i].astype(F32)
-        gq_ref[i * BLOCK : (i + 1) * BLOCK, :] = (grad_query * (1.0 / math.sqrt(HEAD))).astype(BF16)
     store_parts(acc_s, own_ref, halo_ref, gid_ref, gout_ref)
 
 
@@ -534,10 +542,13 @@
 
 def value_back_kernel(
     me_ref, feat_ref, ownv_ref, ret_ref, ownk_ref, rows_ref, o0_ref, o1_ref, o2_ref, o3_ref, gid_ref, wq_ref, wv_ref,
-    gq_ref, accv_s, acck_ref, pre_ref,
+    out_t_ref, back_ref, pair_ref, acck_ref, pre_ref, accv_s, gq_ref,
 ):
     others = (o0_ref, o1_ref, o2_ref, o3_ref)
     parts = [ret_ref[me_ref[0] ^ (1 << m), SLOTS:] for m in range(EXPANDERS)]
+    join_partners(
+        gq_ref, out_t_ref, [back_ref[m, :16] for m in range(EXPANDERS)], pair_ref, 1.0 / math.sqrt(HEAD)
+    )
     accv_s[...] = ownv_ref[...]
     add_halo(accv_s, me_ref, ret_ref, rows_ref, gid_ref)
     add_partners(accv_s, [part[16:] for part in parts], others, COLS)
@@ -550,20 +561,27 @@
 
 
 def key_back_kernel(
-    me_ref, feat_ref, acck_ref, ret_ref, rows_ref, gid_ref, wk_ref, pre_ref, t0_ref, t1_ref, t2_ref, t3_ref, acc_s
+    me_ref, feat_ref, acck_ref, ret_ref, rows_ref, gid_ref, wk_ref, pre_ref, t0_ref, t1_ref, t2_ref, t3_ref,
+    acc_s, own_s, pre_s, sems,
 ):
-    acc_s[...] = acck_ref[...]
+    own_copy = pltpu.make_async_copy(acck_ref, own_s, sems.at[0])
+    pre_copy = pltpu.make_async_copy(pre_ref, pre_s, sems.at[1])
+    own_copy.start()
+    pre_copy.start()
+    acc_s[...] = jnp.zeros((NODES_HERE, COLS), F32)
     add_halo(acc_s, me_ref, ret_ref, rows_ref, gid_ref)
-    grad_key = acc_s[...].astype(BF16)
+    own_copy.wait()
+    grad_key = (acc_s[...] + own_s[...]).astype(BF16)
+    pre_copy.wait()
     for k, out in ((1, t1_ref), (2, t2_ref), (3, t3_ref), (0, t0_ref)):
-        out[...] = (pre_ref[k] + dot_nt(grad_key, wk_ref[feature_part(feat_ref, k), :])).astype(out.dtype)
+        out[...] = (pre_s[k] + dot_nt(grad_key, wk_ref[feature_part(feat_ref, k), :])).astype(out.dtype)
 
 
 def shape(dims, kind=BF16):
     return jax.ShapeDtypeStruct(dims, kind)
 
 
-def call(kernel, ins, outs, args, scratch=(), name=None, flops=0, out_spaces=None, aliases={}):
+def call(kernel, ins, outs, args, scratch=(), name=None, flops=0, out_spaces=None, aliases={}, mib=56):
     cost = pl.CostEstimate(flops=flops, transcendentals=0, bytes_accessed=4_000_000)
     return pl.pallas_call(
         kernel,
@@ -571,7 +589,7 @@
         in_specs=ins,
         out_specs=out_spaces or tuple(vmem() for _ in outs),
         scratch_shapes=list(scratch),
-        compiler_params=params(),
+        compiler_params=params(mib),
         cost_estimate=cost,
         input_output_aliases=aliases,
         name=name,
@@ -597,6 +615,7 @@
         ),
         (me, features, w_query, w_key, w_value, cotangent, rows, exp_list, gids),
         name="project",
+        mib=56,
         flops=3_000_000_000,
         out_spaces=(*(vmem() for _ in range(6)), smem()),
         scratch=[pltpu.VMEM((NODES_HERE, 2 * COLS), BF16)],
@@ -607,10 +626,15 @@
     return call(
         plan_kernel,
         [smem()] * 2,
-        (shape((Q_BLOCKS * LIST,), jnp.int32), shape((Q_BLOCKS,), jnp.int32), shape((LIST,), jnp.int32)),
+        (
+            shape((Q_BLOCKS * LIST,), jnp.int32),
+            shape((Q_BLOCKS,), jnp.int32),
+            shape((Q_BLOCKS,), jnp.int32),
+            shape((LIST,), jnp.int32),
+        ),
         (block_mask.reshape(-1), halo_count.reshape(-1)),
         name="plan",
-        out_spaces=(smem(), smem(), smem()),
+        out_spaces=(smem(), smem(), smem(), smem()),
     )
 
 
@@ -625,24 +649,35 @@
     )
 
 
-def run_finish(me, exp_rows, swaps, cotangent, out_t, scores, lse, local, back_v):
+def run_finish(me, exp_rows, swaps, cotangent, scores, lse, local, back_v):
     anywhere = pl.BlockSpec(memory_space=pl.ANY)
     return call(
         finish_kernel,
-        [smem()] + [vmem()] * 10 + [anywhere],
+        [smem()] + [vmem()] * 9 + [anywhere],
         (
-            shape((NODES_HERE, COLS)),
+            shape((EXPANDERS * Q_BLOCKS, BLOCK, COLS)),
             shape((EXPANDERS, PART_ROWS, BLOCK)),
             shape((Q_BLOCKS, 2 * BLOCK), F32),
             shape((SENDERS, BACK, COLS)),
         ),
-        (me, exp_rows, *swaps, cotangent, out_t, scores, lse, local, back_v),
+        (me, exp_rows, *swaps, cotangent, scores, lse, local, back_v),
         name="finish",
         flops=5_000_000_000,
         out_spaces=(vmem(), vmem(), vmem(), anywhere),
         scratch=[pltpu.SemaphoreType.DMA((EXPANDERS,))],
-        aliases={11: 3},
-    )
+        aliases={10: 3},
+    )
+
+
+def run_attend(out_t, back, value_pairs):
+    return call(
+        attend_kernel,
+        [vmem()] * 3,
+        (shape((NODES_HERE, COLS)),),
+        (out_t, back, value_pairs),
+        name="attend",
+        flops=2_000_000_000,
+    )[0]
 
 
 def run_prepare(query, cotangent):
@@ -655,7 +690,7 @@
 def run_scores(plan, turned_q, own, halo_k, gids, glob):
     return call(
         score_kernel,
-        [smem()] * 3 + [vmem()] * 5,
+        [smem()] * 4 + [vmem()] * 5,
         (
             shape((Q_BLOCKS, 2 * BLOCK), F32),
             shape((KEY_BLOCKS, BLOCK, COLS)),
@@ -682,7 +717,7 @@
     turned_q, _, turned_cot, cot_stack = prepared
     return call(
         value_kernel,
-        [smem()] * 3 + [vmem()] * 8,
+        [smem()] * 4 + [vmem()] * 8,
         (
             shape((NODES_HERE, COLS), F32),
             shape((SENDERS, BACK, COLS)),
@@ -698,43 +733,53 @@
     )
 
 
-def run_keys(plan, keys, turned_k, values, prepared, lse, delta, back, pairs, gids):
+def run_keys(plan, keys, turned_k, values, prepared, lse, delta, gids):
     turned_q, q_stack, turned_cot, _ = prepared
     return call(
         key_kernel,
-        [smem()] * 3 + [vmem()] * 11,
+        [smem()] * 4 + [vmem()] * 9,
         (
-            shape((NODES_HERE, COLS)),
+            shape((Q_BLOCKS, COLS, 2 * BLOCK), F32),
             shape((NODES_HERE, COLS), F32),
             shape((SENDERS, SLOTS, COLS)),
             shape((BLOCK, COLS)),
         ),
-        (*plan, keys, turned_k, values, turned_q, q_stack, turned_cot, lse, delta, back, pairs, gids),
-        scratch=[blocks_of(F32), pltpu.VMEM((Q_BLOCKS, COLS, 2 * BLOCK), F32)],
+        (*plan, keys, turned_k, values, turned_q, q_stack, turned_cot, lse, delta, gids),
+        scratch=[blocks_of(F32)],
         name="keys",
+        mib=56,
         flops=25_000_000_000,
     )
 
 
-def run_value_back(me, feat, own_v, returned_v, own_k, rows, others, gids, w_query, w_value, grad_query):
+def run_value_back(me, feat, own_v, returned_v, own_k, rows, others, gids, w_query, w_value, out_t, back, pairs):
     return call(
         value_back_kernel,
-        [smem()] * 2 + [vmem()] * 12,
-        (shape((NODES_HERE, COLS), F32), shape((NODES_HERE, COLS), F32), shape((4, NODES_HERE, COLS), F32)),
-        (me, feat, own_v, returned_v, own_k, rows, *others, gids, w_query, w_value, grad_query),
+        [smem()] * 2 + [vmem()] * 14,
+        (shape((NODES_HERE, COLS), F32), shape((4, NODES_HERE, COLS), F32)),
+        (me, feat, own_v, returned_v, own_k, rows, *others, gids, w_query, w_value, out_t, back, pairs),
+        scratch=[pltpu.VMEM((NODES_HERE, COLS), F32), pltpu.VMEM((NODES_HERE, COLS), BF16)],
         name="value_back",
+        mib=56,
         flops=12_000_000_000,
-    )[1:]
+    )
 
 
 def run_key_back(me, feat, own_k, returned_k, rows, gids, w_key, pre):
+    anywhere = pl.BlockSpec(memory_space=pl.ANY)
     return call(
         key_back_kernel,
-        [smem()] * 2 + [vmem()] * 6,
+        [smem()] * 2 + [anywhere] + [vmem()] * 4 + [anywhere],
         (shape((NODES_HERE, COLS), F32),) + tuple(shape((NODES_HERE, COLS)) for _ in range(3)),
         (me, feat, own_k, returned_k, rows, gids, w_key, pre),
-        scratch=[pltpu.VMEM((NODES_HERE, COLS), F32)],
+        scratch=[
+            pltpu.VMEM((NODES_HERE, COLS), F32),
+            pltpu.VMEM((NODES_HERE, COLS), F32),
+            pltpu.VMEM((4, NODES_HERE, COLS), F32),
+            pltpu.SemaphoreType.DMA((2,)),
+        ],
         name="key_back",
+        mib=56,
         flops=8_000_000_000,
     )
 
@@ -825,24 +870,24 @@
     away, scores = lax.optimization_barrier((away, scores))
     others = [swapped(away, m) for m in range(EXPANDERS)]
     own_v, back_v, glob_v, out_t, local, lse = run_values(plan, keys, turned_v, prepared, part, scores, gids)
-    out_t, *value_swaps = lax.optimization_barrier((out_t, *value_swaps))
-    attended, back, delta, back_v = run_finish(
-        me, exp_rows, value_swaps, cotangent, out_t, scores, lse, local, back_v
+    local, *value_swaps = lax.optimization_barrier((local, *value_swaps))
+    value_pairs, back, delta, back_v = run_finish(
+        me, exp_rows, value_swaps, cotangent, scores, lse, local, back_v
     )
     returned_v = lax.all_to_all(back_v, "dom", 0, 0, tiled=True)
-    grad_query, own_k, back_k, glob_k = run_keys(
-        plan, keys, turned_k, values, prepared, lse, delta, back, pairs, gids
-    )
+    query_t, own_k, back_k, glob_k = run_keys(plan, keys, turned_k, values, prepared, lse, delta, gids)
     own_k, returned_v, *others = lax.optimization_barrier((own_k, returned_v, *others))
     own_k, own_v = more_grads(rounds, global_ids, my_index, glob_k, glob_v, own_k, own_v)
     back_k, own_k, own_v = lax.optimization_barrier((back_k, own_k, own_v))
     returned_k = lax.all_to_all(back_k, "dom", 0, 0, tiled=True)
     own_k, pre = run_value_back(
-        me, feat, own_v, returned_v, own_k, rows, others, gids, w_query, w_value, grad_query
+        me, feat, own_v, returned_v, own_k, rows, others, gids, w_query, w_value, query_t, back, pairs
     )
     mine, *away = run_key_back(me, feat, own_k, returned_k, rows, gids, w_key, pre)
-    for k, term in enumerate(away, 1):
-        mine = mine + lax.ppermute(term, "feat", [(i, (i + k) % 4) for i in range(4)]).astype(F32)
+    out_t, mine = lax.optimization_barrier((out_t, mine))
+    attended = run_attend(out_t, back, value_pairs)
+    for k in (2, 1, 3):
+        mine = mine + lax.ppermute(away[k - 1], "feat", [(i, (i + k) % 4) for i in range(4)]).astype(F32)
     return (attended, mine.astype(BF16))
 
 

time: 197 us -> 187 us (0.949)
  local copies, waits for them, and re-layouts: 31.3 us -> 4.15 us
  Pallas kernels: 91.5 us -> 111 us
  waiting for transfers between devices: 17.4 us -> 15.2 us
    unnamed x98 -> x28, local copies, waits for them, and re-layouts: 31.3 us -> 3.48 us
    pallas_call x11 -> x12, Pallas kernels: 91.5 us -> 111 us  [call(): pl.pallas_call(kernel, out_shape=outs, in_specs=ins, out_specs=out_spaces...]
    ppermute x3, waiting for transfers between devices: 10.7 us -> 6.93 us  [on_device(): lax.ppermute(away[k - 1], 'feat', [(i, (i + k) % 4) for i in range(4)])]
  transfers between devices with their start and end apart: 19 -> 19, of which waited for: 4 -> 5; matrix products, arithmetic and copies ran while one was open for 0% -> 1% of each run, Pallas kernels for 41% -> 52%
where the time goes in v7:
time: 187 us; the launch traced here: 186 us
  Pallas kernels  111 us (59%)
  starting transfers between devices  51.4 us (27%)
  waiting for transfers between devices  15.2 us (8%)
  local copies, waits for them, and re-layouts  4.15 us (2%)
  other arithmetic  2.43 us (1%)
    pallas_call x12, Pallas kernels, call(): pl.pallas_call(kernel, out_shape=outs, in_specs=ins, out_specs=out_spaces...  111 us
    ppermute x12, starting transfers between devices, swapped(): lax.ppermute(value, 'dom', [(i, i ^ 1 << bit) for i in range(dom_count)])  14.3 us
    all_to_all x1, starting transfers between devices, on_device(): returned_k = lax.all_to_all(back_k, 'dom', 0, 0, tiled=True)  9.23 us
    all_to_all x1, starting transfers between devices, on_device(): returned_v = lax.all_to_all(back_v, 'dom', 0, 0, tiled=True)  8.7 us
    all_to_all x1, starting transfers between devices, on_device(): halo_k = lax.all_to_all(out_k, 'dom', 0, 0, tiled=True)  8.27 us
    ppermute x3, waiting for transfers between devices, on_device(): lax.ppermute(away[k - 1], 'feat', [(i, (i + k) % 4) for i in range(4)])  6.93 us
    ppermute x3, starting transfers between devices, on_device(): lax.ppermute(away[k - 1], 'feat', [(i, (i + k) % 4) for i in range(4)])  6.51 us
    all_to_all x1, waiting for transfers between devices, on_device(): halo_k = lax.all_to_all(out_k, 'dom', 0, 0, tiled=True)  4.33 us
  transfers between devices with their start and end apart: 19, of which 5 were waited for; matrix products, arithmetic and copies ran while one was open for 1% of the time, Pallas kernels for 52%

profile of v7, /device:TPU:0, one launch (start us, length us, event | category | flops | bytes accessed | tf_op | source)
XLA Modules:
  0.0 185.9 jit_solution(516977792014666825)
XLA Ops:
  0.6 0.7 negate_bitcast_fusion
  1.3 0.2 convert_reduce_fusion.1
  1.5 0.0 copy-start.5
  1.5 7.1 %project.1 = (bf16[1024,128]{1,0:T(8,128)(2,1)}, bf16[1024,128]{1,0:T(8,128)(2,1)S(1)}, bf16[1024,128]{1,0:T(8,128)(2,1)S(1)}, bf16[32,144,128]{2,1,0:T(8,128)(2...) custom-call(s32[1]{0:T(128)} %bitcast.15.me_ref, bf16[1024,512]{1,0:T(8,128)(2,1)} %x_ref.1, ...), custom_call_target="tpu_custom_call" | custom-call | flops 3000000000 | bytes 4000000 | tf_op jit(solution)/shard_map/project/pallas_call | solution.py:586
  8.7 0.6 while.34
  9.3 0.0 copy-start.7
  9.3 8.3 %all-to-all-start.2 = ((bf16[32,144,128]{2,1,0:T(8,128)(2,1)}), bf16[32,144,128]{2,1,0:T(8,128)(2,1)S(1)}, u32[]{:S(2)}, u32[]{:S(2)}) async-start(bf16[32,144,128]{2,1,0:T(8,128)(2,1)} %get-tuple-element.672), calls=%async_computation.2 | async-start | bytes 2359296 | tf_op jit(solution)/shard_map/all_to_all | solution.py:859
  17.6 0.4 collective-permute-start
  17.9 1.7 collective-permute-start.1
  19.6 2.7 %collective-permute-start.2 = (bf16[1024,128]{1,0:T(8,128)(2,1)S(1)}, bf16[1024,128]{1,0:T(8,128)(2,1)}, u32[]{:S(2)}, u32[]{:S(2)}) collective-permute-start(bf16[1024,128]{1,0:T(8,128)(2,1)S(1)} %get-tuple-element.1012), channel_id=1, source_target_pairs={{0,16},{4,20},{8,24},{12,28},{16,0},{20,4},{24,8},{28,12},{32,48},... | collective-permute-start | bytes 786440 | tf_op jit(solution)/shard_map/ppermute | solution.py:846
  22.3 1.5 collective-permute-start.3
  23.8 0.7 reshape.638.mask_ref
  24.4 4.5 %plan.1 = (s32[448]{0:T(512)}, s32[8]{0:T(128)}, s32[8]{0:T(128)}, s32[56]{0:T(128)}) custom-call(s32[320]{0:T(512)} %reshape.638.mask_ref, s32[32]{0:T(128)} %bitcast.117), custom_call_target="tpu_custom_call" | custom-call | bytes 4000000 | tf_op jit(solution)/shard_map/plan/pallas_call | solution.py:586
  28.9 2.7 %prepare.1 = (bf16[8,128,256]{2,1,0:T(8,128)(2,1)}, bf16[8,256,128]{2,1,0:T(8,128)(2,1)}, bf16[8,128,256]{2,1,0:T(8,128)(2,1)}, bf16[8,256,128]{2,1,0:T(8,128)(2,1)}) custom-call(bf16[1024,128]{1,0:T(8,128)(2,1)} %get-tuple-element.664.q_ref, bf16[1024,128]{1,0:T(8,128)(2,1)} %cot_ref.5), custom_call_target="tpu_custom_call" | custom-call | flops 2000000000 | bytes 4000000 | tf_op jit(solution)/shard_map/prepare/pallas_call | solution.py:586
  31.7 4.3 %all-to-all-done.2.hk_ref = bf16[32,144,128]{2,1,0:T(8,128)(2,1)S(1)} async-done(((bf16[32,144,128]{2,1,0:T(8,128)(2,1)}), bf16[32,144,128]{2,1,0:T(8,128)(2,1)S(1)}, u32[]{:S(2)}, u32[]{:S(2)}) %all-to-all-start.2) | async-done | bytes 1179680 | tf_op jit(solution)/shard_map/all_to_all | solution.py:859
  36.0 4.3 %all-to-all-start.3 = ((bf16[32,144,128]{2,1,0:T(8,128)(2,1)}), bf16[32,144,128]{2,1,0:T(8,128)(2,1)S(1)}, u32[]{:S(2)}, u32[]{:S(2)}) async-start(bf16[32,144,128]{2,1,0:T(8,128)(2,1)} %get-tuple-element.675), calls=%async_computation.3 | async-start | bytes 2359296 | tf_op jit(solution)/shard_map/all_to_all | solution.py:863
  40.3 15.3 %scores.1 = (f32[8,256]{1,0:T(8,128)}, bf16[42,128,128]{2,1,0:T(8,128)(2,1)}, bf16[42,128,128]{2,1,0:T(8,128)(2,1)}) custom-call(s32[448]{0:T(512)} %get-tuple-element.660.list_ref, s32[8]{0:T(128)} %get-tuple-element.661.groups_ref, s32[8]{0:T(128)} %get-tuple-element.662.tail_ref, s32[56]{0:T(128)} %get-tuple-element.663.live_ref, ...), custom_call_target="tpu_custom_call" | custom-call | flops 12000000000 | bytes 4000000 | tf_op jit(solution)/shard_map/scores/pallas_call | solution.py:586
  55.7 0.4 collective-permute-start.4
  56.1 0.0 collective-permute-done.t0_ref
  56.1 1.8 collective-permute-start.5
  58.0 0.0 collective-permute-done.1.t1_ref
  58.0 3.0 %collective-permute-start.6 = (bf16[1024,128]{1,0:T(8,128)(2,1)S(1)}, bf16[1024,128]{1,0:T(8,128)(2,1)}, u32[]{:S(2)}, u32[]{:S(2)}) collective-permute-start(bf16[1024,128]{1,0:T(8,128)(2,1)S(1)} %get-tuple-element.1007), channel_id=1, source_target_pairs={{0,16},{4,20},{8,24},{12,28},{16,0},{20,4},{24,8},{28,12},{32,48},... | collective-permute-start | bytes 786440 | tf_op jit(solution)/shard_map/ppermute | solution.py:846
  60.9 0.0 collective-permute-done.2.t2_ref
  61.0 0.8 collective-permute-start.7
  61.7 0.0 collective-permute-done.3.t3_ref
  61.8 5.4 %partners.1 = (bf16[32,128,128]{2,1,0:T(8,128)(2,1)}, f32[4,8,256]{2,1,0:T(8,128)}) custom-call(s32[4,1024]{1,0:T(4,128)} %exp_ref.5, bf16[1024,128]{1,0:T(8,128)(2,1)} %copy-done.14, bf16[1024,128]{1,0:T(8,128)(2,1)} %copy-done.15, bf16[1024,128]{1,0:T(8,128)(2,1)} %collective-permute-done.2.t2_ref, bf16[1024,128]{1,0:T(8,128)(2,1)} %collective-permute-done.3.t3_ref, ...), custom_call_target="tpu_custom_call" | custom-call | flops 5000000000 | bytes 4000000 | tf_op jit(solution)/shard_map/partners/pallas_call | solution.py:586
  67.2 1.7 collective-permute-start.10
  68.9 0.0 all-to-all-done.3.hv_ref
  68.9 1.0 copy-done.1
  69.9 4.0 %turn.1 = (bf16[42,128,128]{2,1,0:T(8,128)(2,1)}, bf16[42,128,128]{2,1,0:T(8,128)(2,1)}) custom-call(bf16[1024,128]{1,0:T(8,128)(2,1)S(1)} %get-tuple-element.1007, bf16[32,144,128]{2,1,0:T(8,128)(2,1)} %copy-done.1, s32[1,128]{1,0:T(1,128)S(1)} %bitcast.112, bf16[128,256]{1,0:T(8,128)(2,1)S(1)} %get-tuple-element.673.glob_ref), custom_call_target="tpu_custom_call" | custom-call | flops 2000000000 | bytes 4000000 | tf_op jit(solution)/shard_map/turn/pallas_call | solution.py:586
  73.9 18.6 %values.1 = (f32[1024,128]{1,0:T(8,128)}, bf16[32,176,128]{2,1,0:T(8,128)(2,1)}, bf16[128,128]{1,0:T(8,128)(2,1)}, f32[8,128,256]{2,1,0:T(8,128)}, f32[8,256]{1,0:T(8,128)}, /*index=5*/f32[8,256]{1,0:T(8,128)}) custom-call(s32[448]{0:T(512)} %get-tuple-element.660.list_ref, s32[8]{0:T(128)} %get-tuple-element.661.groups_ref, s32[8]{0:T(128)} %get-tuple-element.662.tail_ref, ...), custom_call_target="tpu_custom_call" | custom-call | flops 20000000000 | bytes 4000000 | tf_op jit(solution)/shard_map/values/pallas_call | solution.py:586
  92.5 0.0 collective-permute-done.4.t0_ref
  92.5 0.3 collective-permute-start.11
  92.8 0.0 collective-permute-done.5.t1_ref
  92.8 0.0 collective-permute-start.8
  92.8 0.0 collective-permute-done.6.t2_ref
  92.8 0.1 collective-permute-start.9
  92.9 0.0 collective-permute-done.7.t3_ref
  92.9 6.2 %finish.1 = (bf16[32,128,128]{2,1,0:T(8,128)(2,1)}, bf16[4,32,128]{2,1,0:T(8,128)(2,1)}, f32[8,256]{1,0:T(8,128)}, bf16[32,176,128]{2,1,0:T(8,128)(2,1)}) custom-call(s32[1]{0:T(128)} %bitcast.15.me_ref, s32[4,1024]{1,0:T(4,128)} %exp_ref.5, bf16[1024,128]{1,0:T(8,128)(2,1)} %collective-permute-done.4.t0_ref, ...), custom_call_target="tpu_custom_call", output_to_operand_aliasing={{3}: (10, {})} | custom-call | flops 5000000000 | bytes 4000000 | tf_op jit(solution)/shard_map/finish/pallas_call | solution.py:586
  99.1 8.7 %all-to-all-start.4 = ((bf16[32,176,128]{2,1,0:T(8,128)(2,1)}), bf16[32,176,128]{2,1,0:T(8,128)(2,1)S(1)}, u32[]{:S(2)}, u32[]{:S(2)}) async-start(bf16[32,176,128]{2,1,0:T(8,128)(2,1)} %get-tuple-element.705), calls=%async_computation.4 | async-start | bytes 2883584 | tf_op jit(solution)/shard_map/all_to_all | solution.py:877
  107.8 0.0 copy-start.6
  107.9 23.6 %keys.1 = (f32[8,128,256]{2,1,0:T(8,128)}, f32[1024,128]{1,0:T(8,128)}, bf16[32,144,128]{2,1,0:T(8,128)(2,1)}, bf16[128,128]{1,0:T(8,128)(2,1)}) custom-call(s32[448]{0:T(512)} %get-tuple-element.660.list_ref, s32[8]{0:T(128)} %get-tuple-element.661.groups_ref, s32[8]{0:T(128)} %get-tuple-element.662.tail_ref, s32[56]{0:T(128)} %get-tuple-element.663.live_ref, ...), custom_call_target="tpu_custom_call" | custom-call | flops 24999999488 | bytes 4000000 | tf_op jit(solution)/shard_map/keys/pallas_call | solution.py:586
  131.5 0.8 pad_maximum_fusion
  132.2 0.0 collective-permute-done.10.o2_ref
  132.2 0.0 collective-permute-done.11.o3_ref
  132.3 0.0 collective-permute-done.8.o0_ref
  132.3 0.0 all-to-all-done.4.ret_ref
  132.3 0.7 copy-done.9
  133.1 0.2 copy-done.10
  133.2 0.5 copy-done
  133.7 0.6 while.35
  134.3 9.2 %all-to-all-start.5 = ((bf16[32,144,128]{2,1,0:T(8,128)(2,1)}), bf16[32,144,128]{2,1,0:T(8,128)(2,1)S(1)}, u32[]{:S(2)}, u32[]{:S(2)}) async-start(bf16[32,144,128]{2,1,0:T(8,128)(2,1)} %get-tuple-element.724), calls=%async_computation.5 | async-start | bytes 2359296 | tf_op jit(solution)/shard_map/all_to_all | solution.py:882
  143.6 14.3 %value_back.1 = (f32[1024,128]{1,0:T(8,128)}, f32[4,1024,128]{2,1,0:T(8,128)}) custom-call(s32[1]{0:T(128)} %bitcast.15.me_ref, s32[1]{0:T(128)} %bitcast.21.feat_ref, f32[1024,128]{1,0:T(8,128)S(1)} %copy-done.13, bf16[32,176,128]{2,1,0:T(8,128)(2,1)} %copy-done, f32[1024,128]{1,0:T(8,128)} %get-tuple-element.715.ownk_ref, s32[32,128]{1,0:T(8,128)} %bitcast.119, ...), custom_call_target="tpu_custom_call" | custom-call | flops 12000000000 | bytes 4000000 | tf_op jit(solution)/shard_map/value_back/pallas_call | solution.py:586
  157.8 3.9 %all-to-all-done.5.ret_ref = bf16[32,144,128]{2,1,0:T(8,128)(2,1)S(1)} async-done(((bf16[32,144,128]{2,1,0:T(8,128)(2,1)}), bf16[32,144,128]{2,1,0:T(8,128)(2,1)S(1)}, u32[]{:S(2)}, u32[]{:S(2)}) %all-to-all-start.5) | async-done | bytes 1179680 | tf_op jit(solution)/shard_map/all_to_all | solution.py:882
  161.7 1.0 copy-done.3
  162.7 6.1 %key_back.1 = (f32[1024,128]{1,0:T(8,128)}, bf16[1024,128]{1,0:T(8,128)(2,1)}, bf16[1024,128]{1,0:T(8,128)(2,1)}, bf16[1024,128]{1,0:T(8,128)(2,1)}) custom-call(s32[1]{0:T(128)} %bitcast.15.me_ref, s32[1]{0:T(128)} %bitcast.21.feat_ref, f32[1024,128]{1,0:T(8,128)} %get-tuple-element.723.acck_ref, bf16[32,144,128]{2,1,0:T(8,128)(2,1)} %copy-done.3, ...), custom_call_target="tpu_custom_call" | custom-call | flops 8000000000 | bytes 4000000 | tf_op jit(solution)/shard_map/key_back/pallas_call | solution.py:586
  168.8 3.3 %collective-permute-start.12 = (bf16[1024,128]{1,0:T(8,128)(2,1)}, bf16[1024,128]{1,0:T(8,128)(2,1)S(1)}, u32[]{:S(2)}, u32[]{:S(2)}) collective-permute-start(bf16[1024,128]{1,0:T(8,128)(2,1)} %get-tuple-element.730), channel_id=1, source_target_pairs={{0,2},{1,3},{2,0},{3,1},{4,6},{5,7},{6,4},{7,5},{8,10},{9,11},{10,... | collective-permute-start | bytes 786440 | tf_op jit(solution)/shard_map/ppermute | solution.py:890
  172.1 0.7 collective-permute-start.13
  172.8 2.6 %collective-permute-start.14 = (bf16[1024,128]{1,0:T(8,128)(2,1)}, bf16[1024,128]{1,0:T(8,128)(2,1)S(1)}, u32[]{:S(2)}, u32[]{:S(2)}) collective-permute-start(bf16[1024,128]{1,0:T(8,128)(2,1)} %get-tuple-element.732), channel_id=1, source_target_pairs={{0,3},{1,0},{2,1},{3,2},{4,7},{5,4},{6,5},{7,6},{8,11},{9,8},{10,9... | collective-permute-start | bytes 786440 | tf_op jit(solution)/shard_map/ppermute | solution.py:890
  175.4 2.8 %attend.1 = bf16[1024,128]{1,0:T(8,128)(2,1)} custom-call(f32[8,128,256]{2,1,0:T(8,128)} %get-tuple-element.727.out_t_ref, bf16[4,32,128]{2,1,0:T(8,128)(2,1)} %get-tuple-element.721.back_ref, bf16[32,128,128]{2,1,0:T(8,128)(2,1)} %get-tuple-element.728.pair_ref), custom_call_target="tpu_custom_call" | custom-call | flops 2000000000 | bytes 4000000 | tf_op jit(solution)/shard_map/attend/pallas_call | solution.py:586
  178.2 1.6 collective-permute-done.12
  179.8 4.9 %collective-permute-done.13 = bf16[1024,128]{1,0:T(8,128)(2,1)S(1)} collective-permute-done((bf16[1024,128]{1,0:T(8,128)(2,1)}, bf16[1024,128]{1,0:T(8,128)(2,1)S(1)}, u32[]{:S(2)}, u32[]{:S(2)}) %collective-permute-start.13) | collective-permute-done | bytes 262176 | tf_op jit(solution)/shard_map/ppermute | solution.py:890
  184.7 0.4 collective-permute-done.14
  185.1 0.8 add_convert_fusion
  (22 shorter events, 0.0 us)
Async XLA Ops:
  1.5 7.2 %copy-start.5 = (s32[128]{0:T(128)S(1)}, s32[128]{0:T(128)}, u32[]{:S(2)}) copy-start(s32[128]{0:T(128)} %param.23) | copy-start | bytes 1540
  9.3 14.5 %copy-start.7 = (s32[8,40]{1,0:T(8,128)S(1)}, s32[8,40]{1,0:T(8,128)}, u32[]{:S(2)}) copy-start(s32[8,40]{1,0:T(8,128)} %param.21) | copy-start | bytes 3844
  9.3 26.7 %all-to-all-start.2 = ((bf16[32,144,128]{2,1,0:T(8,128)(2,1)}), bf16[32,144,128]{2,1,0:T(8,128)(2,1)S(1)}, u32[]{:S(2)}, u32[]{:S(2)}) async-start(bf16[32,144,128]{2,1,0:T(8,128)(2,1)} %get-tuple-element.672), calls=%async_computation.2 | async-start | bytes 2359296 | tf_op jit(solution)/shard_map/all_to_all | solution.py:859
  17.6 38.5 %collective-permute-start = (bf16[1024,128]{1,0:T(8,128)(2,1)S(1)}, bf16[1024,128]{1,0:T(8,128)(2,1)S(1)}, u32[]{:S(2)}, u32[]{:S(2)}) collective-permute-start(bf16[1024,128]{1,0:T(8,128)(2,1)S(1)} %get-tuple-element.1012), channel_id=1, source_target_pairs={{0,4},{4,0},{8,12},{12,8},{16,20},{20,16},{24,28},{28,24},{32,36},... | collective-permute-start | bytes 786440 | tf_op jit(solution)/shard_map/ppermute | solution.py:846
  17.9 40.0 %collective-permute-start.1 = (bf16[1024,128]{1,0:T(8,128)(2,1)S(1)}, bf16[1024,128]{1,0:T(8,128)(2,1)S(1)}, u32[]{:S(2)}, u32[]{:S(2)}) collective-permute-start(bf16[1024,128]{1,0:T(8,128)(2,1)S(1)} %get-tuple-element.1012), channel_id=1, source_target_pairs={{0,8},{4,12},{8,0},{12,4},{16,24},{20,28},{24,16},{28,20},{32,40},... | collective-permute-start | bytes 786440 | tf_op jit(solution)/shard_map/ppermute | solution.py:846
  19.6 41.3 %collective-permute-start.2 = (bf16[1024,128]{1,0:T(8,128)(2,1)S(1)}, bf16[1024,128]{1,0:T(8,128)(2,1)}, u32[]{:S(2)}, u32[]{:S(2)}) collective-permute-start(bf16[1024,128]{1,0:T(8,128)(2,1)S(1)} %get-tuple-element.1012), channel_id=1, source_target_pairs={{0,16},{4,20},{8,24},{12,28},{16,0},{20,4},{24,8},{28,12},{32,48},... | collective-permute-start | bytes 786440 | tf_op jit(solution)/shard_map/ppermute | solution.py:846
  22.3 39.5 %collective-permute-start.3 = (bf16[1024,128]{1,0:T(8,128)(2,1)S(1)}, bf16[1024,128]{1,0:T(8,128)(2,1)}, u32[]{:S(2)}, u32[]{:S(2)}) collective-permute-start(bf16[1024,128]{1,0:T(8,128)(2,1)S(1)} %get-tuple-element.1012), channel_id=1, source_target_pairs={{0,32},{4,36},{8,40},{12,44},{16,48},{20,52},{24,56},{28,60},{32,0... | collective-permute-start | bytes 786440 | tf_op jit(solution)/shard_map/ppermute | solution.py:846
  36.0 4.3 %copy-start.2 = (bf16[32,144,128]{2,1,0:T(8,128)(2,1)}, bf16[32,144,128]{2,1,0:T(8,128)(2,1)S(1)}, u32[]{:S(2)}) copy-start(bf16[32,144,128]{2,1,0:T(8,128)(2,1)S(1)} %all-to-all-done.2.hk_ref) | copy-start | bytes 3538948
  36.0 32.9 %all-to-all-start.3 = ((bf16[32,144,128]{2,1,0:T(8,128)(2,1)}), bf16[32,144,128]{2,1,0:T(8,128)(2,1)S(1)}, u32[]{:S(2)}, u32[]{:S(2)}) async-start(bf16[32,144,128]{2,1,0:T(8,128)(2,1)} %get-tuple-element.675), calls=%async_computation.3 | async-start | bytes 2359296 | tf_op jit(solution)/shard_map/all_to_all | solution.py:863
  55.7 11.5 %copy-start.8 = (bf16[1056,256]{1,0:T(8,128)(2,1)S(1)}, bf16[1056,256]{1,0:T(8,128)(2,1)}, u32[]{:S(2)}) copy-start(bf16[1056,256]{1,0:T(8,128)(2,1)} %get-tuple-element.706) | copy-start | bytes 1622020
  55.7 36.8 %collective-permute-start.4 = (bf16[1024,128]{1,0:T(8,128)(2,1)S(1)}, bf16[1024,128]{1,0:T(8,128)(2,1)}, u32[]{:S(2)}, u32[]{:S(2)}) collective-permute-start(bf16[1024,128]{1,0:T(8,128)(2,1)S(1)} %get-tuple-element.1007), channel_id=1, source_target_pairs={{0,4},{4,0},{8,12},{12,8},{16,20},{20,16},{24,28},{28,24},{32,36},... | collective-permute-start | bytes 786440 | tf_op jit(solution)/shard_map/ppermute | solution.py:846
  56.1 5.6 %copy-start.14 = (bf16[1024,128]{1,0:T(8,128)(2,1)}, bf16[1024,128]{1,0:T(8,128)(2,1)S(1)}, u32[]{:S(2)}) copy-start(bf16[1024,128]{1,0:T(8,128)(2,1)S(1)} %collective-permute-done.t0_ref) | copy-start | bytes 786436
  56.1 36.7 %collective-permute-start.5 = (bf16[1024,128]{1,0:T(8,128)(2,1)S(1)}, bf16[1024,128]{1,0:T(8,128)(2,1)}, u32[]{:S(2)}, u32[]{:S(2)}) collective-permute-start(bf16[1024,128]{1,0:T(8,128)(2,1)S(1)} %get-tuple-element.1007), channel_id=1, source_target_pairs={{0,8},{4,12},{8,0},{12,4},{16,24},{20,28},{24,16},{28,20},{32,40},... | collective-permute-start | bytes 786440 | tf_op jit(solution)/shard_map/ppermute | solution.py:846
  58.0 3.8 %copy-start.15 = (bf16[1024,128]{1,0:T(8,128)(2,1)}, bf16[1024,128]{1,0:T(8,128)(2,1)S(1)}, u32[]{:S(2)}) copy-start(bf16[1024,128]{1,0:T(8,128)(2,1)S(1)} %collective-permute-done.1.t1_ref) | copy-start | bytes 786436
  58.0 34.9 %collective-permute-start.6 = (bf16[1024,128]{1,0:T(8,128)(2,1)S(1)}, bf16[1024,128]{1,0:T(8,128)(2,1)}, u32[]{:S(2)}, u32[]{:S(2)}) collective-permute-start(bf16[1024,128]{1,0:T(8,128)(2,1)S(1)} %get-tuple-element.1007), channel_id=1, source_target_pairs={{0,16},{4,20},{8,24},{12,28},{16,0},{20,4},{24,8},{28,12},{32,48},... | collective-permute-start | bytes 786440 | tf_op jit(solution)/shard_map/ppermute | solution.py:846
  61.0 32.0 %collective-permute-start.7 = (bf16[1024,128]{1,0:T(8,128)(2,1)S(1)}, bf16[1024,128]{1,0:T(8,128)(2,1)}, u32[]{:S(2)}, u32[]{:S(2)}) collective-permute-start(bf16[1024,128]{1,0:T(8,128)(2,1)S(1)} %get-tuple-element.1007), channel_id=1, source_target_pairs={{0,32},{4,36},{8,40},{12,44},{16,48},{20,52},{24,56},{28,60},{32,0... | collective-permute-start | bytes 786440 | tf_op jit(solution)/shard_map/ppermute | solution.py:846
  67.2 65.1 %collective-permute-start.10 = (bf16[1056,256]{1,0:T(8,128)(2,1)S(1)}, bf16[1056,256]{1,0:T(8,128)(2,1)S(1)}, u32[]{:S(2)}, u32[]{:S(2)}) collective-permute-start(bf16[1056,256]{1,0:T(8,128)(2,1)S(1)} %copy-done.8), channel_id=1, source_target_pairs={{0,16},{4,20},{8,24},{12,28},{16,0},{20,4},{24,8},{28,12},{32,48},... | collective-permute-start | bytes 1622024 | tf_op jit(solution)/shard_map/ppermute | solution.py:846
  68.9 1.0 copy-start.1
  92.5 39.8 %collective-permute-start.11 = (bf16[1056,256]{1,0:T(8,128)(2,1)S(1)}, bf16[1056,256]{1,0:T(8,128)(2,1)S(1)}, u32[]{:S(2)}, u32[]{:S(2)}) collective-permute-start(bf16[1056,256]{1,0:T(8,128)(2,1)S(1)} %copy-done.8), channel_id=1, source_target_pairs={{0,32},{4,36},{8,40},{12,44},{16,48},{20,52},{24,56},{28,60},{32,0... | collective-permute-start | bytes 1622024 | tf_op jit(solution)/shard_map/ppermute | solution.py:846
  92.8 39.5 %collective-permute-start.8 = (bf16[1056,256]{1,0:T(8,128)(2,1)S(1)}, bf16[1056,256]{1,0:T(8,128)(2,1)}, u32[]{:S(2)}, u32[]{:S(2)}) collective-permute-start(bf16[1056,256]{1,0:T(8,128)(2,1)S(1)} %copy-done.8), channel_id=1, source_target_pairs={{0,4},{4,0},{8,12},{12,8},{16,20},{20,16},{24,28},{28,24},{32,36},... | collective-permute-start | bytes 1622024 | tf_op jit(solution)/shard_map/ppermute | solution.py:846
  92.8 39.5 %collective-permute-start.9 = (bf16[1056,256]{1,0:T(8,128)(2,1)S(1)}, bf16[1056,256]{1,0:T(8,128)(2,1)}, u32[]{:S(2)}, u32[]{:S(2)}) collective-permute-start(bf16[1056,256]{1,0:T(8,128)(2,1)S(1)} %copy-done.8), channel_id=1, source_target_pairs={{0,8},{4,12},{8,0},{12,4},{16,24},{20,28},{24,16},{28,20},{32,40},... | collective-permute-start | bytes 1622024 | tf_op jit(solution)/shard_map/ppermute | solution.py:846
  99.1 33.2 %all-to-all-start.4 = ((bf16[32,176,128]{2,1,0:T(8,128)(2,1)}), bf16[32,176,128]{2,1,0:T(8,128)(2,1)S(1)}, u32[]{:S(2)}, u32[]{:S(2)}) async-start(bf16[32,176,128]{2,1,0:T(8,128)(2,1)} %get-tuple-element.705), calls=%async_computation.4 | async-start | bytes 2883584 | tf_op jit(solution)/shard_map/all_to_all | solution.py:877
  107.8 23.6 %copy-start.6 = (bf16[128,128]{1,0:T(8,128)(2,1)S(1)}, bf16[128,128]{1,0:T(8,128)(2,1)}, u32[]{:S(2)}) copy-start(bf16[128,128]{1,0:T(8,128)(2,1)} %get-tuple-element.710) | copy-start | bytes 98308
  132.2 0.8 copy-start.9
  132.3 1.0 copy-start.10
  132.3 1.4 copy-start
  134.3 9.3 %copy-start.13 = (f32[1024,128]{1,0:T(8,128)S(1)}, f32[1024,128]{1,0:T(8,128)}, u32[]{:S(2)}) copy-start(f32[1024,128]{1,0:T(8,128)} %get-tuple-element.713.ownv_ref) | copy-start | bytes 1572868
  134.3 27.4 %all-to-all-start.5 = ((bf16[32,144,128]{2,1,0:T(8,128)(2,1)}), bf16[32,144,128]{2,1,0:T(8,128)(2,1)S(1)}, u32[]{:S(2)}, u32[]{:S(2)}) async-start(bf16[32,144,128]{2,1,0:T(8,128)(2,1)} %get-tuple-element.724), calls=%async_computation.5 | async-start | bytes 2359296 | tf_op jit(solution)/shard_map/all_to_all | solution.py:882
  161.7 1.0 copy-start.3
  168.8 11.0 %collective-permute-start.12 = (bf16[1024,128]{1,0:T(8,128)(2,1)}, bf16[1024,128]{1,0:T(8,128)(2,1)S(1)}, u32[]{:S(2)}, u32[]{:S(2)}) collective-permute-start(bf16[1024,128]{1,0:T(8,128)(2,1)} %get-tuple-element.730), channel_id=1, source_target_pairs={{0,2},{1,3},{2,0},{3,1},{4,6},{5,7},{6,4},{7,5},{8,10},{9,11},{10,... | collective-permute-start | bytes 786440 | tf_op jit(solution)/shard_map/ppermute | solution.py:890
  172.1 12.6 %collective-permute-start.13 = (bf16[1024,128]{1,0:T(8,128)(2,1)}, bf16[1024,128]{1,0:T(8,128)(2,1)S(1)}, u32[]{:S(2)}, u32[]{:S(2)}) collective-permute-start(bf16[1024,128]{1,0:T(8,128)(2,1)} %get-tuple-element.731), channel_id=1, source_target_pairs={{0,1},{1,2},{2,3},{3,0},{4,5},{5,6},{6,7},{7,4},{8,9},{9,10},{10,1... | collective-permute-start | bytes 786440 | tf_op jit(solution)/shard_map/ppermute | solution.py:890
  172.8 12.3 %collective-permute-start.14 = (bf16[1024,128]{1,0:T(8,128)(2,1)}, bf16[1024,128]{1,0:T(8,128)(2,1)S(1)}, u32[]{:S(2)}, u32[]{:S(2)}) collective-permute-start(bf16[1024,128]{1,0:T(8,128)(2,1)} %get-tuple-element.732), channel_id=1, source_target_pairs={{0,3},{1,0},{2,1},{3,2},{4,7},{5,4},{6,5},{7,6},{8,11},{9,8},{10,9... | collective-permute-start | bytes 786440 | tf_op jit(solution)/shard_map/ppermute | solution.py:890
  175.4 9.8 %copy-start.4 = (f32[1024,128]{1,0:T(8,128)S(1)}, f32[1024,128]{1,0:T(8,128)}, u32[]{:S(2)}) copy-start(f32[1024,128]{1,0:T(8,128)} %get-tuple-element.729) | copy-start | bytes 1572868

commit v8 on v7

--- a/solution.py
+++ b/solution.py
@@ -19,7 +19,10 @@
 EMPTY_BLOCK = GLOBAL_BLOCK + 1
 KEY_BLOCKS = EMPTY_BLOCK + 1
 GROUP = 8
-PAIR = 4
+PAIR = 8
+SCORE_PAIR = 4
+ITEMS = 2
+MAX_ITEMS = 64
 LIST = 56
 EXTRA = 16
 SLOTS = BLOCK + EXTRA
@@ -105,7 +108,7 @@
 
 def project_kernel(
     me_ref, x_ref, wq_ref, wk_ref, wv_ref, cot_ref, rows_ref, exp_ref, gid_ref, q_ref, k_ref, v_ref, outk_ref, outv_ref,
-    away_ref, rounds_ref, kv_ref,
+    away_ref, rounds_ref, kv_ref, msgk_s, msgv_s, sems,
 ):
     most = jnp.max(owner_ranks(gid_ref[...])[0].astype(F32)).astype(jnp.int32)
     rounds_ref[0] = (most + EXTRA) // EXTRA
@@ -129,17 +132,29 @@
     hot = (jnp.concatenate([mine] * (NODES_HERE // BLOCK), axis=1) == lanes).astype(F32).astype(BF16)
     extra = dot(hot, kv_ref[...]).astype(BF16)
 
+    def sends(t):
+        here = pl.ds(t * GROUP, GROUP)
+        return (
+            pltpu.make_async_copy(msgk_s.at[here], outk_ref.at[here], sems.at[0, t]),
+            pltpu.make_async_copy(msgv_s.at[here], outv_ref.at[here], sems.at[1, t]),
+        )
+
     def gather(t, carry):
         hot = one_hot_of_rows([rows_ref[pl.ds(t * GROUP + u, 1), :] for u in range(GROUP)])
         got = dot(hot, kv_ref[...]).astype(BF16)
         for u in range(GROUP):
-            outk_ref[t * GROUP + u, :BLOCK] = got[u * BLOCK : (u + 1) * BLOCK, :COLS]
-            outv_ref[t * GROUP + u, :BLOCK] = got[u * BLOCK : (u + 1) * BLOCK, COLS:]
-            outk_ref[t * GROUP + u, BLOCK:] = extra[:, :COLS]
-            outv_ref[t * GROUP + u, BLOCK:] = extra[:, COLS:]
+            msgk_s[t * GROUP + u, :BLOCK] = got[u * BLOCK : (u + 1) * BLOCK, :COLS]
+            msgv_s[t * GROUP + u, :BLOCK] = got[u * BLOCK : (u + 1) * BLOCK, COLS:]
+            msgk_s[t * GROUP + u, BLOCK:] = extra[:, :COLS]
+            msgv_s[t * GROUP + u, BLOCK:] = extra[:, COLS:]
+        for send in sends(t):
+            send.start()
         return carry
 
     lax.fori_loop(0, SENDERS // GROUP, gather, 0)
+    for t in range(SENDERS // GROUP):
+        for send in sends(t):
+            send.wait()
 
 
 def gather_partner(exp_ref, m, table):
@@ -250,19 +265,19 @@
     lax.fori_loop(0, Q_BLOCKS, one, 0, unroll=2)
 
 
-def plan_kernel(mask_ref, count_ref, list_ref, groups_ref, tail_ref, live_ref):
+def plan_kernel(mask_ref, halo_ref, list_ref, where_ref, block_ref, count_ref, live_ref):
     for j in range(Q_BLOCKS):
         live_ref[j] = BLOCK
     live_ref[GLOBAL_BLOCK] = BLOCK
     live_ref[EMPTY_BLOCK] = 0
 
     def copy_count(s, carry):
-        live_ref[Q_BLOCKS + s] = count_ref[s]
+        live_ref[Q_BLOCKS + s] = halo_ref[s]
         return carry
 
     lax.fori_loop(0, SENDERS, copy_count, 0)
 
-    def per_block(i, carry):
+    def per_block(i, items):
         list_ref[i * LIST] = GLOBAL_BLOCK
 
         def put(j, n):
@@ -273,24 +288,38 @@
         n = lax.fori_loop(0, GLOBAL_BLOCK, put, 1)
         for extra in range(GROUP):
             list_ref[i * LIST + n + extra] = EMPTY_BLOCK
-        groups_ref[i] = (n + PAIR - 1) // GROUP
-        tail_ref[i] = jnp.logical_and(n % GROUP > 0, n % GROUP <= PAIR).astype(jnp.int32)
-        return carry
-
-    lax.fori_loop(0, Q_BLOCKS, per_block, 0)
-
-
-def fill(dst, dst_t, first_col, own_ref, halo_ref, gid_ref, glob_ref):
+        groups = (n + GROUP - 1) // GROUP
+
+        def item(g, carry):
+            where_ref[items + g] = i * LIST + g * GROUP
+            block_ref[items + g] = i
+            return carry
+
+        lax.fori_loop(0, groups, item, 0)
+        return items + groups
+
+    items = lax.fori_loop(0, Q_BLOCKS, per_block, 0)
+    for u in range(GROUP):
+        list_ref[Q_BLOCKS * LIST + u] = EMPTY_BLOCK
+    for u in range(ITEMS - 1):
+        where_ref[items + u] = Q_BLOCKS * LIST
+        block_ref[items + u] = 0
+    count_ref[0] = (items + ITEMS - 1) // ITEMS
+
+
+def fill(dst, dst_t, first_col,  own_ref, halo_ref, gid_ref, glob_ref):
+    def put(j, block):
+        if dst is not None:
+            dst[j] = block
+        if dst_t is not None:
+            dst_t[j] = block.T
+
     def own(j, carry):
-        block = own_ref[q_rows(j), :]
-        dst[j] = block
-        dst_t[j] = block.T
+        put(j, own_ref[q_rows(j), :])
         return carry
 
     def halo(j, carry):
-        block = halo_ref[j, :BLOCK]
-        dst[Q_BLOCKS + j] = block
-        dst_t[Q_BLOCKS + j] = block.T
+        put(Q_BLOCKS + j, halo_ref[j, :BLOCK])
         return carry
 
     lax.fori_loop(0, Q_BLOCKS, own, 0, unroll=4)
@@ -300,14 +329,8 @@
     hot = (wide == iota((BLOCK, SENDERS * EXTRA), 1)).astype(F32).astype(BF16)
     extra = jnp.concatenate([halo_ref[s, BLOCK:] for s in range(SENDERS)], axis=0)
     rows = (dot(hot, extra) + glob_ref[:, first_col : first_col + COLS].astype(F32)).astype(BF16)
-    dst[GLOBAL_BLOCK] = rows
-    dst_t[GLOBAL_BLOCK] = rows.T
-    dst[EMPTY_BLOCK] = jnp.zeros((BLOCK, COLS), BF16)
-    dst_t[EMPTY_BLOCK] = jnp.zeros((BLOCK, COLS), BF16)
-
-
-def turn_kernel(own_ref, hv_ref, gid_ref, glob_ref, v_ref, vt_ref):
-    fill(v_ref, vt_ref, COLS, own_ref, hv_ref, gid_ref, glob_ref)
+    put(GLOBAL_BLOCK, rows)
+    put(EMPTY_BLOCK, jnp.zeros((BLOCK, COLS), BF16))
 
 
 def stacked(rows):
@@ -340,8 +363,9 @@
     )
 
 
-def block_ids(list_ref, i, g, size):
-    return [list_ref[i * LIST + g * GROUP + u] for u in range(size)]
+def item_of(t, u, list_ref, where_ref, block_ref):
+    where = where_ref[t * ITEMS + u]
+    return block_ref[t * ITEMS + u], [list_ref[where + b] for b in range(GROUP)]
 
 
 def q_rows(i):
@@ -349,43 +373,43 @@
 
 
 def score_kernel(
-    list_ref, groups_ref, tail_ref, live_ref, qt_ref, own_ref, hk_ref, gid_ref, glob_ref, lse_ref, k_s, kt_ref
+    list_ref, where_ref, block_ref, count_ref, live_ref, qt_ref, own_ref, hk_ref, gid_ref, glob_ref, lse_ref, k_s, kt_ref,
+    top_s, total_s,
 ):
     fill(k_s, kt_ref, 0, own_ref, hk_ref, gid_ref, glob_ref)
 
-    def per_block(i, carry):
-        turned_q = qt_ref[i]
-
-        def step(size, g, state):
-            blocks = block_ids(list_ref, i, g, size)
-            new_state = []
-            for u in range(size // PAIR):
-                top, total = state[u]
-                scores = masked_scores(blocks[u * PAIR : (u + 1) * PAIR], k_s, turned_q, live_ref)
-                scores = scores.reshape(PAIR * BLOCK // 8, 8, 2 * BLOCK)
-                new_top = jnp.maximum(top, jnp.max(scores, axis=0))
-                total = total * jnp.exp(top - new_top) + jnp.sum(jnp.exp(scores - new_top[None]), axis=0)
-                new_state.append((new_top, total))
-            return tuple(new_state) + tuple(state[size // PAIR :])
-
-        init = (jnp.full((8, 2 * BLOCK), NEG, F32), jnp.zeros((8, 2 * BLOCK), F32))
-        state = tuple(init for _ in range(GROUP // PAIR))
-        state = lax.fori_loop(0, groups_ref[i], functools.partial(step, GROUP), state)
-        state = lax.fori_loop(groups_ref[i], groups_ref[i] + tail_ref[i], functools.partial(step, PAIR), state)
-        top = jnp.concatenate([t for t, _ in state], axis=0)
-        total = jnp.concatenate([t for _, t in state], axis=0)
+    top_s[...] = jnp.full((Q_BLOCKS, 8, 2 * BLOCK), NEG, F32)
+    total_s[...] = jnp.zeros((Q_BLOCKS, 8, 2 * BLOCK), F32)
+
+    def step(t, carry):
+        for item in range(ITEMS):
+            i, blocks = item_of(t, item, list_ref, where_ref, block_ref)
+            turned_q = qt_ref[i]
+            parts = []
+            for u in range(0, GROUP, SCORE_PAIR):
+                scores = masked_scores(blocks[u : u + SCORE_PAIR], k_s, turned_q, live_ref)
+                scores = scores.reshape(SCORE_PAIR * BLOCK // 8, 8, 2 * BLOCK)
+                top = jnp.max(scores, axis=0)
+                parts.append((top, jnp.sum(jnp.exp(scores - top[None]), axis=0)))
+            parts.append((top_s[i], total_s[i]))
+            best = functools.reduce(jnp.maximum, [top for top, _ in parts])
+            top_s[i] = best
+            total_s[i] = sum(total * jnp.exp(top - best) for top, total in parts)
+        return carry
+
+    lax.fori_loop(0, count_ref[0], step, 0)
+    for i in range(Q_BLOCKS):
+        top = top_s[i]
         best = jnp.max(top, axis=0, keepdims=True)
-        denominator = jnp.sum(total * jnp.exp(top - best), axis=0, keepdims=True)
-        lse_ref[pl.ds(i, 1), :] = best + jnp.log(denominator)
-        return carry
-
-    lax.fori_loop(0, Q_BLOCKS, per_block, 0)
+        denominator = jnp.sum(total_s[i] * jnp.exp(top - best), axis=0, keepdims=True)
+        lse_ref[i : i + 1, :] = best + jnp.log(denominator)
 
 
 def value_kernel(
-    list_ref, groups_ref, tail_ref, live_ref, k_s, vt_s, qt_ref, ct_ref, cs_ref, part_ref, sp_ref, gid_ref,
-    own_ref, halo_ref, gout_ref, out_s, delta_ref, lse_ref, acc_s,
+    list_ref, where_ref, block_ref, count_ref, live_ref, k_s, ownv_ref, hv_ref, glob_ref, qt_ref, ct_ref, cs_ref, part_ref,
+    sp_ref, gid_ref, own_ref, halo_ref, gout_ref, out_s, delta_ref, lse_ref, acc_s, vt_s,
 ):
+    fill(None, vt_s, COLS, ownv_ref, hv_ref, gid_ref, glob_ref)
     clear_blocks(acc_s)
     part = part_ref[...]
     best = part
@@ -396,33 +420,27 @@
         total += jnp.exp(sp_ref[m] - best)
     lse_ref[...] = best + jnp.log(total)
 
-    def per_block(i, carry):
-        turned_q = qt_ref[i]
-        cot_stack = cs_ref[i]
-        lse = lse_ref[pl.ds(i, 1), :]
-        out_s[i] = jnp.zeros((COLS, 2 * BLOCK), F32)
-
-        def step(size, g, carry):
-            blocks = block_ids(list_ref, i, g, size)
-            total = None
-            for u in range(0, size, PAIR):
+    out_s[...] = jnp.zeros((Q_BLOCKS, COLS, 2 * BLOCK), F32)
+
+    def step(t, carry):
+        for item in range(ITEMS):
+            i, blocks = item_of(t, item, list_ref, where_ref, block_ref)
+            turned_q = qt_ref[i]
+            cot_stack = cs_ref[i]
+            lse = lse_ref[pl.ds(i, 1), :]
+            for u in range(0, GROUP, PAIR):
                 pair = blocks[u : u + PAIR]
                 scores = masked_scores(pair, k_s, turned_q, live_ref)
                 weight = jnp.exp(scores - lse).astype(BF16)
-                term = dot(jnp.concatenate([vt_s[b] for b in pair], axis=1), weight)
-                total = term if total is None else total + term
+                out_s[i] += dot(jnp.concatenate([vt_s[b] for b in pair], axis=1), weight)
                 grads = dot(weight, cot_stack)
                 for w, b in enumerate(pair):
                     acc_s[b] += grads[w * BLOCK : (w + 1) * BLOCK]
-            out_s[i] += total
-            return carry
-
-        lax.fori_loop(0, groups_ref[i], functools.partial(step, GROUP), 0)
-        lax.fori_loop(groups_ref[i], groups_ref[i] + tail_ref[i], functools.partial(step, PAIR), 0)
-        delta_ref[pl.ds(i, 1), :] = jnp.sum(out_s[i] * ct_ref[i].astype(F32), axis=0, keepdims=True)
-        return carry
-
-    lax.fori_loop(0, Q_BLOCKS, per_block, 0)
+        return carry
+
+    lax.fori_loop(0, count_ref[0], step, 0)
+    for i in range(Q_BLOCKS):
+        delta_ref[i : i + 1, :] = jnp.sum(out_s[i] * ct_ref[i].astype(F32), axis=0, keepdims=True)
     store_parts(acc_s, own_ref, halo_ref, gid_ref, gout_ref)
 
 
@@ -455,40 +473,34 @@
 
 
 def key_kernel(
-    list_ref, groups_ref, tail_ref, live_ref, k_s, kt_s, v_s, qt_ref, qs_ref, ct_ref, lse_ref, delta_ref, gid_ref,
-    out_s, own_ref, halo_ref, gout_ref, acc_s,
+    list_ref, where_ref, block_ref, count_ref, live_ref, k_s, kt_s, ownv_ref, hv_ref, glob_ref, qt_ref, qs_ref, ct_ref, lse_ref,
+    delta_ref, gid_ref, out_s, own_ref, halo_ref, gout_ref, acc_s, v_s,
 ):
+    fill(v_s, None, COLS, ownv_ref, hv_ref, gid_ref, glob_ref)
     clear_blocks(acc_s)
 
-    def per_block(i, carry):
-        turned_q = qt_ref[i]
-        q_stack = qs_ref[i]
-        turned_cot = ct_ref[i]
-        lse = lse_ref[pl.ds(i, 1), :]
-        delta = delta_ref[pl.ds(i, 1), :]
-        out_s[i] = jnp.zeros((COLS, 2 * BLOCK), F32)
-
-        def step(size, g, carry):
-            blocks = block_ids(list_ref, i, g, size)
-            total = None
-            for u in range(0, size, PAIR):
+    out_s[...] = jnp.zeros((Q_BLOCKS, COLS, 2 * BLOCK), F32)
+
+    def step(t, carry):
+        for item in range(ITEMS):
+            i, blocks = item_of(t, item, list_ref, where_ref, block_ref)
+            turned_q = qt_ref[i]
+            q_stack = qs_ref[i]
+            turned_cot = ct_ref[i]
+            lse = lse_ref[pl.ds(i, 1), :]
+            delta = delta_ref[pl.ds(i, 1), :]
+            for u in range(0, GROUP, PAIR):
                 pair = blocks[u : u + PAIR]
                 scores = masked_scores(pair, k_s, turned_q, live_ref)
                 dprob = dot(jnp.concatenate([v_s[b] for b in pair], axis=0), turned_cot)
                 dscore = (jnp.exp(scores - lse) * (dprob - delta)).astype(BF16)
-                term = dot(jnp.concatenate([kt_s[b] for b in pair], axis=1), dscore)
-                total = term if total is None else total + term
+                out_s[i] += dot(jnp.concatenate([kt_s[b] for b in pair], axis=1), dscore)
                 grads = dot(dscore, q_stack)
                 for w, b in enumerate(pair):
                     acc_s[b] += grads[w * BLOCK : (w + 1) * BLOCK]
-            out_s[i] += total
-            return carry
-
-        lax.fori_loop(0, groups_ref[i], functools.partial(step, GROUP), 0)
-        lax.fori_loop(groups_ref[i], groups_ref[i] + tail_ref[i], functools.partial(step, PAIR), 0)
-        return carry
-
-    lax.fori_loop(0, Q_BLOCKS, per_block, 0)
+        return carry
+
+    lax.fori_loop(0, count_ref[0], step, 0)
     store_parts(acc_s, own_ref, halo_ref, gid_ref, gout_ref)
 
 
@@ -501,7 +513,7 @@
         acc_s[c * BLOCK : (c + 1) * BLOCK, :] += dot(hot, data)
 
 
-def add_halo(acc_s, me_ref, ret_ref, rows_ref, gid_ref):
+def add_halo(acc_s, me_ref, ret_ref, rows_ref, gid_ref, more_ref):
     def halo(t, carry):
         splits = [split_index(rows_ref[pl.ds(t * GROUP + u, 1), :]) for u in range(GROUP)]
         data = jnp.concatenate([ret_ref[t * GROUP + u, :BLOCK] for u in range(GROUP)], axis=0)
@@ -518,6 +530,12 @@
     hot = (mine == iota((EXTRA, NODES_HERE), 1)).astype(F32)
     hot = jnp.concatenate([hot, hot], axis=0).T.astype(BF16)
     acc_s[...] += dot(hot, data)
+    gids = gid_ref[...]
+    local = jnp.where((gids >> 10) == me_ref[0], gids & (NODES_HERE - 1), NODES_HERE)
+    more = more_ref[...]
+    high = more.astype(BF16)
+    low = (more - high.astype(F32)).astype(BF16)
+    scatter_into(acc_s, [split_index(local)] * 2, jnp.concatenate([high, low], axis=0))
 
 
 def add_partners(acc_s, parts, others, first_col):
@@ -542,7 +560,7 @@
 
 def value_back_kernel(
     me_ref, feat_ref, ownv_ref, ret_ref, ownk_ref, rows_ref, o0_ref, o1_ref, o2_ref, o3_ref, gid_ref, wq_ref, wv_ref,
-    out_t_ref, back_ref, pair_ref, acck_ref, pre_ref, accv_s, gq_ref,
+    out_t_ref, back_ref, pair_ref, more_ref, acck_ref, pre_ref, accv_s, gq_ref,
 ):
     others = (o0_ref, o1_ref, o2_ref, o3_ref)
     parts = [ret_ref[me_ref[0] ^ (1 << m), SLOTS:] for m in range(EXPANDERS)]
@@ -550,7 +568,7 @@
         gq_ref, out_t_ref, [back_ref[m, :16] for m in range(EXPANDERS)], pair_ref, 1.0 / math.sqrt(HEAD)
     )
     accv_s[...] = ownv_ref[...]
-    add_halo(accv_s, me_ref, ret_ref, rows_ref, gid_ref)
+    add_halo(accv_s, me_ref, ret_ref, rows_ref, gid_ref, more_ref)
     add_partners(accv_s, [part[16:] for part in parts], others, COLS)
     acck_ref[...] = ownk_ref[...]
     add_partners(acck_ref, [part[:16] for part in parts], others, 0)
@@ -561,7 +579,7 @@
 
 
 def key_back_kernel(
-    me_ref, feat_ref, acck_ref, ret_ref, rows_ref, gid_ref, wk_ref, pre_ref, t0_ref, t1_ref, t2_ref, t3_ref,
+    me_ref, feat_ref, acck_ref, ret_ref, rows_ref, gid_ref, wk_ref, pre_ref, more_ref, t0_ref, t1_ref, t2_ref, t3_ref,
     acc_s, own_s, pre_s, sems,
 ):
     own_copy = pltpu.make_async_copy(acck_ref, own_s, sems.at[0])
@@ -569,7 +587,7 @@
     own_copy.start()
     pre_copy.start()
     acc_s[...] = jnp.zeros((NODES_HERE, COLS), F32)
-    add_halo(acc_s, me_ref, ret_ref, rows_ref, gid_ref)
+    add_halo(acc_s, me_ref, ret_ref, rows_ref, gid_ref, more_ref)
     own_copy.wait()
     grad_key = (acc_s[...] + own_s[...]).astype(BF16)
     pre_copy.wait()
@@ -601,6 +619,7 @@
 
 
 def run_project(me, features, w_query, w_key, w_value, cotangent, rows, exp_list, gids):
+    anywhere = pl.BlockSpec(memory_space=pl.ANY)
     return call(
         project_kernel,
         [smem()] + [vmem()] * 8,
@@ -617,24 +636,25 @@
         name="project",
         mib=56,
         flops=3_000_000_000,
-        out_spaces=(*(vmem() for _ in range(6)), smem()),
-        scratch=[pltpu.VMEM((NODES_HERE, 2 * COLS), BF16)],
+        out_spaces=(vmem(), vmem(), vmem(), anywhere, anywhere, vmem(), smem()),
+        scratch=[
+            pltpu.VMEM((NODES_HERE, 2 * COLS), BF16),
+            pltpu.VMEM((SENDERS, SLOTS, COLS), BF16),
+            pltpu.VMEM((SENDERS, SLOTS, COLS), BF16),
+            pltpu.SemaphoreType.DMA((2, SENDERS // GROUP)),
+        ],
     )
 
 
 def run_plan(block_mask, halo_count):
+    sizes = (Q_BLOCKS * LIST + GROUP, MAX_ITEMS, MAX_ITEMS, 1, KEY_BLOCKS)
     return call(
         plan_kernel,
         [smem()] * 2,
-        (
-            shape((Q_BLOCKS * LIST,), jnp.int32),
-            shape((Q_BLOCKS,), jnp.int32),
-            shape((Q_BLOCKS,), jnp.int32),
-            shape((LIST,), jnp.int32),
-        ),
+        tuple(shape((size,), jnp.int32) for size in sizes),
         (block_mask.reshape(-1), halo_count.reshape(-1)),
         name="plan",
-        out_spaces=(smem(), smem(), smem(), smem()),
+        out_spaces=tuple(smem() for _ in sizes),
     )
 
 
@@ -690,34 +710,24 @@
 def run_scores(plan, turned_q, own, halo_k, gids, glob):
     return call(
         score_kernel,
-        [smem()] * 4 + [vmem()] * 5,
+        [smem()] * 5 + [vmem()] * 5,
         (
             shape((Q_BLOCKS, 2 * BLOCK), F32),
             shape((KEY_BLOCKS, BLOCK, COLS)),
             shape((KEY_BLOCKS, COLS, BLOCK)),
         ),
         (*plan, turned_q, own, halo_k, gids, glob),
+        scratch=[pltpu.VMEM((Q_BLOCKS, 8, 2 * BLOCK), F32)] * 2,
         name="scores",
         flops=12_000_000_000,
     )
 
 
-def run_turn(own, halo_v, gids, glob):
-    return call(
-        turn_kernel,
-        [vmem()] * 4,
-        (shape((KEY_BLOCKS, BLOCK, COLS)), shape((KEY_BLOCKS, COLS, BLOCK))),
-        (own, halo_v, gids, glob),
-        name="turn",
-        flops=2_000_000_000,
-    )
-
-
-def run_values(plan, keys, turned_v, prepared, part, scores, gids):
+def run_values(plan, keys, own_values, halo_v, glob, prepared, part, scores, gids):
     turned_q, _, turned_cot, cot_stack = prepared
     return call(
         value_kernel,
-        [smem()] * 4 + [vmem()] * 8,
+        [smem()] * 5 + [vmem()] * 10,
         (
             shape((NODES_HERE, COLS), F32),
             shape((SENDERS, BACK, COLS)),
@@ -726,38 +736,38 @@
             shape((Q_BLOCKS, 2 * BLOCK), F32),
             shape((Q_BLOCKS, 2 * BLOCK), F32),
         ),
-        (*plan, keys, turned_v, turned_q, turned_cot, cot_stack, part, scores, gids),
-        scratch=[blocks_of(F32)],
+        (*plan, keys, own_values, halo_v, glob, turned_q, turned_cot, cot_stack, part, scores, gids),
+        scratch=[blocks_of(F32), blocks_of(BF16)],
         name="values",
         flops=20_000_000_000,
     )
 
 
-def run_keys(plan, keys, turned_k, values, prepared, lse, delta, gids):
+def run_keys(plan, keys, turned_k, own_values, halo_v, glob, prepared, lse, delta, gids):
     turned_q, q_stack, turned_cot, _ = prepared
     return call(
         key_kernel,
-        [smem()] * 4 + [vmem()] * 9,
+        [smem()] * 5 + [vmem()] * 11,
         (
             shape((Q_BLOCKS, COLS, 2 * BLOCK), F32),
             shape((NODES_HERE, COLS), F32),
             shape((SENDERS, SLOTS, COLS)),
             shape((BLOCK, COLS)),
         ),
-        (*plan, keys, turned_k, values, turned_q, q_stack, turned_cot, lse, delta, gids),
-        scratch=[blocks_of(F32)],
+        (*plan, keys, turned_k, own_values, halo_v, glob, turned_q, q_stack, turned_cot, lse, delta, gids),
+        scratch=[blocks_of(F32), blocks_of(BF16)],
         name="keys",
         mib=56,
         flops=25_000_000_000,
     )
 
 
-def run_value_back(me, feat, own_v, returned_v, own_k, rows, others, gids, w_query, w_value, out_t, back, pairs):
+def run_value_back(me, feat, own_v, returned_v, own_k, rows, others, gids, w_query, w_value, out_t, back, pairs, more):
     return call(
         value_back_kernel,
-        [smem()] * 2 + [vmem()] * 14,
+        [smem()] * 2 + [vmem()] * 15,
         (shape((NODES_HERE, COLS), F32), shape((4, NODES_HERE, COLS), F32)),
-        (me, feat, own_v, returned_v, own_k, rows, *others, gids, w_query, w_value, out_t, back, pairs),
+        (me, feat, own_v, returned_v, own_k, rows, *others, gids, w_query, w_value, out_t, back, pairs, more),
         scratch=[pltpu.VMEM((NODES_HERE, COLS), F32), pltpu.VMEM((NODES_HERE, COLS), BF16)],
         name="value_back",
         mib=56,
@@ -765,13 +775,13 @@
     )
 
 
-def run_key_back(me, feat, own_k, returned_k, rows, gids, w_key, pre):
+def run_key_back(me, feat, own_k, returned_k, rows, gids, w_key, pre, more):
     anywhere = pl.BlockSpec(memory_space=pl.ANY)
     return call(
         key_back_kernel,
-        [smem()] * 2 + [anywhere] + [vmem()] * 4 + [anywhere],
+        [smem()] * 2 + [anywhere] + [vmem()] * 4 + [anywhere, vmem()],
         (shape((NODES_HERE, COLS), F32),) + tuple(shape((NODES_HERE, COLS)) for _ in range(3)),
-        (me, feat, own_k, returned_k, rows, gids, w_key, pre),
+        (me, feat, own_k, returned_k, rows, gids, w_key, pre, more),
         scratch=[
             pltpu.VMEM((NODES_HERE, COLS), F32),
             pltpu.VMEM((NODES_HERE, COLS), F32),
@@ -793,7 +803,7 @@
 def more_globals(rounds, global_ids, my_index, own_k, own_v):
     def body(state):
         r, glob = state
-        owner, rank = ranks(global_ids)
+        owner, rank = ranks(global_ids + jnp.minimum(r, 0))
         slot = rank - r * EXTRA
         here = (slot >= 0) & (slot < EXTRA)
         place = jnp.where((owner == my_index) & here, slot, EXTRA)
@@ -808,22 +818,23 @@
     return lax.while_loop(lambda state: state[0] < rounds, body, start)[1]
 
 
-def more_grads(rounds, global_ids, my_index, part_k, part_v, own_k, own_v):
+def more_grads(rounds, global_ids, my_index, part_k, part_v):
     def body(state):
-        r, own_k, own_v = state
-        owner, rank = ranks(global_ids)
+        r, more_k, more_v = state
+        owner, rank = ranks(global_ids + jnp.minimum(r, 0))
         slot = rank - r * EXTRA
         here = (slot >= 0) & (slot < EXTRA)
-        part = jnp.concatenate([part_k, part_v], axis=1)
         place = jnp.where(here, owner * EXTRA + slot, SENDERS * EXTRA)
-        rows = jnp.zeros((SENDERS * EXTRA + 1, part.shape[1]), BF16).at[place].set(part)[: SENDERS * EXTRA]
-        got = lax.all_to_all(rows.reshape(SENDERS, EXTRA, -1), "dom", 0, 0, tiled=True).astype(F32).sum(0)
-        take = (owner == my_index) & here
-        add = jnp.where(take[:, None], got[jnp.clip(slot, 0, EXTRA - 1)], 0.0)
-        local = global_ids % NODES_HERE
-        return r + 1, own_k.at[local].add(add[:, :COLS]), own_v.at[local].add(add[:, COLS:])
-
-    start = (jnp.asarray(1, jnp.int32), own_k, own_v)
+
+        def summed(part):
+            rows = jnp.zeros((SENDERS * EXTRA + 1, COLS), BF16).at[place].set(part)[: SENDERS * EXTRA]
+            got = lax.all_to_all(rows.reshape(SENDERS, EXTRA, -1), "dom", 0, 0, tiled=True).astype(F32).sum(0)
+            return jnp.where(((owner == my_index) & here)[:, None], got[jnp.clip(slot, 0, EXTRA - 1)], 0.0)
+
+        return r + 1, more_k + summed(part_k), more_v + summed(part_v)
+
+    zeros = jnp.zeros((BLOCK, COLS), F32)
+    start = (jnp.asarray(1, jnp.int32), zeros, zeros)
     return lax.while_loop(lambda state: state[0] < rounds, body, start)[1:]
 
 
@@ -860,30 +871,33 @@
     key_swaps = [swapped(own_keys, m) for m in range(EXPANDERS)]
     plan = run_plan(block_mask, halo_count)
     prepared = run_prepare(query, cotangent)
+    own_values_late, *prepared = lax.optimization_barrier((own_values, *prepared))
+    value_swaps = [swapped(own_values_late, m) for m in range(EXPANDERS)]
     halo_v = lax.all_to_all(out_v, "dom", 0, 0, tiled=True)
     part, keys, turned_k = run_scores(plan, prepared[0], own_keys, halo_k, gids, glob)
-    own_values_late, part = lax.optimization_barrier((own_values, part))
     part, *key_swaps = lax.optimization_barrier((part, *key_swaps))
-    value_swaps = [swapped(own_values_late, m) for m in range(EXPANDERS)]
     pairs, scores = run_partner_keys(exp_rows, key_swaps, query)
-    values, turned_v = run_turn(own_values, halo_v, gids, glob)
     away, scores = lax.optimization_barrier((away, scores))
     others = [swapped(away, m) for m in range(EXPANDERS)]
-    own_v, back_v, glob_v, out_t, local, lse = run_values(plan, keys, turned_v, prepared, part, scores, gids)
+    own_v, back_v, glob_v, out_t, local, lse = run_values(
+        plan, keys, own_values, halo_v, glob, prepared, part, scores, gids
+    )
     local, *value_swaps = lax.optimization_barrier((local, *value_swaps))
     value_pairs, back, delta, back_v = run_finish(
         me, exp_rows, value_swaps, cotangent, scores, lse, local, back_v
     )
     returned_v = lax.all_to_all(back_v, "dom", 0, 0, tiled=True)
-    query_t, own_k, back_k, glob_k = run_keys(plan, keys, turned_k, values, prepared, lse, delta, gids)
-    own_k, returned_v, *others = lax.optimization_barrier((own_k, returned_v, *others))
-    own_k, own_v = more_grads(rounds, global_ids, my_index, glob_k, glob_v, own_k, own_v)
-    back_k, own_k, own_v = lax.optimization_barrier((back_k, own_k, own_v))
+    query_t, own_k, back_k, glob_k = run_keys(
+        plan, keys, turned_k, own_values, halo_v, glob, prepared, lse, delta, gids
+    )
+    glob_k, returned_v, *others = lax.optimization_barrier((glob_k, returned_v, *others))
+    more_k, more_v = more_grads(rounds, global_ids, my_index, glob_k, glob_v)
+    back_k, more_k, more_v = lax.optimization_barrier((back_k, more_k, more_v))
     returned_k = lax.all_to_all(back_k, "dom", 0, 0, tiled=True)
     own_k, pre = run_value_back(
-        me, feat, own_v, returned_v, own_k, rows, others, gids, w_query, w_value, query_t, back, pairs
-    )
-    mine, *away = run_key_back(me, feat, own_k, returned_k, rows, gids, w_key, pre)
+        me, feat, own_v, returned_v, own_k, rows, others, gids, w_query, w_value, query_t, back, pairs, more_v
+    )
+    mine, *away = run_key_back(me, feat, own_k, returned_k, rows, gids, w_key, pre, more_k)
     out_t, mine = lax.optimization_barrier((out_t, mine))
     attended = run_attend(out_t, back, value_pairs)
     for k in (2, 1, 3):

time: 187 us -> 180 us (0.963)
  starting transfers between devices: 51.4 us -> 46.5 us
    pallas_call x12 -> x11, Pallas kernels: 111 us -> 110 us  [call(): pl.pallas_call(kernel, out_shape=outs, in_specs=ins, out_specs=out_spaces...]
    unnamed x28 -> x26, local copies, waits for them, and re-layouts: 3.48 us -> 4.14 us
  transfers between devices with their start and end apart: 19 -> 19, of which waited for: 5 -> 5; matrix products, arithmetic and copies ran while one was open for 1% -> 0% of each run, Pallas kernels for 52% -> 54%
where the time goes in v8:
time: 180 us; the launch traced here: 179 us
  Pallas kernels  110 us (61%)
  starting transfers between devices  46.5 us (26%)
  waiting for transfers between devices  14.6 us (8%)
  local copies, waits for them, and re-layouts  4.82 us (3%)
    pallas_call x11, Pallas kernels, call(): pl.pallas_call(kernel, out_shape=outs, in_specs=ins, out_specs=out_spaces...  110 us
    ppermute x12, starting transfers between devices, swapped(): lax.ppermute(value, 'dom', [(i, i ^ 1 << bit) for i in range(dom_count)])  13 us
    all_to_all x1, starting transfers between devices, on_device(): halo_k = lax.all_to_all(out_k, 'dom', 0, 0, tiled=True)  8.27 us
    all_to_all x1, starting transfers between devices, on_device(): returned_k = lax.all_to_all(back_k, 'dom', 0, 0, tiled=True)  7.4 us
    ppermute x3, waiting for transfers between devices, on_device(): lax.ppermute(away[k - 1], 'feat', [(i, (i + k) % 4) for i in range(4)])  6.92 us
    all_to_all x1, starting transfers between devices, on_device(): returned_v = lax.all_to_all(back_v, 'dom', 0, 0, tiled=True)  6.92 us
    ppermute x3, starting transfers between devices, on_device(): lax.ppermute(away[k - 1], 'feat', [(i, (i + k) % 4) for i in range(4)])  6.51 us
    all_to_all x1, starting transfers between devices, on_device(): halo_v = lax.all_to_all(out_v, 'dom', 0, 0, tiled=True)  4.32 us
  transfers between devices with their start and end apart: 19, of which 5 were waited for; matrix products, arithmetic and copies ran while one was open for 0% of the time, Pallas kernels for 54%

profile of v8, /device:TPU:0, one launch (start us, length us, event | category | flops | bytes accessed | tf_op | source)
XLA Modules:
  0.0 179.1 jit_solution(4824341859572789206)
XLA Ops:
  0.6 0.7 negate_bitcast_fusion
  1.3 7.5 %project.1 = (bf16[1024,128]{1,0:T(8,128)(2,1)}, bf16[1024,128]{1,0:T(8,128)(2,1)S(1)}, bf16[1024,128]{1,0:T(8,128)(2,1)S(1)}, bf16[32,144,128]{2,1,0:T(8,128)(2...) custom-call(s32[1]{0:T(128)} %bitcast.13.me_ref, bf16[1024,512]{1,0:T(8,128)(2,1)} %x_ref.1, ...), custom_call_target="tpu_custom_call" | custom-call | flops 3000000000 | bytes 4000000 | tf_op jit(solution)/shard_map/project/pallas_call | solution.py:604
  8.8 0.0 copy-done.5
  8.8 0.6 while.27
  9.4 8.3 %all-to-all-start.3 = ((bf16[32,144,128]{2,1,0:T(8,128)(2,1)}), bf16[32,144,128]{2,1,0:T(8,128)(2,1)S(1)}, u32[]{:S(2)}, u32[]{:S(2)}) async-start(bf16[32,144,128]{2,1,0:T(8,128)(2,1)} %get-tuple-element.326), calls=%async_computation.3 | async-start | bytes 2359296 | tf_op jit(solution)/shard_map/all_to_all | solution.py:870
  17.7 0.4 collective-permute-start
  18.0 1.7 collective-permute-start.1
  19.7 2.7 %collective-permute-start.2 = (bf16[1024,128]{1,0:T(8,128)(2,1)S(1)}, bf16[1024,128]{1,0:T(8,128)(2,1)}, u32[]{:S(2)}, u32[]{:S(2)}) collective-permute-start(bf16[1024,128]{1,0:T(8,128)(2,1)S(1)} %get-tuple-element.626), channel_id=1, source_target_pairs={{0,16},{4,20},{8,24},{12,28},{16,0},{20,4},{24,8},{28,12},{32,48},... | collective-permute-start | bytes 786440 | tf_op jit(solution)/shard_map/ppermute | solution.py:857
  22.4 1.5 collective-permute-start.3
  23.9 2.7 %prepare.1 = (bf16[8,128,256]{2,1,0:T(8,128)(2,1)}, bf16[8,256,128]{2,1,0:T(8,128)(2,1)}, bf16[8,128,256]{2,1,0:T(8,128)(2,1)}, bf16[8,256,128]{2,1,0:T(8,128)(2,1)}) custom-call(bf16[1024,128]{1,0:T(8,128)(2,1)} %get-tuple-element.315.q_ref, bf16[1024,128]{1,0:T(8,128)(2,1)} %cot_ref.5), custom_call_target="tpu_custom_call" | custom-call | flops 2000000000 | bytes 4000000 | tf_op jit(solution)/shard_map/prepare/pallas_call | solution.py:604
  26.6 0.0 collective-permute-start.4
  26.6 0.7 reshape.399.mask_ref
  27.3 4.7 %plan.1 = (s32[456]{0:T(512)}, s32[64]{0:T(128)}, s32[64]{0:T(128)}, s32[1]{0:T(128)}, s32[42]{0:T(128)}) custom-call(s32[320]{0:T(512)} %reshape.399.mask_ref, s32[32]{0:T(128)} %bitcast.91), custom_call_target="tpu_custom_call" | custom-call | bytes 4000000 | tf_op jit(solution)/shard_map/plan/pallas_call | solution.py:604
  31.9 4.2 %all-to-all-done.3.hk_ref = bf16[32,144,128]{2,1,0:T(8,128)(2,1)S(1)} async-done(((bf16[32,144,128]{2,1,0:T(8,128)(2,1)}), bf16[32,144,128]{2,1,0:T(8,128)(2,1)S(1)}, u32[]{:S(2)}, u32[]{:S(2)}) %all-to-all-start.3) | async-done | bytes 1179680 | tf_op jit(solution)/shard_map/all_to_all | solution.py:870
  36.1 4.3 %all-to-all-start.4 = ((bf16[32,144,128]{2,1,0:T(8,128)(2,1)}), bf16[32,144,128]{2,1,0:T(8,128)(2,1)S(1)}, u32[]{:S(2)}, u32[]{:S(2)}) async-start(bf16[32,144,128]{2,1,0:T(8,128)(2,1)} %get-tuple-element.329), calls=%async_computation.4 | async-start | bytes 2359296 | tf_op jit(solution)/shard_map/all_to_all | solution.py:876
  40.5 14.8 %scores.1 = (f32[8,256]{1,0:T(8,128)}, bf16[42,128,128]{2,1,0:T(8,128)(2,1)}, bf16[42,128,128]{2,1,0:T(8,128)(2,1)}) custom-call(s32[456]{0:T(512)} %get-tuple-element.309.list_ref, s32[64]{0:T(128)} %get-tuple-element.310.where_ref, s32[64]{0:T(128)} %get-tuple-element.311.block_ref, s32[1]{0:T(128)} %get-tuple-element.312.count_ref, ...), custom_call_target="tpu_custom_call" | custom-call | flops 12000000000 | bytes 4000000 | tf_op jit(solution)/shard_map/scores/pallas_call | solution.py:604
  55.3 0.0 collective-permute-done.t0_ref
  55.3 1.8 collective-permute-start.5
  57.1 0.0 collective-permute-done.1.t1_ref
  57.1 1.9 %collective-permute-start.6 = (bf16[1024,128]{1,0:T(8,128)(2,1)S(1)}, bf16[1024,128]{1,0:T(8,128)(2,1)S(1)}, u32[]{:S(2)}, u32[]{:S(2)}) collective-permute-start(bf16[1024,128]{1,0:T(8,128)(2,1)S(1)} %get-tuple-element.621), channel_id=1, source_target_pairs={{0,16},{4,20},{8,24},{12,28},{16,0},{20,4},{24,8},{28,12},{32,48},... | collective-permute-start | bytes 786440 | tf_op jit(solution)/shard_map/ppermute | solution.py:857
  59.0 0.0 collective-permute-done.2.t2_ref
  59.0 1.5 collective-permute-start.7
  60.4 0.0 collective-permute-done.3.t3_ref
  60.4 5.4 %partners.1 = (bf16[32,128,128]{2,1,0:T(8,128)(2,1)}, f32[4,8,256]{2,1,0:T(8,128)}) custom-call(s32[4,1024]{1,0:T(4,128)} %exp_ref.5, bf16[1024,128]{1,0:T(8,128)(2,1)} %collective-permute-done.t0_ref, bf16[1024,128]{1,0:T(8,128)(2,1)} %collective-permute-done.1.t1_ref, bf16[1024,128]{1,0:T(8,128)(2,1)} %collective-permute-done.2.t2_ref, ...), custom_call_target="tpu_custom_call" | custom-call | flops 5000000000 | bytes 4000000 | tf_op jit(solution)/shard_map/partners/pallas_call | solution.py:604
  65.8 0.2 collective-permute-start.10
  66.0 0.0 all-to-all-done.4.hv_ref
  66.0 1.0 copy-done.1
  67.0 18.9 %values.1 = (f32[1024,128]{1,0:T(8,128)}, bf16[32,176,128]{2,1,0:T(8,128)(2,1)}, bf16[128,128]{1,0:T(8,128)(2,1)S(1)}, f32[8,128,256]{2,1,0:T(8,128)}, f32[8,256]{1,0:T(8,128)}, /*index=5*/f32[8,256]{1,0:T(8,128)}) custom-call(s32[456]{0:T(512)} %get-tuple-element.309.list_ref, s32[64]{0:T(128)} %get-tuple-element.310.where_ref, ...), custom_call_target="tpu_custom_call" | custom-call | flops 20000000000 | bytes 4000000 | tf_op jit(solution)/shard_map/values/pallas_call | solution.py:604
  85.9 0.0 collective-permute-done.4.t0_ref
  85.9 0.0 copy-start.9
  85.9 1.2 collective-permute-start.11
  87.0 0.0 collective-permute-done.5.t1_ref
  87.0 0.0 collective-permute-start.8
  87.1 0.0 collective-permute-done.6.t2_ref
  87.1 0.4 collective-permute-start.9
  87.5 0.0 collective-permute-done.7.t3_ref
  87.5 0.3 copy-done.10
  87.8 0.1 copy-done.11
  87.8 0.3 copy-done.12
  88.2 6.2 %finish.1 = (bf16[32,128,128]{2,1,0:T(8,128)(2,1)}, bf16[4,32,128]{2,1,0:T(8,128)(2,1)}, f32[8,256]{1,0:T(8,128)}, bf16[32,176,128]{2,1,0:T(8,128)(2,1)}) custom-call(s32[1]{0:T(128)} %bitcast.13.me_ref, s32[4,1024]{1,0:T(4,128)} %exp_ref.5, bf16[1024,128]{1,0:T(8,128)(2,1)} %copy-done.9, ...), custom_call_target="tpu_custom_call", output_to_operand_aliasing={{3}: (10, {})} | custom-call | flops 5000000000 | bytes 4000000 | tf_op jit(solution)/shard_map/finish/pallas_call | solution.py:604
  94.3 6.9 %all-to-all-start.5 = ((bf16[32,176,128]{2,1,0:T(8,128)(2,1)}), bf16[32,176,128]{2,1,0:T(8,128)(2,1)S(1)}, u32[]{:S(2)}, u32[]{:S(2)}) async-start(bf16[32,176,128]{2,1,0:T(8,128)(2,1)} %get-tuple-element.356), calls=%async_computation.5 | async-start | bytes 2883584 | tf_op jit(solution)/shard_map/all_to_all | solution.py:889
  101.3 25.9 %keys.1 = (f32[8,128,256]{2,1,0:T(8,128)}, f32[1024,128]{1,0:T(8,128)}, bf16[32,144,128]{2,1,0:T(8,128)(2,1)}, bf16[128,128]{1,0:T(8,128)(2,1)S(1)}) custom-call(s32[456]{0:T(512)} %get-tuple-element.309.list_ref, s32[64]{0:T(128)} %get-tuple-element.310.where_ref, s32[64]{0:T(128)} %get-tuple-element.311.block_ref, s32[1]{0:T(128)} %get-tuple-element.312.count_ref, ...), custom_call_target="tpu_custom_call" | custom-call | flops 24999999488 | bytes 4000000 | tf_op jit(solution)/shard_map/keys/pallas_call | solution.py:604
  127.1 0.0 collective-permute-done.10.o2_ref
  127.1 0.0 collective-permute-done.11.o3_ref
  127.2 0.0 collective-permute-done.8.o0_ref
  127.2 0.0 collective-permute-done.9.o1_ref
  127.2 0.0 all-to-all-done.5.ret_ref
  127.2 0.7 copy-done.7
  128.0 0.2 copy-done.8
  128.1 0.4 copy-done
  128.6 0.6 while.28
  129.2 7.4 %all-to-all-start.6 = ((bf16[32,144,128]{2,1,0:T(8,128)(2,1)}), bf16[32,144,128]{2,1,0:T(8,128)(2,1)S(1)}, u32[]{:S(2)}, u32[]{:S(2)}) async-start(bf16[32,144,128]{2,1,0:T(8,128)(2,1)} %get-tuple-element.374), calls=%async_computation.6 | async-start | bytes 2359296 | tf_op jit(solution)/shard_map/all_to_all | solution.py:896
  136.6 14.6 %value_back.1 = (f32[1024,128]{1,0:T(8,128)}, f32[4,1024,128]{2,1,0:T(8,128)}) custom-call(s32[1]{0:T(128)} %bitcast.13.me_ref, s32[1]{0:T(128)} %bitcast.18.feat_ref, f32[1024,128]{1,0:T(8,128)} %get-tuple-element.342.ownv_ref, bf16[32,176,128]{2,1,0:T(8,128)(2,1)} %copy-done, f32[1024,128]{1,0:T(8,128)} %get-tuple-element.359.ownk_ref, ...), custom_call_target="tpu_custom_call" | custom-call | flops 12000000000 | bytes 4000000 | tf_op jit(solution)/shard_map/value_back/pallas_call | solution.py:604
  151.2 3.5 %all-to-all-done.6.ret_ref = bf16[32,144,128]{2,1,0:T(8,128)(2,1)S(1)} async-done(((bf16[32,144,128]{2,1,0:T(8,128)(2,1)}), bf16[32,144,128]{2,1,0:T(8,128)(2,1)S(1)}, u32[]{:S(2)}, u32[]{:S(2)}) %all-to-all-start.6) | async-done | bytes 1179680 | tf_op jit(solution)/shard_map/all_to_all | solution.py:896
  154.7 1.0 copy-done.3
  155.8 6.2 %key_back.1 = (f32[1024,128]{1,0:T(8,128)}, bf16[1024,128]{1,0:T(8,128)(2,1)}, bf16[1024,128]{1,0:T(8,128)(2,1)}, bf16[1024,128]{1,0:T(8,128)(2,1)}) custom-call(s32[1]{0:T(128)} %bitcast.13.me_ref, s32[1]{0:T(128)} %bitcast.18.feat_ref, f32[1024,128]{1,0:T(8,128)} %get-tuple-element.373.acck_ref, bf16[32,144,128]{2,1,0:T(8,128)(2,1)} %copy-done.3, ...), custom_call_target="tpu_custom_call" | custom-call | flops 8000000000 | bytes 4000000 | tf_op jit(solution)/shard_map/key_back/pallas_call | solution.py:604
  162.0 3.3 %collective-permute-start.12 = (bf16[1024,128]{1,0:T(8,128)(2,1)}, bf16[1024,128]{1,0:T(8,128)(2,1)S(1)}, u32[]{:S(2)}, u32[]{:S(2)}) collective-permute-start(bf16[1024,128]{1,0:T(8,128)(2,1)} %get-tuple-element.381), channel_id=1, source_target_pairs={{0,2},{1,3},{2,0},{3,1},{4,6},{5,7},{6,4},{7,5},{8,10},{9,11},{10,... | collective-permute-start | bytes 786440 | tf_op jit(solution)/shard_map/ppermute | solution.py:904
  165.2 0.7 collective-permute-start.13
  165.9 2.6 %collective-permute-start.14 = (bf16[1024,128]{1,0:T(8,128)(2,1)}, bf16[1024,128]{1,0:T(8,128)(2,1)S(1)}, u32[]{:S(2)}, u32[]{:S(2)}) collective-permute-start(bf16[1024,128]{1,0:T(8,128)(2,1)} %get-tuple-element.383), channel_id=1, source_target_pairs={{0,3},{1,0},{2,1},{3,2},{4,7},{5,4},{6,5},{7,6},{8,11},{9,8},{10,9... | collective-permute-start | bytes 786440 | tf_op jit(solution)/shard_map/ppermute | solution.py:904
  168.5 2.8 %attend.1 = bf16[1024,128]{1,0:T(8,128)(2,1)} custom-call(f32[8,128,256]{2,1,0:T(8,128)} %get-tuple-element.378.out_t_ref, bf16[4,32,128]{2,1,0:T(8,128)(2,1)} %get-tuple-element.365.back_ref, bf16[32,128,128]{2,1,0:T(8,128)(2,1)} %get-tuple-element.379.pair_ref), custom_call_target="tpu_custom_call" | custom-call | flops 2000000000 | bytes 4000000 | tf_op jit(solution)/shard_map/attend/pallas_call | solution.py:604
  171.3 1.6 collective-permute-done.12
  172.9 4.9 %collective-permute-done.13 = bf16[1024,128]{1,0:T(8,128)(2,1)S(1)} collective-permute-done((bf16[1024,128]{1,0:T(8,128)(2,1)}, bf16[1024,128]{1,0:T(8,128)(2,1)S(1)}, u32[]{:S(2)}, u32[]{:S(2)}) %collective-permute-start.13) | collective-permute-done | bytes 262176 | tf_op jit(solution)/shard_map/ppermute | solution.py:904
  177.8 0.4 collective-permute-done.14
  178.2 0.8 add_convert_fusion
  (19 shorter events, 0.1 us)
Async XLA Ops:
  1.3 7.5 %copy-start.5 = (s32[128]{0:T(128)S(1)}, s32[128]{0:T(128)}, u32[]{:S(2)}) copy-start(s32[128]{0:T(128)} %param.23) | copy-start | bytes 1540
  9.4 26.7 %all-to-all-start.3 = ((bf16[32,144,128]{2,1,0:T(8,128)(2,1)}), bf16[32,144,128]{2,1,0:T(8,128)(2,1)S(1)}, u32[]{:S(2)}, u32[]{:S(2)}) async-start(bf16[32,144,128]{2,1,0:T(8,128)(2,1)} %get-tuple-element.326), calls=%async_computation.3 | async-start | bytes 2359296 | tf_op jit(solution)/shard_map/all_to_all | solution.py:870
  17.7 37.6 %collective-permute-start = (bf16[1024,128]{1,0:T(8,128)(2,1)S(1)}, bf16[1024,128]{1,0:T(8,128)(2,1)}, u32[]{:S(2)}, u32[]{:S(2)}) collective-permute-start(bf16[1024,128]{1,0:T(8,128)(2,1)S(1)} %get-tuple-element.626), channel_id=1, source_target_pairs={{0,4},{4,0},{8,12},{12,8},{16,20},{20,16},{24,28},{28,24},{32,36},... | collective-permute-start | bytes 786440 | tf_op jit(solution)/shard_map/ppermute | solution.py:857
  18.0 39.0 %collective-permute-start.1 = (bf16[1024,128]{1,0:T(8,128)(2,1)S(1)}, bf16[1024,128]{1,0:T(8,128)(2,1)}, u32[]{:S(2)}, u32[]{:S(2)}) collective-permute-start(bf16[1024,128]{1,0:T(8,128)(2,1)S(1)} %get-tuple-element.626), channel_id=1, source_target_pairs={{0,8},{4,12},{8,0},{12,4},{16,24},{20,28},{24,16},{28,20},{32,40},... | collective-permute-start | bytes 786440 | tf_op jit(solution)/shard_map/ppermute | solution.py:857
  19.7 39.2 %collective-permute-start.2 = (bf16[1024,128]{1,0:T(8,128)(2,1)S(1)}, bf16[1024,128]{1,0:T(8,128)(2,1)}, u32[]{:S(2)}, u32[]{:S(2)}) collective-permute-start(bf16[1024,128]{1,0:T(8,128)(2,1)S(1)} %get-tuple-element.626), channel_id=1, source_target_pairs={{0,16},{4,20},{8,24},{12,28},{16,0},{20,4},{24,8},{28,12},{32,48},... | collective-permute-start | bytes 786440 | tf_op jit(solution)/shard_map/ppermute | solution.py:857
  22.4 38.0 %collective-permute-start.3 = (bf16[1024,128]{1,0:T(8,128)(2,1)S(1)}, bf16[1024,128]{1,0:T(8,128)(2,1)}, u32[]{:S(2)}, u32[]{:S(2)}) collective-permute-start(bf16[1024,128]{1,0:T(8,128)(2,1)S(1)} %get-tuple-element.626), channel_id=1, source_target_pairs={{0,32},{4,36},{8,40},{12,44},{16,48},{20,52},{24,56},{28,60},{32,0... | collective-permute-start | bytes 786440 | tf_op jit(solution)/shard_map/ppermute | solution.py:857
  23.9 2.7 %copy-start.6 = (s32[8,40]{1,0:T(8,128)S(1)}, s32[8,40]{1,0:T(8,128)}, u32[]{:S(2)}) copy-start(s32[8,40]{1,0:T(8,128)} %param.21) | copy-start | bytes 3844
  26.6 59.3 %collective-permute-start.4 = (bf16[1024,128]{1,0:T(8,128)(2,1)S(1)}, bf16[1024,128]{1,0:T(8,128)(2,1)S(1)}, u32[]{:S(2)}, u32[]{:S(2)}) collective-permute-start(bf16[1024,128]{1,0:T(8,128)(2,1)S(1)} %get-tuple-element.621), channel_id=1, source_target_pairs={{0,4},{4,0},{8,12},{12,8},{16,20},{20,16},{24,28},{28,24},{32,36},... | collective-permute-start | bytes 786440 | tf_op jit(solution)/shard_map/ppermute | solution.py:857
  36.1 4.3 %copy-start.2 = (bf16[32,144,128]{2,1,0:T(8,128)(2,1)}, bf16[32,144,128]{2,1,0:T(8,128)(2,1)S(1)}, u32[]{:S(2)}) copy-start(bf16[32,144,128]{2,1,0:T(8,128)(2,1)S(1)} %all-to-all-done.3.hk_ref) | copy-start | bytes 3538948
  36.1 29.9 %all-to-all-start.4 = ((bf16[32,144,128]{2,1,0:T(8,128)(2,1)}), bf16[32,144,128]{2,1,0:T(8,128)(2,1)S(1)}, u32[]{:S(2)}, u32[]{:S(2)}) async-start(bf16[32,144,128]{2,1,0:T(8,128)(2,1)} %get-tuple-element.329), calls=%async_computation.4 | async-start | bytes 2359296 | tf_op jit(solution)/shard_map/all_to_all | solution.py:876
  55.3 31.8 %collective-permute-start.5 = (bf16[1024,128]{1,0:T(8,128)(2,1)S(1)}, bf16[1024,128]{1,0:T(8,128)(2,1)S(1)}, u32[]{:S(2)}, u32[]{:S(2)}) collective-permute-start(bf16[1024,128]{1,0:T(8,128)(2,1)S(1)} %get-tuple-element.621), channel_id=1, source_target_pairs={{0,8},{4,12},{8,0},{12,4},{16,24},{20,28},{24,16},{28,20},{32,40},... | collective-permute-start | bytes 786440 | tf_op jit(solution)/shard_map/ppermute | solution.py:857
  57.1 30.0 %collective-permute-start.6 = (bf16[1024,128]{1,0:T(8,128)(2,1)S(1)}, bf16[1024,128]{1,0:T(8,128)(2,1)S(1)}, u32[]{:S(2)}, u32[]{:S(2)}) collective-permute-start(bf16[1024,128]{1,0:T(8,128)(2,1)S(1)} %get-tuple-element.621), channel_id=1, source_target_pairs={{0,16},{4,20},{8,24},{12,28},{16,0},{20,4},{24,8},{28,12},{32,48},... | collective-permute-start | bytes 786440 | tf_op jit(solution)/shard_map/ppermute | solution.py:857
  59.0 28.5 %collective-permute-start.7 = (bf16[1024,128]{1,0:T(8,128)(2,1)S(1)}, bf16[1024,128]{1,0:T(8,128)(2,1)S(1)}, u32[]{:S(2)}, u32[]{:S(2)}) collective-permute-start(bf16[1024,128]{1,0:T(8,128)(2,1)S(1)} %get-tuple-element.621), channel_id=1, source_target_pairs={{0,32},{4,36},{8,40},{12,44},{16,48},{20,52},{24,56},{28,60},{32,0... | collective-permute-start | bytes 786440 | tf_op jit(solution)/shard_map/ppermute | solution.py:857
  65.8 61.3 %collective-permute-start.10 = (bf16[1056,256]{1,0:T(8,128)(2,1)}, bf16[1056,256]{1,0:T(8,128)(2,1)}, u32[]{:S(2)}, u32[]{:S(2)}) collective-permute-start(bf16[1056,256]{1,0:T(8,128)(2,1)} %get-tuple-element.357), channel_id=1, source_target_pairs={{0,16},{4,20},{8,24},{12,28},{16,0},{20,4},{24,8},{28,12},{32,48},... | collective-permute-start | bytes 1622024 | tf_op jit(solution)/shard_map/ppermute | solution.py:857
  66.0 1.0 copy-start.1
  85.9 1.6 copy-start.9
  85.9 41.3 %collective-permute-start.11 = (bf16[1056,256]{1,0:T(8,128)(2,1)}, bf16[1056,256]{1,0:T(8,128)(2,1)S(1)}, u32[]{:S(2)}, u32[]{:S(2)}) collective-permute-start(bf16[1056,256]{1,0:T(8,128)(2,1)} %get-tuple-element.357), channel_id=1, source_target_pairs={{0,32},{4,36},{8,40},{12,44},{16,48},{20,52},{24,56},{28,60},{32,0... | collective-permute-start | bytes 1622024 | tf_op jit(solution)/shard_map/ppermute | solution.py:857
  87.0 0.7 copy-start.10
  87.0 40.1 %collective-permute-start.8 = (bf16[1056,256]{1,0:T(8,128)(2,1)}, bf16[1056,256]{1,0:T(8,128)(2,1)S(1)}, u32[]{:S(2)}, u32[]{:S(2)}) collective-permute-start(bf16[1056,256]{1,0:T(8,128)(2,1)} %get-tuple-element.357), channel_id=1, source_target_pairs={{0,4},{4,0},{8,12},{12,8},{16,20},{20,16},{24,28},{28,24},{32,36},... | collective-permute-start | bytes 1622024 | tf_op jit(solution)/shard_map/ppermute | solution.py:857
  87.1 0.8 copy-start.11
  87.1 40.1 %collective-permute-start.9 = (bf16[1056,256]{1,0:T(8,128)(2,1)}, bf16[1056,256]{1,0:T(8,128)(2,1)}, u32[]{:S(2)}, u32[]{:S(2)}) collective-permute-start(bf16[1056,256]{1,0:T(8,128)(2,1)} %get-tuple-element.357), channel_id=1, source_target_pairs={{0,8},{4,12},{8,0},{12,4},{16,24},{20,28},{24,16},{28,20},{32,40},... | collective-permute-start | bytes 1622024 | tf_op jit(solution)/shard_map/ppermute | solution.py:857
  87.5 0.7 copy-start.12
  94.3 32.8 %all-to-all-start.5 = ((bf16[32,176,128]{2,1,0:T(8,128)(2,1)}), bf16[32,176,128]{2,1,0:T(8,128)(2,1)S(1)}, u32[]{:S(2)}, u32[]{:S(2)}) async-start(bf16[32,176,128]{2,1,0:T(8,128)(2,1)} %get-tuple-element.356), calls=%async_computation.5 | async-start | bytes 2883584 | tf_op jit(solution)/shard_map/all_to_all | solution.py:889
  127.1 0.8 copy-start.7
  127.2 1.0 copy-start.8
  127.2 1.4 copy-start
  129.2 25.6 %all-to-all-start.6 = ((bf16[32,144,128]{2,1,0:T(8,128)(2,1)}), bf16[32,144,128]{2,1,0:T(8,128)(2,1)S(1)}, u32[]{:S(2)}, u32[]{:S(2)}) async-start(bf16[32,144,128]{2,1,0:T(8,128)(2,1)} %get-tuple-element.374), calls=%async_computation.6 | async-start | bytes 2359296 | tf_op jit(solution)/shard_map/all_to_all | solution.py:896
  154.7 1.0 copy-start.3
  162.0 11.0 %collective-permute-start.12 = (bf16[1024,128]{1,0:T(8,128)(2,1)}, bf16[1024,128]{1,0:T(8,128)(2,1)S(1)}, u32[]{:S(2)}, u32[]{:S(2)}) collective-permute-start(bf16[1024,128]{1,0:T(8,128)(2,1)} %get-tuple-element.381), channel_id=1, source_target_pairs={{0,2},{1,3},{2,0},{3,1},{4,6},{5,7},{6,4},{7,5},{8,10},{9,11},{10,... | collective-permute-start | bytes 786440 | tf_op jit(solution)/shard_map/ppermute | solution.py:904
  165.2 12.6 %collective-permute-start.13 = (bf16[1024,128]{1,0:T(8,128)(2,1)}, bf16[1024,128]{1,0:T(8,128)(2,1)S(1)}, u32[]{:S(2)}, u32[]{:S(2)}) collective-permute-start(bf16[1024,128]{1,0:T(8,128)(2,1)} %get-tuple-element.382), channel_id=1, source_target_pairs={{0,1},{1,2},{2,3},{3,0},{4,5},{5,6},{6,7},{7,4},{8,9},{9,10},{10,1... | collective-permute-start | bytes 786440 | tf_op jit(solution)/shard_map/ppermute | solution.py:904
  165.9 12.3 %collective-permute-start.14 = (bf16[1024,128]{1,0:T(8,128)(2,1)}, bf16[1024,128]{1,0:T(8,128)(2,1)S(1)}, u32[]{:S(2)}, u32[]{:S(2)}) collective-permute-start(bf16[1024,128]{1,0:T(8,128)(2,1)} %get-tuple-element.383), channel_id=1, source_target_pairs={{0,3},{1,0},{2,1},{3,2},{4,7},{5,4},{6,5},{7,6},{8,11},{9,8},{10,9... | collective-permute-start | bytes 786440 | tf_op jit(solution)/shard_map/ppermute | solution.py:904
  168.5 9.8 %copy-start.4 = (f32[1024,128]{1,0:T(8,128)S(1)}, f32[1024,128]{1,0:T(8,128)}, u32[]{:S(2)}) copy-start(f32[1024,128]{1,0:T(8,128)} %get-tuple-element.380) | copy-start | bytes 1572868

commit v9 on v8

--- a/solution.py
+++ b/solution.py
@@ -23,6 +23,7 @@
 SCORE_PAIR = 4
 ITEMS = 2
 MAX_ITEMS = 64
+TOGETHER = (0, 3)
 LIST = 56
 EXTRA = 16
 SLOTS = BLOCK + EXTRA
@@ -107,8 +108,8 @@
 
 
 def project_kernel(
-    me_ref, x_ref, wq_ref, wk_ref, wv_ref, cot_ref, rows_ref, exp_ref, gid_ref, q_ref, k_ref, v_ref, outk_ref, outv_ref,
-    away_ref, rounds_ref, kv_ref, msgk_s, msgv_s, sems,
+    me_ref, x_ref, wq_ref, wk_ref, wv_ref, cot_ref, rows_ref, exp_ref, gid_ref, q_ref, k_ref, v_ref, kv_ref, outk_ref, outv_ref,
+    away_ref, rounds_ref, msgk_s, msgv_s, sems,
 ):
     most = jnp.max(owner_ranks(gid_ref[...])[0].astype(F32)).astype(jnp.int32)
     rounds_ref[0] = (most + EXTRA) // EXTRA
@@ -157,11 +158,11 @@
             send.wait()
 
 
-def gather_partner(exp_ref, m, table):
+def gather_partner(exp_ref, m, table, first_col=0):
     blocks = []
     for t in range(0, Q_BLOCKS, 4):
         hot = one_hot_of_rows([exp_row(exp_ref, m, t + u) for u in range(4)])
-        got = dot(hot, table[...]).astype(BF16)
+        got = dot(hot, table[:, first_col : first_col + COLS]).astype(BF16)
         blocks += [got[u * BLOCK : (u + 1) * BLOCK] for u in range(4)]
     return blocks
 
@@ -203,7 +204,7 @@
     delta = local_ref[...]
     probs, dprobs = [], []
     for m, table in enumerate((t0_ref, t1_ref, t2_ref, t3_ref)):
-        blocks = gather_partner(exp_ref, m, table)
+        blocks = gather_partner(exp_ref, m, table, table.shape[1] - COLS)
         prob = jnp.exp(sp_ref[m] - lse)
         dprob = head_sums(cot_ref, blocks, picks)
         delta += prob * dprob
@@ -627,6 +628,7 @@
             shape((NODES_HERE, COLS)),
             shape((NODES_HERE, COLS)),
             shape((NODES_HERE, COLS)),
+            shape((NODES_HERE, 2 * COLS)),
             shape((SENDERS, SLOTS, COLS)),
             shape((SENDERS, SLOTS, COLS)),
             shape((NODES_HERE + EXPANDERS * Q_BLOCKS, 2 * COLS)),
@@ -636,9 +638,8 @@
         name="project",
         mib=56,
         flops=3_000_000_000,
-        out_spaces=(vmem(), vmem(), vmem(), anywhere, anywhere, vmem(), smem()),
+        out_spaces=(vmem(), vmem(), vmem(), vmem(), anywhere, anywhere, vmem(), smem()),
         scratch=[
-            pltpu.VMEM((NODES_HERE, 2 * COLS), BF16),
             pltpu.VMEM((SENDERS, SLOTS, COLS), BF16),
             pltpu.VMEM((SENDERS, SLOTS, COLS), BF16),
             pltpu.SemaphoreType.DMA((2, SENDERS // GROUP)),
@@ -776,7 +777,7 @@
 
 
 def run_key_back(me, feat, own_k, returned_k, rows, gids, w_key, pre, more):
-    anywhere = pl.BlockSpec(memory_space=pl.ANY)
+    anywhere = pl.BlockSpec(memory_space=pltpu.HBM)
     return call(
         key_back_kernel,
         [smem()] * 2 + [anywhere] + [vmem()] * 4 + [anywhere, vmem()],
@@ -789,7 +790,7 @@
             pltpu.SemaphoreType.DMA((2,)),
         ],
         name="key_back",
-        mib=56,
+        mib=20,
         flops=8_000_000_000,
     )
 
@@ -803,11 +804,12 @@
 def more_globals(rounds, global_ids, my_index, own_k, own_v):
     def body(state):
         r, glob = state
-        owner, rank = ranks(global_ids + jnp.minimum(r, 0))
+        ids = global_ids + jnp.minimum(r, 0)
+        owner, rank = ranks(ids)
         slot = rank - r * EXTRA
         here = (slot >= 0) & (slot < EXTRA)
         place = jnp.where((owner == my_index) & here, slot, EXTRA)
-        local = jnp.where(here, global_ids % NODES_HERE, 0)
+        local = jnp.where(here, ids % NODES_HERE, 0)
         found = jnp.concatenate([own_k[local], own_v[local]], axis=1)
         rows = jnp.zeros((EXTRA + 1, 2 * COLS), BF16).at[place].set(found)[:EXTRA]
         got = lax.all_to_all(jnp.broadcast_to(rows[None], (SENDERS, *rows.shape)), "dom", 0, 0, tiled=True)
@@ -821,7 +823,8 @@
 def more_grads(rounds, global_ids, my_index, part_k, part_v):
     def body(state):
         r, more_k, more_v = state
-        owner, rank = ranks(global_ids + jnp.minimum(r, 0))
+        ids = global_ids + jnp.minimum(r, 0)
+        owner, rank = ranks(ids)
         slot = rank - r * EXTRA
         here = (slot >= 0) & (slot < EXTRA)
         place = jnp.where(here, owner * EXTRA + slot, SENDERS * EXTRA)
@@ -861,18 +864,18 @@
     me = my_index.reshape(1).astype(jnp.int32)
     feat = lax.axis_index("feat").reshape(1).astype(jnp.int32)
 
-    query, own_keys, own_values, out_k, out_v, away, rounds = run_project(
+    query, own_keys, own_values, paired, out_k, out_v, away, rounds = run_project(
         me, features, w_query, w_key, w_value, cotangent, rows, exp_rows, gids
     )
     rounds = rounds[0]
     glob = more_globals(rounds, global_ids, my_index, own_keys, own_values)
     out_k, out_v, glob = lax.optimization_barrier((out_k, out_v, glob))
     halo_k = lax.all_to_all(out_k, "dom", 0, 0, tiled=True)
-    key_swaps = [swapped(own_keys, m) for m in range(EXPANDERS)]
+    key_swaps = [swapped(paired if m in TOGETHER else own_keys, m) for m in range(EXPANDERS)]
     plan = run_plan(block_mask, halo_count)
     prepared = run_prepare(query, cotangent)
     own_values_late, *prepared = lax.optimization_barrier((own_values, *prepared))
-    value_swaps = [swapped(own_values_late, m) for m in range(EXPANDERS)]
+    value_swaps = {m: swapped(own_values_late, m) for m in range(EXPANDERS) if m not in TOGETHER}
     halo_v = lax.all_to_all(out_v, "dom", 0, 0, tiled=True)
     part, keys, turned_k = run_scores(plan, prepared[0], own_keys, halo_k, gids, glob)
     part, *key_swaps = lax.optimization_barrier((part, *key_swaps))
@@ -882,7 +885,8 @@
     own_v, back_v, glob_v, out_t, local, lse = run_values(
         plan, keys, own_values, halo_v, glob, prepared, part, scores, gids
     )
-    local, *value_swaps = lax.optimization_barrier((local, *value_swaps))
+    local, value_swaps = lax.optimization_barrier((local, value_swaps))
+    value_swaps = [value_swaps.get(m, key_swaps[m]) for m in range(EXPANDERS)]
     value_pairs, back, delta, back_v = run_finish(
         me, exp_rows, value_swaps, cotangent, scores, lse, local, back_v
     )

time: 180 us -> 180 us (level)
  Pallas kernels: 110 us -> 105 us
  waiting for transfers between devices: 14.6 us -> 17.6 us
    pallas_call x11, Pallas kernels: 110 us -> 105 us  [call(): pl.pallas_call(kernel, out_shape=outs, in_specs=ins, out_specs=out_spaces...]
    ppermute x3, waiting for transfers between devices: 6.92 us -> 10 us  [on_device(): lax.ppermute(away[k - 1], 'feat', [(i, (i + k) % 4) for i in range(4)])]
    ppermute x12 -> x10, starting transfers between devices: 13 us -> 14.4 us  [swapped(): lax.ppermute(value, 'dom', [(i, i ^ 1 << bit) for i in range(dom_count)])]
  transfers between devices with their start and end apart: 19 -> 17, of which waited for: 5 -> 4; matrix products, arithmetic and copies ran while one was open for 0% -> 0% of each run, Pallas kernels for 54% -> 52%
where the time goes in v9:
time: 180 us; the launch traced here: 179 us
  Pallas kernels  105 us (58%)
  starting transfers between devices  47.8 us (27%)
  waiting for transfers between devices  17.6 us (10%)
  local copies, waits for them, and re-layouts  6.3 us (4%)
    pallas_call x11, Pallas kernels, call(): pl.pallas_call(kernel, out_shape=outs, in_specs=ins, out_specs=out_spaces...  105 us
    ppermute x10, starting transfers between devices, swapped(): lax.ppermute(value, 'dom', [(i, i ^ 1 << bit) for i in range(dom_count)])  14.4 us
    ppermute x3, waiting for transfers between devices, on_device(): lax.ppermute(away[k - 1], 'feat', [(i, (i + k) % 4) for i in range(4)])  10 us
    all_to_all x1, starting transfers between devices, on_device(): returned_k = lax.all_to_all(back_k, 'dom', 0, 0, tiled=True)  9.17 us
    all_to_all x1, starting transfers between devices, on_device(): halo_k = lax.all_to_all(out_k, 'dom', 0, 0, tiled=True)  8.38 us
    all_to_all x1, starting transfers between devices, on_device(): returned_v = lax.all_to_all(back_v, 'dom', 0, 0, tiled=True)  6.29 us
    unnamed x26, local copies, waits for them, and re-layouts  5.62 us
    ppermute x3, starting transfers between devices, on_device(): lax.ppermute(away[k - 1], 'feat', [(i, (i + k) % 4) for i in range(4)])  5.31 us
  transfers between devices with their start and end apart: 17, of which 4 were waited for; matrix products, arithmetic and copies ran while one was open for 0% of the time, Pallas kernels for 52%

profile of v9, /device:TPU:0, one launch (start us, length us, event | category | flops | bytes accessed | tf_op | source)
XLA Modules:
  0.0 179.5 jit_solution(2563381778435138867)
XLA Ops:
  0.6 0.0 copy-start.7
  0.6 7.7 %project.1 = (bf16[1024,128]{1,0:T(8,128)(2,1)}, bf16[1024,128]{1,0:T(8,128)(2,1)S(1)}, bf16[1024,128]{1,0:T(8,128)(2,1)S(1)}, bf16[1024,256]{1,0:T(8,128)(2,1)}...) custom-call(s32[1]{0:T(128)} %bitcast.13.me_ref, ...), custom_call_target="tpu_custom_call" | custom-call | flops 3000000000 | bytes 4000000 | tf_op jit(solution)/shard_map/project/pallas_call | solution.py:605
  8.4 0.0 copy-done.7
  8.4 0.6 while.26
  9.0 0.0 copy-start.11
  9.0 8.4 %all-to-all-start.3 = ((bf16[32,144,128]{2,1,0:T(8,128)(2,1)}), bf16[32,144,128]{2,1,0:T(8,128)(2,1)S(1)}, u32[]{:S(2)}, u32[]{:S(2)}) async-start(bf16[32,144,128]{2,1,0:T(8,128)(2,1)} %get-tuple-element.291), calls=%async_computation.3 | async-start | bytes 2359296 | tf_op jit(solution)/shard_map/all_to_all | solution.py:873
  17.4 1.9 %collective-permute-start.1 = (bf16[1024,128]{1,0:T(8,128)(2,1)S(1)}, bf16[1024,128]{1,0:T(8,128)(2,1)}, u32[]{:S(2)}, u32[]{:S(2)}) collective-permute-start(bf16[1024,128]{1,0:T(8,128)(2,1)S(1)} %get-tuple-element.587), channel_id=1, source_target_pairs={{0,8},{4,12},{8,0},{12,4},{16,24},{20,28},{24,16},{28,20},{32,40},... | collective-permute-start | bytes 786440 | tf_op jit(solution)/shard_map/ppermute | solution.py:860
  19.3 2.7 %collective-permute-start.2 = (bf16[1024,128]{1,0:T(8,128)(2,1)S(1)}, bf16[1024,128]{1,0:T(8,128)(2,1)}, u32[]{:S(2)}, u32[]{:S(2)}) collective-permute-start(bf16[1024,128]{1,0:T(8,128)(2,1)S(1)} %get-tuple-element.587), channel_id=1, source_target_pairs={{0,16},{4,20},{8,24},{12,28},{16,0},{20,4},{24,8},{28,12},{32,48},... | collective-permute-start | bytes 786440 | tf_op jit(solution)/shard_map/ppermute | solution.py:860
  22.0 0.0 collective-permute-start
  22.0 1.5 collective-permute-start.3
  23.5 2.7 %prepare.1 = (bf16[8,128,256]{2,1,0:T(8,128)(2,1)}, bf16[8,256,128]{2,1,0:T(8,128)(2,1)}, bf16[8,128,256]{2,1,0:T(8,128)(2,1)}, bf16[8,256,128]{2,1,0:T(8,128)(2,1)}) custom-call(bf16[1024,128]{1,0:T(8,128)(2,1)} %get-tuple-element.280.q_ref, bf16[1024,128]{1,0:T(8,128)(2,1)} %cot_ref.5), custom_call_target="tpu_custom_call" | custom-call | flops 2000000000 | bytes 4000000 | tf_op jit(solution)/shard_map/prepare/pallas_call | solution.py:605
  26.2 0.3 collective-permute-start.4
  26.4 0.7 reshape.383.mask_ref
  27.1 4.7 %plan.1 = (s32[456]{0:T(512)}, s32[64]{0:T(128)}, s32[64]{0:T(128)}, s32[1]{0:T(128)}, s32[42]{0:T(128)}) custom-call(s32[320]{0:T(512)} %reshape.383.mask_ref, s32[32]{0:T(128)} %bitcast.100), custom_call_target="tpu_custom_call" | custom-call | bytes 4000000 | tf_op jit(solution)/shard_map/plan/pallas_call | solution.py:605
  31.7 4.1 %all-to-all-done.3.hk_ref = bf16[32,144,128]{2,1,0:T(8,128)(2,1)S(1)} async-done(((bf16[32,144,128]{2,1,0:T(8,128)(2,1)}), bf16[32,144,128]{2,1,0:T(8,128)(2,1)S(1)}, u32[]{:S(2)}, u32[]{:S(2)}) %all-to-all-start.3) | async-done | bytes 1179680 | tf_op jit(solution)/shard_map/all_to_all | solution.py:873
  35.9 4.3 %all-to-all-start.4 = ((bf16[32,144,128]{2,1,0:T(8,128)(2,1)}), bf16[32,144,128]{2,1,0:T(8,128)(2,1)S(1)}, u32[]{:S(2)}, u32[]{:S(2)}) async-start(bf16[32,144,128]{2,1,0:T(8,128)(2,1)} %get-tuple-element.294), calls=%async_computation.4 | async-start | bytes 2359296 | tf_op jit(solution)/shard_map/all_to_all | solution.py:879
  40.2 0.0 copy-done.6
  40.2 14.1 %scores.1 = (f32[8,256]{1,0:T(8,128)}, bf16[42,128,128]{2,1,0:T(8,128)(2,1)}, bf16[42,128,128]{2,1,0:T(8,128)(2,1)}) custom-call(s32[456]{0:T(512)} %get-tuple-element.274.list_ref, s32[64]{0:T(128)} %get-tuple-element.275.where_ref, s32[64]{0:T(128)} %get-tuple-element.276.block_ref, s32[1]{0:T(128)} %get-tuple-element.277.count_ref, ...), custom_call_target="tpu_custom_call" | custom-call | flops 12000000000 | bytes 4000000 | tf_op jit(solution)/shard_map/scores/pallas_call | solution.py:605
  54.3 0.0 collective-permute-done.1.t1_ref
  54.3 3.3 %collective-permute-start.5 = (bf16[1024,128]{1,0:T(8,128)(2,1)S(1)}, bf16[1024,128]{1,0:T(8,128)(2,1)S(1)}, u32[]{:S(2)}, u32[]{:S(2)}) collective-permute-start(bf16[1024,128]{1,0:T(8,128)(2,1)S(1)} %get-tuple-element.584), channel_id=1, source_target_pairs={{0,16},{4,20},{8,24},{12,28},{16,0},{20,4},{24,8},{28,12},{32,48},... | collective-permute-start | bytes 786440 | tf_op jit(solution)/shard_map/ppermute | solution.py:860
  57.6 0.0 collective-permute-done.2.t2_ref
  57.6 0.0 collective-permute-done.t0_ref
  57.6 0.0 collective-permute-done.3.t3_ref
  57.6 5.5 %partners.1 = (bf16[32,128,128]{2,1,0:T(8,128)(2,1)}, f32[4,8,256]{2,1,0:T(8,128)}) custom-call(s32[4,1024]{1,0:T(4,128)} %exp_ref.5, bf16[1024,256]{1,0:T(8,128)(2,1)} %collective-permute-done.t0_ref, bf16[1024,128]{1,0:T(8,128)(2,1)} %collective-permute-done.1.t1_ref, bf16[1024,128]{1,0:T(8,128)(2,1)} %collective-permute-done.2.t2_ref, ...), custom_call_target="tpu_custom_call" | custom-call | flops 5000000000 | bytes 4000000 | tf_op jit(solution)/shard_map/partners/pallas_call | solution.py:605
  63.1 0.0 copy-done.9
  63.1 0.0 collective-permute-start.6
  63.1 0.7 collective-permute-start.7
  63.7 2.6 %collective-permute-start.8 = (bf16[1056,256]{1,0:T(8,128)(2,1)S(1)}, bf16[1056,256]{1,0:T(8,128)(2,1)}, u32[]{:S(2)}, u32[]{:S(2)}) collective-permute-start(bf16[1056,256]{1,0:T(8,128)(2,1)S(1)} %copy-done.9), channel_id=1, source_target_pairs={{0,16},{4,20},{8,24},{12,28},{16,0},{20,4},{24,8},{28,12},{32,48},... | collective-permute-start | bytes 1622024 | tf_op jit(solution)/shard_map/ppermute | solution.py:860
  66.3 0.0 all-to-all-done.4.hv_ref
  66.3 1.0 copy-done.5
  67.4 17.9 %values.1 = (f32[1024,128]{1,0:T(8,128)}, bf16[32,176,128]{2,1,0:T(8,128)(2,1)}, bf16[128,128]{1,0:T(8,128)(2,1)S(1)}, f32[8,128,256]{2,1,0:T(8,128)}, f32[8,256]{1,0:T(8,128)}, /*index=5*/f32[8,256]{1,0:T(8,128)}) custom-call(s32[456]{0:T(512)} %get-tuple-element.274.list_ref, s32[64]{0:T(128)} %get-tuple-element.275.where_ref, ...), custom_call_target="tpu_custom_call" | custom-call | flops 20000000000 | bytes 4000000 | tf_op jit(solution)/shard_map/values/pallas_call | solution.py:605
  85.3 0.0 collective-permute-done.4.t1_ref
  85.3 1.5 collective-permute-start.9
  86.9 0.0 collective-permute-done.5.t2_ref
  86.9 0.7 copy-done.12
  87.6 6.3 %finish.1 = (bf16[32,128,128]{2,1,0:T(8,128)(2,1)}, bf16[4,32,128]{2,1,0:T(8,128)(2,1)}, f32[8,256]{1,0:T(8,128)}, bf16[32,176,128]{2,1,0:T(8,128)(2,1)}) custom-call(s32[1]{0:T(128)} %bitcast.13.me_ref, s32[4,1024]{1,0:T(4,128)} %exp_ref.5, bf16[1024,256]{1,0:T(8,128)(2,1)} %collective-permute-done.t0_ref, ...), custom_call_target="tpu_custom_call", output_to_operand_aliasing={{3}: (10, {})} | custom-call | flops 5000000000 | bytes 4000000 | tf_op jit(solution)/shard_map/finish/pallas_call | solution.py:605
  93.9 6.3 %all-to-all-start.5 = ((bf16[32,176,128]{2,1,0:T(8,128)(2,1)}), bf16[32,176,128]{2,1,0:T(8,128)(2,1)S(1)}, u32[]{:S(2)}, u32[]{:S(2)}) async-start(bf16[32,176,128]{2,1,0:T(8,128)(2,1)} %get-tuple-element.320), calls=%async_computation.5 | async-start | bytes 2883584 | tf_op jit(solution)/shard_map/all_to_all | solution.py:893
  100.2 24.3 %keys.1 = (f32[8,128,256]{2,1,0:T(8,128)}, f32[1024,128]{1,0:T(8,128)}, bf16[32,144,128]{2,1,0:T(8,128)(2,1)}, bf16[128,128]{1,0:T(8,128)(2,1)S(1)}) custom-call(s32[456]{0:T(512)} %get-tuple-element.274.list_ref, s32[64]{0:T(128)} %get-tuple-element.275.where_ref, s32[64]{0:T(128)} %get-tuple-element.276.block_ref, s32[1]{0:T(128)} %get-tuple-element.277.count_ref, ...), custom_call_target="tpu_custom_call" | custom-call | flops 24999999488 | bytes 4000000 | tf_op jit(solution)/shard_map/keys/pallas_call | solution.py:605
  124.5 0.0 collective-permute-done.6.o0_ref
  124.5 0.0 collective-permute-done.7.o1_ref
  124.5 0.0 collective-permute-done.8.o2_ref
  124.5 0.0 collective-permute-done.9.o3_ref
  124.5 0.0 copy-start.10
  124.5 0.0 all-to-all-done.5.ret_ref
  124.6 0.7 copy-done.10
  125.3 0.5 copy-done.4
  125.8 0.6 while.27
  126.4 9.2 %all-to-all-start.6 = ((bf16[32,144,128]{2,1,0:T(8,128)(2,1)}), bf16[32,144,128]{2,1,0:T(8,128)(2,1)S(1)}, u32[]{:S(2)}, u32[]{:S(2)}) async-start(bf16[32,144,128]{2,1,0:T(8,128)(2,1)} %get-tuple-element.338), calls=%async_computation.6 | async-start | bytes 2359296 | tf_op jit(solution)/shard_map/all_to_all | solution.py:900
  135.6 0.0 copy-start
  135.6 0.0 copy-start.1
  135.6 14.7 %value_back.1 = (f32[1024,128]{1,0:T(8,128)}, f32[4,1024,128]{2,1,0:T(8,128)}) custom-call(s32[1]{0:T(128)} %bitcast.13.me_ref, s32[1]{0:T(128)} %bitcast.17.feat_ref, f32[1024,128]{1,0:T(8,128)} %get-tuple-element.308.ownv_ref, bf16[32,176,128]{2,1,0:T(8,128)(2,1)} %copy-done.4, f32[1024,128]{1,0:T(8,128)} %get-tuple-element.323.ownk_ref, ...), custom_call_target="tpu_custom_call" | custom-call | flops 12000000000 | bytes 4000000 | tf_op jit(solution)/shard_map/value_back/pallas_call | solution.py:605
  150.3 3.4 %all-to-all-done.6.ret_ref = bf16[32,144,128]{2,1,0:T(8,128)(2,1)S(1)} async-done(((bf16[32,144,128]{2,1,0:T(8,128)(2,1)}), bf16[32,144,128]{2,1,0:T(8,128)(2,1)S(1)}, u32[]{:S(2)}, u32[]{:S(2)}) %all-to-all-start.6) | async-done | bytes 1179680 | tf_op jit(solution)/shard_map/all_to_all | solution.py:900
  153.8 0.0 copy-done.1
  153.8 1.6 copy-done.2
  155.4 1.0 copy-done.3
  156.4 4.1 %key_back.1 = (f32[1024,128]{1,0:T(8,128)S(1)}, bf16[1024,128]{1,0:T(8,128)(2,1)S(1)}, bf16[1024,128]{1,0:T(8,128)(2,1)S(1)}, bf16[1024,128]{1,0:T(8,128)(2,1)S(1)}) custom-call(s32[1]{0:T(128)} %bitcast.13.me_ref, s32[1]{0:T(128)} %bitcast.17.feat_ref, f32[1024,128]{1,0:T(8,128)S(1)} %copy-done.3, bf16[32,144,128]{2,1,0:T(8,128)(2,1)S(1)} %all-to-all-done.6.ret_ref, ...), custom_call_target="tpu_custom_call" | custom-call | flops 8000000000 | bytes 4000000 | tf_op jit(solution)/shard_map/key_back/pallas_call | solution.py:605
  160.5 3.1 %collective-permute-start.12 = (bf16[1024,128]{1,0:T(8,128)(2,1)S(1)}, bf16[1024,128]{1,0:T(8,128)(2,1)S(1)}, u32[]{:S(2)}, u32[]{:S(2)}) collective-permute-start(bf16[1024,128]{1,0:T(8,128)(2,1)S(1)} %get-tuple-element.347), channel_id=1, source_target_pairs={{0,3},{1,0},{2,1},{3,2},{4,7},{5,4},{6,5},{7,6},{8,11},{9,8},{10,9... | collective-permute-start | bytes 786440 | tf_op jit(solution)/shard_map/ppermute | solution.py:908
  163.6 0.0 collective-permute-start.11
  163.7 2.2 %collective-permute-start.10 = (bf16[1024,128]{1,0:T(8,128)(2,1)S(1)}, bf16[1024,128]{1,0:T(8,128)(2,1)S(1)}, u32[]{:S(2)}, u32[]{:S(2)}) collective-permute-start(bf16[1024,128]{1,0:T(8,128)(2,1)S(1)} %get-tuple-element.345), channel_id=1, source_target_pairs={{0,2},{1,3},{2,0},{3,1},{4,6},{5,7},{6,4},{7,5},{8,10},{9,11},{10,... | collective-permute-start | bytes 786440 | tf_op jit(solution)/shard_map/ppermute | solution.py:908
  165.9 2.8 %attend.1 = bf16[1024,128]{1,0:T(8,128)(2,1)} custom-call(f32[8,128,256]{2,1,0:T(8,128)} %get-tuple-element.342.out_t_ref, bf16[4,32,128]{2,1,0:T(8,128)(2,1)} %get-tuple-element.329.back_ref, bf16[32,128,128]{2,1,0:T(8,128)(2,1)} %get-tuple-element.343.pair_ref), custom_call_target="tpu_custom_call" | custom-call | flops 2000000000 | bytes 4000000 | tf_op jit(solution)/shard_map/attend/pallas_call | solution.py:605
  168.6 6.6 %collective-permute-done.12 = bf16[1024,128]{1,0:T(8,128)(2,1)S(1)} collective-permute-done((bf16[1024,128]{1,0:T(8,128)(2,1)S(1)}, bf16[1024,128]{1,0:T(8,128)(2,1)S(1)}, u32[]{:S(2)}, u32[]{:S(2)}) %collective-permute-start.12) | collective-permute-done | bytes 262176 | tf_op jit(solution)/shard_map/ppermute | solution.py:908
  175.3 3.4 %collective-permute-done.11 = bf16[1024,128]{1,0:T(8,128)(2,1)S(1)} collective-permute-done((bf16[1024,128]{1,0:T(8,128)(2,1)S(1)}, bf16[1024,128]{1,0:T(8,128)(2,1)S(1)}, u32[]{:S(2)}, u32[]{:S(2)}) %collective-permute-start.11) | collective-permute-done | bytes 262176 | tf_op jit(solution)/shard_map/ppermute | solution.py:908
  178.7 0.0 collective-permute-done.10
  178.7 0.8 add_convert_fusion
  (14 shorter events, 0.0 us)
Async XLA Ops:
  0.6 7.7 %copy-start.7 = (s32[128]{0:T(128)S(1)}, s32[128]{0:T(128)}, u32[]{:S(2)}) copy-start(s32[128]{0:T(128)} %param.23) | copy-start | bytes 1540
  9.0 12.9 %copy-start.11 = (bf16[1024,256]{1,0:T(8,128)(2,1)S(1)}, bf16[1024,256]{1,0:T(8,128)(2,1)}, u32[]{:S(2)}) copy-start(bf16[1024,256]{1,0:T(8,128)(2,1)} %get-tuple-element.298) | copy-start | bytes 1572868
  9.0 26.8 %all-to-all-start.3 = ((bf16[32,144,128]{2,1,0:T(8,128)(2,1)}), bf16[32,144,128]{2,1,0:T(8,128)(2,1)S(1)}, u32[]{:S(2)}, u32[]{:S(2)}) async-start(bf16[32,144,128]{2,1,0:T(8,128)(2,1)} %get-tuple-element.291), calls=%async_computation.3 | async-start | bytes 2359296 | tf_op jit(solution)/shard_map/all_to_all | solution.py:873
  17.4 36.8 %collective-permute-start.1 = (bf16[1024,128]{1,0:T(8,128)(2,1)S(1)}, bf16[1024,128]{1,0:T(8,128)(2,1)}, u32[]{:S(2)}, u32[]{:S(2)}) collective-permute-start(bf16[1024,128]{1,0:T(8,128)(2,1)S(1)} %get-tuple-element.587), channel_id=1, source_target_pairs={{0,8},{4,12},{8,0},{12,4},{16,24},{20,28},{24,16},{28,20},{32,40},... | collective-permute-start | bytes 786440 | tf_op jit(solution)/shard_map/ppermute | solution.py:860
  19.3 38.3 %collective-permute-start.2 = (bf16[1024,128]{1,0:T(8,128)(2,1)S(1)}, bf16[1024,128]{1,0:T(8,128)(2,1)}, u32[]{:S(2)}, u32[]{:S(2)}) collective-permute-start(bf16[1024,128]{1,0:T(8,128)(2,1)S(1)} %get-tuple-element.587), channel_id=1, source_target_pairs={{0,16},{4,20},{8,24},{12,28},{16,0},{20,4},{24,8},{28,12},{32,48},... | collective-permute-start | bytes 786440 | tf_op jit(solution)/shard_map/ppermute | solution.py:860
  22.0 35.6 %collective-permute-start = (bf16[1024,256]{1,0:T(8,128)(2,1)S(1)}, bf16[1024,256]{1,0:T(8,128)(2,1)}, u32[]{:S(2)}, u32[]{:S(2)}) collective-permute-start(bf16[1024,256]{1,0:T(8,128)(2,1)S(1)} %copy-done.11), channel_id=1, source_target_pairs={{0,4},{4,0},{8,12},{12,8},{16,20},{20,16},{24,28},{28,24},{32,36},... | collective-permute-start | bytes 1572872 | tf_op jit(solution)/shard_map/ppermute | solution.py:860
  22.0 35.6 %collective-permute-start.3 = (bf16[1024,256]{1,0:T(8,128)(2,1)S(1)}, bf16[1024,256]{1,0:T(8,128)(2,1)}, u32[]{:S(2)}, u32[]{:S(2)}) collective-permute-start(bf16[1024,256]{1,0:T(8,128)(2,1)S(1)} %copy-done.11), channel_id=1, source_target_pairs={{0,32},{4,36},{8,40},{12,44},{16,48},{20,52},{24,56},{28,60},{32,0... | collective-permute-start | bytes 1572872 | tf_op jit(solution)/shard_map/ppermute | solution.py:860
  23.4 3.0 %copy-start.8 = (s32[8,40]{1,0:T(8,128)S(1)}, s32[8,40]{1,0:T(8,128)}, u32[]{:S(2)}) copy-start(s32[8,40]{1,0:T(8,128)} %param.21) | copy-start | bytes 3844
  26.2 59.2 %collective-permute-start.4 = (bf16[1024,128]{1,0:T(8,128)(2,1)S(1)}, bf16[1024,128]{1,0:T(8,128)(2,1)}, u32[]{:S(2)}, u32[]{:S(2)}) collective-permute-start(bf16[1024,128]{1,0:T(8,128)(2,1)S(1)} %get-tuple-element.584), channel_id=1, source_target_pairs={{0,8},{4,12},{8,0},{12,4},{16,24},{20,28},{24,16},{28,20},{32,40},... | collective-permute-start | bytes 786440 | tf_op jit(solution)/shard_map/ppermute | solution.py:860
  35.8 4.3 %copy-start.6 = (bf16[32,144,128]{2,1,0:T(8,128)(2,1)}, bf16[32,144,128]{2,1,0:T(8,128)(2,1)S(1)}, u32[]{:S(2)}) copy-start(bf16[32,144,128]{2,1,0:T(8,128)(2,1)S(1)} %all-to-all-done.3.hk_ref) | copy-start | bytes 3538948
  35.9 30.5 %all-to-all-start.4 = ((bf16[32,144,128]{2,1,0:T(8,128)(2,1)}), bf16[32,144,128]{2,1,0:T(8,128)(2,1)S(1)}, u32[]{:S(2)}, u32[]{:S(2)}) async-start(bf16[32,144,128]{2,1,0:T(8,128)(2,1)} %get-tuple-element.294), calls=%async_computation.4 | async-start | bytes 2359296 | tf_op jit(solution)/shard_map/all_to_all | solution.py:879
  54.3 32.6 %collective-permute-start.5 = (bf16[1024,128]{1,0:T(8,128)(2,1)S(1)}, bf16[1024,128]{1,0:T(8,128)(2,1)S(1)}, u32[]{:S(2)}, u32[]{:S(2)}) collective-permute-start(bf16[1024,128]{1,0:T(8,128)(2,1)S(1)} %get-tuple-element.584), channel_id=1, source_target_pairs={{0,16},{4,20},{8,24},{12,28},{16,0},{20,4},{24,8},{28,12},{32,48},... | collective-permute-start | bytes 786440 | tf_op jit(solution)/shard_map/ppermute | solution.py:860
  57.6 5.5 %copy-start.9 = (bf16[1056,256]{1,0:T(8,128)(2,1)S(1)}, bf16[1056,256]{1,0:T(8,128)(2,1)}, u32[]{:S(2)}) copy-start(bf16[1056,256]{1,0:T(8,128)(2,1)} %get-tuple-element.321) | copy-start | bytes 1622020
  63.1 61.4 %collective-permute-start.6 = (bf16[1056,256]{1,0:T(8,128)(2,1)S(1)}, bf16[1056,256]{1,0:T(8,128)(2,1)}, u32[]{:S(2)}, u32[]{:S(2)}) collective-permute-start(bf16[1056,256]{1,0:T(8,128)(2,1)S(1)} %copy-done.9), channel_id=1, source_target_pairs={{0,4},{4,0},{8,12},{12,8},{16,20},{20,16},{24,28},{28,24},{32,36},... | collective-permute-start | bytes 1622024 | tf_op jit(solution)/shard_map/ppermute | solution.py:860
  63.1 61.4 %collective-permute-start.7 = (bf16[1056,256]{1,0:T(8,128)(2,1)S(1)}, bf16[1056,256]{1,0:T(8,128)(2,1)}, u32[]{:S(2)}, u32[]{:S(2)}) collective-permute-start(bf16[1056,256]{1,0:T(8,128)(2,1)S(1)} %copy-done.9), channel_id=1, source_target_pairs={{0,8},{4,12},{8,0},{12,4},{16,24},{20,28},{24,16},{28,20},{32,40},... | collective-permute-start | bytes 1622024 | tf_op jit(solution)/shard_map/ppermute | solution.py:860
  63.7 60.8 %collective-permute-start.8 = (bf16[1056,256]{1,0:T(8,128)(2,1)S(1)}, bf16[1056,256]{1,0:T(8,128)(2,1)}, u32[]{:S(2)}, u32[]{:S(2)}) collective-permute-start(bf16[1056,256]{1,0:T(8,128)(2,1)S(1)} %copy-done.9), channel_id=1, source_target_pairs={{0,16},{4,20},{8,24},{12,28},{16,0},{20,4},{24,8},{28,12},{32,48},... | collective-permute-start | bytes 1622024 | tf_op jit(solution)/shard_map/ppermute | solution.py:860
  66.3 1.0 copy-start.5
  85.3 39.2 %collective-permute-start.9 = (bf16[1056,256]{1,0:T(8,128)(2,1)S(1)}, bf16[1056,256]{1,0:T(8,128)(2,1)S(1)}, u32[]{:S(2)}, u32[]{:S(2)}) collective-permute-start(bf16[1056,256]{1,0:T(8,128)(2,1)S(1)} %copy-done.9), channel_id=1, source_target_pairs={{0,32},{4,36},{8,40},{12,44},{16,48},{20,52},{24,56},{28,60},{32,0... | collective-permute-start | bytes 1622024 | tf_op jit(solution)/shard_map/ppermute | solution.py:860
  86.9 0.7 copy-start.12
  93.9 30.6 %all-to-all-start.5 = ((bf16[32,176,128]{2,1,0:T(8,128)(2,1)}), bf16[32,176,128]{2,1,0:T(8,128)(2,1)S(1)}, u32[]{:S(2)}, u32[]{:S(2)}) async-start(bf16[32,176,128]{2,1,0:T(8,128)(2,1)} %get-tuple-element.320), calls=%async_computation.5 | async-start | bytes 2883584 | tf_op jit(solution)/shard_map/all_to_all | solution.py:893
  124.5 0.8 copy-start.10
  124.6 1.2 copy-start.4
  126.4 27.3 %all-to-all-start.6 = ((bf16[32,144,128]{2,1,0:T(8,128)(2,1)}), bf16[32,144,128]{2,1,0:T(8,128)(2,1)S(1)}, u32[]{:S(2)}, u32[]{:S(2)}) async-start(bf16[32,144,128]{2,1,0:T(8,128)(2,1)} %get-tuple-element.338), calls=%async_computation.6 | async-start | bytes 2359296 | tf_op jit(solution)/shard_map/all_to_all | solution.py:900
  135.6 18.2 %copy-start = (bf16[512,128]{1,0:T(8,128)(2,1)S(1)}, bf16[512,128]{1,0:T(8,128)(2,1)}, u32[]{:S(2)}) copy-start(bf16[512,128]{1,0:T(8,128)(2,1)} %wk_ref.3) | copy-start | bytes 393220
  135.6 18.1 %copy-start.1 = (s32[1,32,128]{2,1,0:T(8,128)S(1)}, s32[1,32,128]{2,1,0:T(8,128)}, u32[]{:S(2)}) copy-start(s32[1,32,128]{2,1,0:T(8,128)} %param.19) | copy-start | bytes 49156
  153.8 1.6 copy-start.2
  155.4 1.0 copy-start.3
  160.5 14.7 %collective-permute-start.12 = (bf16[1024,128]{1,0:T(8,128)(2,1)S(1)}, bf16[1024,128]{1,0:T(8,128)(2,1)S(1)}, u32[]{:S(2)}, u32[]{:S(2)}) collective-permute-start(bf16[1024,128]{1,0:T(8,128)(2,1)S(1)} %get-tuple-element.347), channel_id=1, source_target_pairs={{0,3},{1,0},{2,1},{3,2},{4,7},{5,4},{6,5},{7,6},{8,11},{9,8},{10,9... | collective-permute-start | bytes 786440 | tf_op jit(solution)/shard_map/ppermute | solution.py:908
  163.6 15.0 %collective-permute-start.11 = (bf16[1024,128]{1,0:T(8,128)(2,1)S(1)}, bf16[1024,128]{1,0:T(8,128)(2,1)S(1)}, u32[]{:S(2)}, u32[]{:S(2)}) collective-permute-start(bf16[1024,128]{1,0:T(8,128)(2,1)S(1)} %get-tuple-element.346), channel_id=1, source_target_pairs={{0,1},{1,2},{2,3},{3,0},{4,5},{5,6},{6,7},{7,4},{8,9},{9,10},{10,1... | collective-permute-start | bytes 786440 | tf_op jit(solution)/shard_map/ppermute | solution.py:908
  163.7 15.0 %collective-permute-start.10 = (bf16[1024,128]{1,0:T(8,128)(2,1)S(1)}, bf16[1024,128]{1,0:T(8,128)(2,1)S(1)}, u32[]{:S(2)}, u32[]{:S(2)}) collective-permute-start(bf16[1024,128]{1,0:T(8,128)(2,1)S(1)} %get-tuple-element.345), channel_id=1, source_target_pairs={{0,2},{1,3},{2,0},{3,1},{4,6},{5,7},{6,4},{7,5},{8,10},{9,11},{10,... | collective-permute-start | bytes 786440 | tf_op jit(solution)/shard_map/ppermute | solution.py:908

commit v10 on v9

--- a/solution.py
+++ b/solution.py
@@ -40,6 +40,22 @@
 
 def vmem():
     return pl.BlockSpec(memory_space=pltpu.VMEM)
+
+
+def anywhere():
+    return pl.BlockSpec(memory_space=pl.ANY)
+
+
+def start_copies(pairs, sems):
+    copies = [pltpu.make_async_copy(src, dst, sems.at[n]) for n, (src, dst) in enumerate(pairs)]
+    for copy in copies:
+        copy.start()
+    return copies
+
+
+def wait_all(copies):
+    for copy in copies:
+        copy.wait()
 
 
 def smem():
@@ -182,13 +198,17 @@
     return flat(dot(jnp.concatenate(parts, axis=1), picks).T)
 
 
-def partner_key_kernel(exp_ref, t0_ref, t1_ref, t2_ref, t3_ref, q_ref, out_ref, sp_ref):
+def partner_key_kernel(exp_ref, t0_ref, t1_ref, t2_ref, t3_ref, q_ref, out_ref, sp_ref, pair_s, sems):
     picks = sum_picks()
+    copies = []
     for m, table in enumerate((t0_ref, t1_ref, t2_ref, t3_ref)):
         blocks = gather_partner(exp_ref, m, table)
         for i, block in enumerate(blocks):
-            out_ref[m * Q_BLOCKS + i] = block
+            pair_s[m * Q_BLOCKS + i] = block
+        here = pl.ds(m * Q_BLOCKS, Q_BLOCKS)
+        copies += start_copies([(pair_s.at[here], out_ref.at[here])], sems.at[pl.ds(m, 1)])
         sp_ref[m] = head_sums(q_ref, blocks, picks)
+    wait_all(copies)
 
 
 def head_picks(i):
@@ -374,10 +394,11 @@
 
 
 def score_kernel(
-    list_ref, where_ref, block_ref, count_ref, live_ref, qt_ref, own_ref, hk_ref, gid_ref, glob_ref, lse_ref, k_s, kt_ref,
-    top_s, total_s,
+    list_ref, where_ref, block_ref, count_ref, live_ref, qt_ref, own_ref, hk_ref, gid_ref, glob_ref, lse_ref, k_ref, kt_ref,
+    top_s, total_s, k_s, kt_s, sems,
 ):
-    fill(k_s, kt_ref, 0, own_ref, hk_ref, gid_ref, glob_ref)
+    fill(k_s, kt_s, 0, own_ref, hk_ref, gid_ref, glob_ref)
+    copies = start_copies([(k_s, k_ref), (kt_s, kt_ref)], sems)
 
     top_s[...] = jnp.full((Q_BLOCKS, 8, 2 * BLOCK), NEG, F32)
     total_s[...] = jnp.zeros((Q_BLOCKS, 8, 2 * BLOCK), F32)
@@ -404,12 +425,15 @@
         best = jnp.max(top, axis=0, keepdims=True)
         denominator = jnp.sum(total_s[i] * jnp.exp(top - best), axis=0, keepdims=True)
         lse_ref[i : i + 1, :] = best + jnp.log(denominator)
+    wait_all(copies)
 
 
 def value_kernel(
-    list_ref, where_ref, block_ref, count_ref, live_ref, k_s, ownv_ref, hv_ref, glob_ref, qt_ref, ct_ref, cs_ref, part_ref,
-    sp_ref, gid_ref, own_ref, halo_ref, gout_ref, out_s, delta_ref, lse_ref, acc_s, vt_s,
+    list_ref, where_ref, block_ref, count_ref, live_ref, k_in, ownv_ref, hv_ref, glob_ref, qt_in, ct_in, cs_in, part_ref,
+    sp_ref, gid_ref, own_ref, halo_ref, gout_ref, out_ref, delta_ref, lse_ref, acc_s, vt_s, k_s, qt_ref, ct_ref, cs_ref,
+    in_sems, out_s, halo_s, sems,
 ):
+    loads = start_copies([(k_in, k_s), (qt_in, qt_ref), (cs_in, cs_ref), (ct_in, ct_ref)], in_sems)
     fill(None, vt_s, COLS, ownv_ref, hv_ref, gid_ref, glob_ref)
     clear_blocks(acc_s)
     part = part_ref[...]
@@ -420,6 +444,7 @@
     for m in range(EXPANDERS):
         total += jnp.exp(sp_ref[m] - best)
     lse_ref[...] = best + jnp.log(total)
+    wait_all(loads)
 
     out_s[...] = jnp.zeros((Q_BLOCKS, COLS, 2 * BLOCK), F32)
 
@@ -440,9 +465,11 @@
         return carry
 
     lax.fori_loop(0, count_ref[0], step, 0)
+    out_copy = pltpu.make_async_copy(out_s, out_ref, sems.at[1 + SENDERS // GROUP])
+    out_copy.start()
     for i in range(Q_BLOCKS):
         delta_ref[i : i + 1, :] = jnp.sum(out_s[i] * ct_ref[i].astype(F32), axis=0, keepdims=True)
-    store_parts(acc_s, own_ref, halo_ref, gid_ref, gout_ref)
+    wait_all(store_parts(acc_s, own_ref, halo_ref, gid_ref, gout_ref, halo_s, sems) + [out_copy])
 
 
 def clear_blocks(acc_s):
@@ -453,32 +480,39 @@
     lax.fori_loop(0, KEY_BLOCKS, clear, 0, unroll=2)
 
 
-def store_parts(acc_s, own_ref, halo_ref, gid_ref, gout_ref):
-    def own(j, carry):
-        own_ref[q_rows(j), :] = acc_s[j]
-        return carry
-
-    def halo(j, carry):
-        halo_ref[j, :BLOCK] = acc_s[Q_BLOCKS + j].astype(BF16)
-        return carry
-
-    lax.fori_loop(0, Q_BLOCKS, own, 0, unroll=2)
-    lax.fori_loop(0, SENDERS, halo, 0, unroll=4)
+def store_parts(acc_s, own_ref, halo_ref, gid_ref, gout_ref, halo_s, sems):
+    copies = start_copies([(acc_s.at[pl.ds(0, Q_BLOCKS)], own_ref)], sems)
     grads = acc_s[GLOBAL_BLOCK].astype(BF16)
     gout_ref[...] = grads
     slot_row = owner_ranks(gid_ref[...])[1]
     hot = (iota((SENDERS * EXTRA, BLOCK), 0) == slot_row).astype(F32).astype(BF16)
     extra = dot(hot, grads).astype(BF16)
-    for s in range(SENDERS):
-        halo_ref[s, BLOCK:SLOTS] = extra[s * EXTRA : (s + 1) * EXTRA]
+    for t in range(SENDERS // GROUP):
+        for s in range(t * GROUP, (t + 1) * GROUP):
+            halo_s[s, :BLOCK] = acc_s[Q_BLOCKS + s].astype(BF16)
+            halo_s[s, BLOCK:] = extra[s * EXTRA : (s + 1) * EXTRA]
+        here = pl.ds(t * GROUP, GROUP)
+        copy = pltpu.make_async_copy(halo_s.at[here], halo_ref.at[here, pl.ds(0, SLOTS)], sems.at[1 + t])
+        copy.start()
+        copies.append(copy)
+    return copies
+
+
+def part_scratch():
+    return [pltpu.VMEM((SENDERS, SLOTS, COLS), BF16), pltpu.SemaphoreType.DMA((2 + SENDERS // GROUP,))]
 
 
 def key_kernel(
-    list_ref, where_ref, block_ref, count_ref, live_ref, k_s, kt_s, ownv_ref, hv_ref, glob_ref, qt_ref, qs_ref, ct_ref, lse_ref,
-    delta_ref, gid_ref, out_s, own_ref, halo_ref, gout_ref, acc_s, v_s,
+    list_ref, where_ref, block_ref, count_ref, live_ref, k_in, kt_in, ownv_ref, hv_ref, glob_ref, qt_in, qs_in, ct_in, lse_ref,
+    delta_ref, gid_ref, out_ref, own_ref, halo_ref, gout_ref, acc_s, v_s, k_s, kt_s, qt_ref, qs_ref, ct_ref, in_sems,
+    out_s, halo_s, sems,
 ):
+    loads = start_copies(
+        [(k_in, k_s), (qt_in, qt_ref), (ct_in, ct_ref), (kt_in, kt_s), (qs_in, qs_ref)], in_sems
+    )
     fill(v_s, None, COLS, ownv_ref, hv_ref, gid_ref, glob_ref)
     clear_blocks(acc_s)
+    wait_all(loads)
 
     out_s[...] = jnp.zeros((Q_BLOCKS, COLS, 2 * BLOCK), F32)
 
@@ -502,7 +536,9 @@
         return carry
 
     lax.fori_loop(0, count_ref[0], step, 0)
-    store_parts(acc_s, own_ref, halo_ref, gid_ref, gout_ref)
+    out_copy = pltpu.make_async_copy(out_s, out_ref, sems.at[1 + SENDERS // GROUP])
+    out_copy.start()
+    wait_all(store_parts(acc_s, own_ref, halo_ref, gid_ref, gout_ref, halo_s, sems) + [out_copy])
 
 
 def scatter_into(acc_s, splits, data):
@@ -620,7 +656,6 @@
 
 
 def run_project(me, features, w_query, w_key, w_value, cotangent, rows, exp_list, gids):
-    anywhere = pl.BlockSpec(memory_space=pl.ANY)
     return call(
         project_kernel,
         [smem()] + [vmem()] * 8,
@@ -638,7 +673,7 @@
         name="project",
         mib=56,
         flops=3_000_000_000,
-        out_spaces=(vmem(), vmem(), vmem(), vmem(), anywhere, anywhere, vmem(), smem()),
+        out_spaces=(vmem(), vmem(), vmem(), vmem(), anywhere(), anywhere(), vmem(), smem()),
         scratch=[
             pltpu.VMEM((SENDERS, SLOTS, COLS), BF16),
             pltpu.VMEM((SENDERS, SLOTS, COLS), BF16),
@@ -666,6 +701,11 @@
         (shape((EXPANDERS * Q_BLOCKS, BLOCK, COLS)), shape((EXPANDERS, Q_BLOCKS, 2 * BLOCK), F32)),
         (exp_rows, *swaps, query),
         name="partners",
+        out_spaces=(anywhere(), vmem()),
+        scratch=[
+            pltpu.VMEM((EXPANDERS * Q_BLOCKS, BLOCK, COLS), BF16),
+            pltpu.SemaphoreType.DMA((EXPANDERS,)),
+        ],
         flops=5_000_000_000,
     )
 
@@ -718,7 +758,9 @@
             shape((KEY_BLOCKS, COLS, BLOCK)),
         ),
         (*plan, turned_q, own, halo_k, gids, glob),
-        scratch=[pltpu.VMEM((Q_BLOCKS, 8, 2 * BLOCK), F32)] * 2,
+        scratch=[pltpu.VMEM((Q_BLOCKS, 8, 2 * BLOCK), F32)] * 2
+        + [blocks_of(BF16), blocks_of(BF16), pltpu.SemaphoreType.DMA((2,))],
+        out_spaces=(vmem(), anywhere(), anywhere()),
         name="scores",
         flops=12_000_000_000,
     )
@@ -728,9 +770,9 @@
     turned_q, _, turned_cot, cot_stack = prepared
     return call(
         value_kernel,
-        [smem()] * 5 + [vmem()] * 10,
+        [smem()] * 5 + [anywhere()] + [vmem()] * 3 + [anywhere()] * 3 + [vmem()] * 3,
         (
-            shape((NODES_HERE, COLS), F32),
+            shape((Q_BLOCKS, BLOCK, COLS), F32),
             shape((SENDERS, BACK, COLS)),
             shape((BLOCK, COLS)),
             shape((Q_BLOCKS, COLS, 2 * BLOCK), F32),
@@ -738,7 +780,12 @@
             shape((Q_BLOCKS, 2 * BLOCK), F32),
         ),
         (*plan, keys, own_values, halo_v, glob, turned_q, turned_cot, cot_stack, part, scores, gids),
-        scratch=[blocks_of(F32), blocks_of(BF16)],
+        scratch=[
+            blocks_of(F32), blocks_of(BF16), blocks_of(BF16), pltpu.VMEM((Q_BLOCKS, COLS, 2 * BLOCK), BF16), pltpu.VMEM((Q_BLOCKS, COLS, 2 * BLOCK), BF16),
+            pltpu.VMEM((Q_BLOCKS, 2 * BLOCK, COLS), BF16), pltpu.SemaphoreType.DMA((4,)), pltpu.VMEM((Q_BLOCKS, COLS, 2 * BLOCK), F32),
+            *part_scratch(),
+        ],
+        out_spaces=(anywhere(), anywhere(), vmem(), anywhere(), vmem(), vmem()),
         name="values",
         flops=20_000_000_000,
     )
@@ -748,15 +795,20 @@
     turned_q, q_stack, turned_cot, _ = prepared
     return call(
         key_kernel,
-        [smem()] * 5 + [vmem()] * 11,
+        [smem()] * 5 + [anywhere()] * 2 + [vmem()] * 3 + [anywhere()] * 3 + [vmem()] * 3,
         (
             shape((Q_BLOCKS, COLS, 2 * BLOCK), F32),
-            shape((NODES_HERE, COLS), F32),
+            shape((Q_BLOCKS, BLOCK, COLS), F32),
             shape((SENDERS, SLOTS, COLS)),
             shape((BLOCK, COLS)),
         ),
         (*plan, keys, turned_k, own_values, halo_v, glob, turned_q, q_stack, turned_cot, lse, delta, gids),
-        scratch=[blocks_of(F32), blocks_of(BF16)],
+        scratch=[
+            blocks_of(F32), blocks_of(BF16), blocks_of(BF16), blocks_of(BF16), pltpu.VMEM((Q_BLOCKS, COLS, 2 * BLOCK), BF16),
+            pltpu.VMEM((Q_BLOCKS, 2 * BLOCK, COLS), BF16), pltpu.VMEM((Q_BLOCKS, COLS, 2 * BLOCK), BF16), pltpu.SemaphoreType.DMA((5,)), pltpu.VMEM((Q_BLOCKS, COLS, 2 * BLOCK), F32),
+            *part_scratch(),
+        ],
+        out_spaces=(anywhere(), anywhere(), anywhere(), vmem()),
         name="keys",
         mib=56,
         flops=25_000_000_000,
@@ -768,7 +820,7 @@
         value_back_kernel,
         [smem()] * 2 + [vmem()] * 15,
         (shape((NODES_HERE, COLS), F32), shape((4, NODES_HERE, COLS), F32)),
-        (me, feat, own_v, returned_v, own_k, rows, *others, gids, w_query, w_value, out_t, back, pairs, more),
+        (me, feat, own_v.reshape(NODES_HERE, COLS), returned_v, own_k.reshape(NODES_HERE, COLS), rows, *others, gids, w_query, w_value, out_t, back, pairs, more),
         scratch=[pltpu.VMEM((NODES_HERE, COLS), F32), pltpu.VMEM((NODES_HERE, COLS), BF16)],
         name="value_back",
         mib=56,

time: 180 us -> 180 us (level)
  transfers between devices with their start and end apart: 17 -> 17, of which waited for: 4 -> 4; matrix products, arithmetic and copies ran while one was open for 0% -> 0% of each run, Pallas kernels for 52% -> 51%
where the time goes in v10:
time: 180 us
  Pallas kernels  104 us (58%)
  starting transfers between devices  49.1 us (27%)
  waiting for transfers between devices  17.6 us (10%)
  local copies, waits for them, and re-layouts  6.3 us (4%)
    pallas_call x11, Pallas kernels, call(): pl.pallas_call(kernel, out_shape=outs, in_specs=ins, out_specs=out_spaces...  104 us
    ppermute x10, starting transfers between devices, swapped(): lax.ppermute(value, 'dom', [(i, i ^ 1 << bit) for i in range(dom_count)])  13.6 us
    all_to_all x1, starting transfers between devices, on_device(): returned_k = lax.all_to_all(back_k, 'dom', 0, 0, tiled=True)  10.5 us
    ppermute x3, waiting for transfers between devices, on_device(): lax.ppermute(away[k - 1], 'feat', [(i, (i + k) % 4) for i in range(4)])  10 us
    all_to_all x1, starting transfers between devices, on_device(): halo_k = lax.all_to_all(out_k, 'dom', 0, 0, tiled=True)  8.38 us
    all_to_all x1, starting transfers between devices, on_device(): returned_v = lax.all_to_all(back_v, 'dom', 0, 0, tiled=True)  6.98 us
    unnamed x26, local copies, waits for them, and re-layouts  5.62 us
    ppermute x3, starting transfers between devices, on_device(): lax.ppermute(away[k - 1], 'feat', [(i, (i + k) % 4) for i in range(4)])  5.31 us
  transfers between devices with their start and end apart: 17, of which 4 were waited for; matrix products, arithmetic and copies ran while one was open for 0% of the time, Pallas kernels for 51%

profile of v10, /device:TPU:0, one launch (start us, length us, event | category | flops | bytes accessed | tf_op | source)
XLA Modules:
  0.0 180.1 jit_solution(11117832823071627449)
XLA Ops:
  0.6 0.0 copy-start.7
  0.6 7.7 %project.1 = (bf16[1024,128]{1,0:T(8,128)(2,1)}, bf16[1024,128]{1,0:T(8,128)(2,1)S(1)}, bf16[1024,128]{1,0:T(8,128)(2,1)S(1)}, bf16[1024,256]{1,0:T(8,128)(2,1)}...) custom-call(s32[1]{0:T(128)} %bitcast.13.me_ref, ...), custom_call_target="tpu_custom_call" | custom-call | flops 3000000000 | bytes 4000000 | tf_op jit(solution)/shard_map/project/pallas_call | solution.py:641
  8.4 0.0 copy-done.7
  8.4 0.6 while.26
  9.0 0.0 copy-start.11
  9.0 8.4 %all-to-all-start.3 = ((bf16[32,144,128]{2,1,0:T(8,128)(2,1)}), bf16[32,144,128]{2,1,0:T(8,128)(2,1)S(1)}, u32[]{:S(2)}, u32[]{:S(2)}) async-start(bf16[32,144,128]{2,1,0:T(8,128)(2,1)} %get-tuple-element.291), calls=%async_computation.3 | async-start | bytes 2359296 | tf_op jit(solution)/shard_map/all_to_all | solution.py:925
  17.4 1.9 %collective-permute-start.1 = (bf16[1024,128]{1,0:T(8,128)(2,1)S(1)}, bf16[1024,128]{1,0:T(8,128)(2,1)}, u32[]{:S(2)}, u32[]{:S(2)}) collective-permute-start(bf16[1024,128]{1,0:T(8,128)(2,1)S(1)} %get-tuple-element.587), channel_id=1, source_target_pairs={{0,8},{4,12},{8,0},{12,4},{16,24},{20,28},{24,16},{28,20},{32,40},... | collective-permute-start | bytes 786440 | tf_op jit(solution)/shard_map/ppermute | solution.py:912
  19.3 2.7 %collective-permute-start.2 = (bf16[1024,128]{1,0:T(8,128)(2,1)S(1)}, bf16[1024,128]{1,0:T(8,128)(2,1)}, u32[]{:S(2)}, u32[]{:S(2)}) collective-permute-start(bf16[1024,128]{1,0:T(8,128)(2,1)S(1)} %get-tuple-element.587), channel_id=1, source_target_pairs={{0,16},{4,20},{8,24},{12,28},{16,0},{20,4},{24,8},{28,12},{32,48},... | collective-permute-start | bytes 786440 | tf_op jit(solution)/shard_map/ppermute | solution.py:912
  22.0 0.0 collective-permute-start
  22.0 1.5 collective-permute-start.3
  23.5 2.7 %prepare.1 = (bf16[8,128,256]{2,1,0:T(8,128)(2,1)}, bf16[8,256,128]{2,1,0:T(8,128)(2,1)}, bf16[8,128,256]{2,1,0:T(8,128)(2,1)}, bf16[8,256,128]{2,1,0:T(8,128)(2,1)}) custom-call(bf16[1024,128]{1,0:T(8,128)(2,1)} %get-tuple-element.280.q_ref, bf16[1024,128]{1,0:T(8,128)(2,1)} %cot_ref.5), custom_call_target="tpu_custom_call" | custom-call | flops 2000000000 | bytes 4000000 | tf_op jit(solution)/shard_map/prepare/pallas_call | solution.py:641
  26.2 0.3 collective-permute-start.4
  26.4 0.7 reshape.389.mask_ref
  27.1 4.7 %plan.1 = (s32[456]{0:T(512)}, s32[64]{0:T(128)}, s32[64]{0:T(128)}, s32[1]{0:T(128)}, s32[42]{0:T(128)}) custom-call(s32[320]{0:T(512)} %reshape.389.mask_ref, s32[32]{0:T(128)} %bitcast.102), custom_call_target="tpu_custom_call" | custom-call | bytes 4000000 | tf_op jit(solution)/shard_map/plan/pallas_call | solution.py:641
  31.7 4.1 %all-to-all-done.3.hk_ref = bf16[32,144,128]{2,1,0:T(8,128)(2,1)S(1)} async-done(((bf16[32,144,128]{2,1,0:T(8,128)(2,1)}), bf16[32,144,128]{2,1,0:T(8,128)(2,1)S(1)}, u32[]{:S(2)}, u32[]{:S(2)}) %all-to-all-start.3) | async-done | bytes 1179680 | tf_op jit(solution)/shard_map/all_to_all | solution.py:925
  35.9 4.3 %all-to-all-start.4 = ((bf16[32,144,128]{2,1,0:T(8,128)(2,1)}), bf16[32,144,128]{2,1,0:T(8,128)(2,1)S(1)}, u32[]{:S(2)}, u32[]{:S(2)}) async-start(bf16[32,144,128]{2,1,0:T(8,128)(2,1)} %get-tuple-element.294), calls=%async_computation.4 | async-start | bytes 2359296 | tf_op jit(solution)/shard_map/all_to_all | solution.py:931
  40.2 0.0 copy-done.6
  40.2 13.1 %scores.1 = (f32[8,256]{1,0:T(8,128)}, bf16[42,128,128]{2,1,0:T(8,128)(2,1)}, bf16[42,128,128]{2,1,0:T(8,128)(2,1)}) custom-call(s32[456]{0:T(512)} %get-tuple-element.274.list_ref, s32[64]{0:T(128)} %get-tuple-element.275.where_ref, s32[64]{0:T(128)} %get-tuple-element.276.block_ref, s32[1]{0:T(128)} %get-tuple-element.277.count_ref, ...), custom_call_target="tpu_custom_call" | custom-call | flops 12000000000 | bytes 4000000 | tf_op jit(solution)/shard_map/scores/pallas_call | solution.py:641
  53.3 0.0 collective-permute-done.1.t1_ref
  53.3 3.4 %collective-permute-start.5 = (bf16[1024,128]{1,0:T(8,128)(2,1)S(1)}, bf16[1024,128]{1,0:T(8,128)(2,1)S(1)}, u32[]{:S(2)}, u32[]{:S(2)}) collective-permute-start(bf16[1024,128]{1,0:T(8,128)(2,1)S(1)} %get-tuple-element.584), channel_id=1, source_target_pairs={{0,16},{4,20},{8,24},{12,28},{16,0},{20,4},{24,8},{28,12},{32,48},... | collective-permute-start | bytes 786440 | tf_op jit(solution)/shard_map/ppermute | solution.py:912
  56.7 0.0 collective-permute-done.2.t2_ref
  56.7 0.0 collective-permute-done.t0_ref
  56.7 0.0 collective-permute-done.3.t3_ref
  56.7 0.0 copy-start.9
  56.7 5.9 %partners.1 = (bf16[32,128,128]{2,1,0:T(8,128)(2,1)}, f32[4,8,256]{2,1,0:T(8,128)}) custom-call(s32[4,1024]{1,0:T(4,128)} %exp_ref.5, bf16[1024,256]{1,0:T(8,128)(2,1)} %collective-permute-done.t0_ref, bf16[1024,128]{1,0:T(8,128)(2,1)} %collective-permute-done.1.t1_ref, bf16[1024,128]{1,0:T(8,128)(2,1)} %collective-permute-done.2.t2_ref, ...), custom_call_target="tpu_custom_call" | custom-call | flops 5000000000 | bytes 4000000 | tf_op jit(solution)/shard_map/partners/pallas_call | solution.py:641
  62.6 0.1 collective-permute-start.6
  62.7 0.6 collective-permute-start.7
  63.3 1.9 %collective-permute-start.8 = (bf16[1056,256]{1,0:T(8,128)(2,1)S(1)}, bf16[1056,256]{1,0:T(8,128)(2,1)}, u32[]{:S(2)}, u32[]{:S(2)}) collective-permute-start(bf16[1056,256]{1,0:T(8,128)(2,1)S(1)} %copy-done.9), channel_id=1, source_target_pairs={{0,16},{4,20},{8,24},{12,28},{16,0},{20,4},{24,8},{28,12},{32,48},... | collective-permute-start | bytes 1622024 | tf_op jit(solution)/shard_map/ppermute | solution.py:912
  65.2 0.0 all-to-all-done.4.hv_ref
  65.2 1.0 copy-done.5
  66.2 17.6 %values.1 = (f32[8,128,128]{2,1,0:T(8,128)}, bf16[32,176,128]{2,1,0:T(8,128)(2,1)}, bf16[128,128]{1,0:T(8,128)(2,1)S(1)}, f32[8,128,256]{2,1,0:T(8,128)}, f32[8,256]{1,0:T(8,128)}, /*index=5*/f32[8,256]{1,0:T(8,128)}) custom-call(s32[456]{0:T(512)} %get-tuple-element.274.list_ref, s32[64]{0:T(128)} %get-tuple-element.275.where_ref, ...), custom_call_target="tpu_custom_call" | custom-call | flops 20000000000 | bytes 4000000 | tf_op jit(solution)/shard_map/values/pallas_call | solution.py:641
  83.8 0.0 collective-permute-done.4.t1_ref
  83.8 1.4 collective-permute-start.9
  85.1 0.0 collective-permute-done.5.t2_ref
  85.2 0.7 copy-done.12
  85.9 6.3 %finish.1 = (bf16[32,128,128]{2,1,0:T(8,128)(2,1)}, bf16[4,32,128]{2,1,0:T(8,128)(2,1)}, f32[8,256]{1,0:T(8,128)}, bf16[32,176,128]{2,1,0:T(8,128)(2,1)}) custom-call(s32[1]{0:T(128)} %bitcast.13.me_ref, s32[4,1024]{1,0:T(4,128)} %exp_ref.5, bf16[1024,256]{1,0:T(8,128)(2,1)} %collective-permute-done.t0_ref, ...), custom_call_target="tpu_custom_call", output_to_operand_aliasing={{3}: (10, {})} | custom-call | flops 5000000000 | bytes 4000000 | tf_op jit(solution)/shard_map/finish/pallas_call | solution.py:641
  92.2 7.0 %all-to-all-start.5 = ((bf16[32,176,128]{2,1,0:T(8,128)(2,1)}), bf16[32,176,128]{2,1,0:T(8,128)(2,1)S(1)}, u32[]{:S(2)}, u32[]{:S(2)}) async-start(bf16[32,176,128]{2,1,0:T(8,128)(2,1)} %get-tuple-element.320), calls=%async_computation.5 | async-start | bytes 2883584 | tf_op jit(solution)/shard_map/all_to_all | solution.py:945
  99.2 24.6 %keys.1 = (f32[8,128,256]{2,1,0:T(8,128)}, f32[8,128,128]{2,1,0:T(8,128)}, bf16[32,144,128]{2,1,0:T(8,128)(2,1)}, bf16[128,128]{1,0:T(8,128)(2,1)S(1)}) custom-call(s32[456]{0:T(512)} %get-tuple-element.274.list_ref, s32[64]{0:T(128)} %get-tuple-element.275.where_ref, s32[64]{0:T(128)} %get-tuple-element.276.block_ref, s32[1]{0:T(128)} %get-tuple-element.277.count_ref, ...), custom_call_target="tpu_custom_call" | custom-call | flops 24999999488 | bytes 4000000 | tf_op jit(solution)/shard_map/keys/pallas_call | solution.py:641
  123.7 0.0 collective-permute-done.6.o0_ref
  123.7 0.0 collective-permute-done.7.o1_ref
  123.8 0.0 collective-permute-done.8.o2_ref
  123.8 0.0 collective-permute-done.9.o3_ref
  123.8 0.0 copy-start.10
  123.8 0.0 all-to-all-done.5.ret_ref
  123.8 0.7 copy-done.10
  124.6 0.5 copy-done.4
  125.0 0.6 while.27
  125.7 10.5 %all-to-all-start.6 = ((bf16[32,144,128]{2,1,0:T(8,128)(2,1)}), bf16[32,144,128]{2,1,0:T(8,128)(2,1)S(1)}, u32[]{:S(2)}, u32[]{:S(2)}) async-start(bf16[32,144,128]{2,1,0:T(8,128)(2,1)} %get-tuple-element.338), calls=%async_computation.6 | async-start | bytes 2359296 | tf_op jit(solution)/shard_map/all_to_all | solution.py:952
  136.2 0.0 copy-start
  136.2 0.0 copy-start.1
  136.2 14.7 %value_back.1 = (f32[1024,128]{1,0:T(8,128)}, f32[4,1024,128]{2,1,0:T(8,128)}) custom-call(s32[1]{0:T(128)} %bitcast.13.me_ref, s32[1]{0:T(128)} %bitcast.17.feat_ref, f32[1024,128]{1,0:T(8,128)} %bitcast.103, bf16[32,176,128]{2,1,0:T(8,128)(2,1)} %copy-done.4, f32[1024,128]{1,0:T(8,128)} %bitcast.104, s32[32,128]{1,0:T(8,128)} %bitcast.93, ...), custom_call_target="tpu_custom_call" | custom-call | flops 12000000000 | bytes 4000000 | tf_op jit(solution)/shard_map/value_back/pallas_call | solution.py:641
  150.9 3.5 %all-to-all-done.6.ret_ref = bf16[32,144,128]{2,1,0:T(8,128)(2,1)S(1)} async-done(((bf16[32,144,128]{2,1,0:T(8,128)(2,1)}), bf16[32,144,128]{2,1,0:T(8,128)(2,1)S(1)}, u32[]{:S(2)}, u32[]{:S(2)}) %all-to-all-start.6) | async-done | bytes 1179680 | tf_op jit(solution)/shard_map/all_to_all | solution.py:952
  154.3 0.0 copy-done
  154.3 1.6 copy-done.2
  155.9 1.0 copy-done.3
  157.0 4.1 %key_back.1 = (f32[1024,128]{1,0:T(8,128)S(1)}, bf16[1024,128]{1,0:T(8,128)(2,1)S(1)}, bf16[1024,128]{1,0:T(8,128)(2,1)S(1)}, bf16[1024,128]{1,0:T(8,128)(2,1)S(1)}) custom-call(s32[1]{0:T(128)} %bitcast.13.me_ref, s32[1]{0:T(128)} %bitcast.17.feat_ref, f32[1024,128]{1,0:T(8,128)S(1)} %copy-done.3, bf16[32,144,128]{2,1,0:T(8,128)(2,1)S(1)} %all-to-all-done.6.ret_ref, ...), custom_call_target="tpu_custom_call" | custom-call | flops 8000000000 | bytes 4000000 | tf_op jit(solution)/shard_map/key_back/pallas_call | solution.py:641
  161.1 3.1 %collective-permute-start.12 = (bf16[1024,128]{1,0:T(8,128)(2,1)S(1)}, bf16[1024,128]{1,0:T(8,128)(2,1)S(1)}, u32[]{:S(2)}, u32[]{:S(2)}) collective-permute-start(bf16[1024,128]{1,0:T(8,128)(2,1)S(1)} %get-tuple-element.347), channel_id=1, source_target_pairs={{0,3},{1,0},{2,1},{3,2},{4,7},{5,4},{6,5},{7,6},{8,11},{9,8},{10,9... | collective-permute-start | bytes 786440 | tf_op jit(solution)/shard_map/ppermute | solution.py:960
  164.2 0.0 collective-permute-start.11
  164.2 2.2 %collective-permute-start.10 = (bf16[1024,128]{1,0:T(8,128)(2,1)S(1)}, bf16[1024,128]{1,0:T(8,128)(2,1)S(1)}, u32[]{:S(2)}, u32[]{:S(2)}) collective-permute-start(bf16[1024,128]{1,0:T(8,128)(2,1)S(1)} %get-tuple-element.345), channel_id=1, source_target_pairs={{0,2},{1,3},{2,0},{3,1},{4,6},{5,7},{6,4},{7,5},{8,10},{9,11},{10,... | collective-permute-start | bytes 786440 | tf_op jit(solution)/shard_map/ppermute | solution.py:960
  166.4 2.8 %attend.1 = bf16[1024,128]{1,0:T(8,128)(2,1)} custom-call(f32[8,128,256]{2,1,0:T(8,128)} %get-tuple-element.342.out_t_ref, bf16[4,32,128]{2,1,0:T(8,128)(2,1)} %get-tuple-element.329.back_ref, bf16[32,128,128]{2,1,0:T(8,128)(2,1)} %get-tuple-element.343.pair_ref), custom_call_target="tpu_custom_call" | custom-call | flops 2000000000 | bytes 4000000 | tf_op jit(solution)/shard_map/attend/pallas_call | solution.py:641
  169.2 6.6 %collective-permute-done.12 = bf16[1024,128]{1,0:T(8,128)(2,1)S(1)} collective-permute-done((bf16[1024,128]{1,0:T(8,128)(2,1)S(1)}, bf16[1024,128]{1,0:T(8,128)(2,1)S(1)}, u32[]{:S(2)}, u32[]{:S(2)}) %collective-permute-start.12) | collective-permute-done | bytes 262176 | tf_op jit(solution)/shard_map/ppermute | solution.py:960
  175.8 3.4 %collective-permute-done.11 = bf16[1024,128]{1,0:T(8,128)(2,1)S(1)} collective-permute-done((bf16[1024,128]{1,0:T(8,128)(2,1)S(1)}, bf16[1024,128]{1,0:T(8,128)(2,1)S(1)}, u32[]{:S(2)}, u32[]{:S(2)}) %collective-permute-start.11) | collective-permute-done | bytes 262176 | tf_op jit(solution)/shard_map/ppermute | solution.py:960
  179.2 0.0 collective-permute-done.10
  179.2 0.8 add_convert_fusion
  (14 shorter events, 0.0 us)
Async XLA Ops:
  0.6 7.7 %copy-start.7 = (s32[128]{0:T(128)S(1)}, s32[128]{0:T(128)}, u32[]{:S(2)}) copy-start(s32[128]{0:T(128)} %param.23) | copy-start | bytes 1540
  9.0 12.9 %copy-start.11 = (bf16[1024,256]{1,0:T(8,128)(2,1)S(1)}, bf16[1024,256]{1,0:T(8,128)(2,1)}, u32[]{:S(2)}) copy-start(bf16[1024,256]{1,0:T(8,128)(2,1)} %get-tuple-element.298) | copy-start | bytes 1572868
  9.0 26.8 %all-to-all-start.3 = ((bf16[32,144,128]{2,1,0:T(8,128)(2,1)}), bf16[32,144,128]{2,1,0:T(8,128)(2,1)S(1)}, u32[]{:S(2)}, u32[]{:S(2)}) async-start(bf16[32,144,128]{2,1,0:T(8,128)(2,1)} %get-tuple-element.291), calls=%async_computation.3 | async-start | bytes 2359296 | tf_op jit(solution)/shard_map/all_to_all | solution.py:925
  17.4 35.9 %collective-permute-start.1 = (bf16[1024,128]{1,0:T(8,128)(2,1)S(1)}, bf16[1024,128]{1,0:T(8,128)(2,1)}, u32[]{:S(2)}, u32[]{:S(2)}) collective-permute-start(bf16[1024,128]{1,0:T(8,128)(2,1)S(1)} %get-tuple-element.587), channel_id=1, source_target_pairs={{0,8},{4,12},{8,0},{12,4},{16,24},{20,28},{24,16},{28,20},{32,40},... | collective-permute-start | bytes 786440 | tf_op jit(solution)/shard_map/ppermute | solution.py:912
  19.3 37.4 %collective-permute-start.2 = (bf16[1024,128]{1,0:T(8,128)(2,1)S(1)}, bf16[1024,128]{1,0:T(8,128)(2,1)}, u32[]{:S(2)}, u32[]{:S(2)}) collective-permute-start(bf16[1024,128]{1,0:T(8,128)(2,1)S(1)} %get-tuple-element.587), channel_id=1, source_target_pairs={{0,16},{4,20},{8,24},{12,28},{16,0},{20,4},{24,8},{28,12},{32,48},... | collective-permute-start | bytes 786440 | tf_op jit(solution)/shard_map/ppermute | solution.py:912
  22.0 34.7 %collective-permute-start = (bf16[1024,256]{1,0:T(8,128)(2,1)S(1)}, bf16[1024,256]{1,0:T(8,128)(2,1)}, u32[]{:S(2)}, u32[]{:S(2)}) collective-permute-start(bf16[1024,256]{1,0:T(8,128)(2,1)S(1)} %copy-done.11), channel_id=1, source_target_pairs={{0,4},{4,0},{8,12},{12,8},{16,20},{20,16},{24,28},{28,24},{32,36},... | collective-permute-start | bytes 1572872 | tf_op jit(solution)/shard_map/ppermute | solution.py:912
  22.0 34.7 %collective-permute-start.3 = (bf16[1024,256]{1,0:T(8,128)(2,1)S(1)}, bf16[1024,256]{1,0:T(8,128)(2,1)}, u32[]{:S(2)}, u32[]{:S(2)}) collective-permute-start(bf16[1024,256]{1,0:T(8,128)(2,1)S(1)} %copy-done.11), channel_id=1, source_target_pairs={{0,32},{4,36},{8,40},{12,44},{16,48},{20,52},{24,56},{28,60},{32,0... | collective-permute-start | bytes 1572872 | tf_op jit(solution)/shard_map/ppermute | solution.py:912
  23.4 3.0 %copy-start.8 = (s32[8,40]{1,0:T(8,128)S(1)}, s32[8,40]{1,0:T(8,128)}, u32[]{:S(2)}) copy-start(s32[8,40]{1,0:T(8,128)} %param.21) | copy-start | bytes 3844
  26.2 57.6 %collective-permute-start.4 = (bf16[1024,128]{1,0:T(8,128)(2,1)S(1)}, bf16[1024,128]{1,0:T(8,128)(2,1)}, u32[]{:S(2)}, u32[]{:S(2)}) collective-permute-start(bf16[1024,128]{1,0:T(8,128)(2,1)S(1)} %get-tuple-element.584), channel_id=1, source_target_pairs={{0,8},{4,12},{8,0},{12,4},{16,24},{20,28},{24,16},{28,20},{32,40},... | collective-permute-start | bytes 786440 | tf_op jit(solution)/shard_map/ppermute | solution.py:912
  35.8 4.3 %copy-start.6 = (bf16[32,144,128]{2,1,0:T(8,128)(2,1)}, bf16[32,144,128]{2,1,0:T(8,128)(2,1)S(1)}, u32[]{:S(2)}) copy-start(bf16[32,144,128]{2,1,0:T(8,128)(2,1)S(1)} %all-to-all-done.3.hk_ref) | copy-start | bytes 3538948
  35.9 29.3 %all-to-all-start.4 = ((bf16[32,144,128]{2,1,0:T(8,128)(2,1)}), bf16[32,144,128]{2,1,0:T(8,128)(2,1)S(1)}, u32[]{:S(2)}, u32[]{:S(2)}) async-start(bf16[32,144,128]{2,1,0:T(8,128)(2,1)} %get-tuple-element.294), calls=%async_computation.4 | async-start | bytes 2359296 | tf_op jit(solution)/shard_map/all_to_all | solution.py:931
  53.3 31.9 %collective-permute-start.5 = (bf16[1024,128]{1,0:T(8,128)(2,1)S(1)}, bf16[1024,128]{1,0:T(8,128)(2,1)S(1)}, u32[]{:S(2)}, u32[]{:S(2)}) collective-permute-start(bf16[1024,128]{1,0:T(8,128)(2,1)S(1)} %get-tuple-element.584), channel_id=1, source_target_pairs={{0,16},{4,20},{8,24},{12,28},{16,0},{20,4},{24,8},{28,12},{32,48},... | collective-permute-start | bytes 786440 | tf_op jit(solution)/shard_map/ppermute | solution.py:912
  56.7 5.9 %copy-start.9 = (bf16[1056,256]{1,0:T(8,128)(2,1)S(1)}, bf16[1056,256]{1,0:T(8,128)(2,1)}, u32[]{:S(2)}) copy-start(bf16[1056,256]{1,0:T(8,128)(2,1)} %get-tuple-element.321) | copy-start | bytes 1622020
  62.6 61.2 %collective-permute-start.6 = (bf16[1056,256]{1,0:T(8,128)(2,1)S(1)}, bf16[1056,256]{1,0:T(8,128)(2,1)}, u32[]{:S(2)}, u32[]{:S(2)}) collective-permute-start(bf16[1056,256]{1,0:T(8,128)(2,1)S(1)} %copy-done.9), channel_id=1, source_target_pairs={{0,4},{4,0},{8,12},{12,8},{16,20},{20,16},{24,28},{28,24},{32,36},... | collective-permute-start | bytes 1622024 | tf_op jit(solution)/shard_map/ppermute | solution.py:912
  62.7 61.1 %collective-permute-start.7 = (bf16[1056,256]{1,0:T(8,128)(2,1)S(1)}, bf16[1056,256]{1,0:T(8,128)(2,1)}, u32[]{:S(2)}, u32[]{:S(2)}) collective-permute-start(bf16[1056,256]{1,0:T(8,128)(2,1)S(1)} %copy-done.9), channel_id=1, source_target_pairs={{0,8},{4,12},{8,0},{12,4},{16,24},{20,28},{24,16},{28,20},{32,40},... | collective-permute-start | bytes 1622024 | tf_op jit(solution)/shard_map/ppermute | solution.py:912
  63.3 60.5 %collective-permute-start.8 = (bf16[1056,256]{1,0:T(8,128)(2,1)S(1)}, bf16[1056,256]{1,0:T(8,128)(2,1)}, u32[]{:S(2)}, u32[]{:S(2)}) collective-permute-start(bf16[1056,256]{1,0:T(8,128)(2,1)S(1)} %copy-done.9), channel_id=1, source_target_pairs={{0,16},{4,20},{8,24},{12,28},{16,0},{20,4},{24,8},{28,12},{32,48},... | collective-permute-start | bytes 1622024 | tf_op jit(solution)/shard_map/ppermute | solution.py:912
  65.2 1.0 copy-start.5
  83.8 40.0 %collective-permute-start.9 = (bf16[1056,256]{1,0:T(8,128)(2,1)S(1)}, bf16[1056,256]{1,0:T(8,128)(2,1)S(1)}, u32[]{:S(2)}, u32[]{:S(2)}) collective-permute-start(bf16[1056,256]{1,0:T(8,128)(2,1)S(1)} %copy-done.9), channel_id=1, source_target_pairs={{0,32},{4,36},{8,40},{12,44},{16,48},{20,52},{24,56},{28,60},{32,0... | collective-permute-start | bytes 1622024 | tf_op jit(solution)/shard_map/ppermute | solution.py:912
  85.2 0.7 copy-start.12
  92.2 31.6 %all-to-all-start.5 = ((bf16[32,176,128]{2,1,0:T(8,128)(2,1)}), bf16[32,176,128]{2,1,0:T(8,128)(2,1)S(1)}, u32[]{:S(2)}, u32[]{:S(2)}) async-start(bf16[32,176,128]{2,1,0:T(8,128)(2,1)} %get-tuple-element.320), calls=%async_computation.5 | async-start | bytes 2883584 | tf_op jit(solution)/shard_map/all_to_all | solution.py:945
  123.8 0.8 copy-start.10
  123.8 1.2 copy-start.4
  125.7 28.6 %all-to-all-start.6 = ((bf16[32,144,128]{2,1,0:T(8,128)(2,1)}), bf16[32,144,128]{2,1,0:T(8,128)(2,1)S(1)}, u32[]{:S(2)}, u32[]{:S(2)}) async-start(bf16[32,144,128]{2,1,0:T(8,128)(2,1)} %get-tuple-element.338), calls=%async_computation.6 | async-start | bytes 2359296 | tf_op jit(solution)/shard_map/all_to_all | solution.py:952
  136.2 18.2 %copy-start = (bf16[512,128]{1,0:T(8,128)(2,1)S(1)}, bf16[512,128]{1,0:T(8,128)(2,1)}, u32[]{:S(2)}) copy-start(bf16[512,128]{1,0:T(8,128)(2,1)} %wk_ref.3) | copy-start | bytes 393220
  136.2 18.1 %copy-start.1 = (s32[1,32,128]{2,1,0:T(8,128)S(1)}, s32[1,32,128]{2,1,0:T(8,128)}, u32[]{:S(2)}) copy-start(s32[1,32,128]{2,1,0:T(8,128)} %param.19) | copy-start | bytes 49156
  154.3 1.6 copy-start.2
  155.9 1.0 copy-start.3
  161.1 14.7 %collective-permute-start.12 = (bf16[1024,128]{1,0:T(8,128)(2,1)S(1)}, bf16[1024,128]{1,0:T(8,128)(2,1)S(1)}, u32[]{:S(2)}, u32[]{:S(2)}) collective-permute-start(bf16[1024,128]{1,0:T(8,128)(2,1)S(1)} %get-tuple-element.347), channel_id=1, source_target_pairs={{0,3},{1,0},{2,1},{3,2},{4,7},{5,4},{6,5},{7,6},{8,11},{9,8},{10,9... | collective-permute-start | bytes 786440 | tf_op jit(solution)/shard_map/ppermute | solution.py:960
  164.2 15.0 %collective-permute-start.11 = (bf16[1024,128]{1,0:T(8,128)(2,1)S(1)}, bf16[1024,128]{1,0:T(8,128)(2,1)S(1)}, u32[]{:S(2)}, u32[]{:S(2)}) collective-permute-start(bf16[1024,128]{1,0:T(8,128)(2,1)S(1)} %get-tuple-element.346), channel_id=1, source_target_pairs={{0,1},{1,2},{2,3},{3,0},{4,5},{5,6},{6,7},{7,4},{8,9},{9,10},{10,1... | collective-permute-start | bytes 786440 | tf_op jit(solution)/shard_map/ppermute | solution.py:960
  164.2 15.0 %collective-permute-start.10 = (bf16[1024,128]{1,0:T(8,128)(2,1)S(1)}, bf16[1024,128]{1,0:T(8,128)(2,1)S(1)}, u32[]{:S(2)}, u32[]{:S(2)}) collective-permute-start(bf16[1024,128]{1,0:T(8,128)(2,1)S(1)} %get-tuple-element.345), channel_id=1, source_target_pairs={{0,2},{1,3},{2,0},{3,1},{4,6},{5,7},{6,4},{7,5},{8,10},{9,11},{10,... | collective-permute-start | bytes 786440 | tf_op jit(solution)/shard_map/ppermute | solution.py:960

commit v11 on v10

--- a/solution.py
+++ b/solution.py
@@ -124,8 +124,8 @@
 
 
 def project_kernel(
-    me_ref, x_ref, wq_ref, wk_ref, wv_ref, cot_ref, rows_ref, exp_ref, gid_ref, q_ref, k_ref, v_ref, kv_ref, outk_ref, outv_ref,
-    away_ref, rounds_ref, msgk_s, msgv_s, sems,
+    me_ref, x_ref, wq_ref, wk_ref, wv_ref, cot_ref, rows_ref, exp_ref, gid_ref, q_out, k_out, v_out, kv_out, outk_ref, outv_ref,
+    away_out, rounds_ref, msgk_s, msgv_s, sems, q_ref, k_ref, v_ref, kv_ref, away_ref, out_sems,
 ):
     most = jnp.max(owner_ranks(gid_ref[...])[0].astype(F32)).astype(jnp.int32)
     rounds_ref[0] = (most + EXTRA) // EXTRA
@@ -144,6 +144,9 @@
         low, high = split_index(jnp.concatenate([exp_row(exp_ref, m, i) for i in range(Q_BLOCKS)], axis=0))
         away_ref[NODES_HERE + m * Q_BLOCKS : NODES_HERE + (m + 1) * Q_BLOCKS, :COLS] = low
         away_ref[NODES_HERE + m * Q_BLOCKS : NODES_HERE + (m + 1) * Q_BLOCKS, COLS:] = high
+    copies = start_copies(
+        [(k_ref, k_out), (kv_ref, kv_out), (v_ref, v_out), (q_ref, q_out), (away_ref, away_out)], out_sems
+    )
     mine = jnp.broadcast_to(mine_columns(gid_ref[...], me_ref[0]), (EXTRA, BLOCK))
     lanes = iota((EXTRA, NODES_HERE), 1)
     hot = (jnp.concatenate([mine] * (NODES_HERE // BLOCK), axis=1) == lanes).astype(F32).astype(BF16)
@@ -172,6 +175,7 @@
     for t in range(SENDERS // GROUP):
         for send in sends(t):
             send.wait()
+    wait_all(copies)
 
 
 def gather_partner(exp_ref, m, table, first_col=0):
@@ -597,7 +601,7 @@
 
 def value_back_kernel(
     me_ref, feat_ref, ownv_ref, ret_ref, ownk_ref, rows_ref, o0_ref, o1_ref, o2_ref, o3_ref, gid_ref, wq_ref, wv_ref,
-    out_t_ref, back_ref, pair_ref, more_ref, acck_ref, pre_ref, accv_s, gq_ref,
+    out_t_ref, back_ref, pair_ref, more_ref, pre_ref, accv_s, gq_ref,
 ):
     others = (o0_ref, o1_ref, o2_ref, o3_ref)
     parts = [ret_ref[me_ref[0] ^ (1 << m), SLOTS:] for m in range(EXPANDERS)]
@@ -607,6 +611,7 @@
     accv_s[...] = ownv_ref[...]
     add_halo(accv_s, me_ref, ret_ref, rows_ref, gid_ref, more_ref)
     add_partners(accv_s, [part[16:] for part in parts], others, COLS)
+    acck_ref = pre_ref.at[4]
     acck_ref[...] = ownk_ref[...]
     add_partners(acck_ref, [part[:16] for part in parts], others, 0)
     grad_value = accv_s[...].astype(BF16)
@@ -616,18 +621,14 @@
 
 
 def key_back_kernel(
-    me_ref, feat_ref, acck_ref, ret_ref, rows_ref, gid_ref, wk_ref, pre_ref, more_ref, t0_ref, t1_ref, t2_ref, t3_ref,
-    acc_s, own_s, pre_s, sems,
+    me_ref, feat_ref, ret_ref, rows_ref, gid_ref, wk_ref, pre_ref, more_ref, t0_ref, t1_ref, t2_ref, t3_ref,
+    acc_s, pre_s, sems,
 ):
-    own_copy = pltpu.make_async_copy(acck_ref, own_s, sems.at[0])
-    pre_copy = pltpu.make_async_copy(pre_ref, pre_s, sems.at[1])
-    own_copy.start()
-    pre_copy.start()
+    copies = start_copies([(pre_ref, pre_s)], sems)
     acc_s[...] = jnp.zeros((NODES_HERE, COLS), F32)
     add_halo(acc_s, me_ref, ret_ref, rows_ref, gid_ref, more_ref)
-    own_copy.wait()
-    grad_key = (acc_s[...] + own_s[...]).astype(BF16)
-    pre_copy.wait()
+    wait_all(copies)
+    grad_key = (acc_s[...] + pre_s[4]).astype(BF16)
     for k, out in ((1, t1_ref), (2, t2_ref), (3, t3_ref), (0, t0_ref)):
         out[...] = (pre_s[k] + dot_nt(grad_key, wk_ref[feature_part(feat_ref, k), :])).astype(out.dtype)
 
@@ -673,11 +674,17 @@
         name="project",
         mib=56,
         flops=3_000_000_000,
-        out_spaces=(vmem(), vmem(), vmem(), vmem(), anywhere(), anywhere(), vmem(), smem()),
+        out_spaces=(*(anywhere() for _ in range(7)), smem()),
         scratch=[
             pltpu.VMEM((SENDERS, SLOTS, COLS), BF16),
             pltpu.VMEM((SENDERS, SLOTS, COLS), BF16),
             pltpu.SemaphoreType.DMA((2, SENDERS // GROUP)),
+            pltpu.VMEM((NODES_HERE, COLS), BF16),
+            pltpu.VMEM((NODES_HERE, COLS), BF16),
+            pltpu.VMEM((NODES_HERE, COLS), BF16),
+            pltpu.VMEM((NODES_HERE, 2 * COLS), BF16),
+            pltpu.VMEM((NODES_HERE + EXPANDERS * Q_BLOCKS, 2 * COLS), BF16),
+            pltpu.SemaphoreType.DMA((5,)),
         ],
     )
 
@@ -819,27 +826,26 @@
     return call(
         value_back_kernel,
         [smem()] * 2 + [vmem()] * 15,
-        (shape((NODES_HERE, COLS), F32), shape((4, NODES_HERE, COLS), F32)),
+        (shape((5, NODES_HERE, COLS), F32),),
         (me, feat, own_v.reshape(NODES_HERE, COLS), returned_v, own_k.reshape(NODES_HERE, COLS), rows, *others, gids, w_query, w_value, out_t, back, pairs, more),
         scratch=[pltpu.VMEM((NODES_HERE, COLS), F32), pltpu.VMEM((NODES_HERE, COLS), BF16)],
         name="value_back",
         mib=56,
         flops=12_000_000_000,
-    )
-
-
-def run_key_back(me, feat, own_k, returned_k, rows, gids, w_key, pre, more):
+    )[0]
+
+
+def run_key_back(me, feat, returned_k, rows, gids, w_key, pre, more):
     anywhere = pl.BlockSpec(memory_space=pltpu.HBM)
     return call(
         key_back_kernel,
-        [smem()] * 2 + [anywhere] + [vmem()] * 4 + [anywhere, vmem()],
+        [smem()] * 2 + [vmem()] * 4 + [anywhere, vmem()],
         (shape((NODES_HERE, COLS), F32),) + tuple(shape((NODES_HERE, COLS)) for _ in range(3)),
-        (me, feat, own_k, returned_k, rows, gids, w_key, pre, more),
+        (me, feat, returned_k, rows, gids, w_key, pre, more),
         scratch=[
             pltpu.VMEM((NODES_HERE, COLS), F32),
-            pltpu.VMEM((NODES_HERE, COLS), F32),
-            pltpu.VMEM((4, NODES_HERE, COLS), F32),
-            pltpu.SemaphoreType.DMA((2,)),
+            pltpu.VMEM((5, NODES_HERE, COLS), F32),
+            pltpu.SemaphoreType.DMA((1,)),
         ],
         name="key_back",
         mib=20,
@@ -950,10 +956,10 @@
     more_k, more_v = more_grads(rounds, global_ids, my_index, glob_k, glob_v)
     back_k, more_k, more_v = lax.optimization_barrier((back_k, more_k, more_v))
     returned_k = lax.all_to_all(back_k, "dom", 0, 0, tiled=True)
-    own_k, pre = run_value_back(
+    pre = run_value_back(
         me, feat, own_v, returned_v, own_k, rows, others, gids, w_query, w_value, query_t, back, pairs, more_v
     )
-    mine, *away = run_key_back(me, feat, own_k, returned_k, rows, gids, w_key, pre, more_k)
+    mine, *away = run_key_back(me, feat, returned_k, rows, gids, w_key, pre, more_k)
     out_t, mine = lax.optimization_barrier((out_t, mine))
     attended = run_attend(out_t, back, value_pairs)
     for k in (2, 1, 3):

time: 180 us -> 179 us (level)
  starting transfers between devices: 49.1 us -> 53.7 us
  Pallas kernels: 104 us -> 101 us
    ppermute x10, starting transfers between devices: 13.6 us -> 17.4 us  [swapped(): lax.ppermute(value, 'dom', [(i, i ^ 1 << bit) for i in range(dom_count)])]
    pallas_call x11, Pallas kernels: 104 us -> 101 us  [call(): pl.pallas_call(kernel, out_shape=outs, in_specs=ins, out_specs=out_spaces...]
    unnamed x26 -> x24, local copies, waits for them, and re-layouts: 5.62 us -> 4.72 us
  transfers between devices with their start and end apart: 17 -> 17, of which waited for: 4 -> 4; matrix products, arithmetic and copies ran while one was open for 0% -> 0% of each run, Pallas kernels for 51% -> 49%
where the time goes in v11:
time: 179 us; the launch traced here: 180 us
  Pallas kernels  101 us (56%)
  starting transfers between devices  53.7 us (30%)
  waiting for transfers between devices  17.5 us (10%)
  local copies, waits for them, and re-layouts  5.4 us (3%)
    pallas_call x11, Pallas kernels, call(): pl.pallas_call(kernel, out_shape=outs, in_specs=ins, out_specs=out_spaces...  101 us
    ppermute x10, starting transfers between devices, swapped(): lax.ppermute(value, 'dom', [(i, i ^ 1 << bit) for i in range(dom_count)])  17.4 us
    all_to_all x1, starting transfers between devices, on_device(): returned_k = lax.all_to_all(back_k, 'dom', 0, 0, tiled=True)  12.3 us
    ppermute x3, waiting for transfers between devices, on_device(): lax.ppermute(away[k - 1], 'feat', [(i, (i + k) % 4) for i in range(4)])  10 us
    all_to_all x1, starting transfers between devices, on_device(): halo_k = lax.all_to_all(out_k, 'dom', 0, 0, tiled=True)  8.4 us
    all_to_all x1, starting transfers between devices, on_device(): returned_v = lax.all_to_all(back_v, 'dom', 0, 0, tiled=True)  6.02 us
    ppermute x3, starting transfers between devices, on_device(): lax.ppermute(away[k - 1], 'feat', [(i, (i + k) % 4) for i in range(4)])  5.28 us
    unnamed x24, local copies, waits for them, and re-layouts  4.72 us
  transfers between devices with their start and end apart: 17, of which 4 were waited for; matrix products, arithmetic and copies ran while one was open for 0% of the time, Pallas kernels for 49%

profile of v11, /device:TPU:0, one launch (start us, length us, event | category | flops | bytes accessed | tf_op | source)
XLA Modules:
  0.0 180.3 jit_solution(12322449744943574707)
XLA Ops:
  0.6 0.0 copy-start.6
  0.6 7.6 %project.1 = (bf16[1024,128]{1,0:T(8,128)(2,1)}, bf16[1024,128]{1,0:T(8,128)(2,1)S(1)}, bf16[1024,128]{1,0:T(8,128)(2,1)S(1)}, bf16[1024,256]{1,0:T(8,128)(2,1)}...) custom-call(s32[1]{0:T(128)} %bitcast.13.me_ref, ...), custom_call_target="tpu_custom_call" | custom-call | flops 3000000000 | bytes 4000000 | tf_op jit(solution)/shard_map/project/pallas_call | solution.py:642
  8.2 0.0 copy-done.6
  8.2 0.6 while.26
  8.9 0.0 copy-start.10
  8.9 8.4 %all-to-all-start.3 = ((bf16[32,144,128]{2,1,0:T(8,128)(2,1)}), bf16[32,144,128]{2,1,0:T(8,128)(2,1)S(1)}, u32[]{:S(2)}, u32[]{:S(2)}) async-start(bf16[32,144,128]{2,1,0:T(8,128)(2,1)} %get-tuple-element.289), calls=%async_computation.3 | async-start | bytes 2359296 | tf_op jit(solution)/shard_map/all_to_all | solution.py:931
  17.3 1.9 %collective-permute-start.1 = (bf16[1024,128]{1,0:T(8,128)(2,1)S(1)}, bf16[1024,128]{1,0:T(8,128)(2,1)}, u32[]{:S(2)}, u32[]{:S(2)}) collective-permute-start(bf16[1024,128]{1,0:T(8,128)(2,1)S(1)} %get-tuple-element.583), channel_id=1, source_target_pairs={{0,8},{4,12},{8,0},{12,4},{16,24},{20,28},{24,16},{28,20},{32,40},... | collective-permute-start | bytes 786440 | tf_op jit(solution)/shard_map/ppermute | solution.py:918
  19.2 2.7 %collective-permute-start.2 = (bf16[1024,128]{1,0:T(8,128)(2,1)S(1)}, bf16[1024,128]{1,0:T(8,128)(2,1)}, u32[]{:S(2)}, u32[]{:S(2)}) collective-permute-start(bf16[1024,128]{1,0:T(8,128)(2,1)S(1)} %get-tuple-element.583), channel_id=1, source_target_pairs={{0,16},{4,20},{8,24},{12,28},{16,0},{20,4},{24,8},{28,12},{32,48},... | collective-permute-start | bytes 786440 | tf_op jit(solution)/shard_map/ppermute | solution.py:918
  21.8 0.0 copy-done.10
  21.8 0.0 collective-permute-start
  21.8 1.5 collective-permute-start.3
  23.3 2.7 %prepare.1 = (bf16[8,128,256]{2,1,0:T(8,128)(2,1)}, bf16[8,256,128]{2,1,0:T(8,128)(2,1)}, bf16[8,128,256]{2,1,0:T(8,128)(2,1)}, bf16[8,256,128]{2,1,0:T(8,128)(2,1)}) custom-call(bf16[1024,128]{1,0:T(8,128)(2,1)} %get-tuple-element.278.q_ref, bf16[1024,128]{1,0:T(8,128)(2,1)} %cot_ref.5), custom_call_target="tpu_custom_call" | custom-call | flops 2000000000 | bytes 4000000 | tf_op jit(solution)/shard_map/prepare/pallas_call | solution.py:642
  26.0 0.3 collective-permute-start.4
  26.3 0.0 copy-done.7
  26.3 0.7 reshape.389.mask_ref
  26.9 4.7 %plan.1 = (s32[456]{0:T(512)}, s32[64]{0:T(128)}, s32[64]{0:T(128)}, s32[1]{0:T(128)}, s32[42]{0:T(128)}) custom-call(s32[320]{0:T(512)} %reshape.389.mask_ref, s32[32]{0:T(128)} %bitcast.102), custom_call_target="tpu_custom_call" | custom-call | bytes 4000000 | tf_op jit(solution)/shard_map/plan/pallas_call | solution.py:642
  31.6 4.1 %all-to-all-done.3.hk_ref = bf16[32,144,128]{2,1,0:T(8,128)(2,1)S(1)} async-done(((bf16[32,144,128]{2,1,0:T(8,128)(2,1)}), bf16[32,144,128]{2,1,0:T(8,128)(2,1)S(1)}, u32[]{:S(2)}, u32[]{:S(2)}) %all-to-all-start.3) | async-done | bytes 1179680 | tf_op jit(solution)/shard_map/all_to_all | solution.py:931
  35.7 4.3 %all-to-all-start.4 = ((bf16[32,144,128]{2,1,0:T(8,128)(2,1)}), bf16[32,144,128]{2,1,0:T(8,128)(2,1)S(1)}, u32[]{:S(2)}, u32[]{:S(2)}) async-start(bf16[32,144,128]{2,1,0:T(8,128)(2,1)} %get-tuple-element.292), calls=%async_computation.4 | async-start | bytes 2359296 | tf_op jit(solution)/shard_map/all_to_all | solution.py:937
  40.0 0.0 copy-done.5
  40.0 12.3 %scores.1 = (f32[8,256]{1,0:T(8,128)}, bf16[42,128,128]{2,1,0:T(8,128)(2,1)}, bf16[42,128,128]{2,1,0:T(8,128)(2,1)}) custom-call(s32[456]{0:T(512)} %get-tuple-element.272.list_ref, s32[64]{0:T(128)} %get-tuple-element.273.where_ref, s32[64]{0:T(128)} %get-tuple-element.274.block_ref, s32[1]{0:T(128)} %get-tuple-element.275.count_ref, ...), custom_call_target="tpu_custom_call" | custom-call | flops 12000000000 | bytes 4000000 | tf_op jit(solution)/shard_map/scores/pallas_call | solution.py:642
  52.4 0.0 collective-permute-done.1.t1_ref
  52.4 4.9 %collective-permute-start.5 = (bf16[1024,128]{1,0:T(8,128)(2,1)S(1)}, bf16[1024,128]{1,0:T(8,128)(2,1)S(1)}, u32[]{:S(2)}, u32[]{:S(2)}) collective-permute-start(bf16[1024,128]{1,0:T(8,128)(2,1)S(1)} %get-tuple-element.580), channel_id=1, source_target_pairs={{0,16},{4,20},{8,24},{12,28},{16,0},{20,4},{24,8},{28,12},{32,48},... | collective-permute-start | bytes 786440 | tf_op jit(solution)/shard_map/ppermute | solution.py:918
  57.3 0.0 collective-permute-done.2.t2_ref
  57.3 0.0 collective-permute-done.t0_ref
  57.3 0.0 collective-permute-done.3.t3_ref
  57.3 0.0 copy-start.8
  57.3 5.9 %partners.1 = (bf16[32,128,128]{2,1,0:T(8,128)(2,1)}, f32[4,8,256]{2,1,0:T(8,128)}) custom-call(s32[4,1024]{1,0:T(4,128)} %exp_ref.5, bf16[1024,256]{1,0:T(8,128)(2,1)} %collective-permute-done.t0_ref, bf16[1024,128]{1,0:T(8,128)(2,1)} %collective-permute-done.1.t1_ref, bf16[1024,128]{1,0:T(8,128)(2,1)} %collective-permute-done.2.t2_ref, ...), custom_call_target="tpu_custom_call" | custom-call | flops 5000000000 | bytes 4000000 | tf_op jit(solution)/shard_map/partners/pallas_call | solution.py:642
  63.2 0.1 collective-permute-start.6
  63.3 0.1 collective-permute-start.7
  63.4 1.9 %collective-permute-start.8 = (bf16[1056,256]{1,0:T(8,128)(2,1)S(1)}, bf16[1056,256]{1,0:T(8,128)(2,1)}, u32[]{:S(2)}, u32[]{:S(2)}) collective-permute-start(bf16[1056,256]{1,0:T(8,128)(2,1)S(1)} %copy-done.8), channel_id=1, source_target_pairs={{0,16},{4,20},{8,24},{12,28},{16,0},{20,4},{24,8},{28,12},{32,48},... | collective-permute-start | bytes 1622024 | tf_op jit(solution)/shard_map/ppermute | solution.py:918
  65.2 0.0 all-to-all-done.4.hv_ref
  65.2 1.0 copy-done.4
  66.3 16.6 %values.1 = (f32[8,128,128]{2,1,0:T(8,128)}, bf16[32,176,128]{2,1,0:T(8,128)(2,1)}, bf16[128,128]{1,0:T(8,128)(2,1)S(1)}, f32[8,128,256]{2,1,0:T(8,128)}, f32[8,256]{1,0:T(8,128)}, /*index=5*/f32[8,256]{1,0:T(8,128)}) custom-call(s32[456]{0:T(512)} %get-tuple-element.272.list_ref, s32[64]{0:T(128)} %get-tuple-element.273.where_ref, ...), custom_call_target="tpu_custom_call" | custom-call | flops 20000000000 | bytes 4000000 | tf_op jit(solution)/shard_map/values/pallas_call | solution.py:642
  82.9 0.0 collective-permute-done.4.t1_ref
  82.9 4.2 %collective-permute-start.9 = (bf16[1056,256]{1,0:T(8,128)(2,1)S(1)}, bf16[1056,256]{1,0:T(8,128)(2,1)S(1)}, u32[]{:S(2)}, u32[]{:S(2)}) collective-permute-start(bf16[1056,256]{1,0:T(8,128)(2,1)S(1)} %copy-done.8), channel_id=1, source_target_pairs={{0,32},{4,36},{8,40},{12,44},{16,48},{20,52},{24,56},{28,60},{32,0... | collective-permute-start | bytes 1622024 | tf_op jit(solution)/shard_map/ppermute | solution.py:918
  87.1 0.0 collective-permute-done.5.t2_ref
  87.1 0.7 copy-done.11
  87.8 6.3 %finish.1 = (bf16[32,128,128]{2,1,0:T(8,128)(2,1)}, bf16[4,32,128]{2,1,0:T(8,128)(2,1)}, f32[8,256]{1,0:T(8,128)}, bf16[32,176,128]{2,1,0:T(8,128)(2,1)}) custom-call(s32[1]{0:T(128)} %bitcast.13.me_ref, s32[4,1024]{1,0:T(4,128)} %exp_ref.5, bf16[1024,256]{1,0:T(8,128)(2,1)} %collective-permute-done.t0_ref, ...), custom_call_target="tpu_custom_call", output_to_operand_aliasing={{3}: (10, {})} | custom-call | flops 5000000000 | bytes 4000000 | tf_op jit(solution)/shard_map/finish/pallas_call | solution.py:642
  94.1 6.0 %all-to-all-start.5 = ((bf16[32,176,128]{2,1,0:T(8,128)(2,1)}), bf16[32,176,128]{2,1,0:T(8,128)(2,1)S(1)}, u32[]{:S(2)}, u32[]{:S(2)}) async-start(bf16[32,176,128]{2,1,0:T(8,128)(2,1)} %get-tuple-element.318), calls=%async_computation.5 | async-start | bytes 2883584 | tf_op jit(solution)/shard_map/all_to_all | solution.py:951
  100.2 23.0 %keys.1 = (f32[8,128,256]{2,1,0:T(8,128)}, f32[8,128,128]{2,1,0:T(8,128)}, bf16[32,144,128]{2,1,0:T(8,128)(2,1)}, bf16[128,128]{1,0:T(8,128)(2,1)S(1)}) custom-call(s32[456]{0:T(512)} %get-tuple-element.272.list_ref, s32[64]{0:T(128)} %get-tuple-element.273.where_ref, s32[64]{0:T(128)} %get-tuple-element.274.block_ref, s32[1]{0:T(128)} %get-tuple-element.275.count_ref, ...), custom_call_target="tpu_custom_call" | custom-call | flops 24999999488 | bytes 4000000 | tf_op jit(solution)/shard_map/keys/pallas_call | solution.py:642
  123.1 0.0 collective-permute-done.6.o0_ref
  123.1 0.0 collective-permute-done.7.o1_ref
  123.2 0.0 collective-permute-done.8.o2_ref
  123.2 0.0 collective-permute-done.9.o3_ref
  123.2 0.0 copy-start.9
  123.2 0.0 all-to-all-done.5.ret_ref
  123.2 0.8 copy-done.9
  124.0 0.5 copy-done.3
  124.4 0.6 while.27
  125.1 12.3 %all-to-all-start.6 = ((bf16[32,144,128]{2,1,0:T(8,128)(2,1)}), bf16[32,144,128]{2,1,0:T(8,128)(2,1)S(1)}, u32[]{:S(2)}, u32[]{:S(2)}) async-start(bf16[32,144,128]{2,1,0:T(8,128)(2,1)} %get-tuple-element.324), calls=%async_computation.6 | async-start | bytes 2359296 | tf_op jit(solution)/shard_map/all_to_all | solution.py:958
  137.4 0.0 copy-start
  137.4 0.0 copy-start.1
  137.4 14.8 %value_back.1.pre_ref = f32[5,1024,128]{2,1,0:T(8,128)} custom-call(s32[1]{0:T(128)} %bitcast.13.me_ref, s32[1]{0:T(128)} %bitcast.17.feat_ref, f32[1024,128]{1,0:T(8,128)} %bitcast.103, bf16[32,176,128]{2,1,0:T(8,128)(2,1)} %copy-done.3, f32[1024,128]{1,0:T(8,128)} %bitcast.104, s32[32,128]{1,0:T(8,128)} %bitcast.93, ...), custom_call_target="tpu_custom_call" | custom-call | flops 12000000000 | bytes 4000000 | tf_op jit(solution)/shard_map/value_back/pallas_call | solution.py:642
  152.2 3.3 %all-to-all-done.6.ret_ref = bf16[32,144,128]{2,1,0:T(8,128)(2,1)S(1)} async-done(((bf16[32,144,128]{2,1,0:T(8,128)(2,1)}), bf16[32,144,128]{2,1,0:T(8,128)(2,1)S(1)}, u32[]{:S(2)}, u32[]{:S(2)}) %all-to-all-start.6) | async-done | bytes 1179680 | tf_op jit(solution)/shard_map/all_to_all | solution.py:958
  155.5 1.7 copy-done.2
  157.3 4.1 %key_back.1 = (f32[1024,128]{1,0:T(8,128)S(1)}, bf16[1024,128]{1,0:T(8,128)(2,1)S(1)}, bf16[1024,128]{1,0:T(8,128)(2,1)S(1)}, bf16[1024,128]{1,0:T(8,128)(2,1)S(1)}) custom-call(s32[1]{0:T(128)} %bitcast.13.me_ref, s32[1]{0:T(128)} %bitcast.17.feat_ref, bf16[32,144,128]{2,1,0:T(8,128)(2,1)S(1)} %all-to-all-done.6.ret_ref, s32[32,128]{1,0:T(8,128)S(1)} %bitcast.94, ...), custom_call_target="tpu_custom_call" | custom-call | flops 8000000000 | bytes 4000000 | tf_op jit(solution)/shard_map/key_back/pallas_call | solution.py:642
  161.3 3.1 %collective-permute-start.12 = (bf16[1024,128]{1,0:T(8,128)(2,1)S(1)}, bf16[1024,128]{1,0:T(8,128)(2,1)S(1)}, u32[]{:S(2)}, u32[]{:S(2)}) collective-permute-start(bf16[1024,128]{1,0:T(8,128)(2,1)S(1)} %get-tuple-element.343), channel_id=1, source_target_pairs={{0,3},{1,0},{2,1},{3,2},{4,7},{5,4},{6,5},{7,6},{8,11},{9,8},{10,9... | collective-permute-start | bytes 786440 | tf_op jit(solution)/shard_map/ppermute | solution.py:966
  164.4 0.0 collective-permute-start.11
  164.4 2.2 %collective-permute-start.10 = (bf16[1024,128]{1,0:T(8,128)(2,1)S(1)}, bf16[1024,128]{1,0:T(8,128)(2,1)S(1)}, u32[]{:S(2)}, u32[]{:S(2)}) collective-permute-start(bf16[1024,128]{1,0:T(8,128)(2,1)S(1)} %get-tuple-element.341), channel_id=1, source_target_pairs={{0,2},{1,3},{2,0},{3,1},{4,6},{5,7},{6,4},{7,5},{8,10},{9,11},{10,... | collective-permute-start | bytes 786440 | tf_op jit(solution)/shard_map/ppermute | solution.py:966
  166.6 2.8 %attend.1 = bf16[1024,128]{1,0:T(8,128)(2,1)} custom-call(f32[8,128,256]{2,1,0:T(8,128)} %get-tuple-element.338.out_t_ref, bf16[4,32,128]{2,1,0:T(8,128)(2,1)} %get-tuple-element.333.back_ref, bf16[32,128,128]{2,1,0:T(8,128)(2,1)} %get-tuple-element.339.pair_ref), custom_call_target="tpu_custom_call" | custom-call | flops 2000000000 | bytes 4000000 | tf_op jit(solution)/shard_map/attend/pallas_call | solution.py:642
  169.4 6.6 %collective-permute-done.12 = bf16[1024,128]{1,0:T(8,128)(2,1)S(1)} collective-permute-done((bf16[1024,128]{1,0:T(8,128)(2,1)S(1)}, bf16[1024,128]{1,0:T(8,128)(2,1)S(1)}, u32[]{:S(2)}, u32[]{:S(2)}) %collective-permute-start.12) | collective-permute-done | bytes 262176 | tf_op jit(solution)/shard_map/ppermute | solution.py:966
  176.0 3.4 %collective-permute-done.11 = bf16[1024,128]{1,0:T(8,128)(2,1)S(1)} collective-permute-done((bf16[1024,128]{1,0:T(8,128)(2,1)S(1)}, bf16[1024,128]{1,0:T(8,128)(2,1)S(1)}, u32[]{:S(2)}, u32[]{:S(2)}) %collective-permute-start.11) | collective-permute-done | bytes 262176 | tf_op jit(solution)/shard_map/ppermute | solution.py:966
  179.4 0.0 collective-permute-done.10
  179.4 0.8 add_convert_fusion
  (12 shorter events, 0.0 us)
Async XLA Ops:
  0.6 7.6 %copy-start.6 = (s32[128]{0:T(128)S(1)}, s32[128]{0:T(128)}, u32[]{:S(2)}) copy-start(s32[128]{0:T(128)} %param.23) | copy-start | bytes 1540
  8.9 13.0 %copy-start.10 = (bf16[1024,256]{1,0:T(8,128)(2,1)S(1)}, bf16[1024,256]{1,0:T(8,128)(2,1)}, u32[]{:S(2)}) copy-start(bf16[1024,256]{1,0:T(8,128)(2,1)} %get-tuple-element.296) | copy-start | bytes 1572868
  8.9 26.8 %all-to-all-start.3 = ((bf16[32,144,128]{2,1,0:T(8,128)(2,1)}), bf16[32,144,128]{2,1,0:T(8,128)(2,1)S(1)}, u32[]{:S(2)}, u32[]{:S(2)}) async-start(bf16[32,144,128]{2,1,0:T(8,128)(2,1)} %get-tuple-element.289), calls=%async_computation.3 | async-start | bytes 2359296 | tf_op jit(solution)/shard_map/all_to_all | solution.py:931
  17.3 35.1 %collective-permute-start.1 = (bf16[1024,128]{1,0:T(8,128)(2,1)S(1)}, bf16[1024,128]{1,0:T(8,128)(2,1)}, u32[]{:S(2)}, u32[]{:S(2)}) collective-permute-start(bf16[1024,128]{1,0:T(8,128)(2,1)S(1)} %get-tuple-element.583), channel_id=1, source_target_pairs={{0,8},{4,12},{8,0},{12,4},{16,24},{20,28},{24,16},{28,20},{32,40},... | collective-permute-start | bytes 786440 | tf_op jit(solution)/shard_map/ppermute | solution.py:918
  19.2 38.1 %collective-permute-start.2 = (bf16[1024,128]{1,0:T(8,128)(2,1)S(1)}, bf16[1024,128]{1,0:T(8,128)(2,1)}, u32[]{:S(2)}, u32[]{:S(2)}) collective-permute-start(bf16[1024,128]{1,0:T(8,128)(2,1)S(1)} %get-tuple-element.583), channel_id=1, source_target_pairs={{0,16},{4,20},{8,24},{12,28},{16,0},{20,4},{24,8},{28,12},{32,48},... | collective-permute-start | bytes 786440 | tf_op jit(solution)/shard_map/ppermute | solution.py:918
  21.8 35.4 %collective-permute-start = (bf16[1024,256]{1,0:T(8,128)(2,1)S(1)}, bf16[1024,256]{1,0:T(8,128)(2,1)}, u32[]{:S(2)}, u32[]{:S(2)}) collective-permute-start(bf16[1024,256]{1,0:T(8,128)(2,1)S(1)} %copy-done.10), channel_id=1, source_target_pairs={{0,4},{4,0},{8,12},{12,8},{16,20},{20,16},{24,28},{28,24},{32,36},... | collective-permute-start | bytes 1572872 | tf_op jit(solution)/shard_map/ppermute | solution.py:918
  21.8 35.4 %collective-permute-start.3 = (bf16[1024,256]{1,0:T(8,128)(2,1)S(1)}, bf16[1024,256]{1,0:T(8,128)(2,1)}, u32[]{:S(2)}, u32[]{:S(2)}) collective-permute-start(bf16[1024,256]{1,0:T(8,128)(2,1)S(1)} %copy-done.10), channel_id=1, source_target_pairs={{0,32},{4,36},{8,40},{12,44},{16,48},{20,52},{24,56},{28,60},{32,0... | collective-permute-start | bytes 1572872 | tf_op jit(solution)/shard_map/ppermute | solution.py:918
  23.3 2.9 %copy-start.7 = (s32[8,40]{1,0:T(8,128)S(1)}, s32[8,40]{1,0:T(8,128)}, u32[]{:S(2)}) copy-start(s32[8,40]{1,0:T(8,128)} %param.21) | copy-start | bytes 3844
  26.0 56.9 %collective-permute-start.4 = (bf16[1024,128]{1,0:T(8,128)(2,1)S(1)}, bf16[1024,128]{1,0:T(8,128)(2,1)}, u32[]{:S(2)}, u32[]{:S(2)}) collective-permute-start(bf16[1024,128]{1,0:T(8,128)(2,1)S(1)} %get-tuple-element.580), channel_id=1, source_target_pairs={{0,8},{4,12},{8,0},{12,4},{16,24},{20,28},{24,16},{28,20},{32,40},... | collective-permute-start | bytes 786440 | tf_op jit(solution)/shard_map/ppermute | solution.py:918
  35.7 4.3 %copy-start.5 = (bf16[32,144,128]{2,1,0:T(8,128)(2,1)}, bf16[32,144,128]{2,1,0:T(8,128)(2,1)S(1)}, u32[]{:S(2)}) copy-start(bf16[32,144,128]{2,1,0:T(8,128)(2,1)S(1)} %all-to-all-done.3.hk_ref) | copy-start | bytes 3538948
  35.7 29.5 %all-to-all-start.4 = ((bf16[32,144,128]{2,1,0:T(8,128)(2,1)}), bf16[32,144,128]{2,1,0:T(8,128)(2,1)S(1)}, u32[]{:S(2)}, u32[]{:S(2)}) async-start(bf16[32,144,128]{2,1,0:T(8,128)(2,1)} %get-tuple-element.292), calls=%async_computation.4 | async-start | bytes 2359296 | tf_op jit(solution)/shard_map/all_to_all | solution.py:937
  52.4 34.7 %collective-permute-start.5 = (bf16[1024,128]{1,0:T(8,128)(2,1)S(1)}, bf16[1024,128]{1,0:T(8,128)(2,1)S(1)}, u32[]{:S(2)}, u32[]{:S(2)}) collective-permute-start(bf16[1024,128]{1,0:T(8,128)(2,1)S(1)} %get-tuple-element.580), channel_id=1, source_target_pairs={{0,16},{4,20},{8,24},{12,28},{16,0},{20,4},{24,8},{28,12},{32,48},... | collective-permute-start | bytes 786440 | tf_op jit(solution)/shard_map/ppermute | solution.py:918
  57.3 5.9 %copy-start.8 = (bf16[1056,256]{1,0:T(8,128)(2,1)S(1)}, bf16[1056,256]{1,0:T(8,128)(2,1)}, u32[]{:S(2)}) copy-start(bf16[1056,256]{1,0:T(8,128)(2,1)} %get-tuple-element.319) | copy-start | bytes 1622020
  63.2 59.9 %collective-permute-start.6 = (bf16[1056,256]{1,0:T(8,128)(2,1)S(1)}, bf16[1056,256]{1,0:T(8,128)(2,1)}, u32[]{:S(2)}, u32[]{:S(2)}) collective-permute-start(bf16[1056,256]{1,0:T(8,128)(2,1)S(1)} %copy-done.8), channel_id=1, source_target_pairs={{0,4},{4,0},{8,12},{12,8},{16,20},{20,16},{24,28},{28,24},{32,36},... | collective-permute-start | bytes 1622024 | tf_op jit(solution)/shard_map/ppermute | solution.py:918
  63.3 59.9 %collective-permute-start.7 = (bf16[1056,256]{1,0:T(8,128)(2,1)S(1)}, bf16[1056,256]{1,0:T(8,128)(2,1)}, u32[]{:S(2)}, u32[]{:S(2)}) collective-permute-start(bf16[1056,256]{1,0:T(8,128)(2,1)S(1)} %copy-done.8), channel_id=1, source_target_pairs={{0,8},{4,12},{8,0},{12,4},{16,24},{20,28},{24,16},{28,20},{32,40},... | collective-permute-start | bytes 1622024 | tf_op jit(solution)/shard_map/ppermute | solution.py:918
  63.4 59.8 %collective-permute-start.8 = (bf16[1056,256]{1,0:T(8,128)(2,1)S(1)}, bf16[1056,256]{1,0:T(8,128)(2,1)}, u32[]{:S(2)}, u32[]{:S(2)}) collective-permute-start(bf16[1056,256]{1,0:T(8,128)(2,1)S(1)} %copy-done.8), channel_id=1, source_target_pairs={{0,16},{4,20},{8,24},{12,28},{16,0},{20,4},{24,8},{28,12},{32,48},... | collective-permute-start | bytes 1622024 | tf_op jit(solution)/shard_map/ppermute | solution.py:918
  65.2 1.0 copy-start.4
  82.9 40.3 %collective-permute-start.9 = (bf16[1056,256]{1,0:T(8,128)(2,1)S(1)}, bf16[1056,256]{1,0:T(8,128)(2,1)S(1)}, u32[]{:S(2)}, u32[]{:S(2)}) collective-permute-start(bf16[1056,256]{1,0:T(8,128)(2,1)S(1)} %copy-done.8), channel_id=1, source_target_pairs={{0,32},{4,36},{8,40},{12,44},{16,48},{20,52},{24,56},{28,60},{32,0... | collective-permute-start | bytes 1622024 | tf_op jit(solution)/shard_map/ppermute | solution.py:918
  87.1 0.7 copy-start.11
  94.1 29.0 %all-to-all-start.5 = ((bf16[32,176,128]{2,1,0:T(8,128)(2,1)}), bf16[32,176,128]{2,1,0:T(8,128)(2,1)S(1)}, u32[]{:S(2)}, u32[]{:S(2)}) async-start(bf16[32,176,128]{2,1,0:T(8,128)(2,1)} %get-tuple-element.318), calls=%async_computation.5 | async-start | bytes 2883584 | tf_op jit(solution)/shard_map/all_to_all | solution.py:951
  123.2 0.8 copy-start.9
  123.2 1.2 copy-start.3
  125.1 30.4 %all-to-all-start.6 = ((bf16[32,144,128]{2,1,0:T(8,128)(2,1)}), bf16[32,144,128]{2,1,0:T(8,128)(2,1)S(1)}, u32[]{:S(2)}, u32[]{:S(2)}) async-start(bf16[32,144,128]{2,1,0:T(8,128)(2,1)} %get-tuple-element.324), calls=%async_computation.6 | async-start | bytes 2359296 | tf_op jit(solution)/shard_map/all_to_all | solution.py:958
  137.4 18.2 %copy-start = (bf16[512,128]{1,0:T(8,128)(2,1)S(1)}, bf16[512,128]{1,0:T(8,128)(2,1)}, u32[]{:S(2)}) copy-start(bf16[512,128]{1,0:T(8,128)(2,1)} %wk_ref.3) | copy-start | bytes 393220
  137.4 18.1 %copy-start.1 = (s32[1,32,128]{2,1,0:T(8,128)S(1)}, s32[1,32,128]{2,1,0:T(8,128)}, u32[]{:S(2)}) copy-start(s32[1,32,128]{2,1,0:T(8,128)} %param.19) | copy-start | bytes 49156
  155.5 1.7 copy-start.2
  161.3 14.7 %collective-permute-start.12 = (bf16[1024,128]{1,0:T(8,128)(2,1)S(1)}, bf16[1024,128]{1,0:T(8,128)(2,1)S(1)}, u32[]{:S(2)}, u32[]{:S(2)}) collective-permute-start(bf16[1024,128]{1,0:T(8,128)(2,1)S(1)} %get-tuple-element.343), channel_id=1, source_target_pairs={{0,3},{1,0},{2,1},{3,2},{4,7},{5,4},{6,5},{7,6},{8,11},{9,8},{10,9... | collective-permute-start | bytes 786440 | tf_op jit(solution)/shard_map/ppermute | solution.py:966
  164.4 15.0 %collective-permute-start.11 = (bf16[1024,128]{1,0:T(8,128)(2,1)S(1)}, bf16[1024,128]{1,0:T(8,128)(2,1)S(1)}, u32[]{:S(2)}, u32[]{:S(2)}) collective-permute-start(bf16[1024,128]{1,0:T(8,128)(2,1)S(1)} %get-tuple-element.342), channel_id=1, source_target_pairs={{0,1},{1,2},{2,3},{3,0},{4,5},{5,6},{6,7},{7,4},{8,9},{9,10},{10,1... | collective-permute-start | bytes 786440 | tf_op jit(solution)/shard_map/ppermute | solution.py:966
  164.4 15.0 %collective-permute-start.10 = (bf16[1024,128]{1,0:T(8,128)(2,1)S(1)}, bf16[1024,128]{1,0:T(8,128)(2,1)S(1)}, u32[]{:S(2)}, u32[]{:S(2)}) collective-permute-start(bf16[1024,128]{1,0:T(8,128)(2,1)S(1)} %get-tuple-element.341), channel_id=1, source_target_pairs={{0,2},{1,3},{2,0},{3,1},{4,6},{5,7},{6,4},{7,5},{8,10},{9,11},{10,... | collective-permute-start | bytes 786440 | tf_op jit(solution)/shard_map/ppermute | solution.py:966
